TPU v7x, 32 devices: a whole 2x2x4 slice. The times are simulated.
32 devices in a mesh: ctx: 8 (over y, x, core), shard: 4 (over z).
Axes of the slice: x: 2, y: 2, z: 4, core: 2. Of those that a mesh axis runs over, the one named last changes fastest.
Arguments:
- hidden_in: bfloat16 [8, 1024, 768], P('shard', 'ctx'), may hold values from -6 to 6
- block_of: int32 [16], replicated, may hold values from 0 to 15, each once
- lengths: int32 [8], replicated, may hold values from 256 to 1024, as said below
- attn_latent: float32 [4, 768, 768], P(None, 'shard'), may hold values from -1.25 to 1.25
- ffn_in_latent: float32 [768, 3072], P('shard'), may hold values from -1.25 to 1.25
- ffn_out_latent: float32 [3072, 768], P('shard'), may hold values from -1.25 to 1.25
- student_vec: float32 [12, 768], replicated
- teacher_attn: bfloat16 [4, 768, 768], P(None, 'shard'), may hold values from -0.3125 to 0.3125
- teacher_ffn_in: bfloat16 [768, 3072], P('shard'), may hold values from -0.21875 to 0.21875
- teacher_ffn_out: bfloat16 [3072, 768], P('shard'), may hold values from -0.109375 to 0.109375
- teacher_vec: float32 [12, 768], replicated
Outputs:
- output: bfloat16 [8, 1024, 768], P('shard', 'ctx')
- statistics: float32 [4], replicated
- grad_hidden: float32 [8, 1024, 768], P('shard', 'ctx')
- grad_attn_latent: float32 [4, 768, 768], P(None, 'shard')
- grad_ffn_in_latent: float32 [768, 3072], P('shard')
- grad_ffn_out_latent: float32 [3072, 768], P('shard')
- grad_student_vec: float32 [11, 768], replicated
- grad_query_bias: float32 [768], replicated
Inputs may be any that keep to these rules, and one draw needn't show every extreme that they name: `block_of`: every block of 64 places of a sequence is named once; entry q holds the block that lies at layout places q * 64 to (q + 1) * 64 - 1, the same for every sequence. `lengths`: A token is valid where its place is below its sequence's length; some sequence has length 1024.
All inputs are finite; a program needn't handle non-finite values.
Results may differ from a plain program's by a relative error of at most 0.0097.
Values may be sent and summed in bfloat16 or wider, within the bound.
No kernel may reach another device: no remote copies, remote signals or barrier semaphores. Data moves between devices by JAX's collectives and lax.ppermute only.
A program may use at most 320 MiB of HBM per device.

v0:
```python
import jax
import jax.numpy as jnp
from jax import lax
from jax.sharding import PartitionSpec as P

D = 768
HEADS = 12
HEAD_DIM = 64
FF = 3072
BLK = 64


norm_eps = 1e-05
attn_gains = (2.0, 2.0, 1.0, 4.0)
heads_block = 4
masked_score = -1e30


def layer_norm(values, gain, shift):
    middle = jnp.mean(values, axis=-1, keepdims=True)
    centred = values - middle
    spread = jnp.mean(centred * centred, axis=-1, keepdims=True)
    return centred * lax.rsqrt(spread + norm_eps) * gain + shift


def gelu_exact(values):
    return jax.nn.gelu(values, approximate=False)


def matmul(left_side, right_side):
    return jnp.dot(left_side, right_side, preferred_element_type=jnp.float32)


def left_product(left_side, right_side):
    return lax.dot_general(
        left_side, right_side, (((0,), (0,)), ((), ())), preferred_element_type=jnp.float32
    )


def right_product(left_side, right_side):
    return lax.dot_general(
        left_side, right_side, (((1,), (1,)), ((), ())), preferred_element_type=jnp.float32
    )


def binarize(latent, column_sum, gain, fan_in):
    return (gain * (column_sum / fan_in) * jnp.sign(latent) * fan_in ** (-0.5)).astype(jnp.bfloat16)


def positions_of(block_of):
    return (block_of[:, None] * BLK + jnp.arange(BLK, dtype=jnp.int32)[None, :]).reshape(
        block_of.shape[0] * BLK
    )


def split_heads(row_matrix, head_group):
    begin = head_group * heads_block * HEAD_DIM
    piece = row_matrix[:, begin : begin + heads_block * HEAD_DIM]
    return piece.reshape(row_matrix.shape[0], heads_block, HEAD_DIM)


def join_heads(parts_list):
    return jnp.concatenate(
        [part_one.reshape(part_one.shape[0], heads_block * HEAD_DIM) for part_one in parts_list],
        axis=1,
    )


def attend_forward(query_rows, key_all, value_all, query_pos, key_pos):
    score_scale = HEAD_DIM ** (-0.5)
    allowed = (query_pos[:, None] >= key_pos[None, :])[None]
    head_outs = []
    log_sums = []
    for head_group in range(HEADS // heads_block):
        q_heads = split_heads(query_rows, head_group)
        k_heads = split_heads(key_all, head_group)
        v_heads = split_heads(value_all, head_group)
        scores = (
            jnp.einsum("qhd,khd->hqk", q_heads, k_heads, preferred_element_type=jnp.float32)
            * score_scale
        )
        scores = jnp.where(allowed, scores, masked_score)
        row_peak = jnp.max(scores, axis=-1, keepdims=True)
        row_total = jnp.sum(jnp.exp(scores - row_peak), axis=-1, keepdims=True)
        log_total = row_peak + jnp.log(row_total)
        prob_rows = jnp.exp(scores - log_total).astype(jnp.bfloat16)
        head_outs.append(
            jnp.einsum("hqk,khd->qhd", prob_rows, v_heads, preferred_element_type=jnp.float32)
        )
        log_sums.append(log_total[..., 0])
    return (join_heads(head_outs), jnp.concatenate(log_sums, axis=0))


def attend_query_back(query_rows, key_all, value_all, grad_rows, log_sums, query_pos, key_pos):
    score_scale = HEAD_DIM ** (-0.5)
    allowed = (query_pos[:, None] >= key_pos[None, :])[None]
    grad_q_parts = []
    delta_parts = []
    grad_k_parts = []
    grad_v_parts = []
    for head_group in range(HEADS // heads_block):
        head_span = slice(head_group * heads_block, (head_group + 1) * heads_block)
        q_heads = split_heads(query_rows, head_group)
        k_heads = split_heads(key_all, head_group)
        v_heads = split_heads(value_all, head_group)
        g_heads = split_heads(grad_rows, head_group)
        scores = (
            jnp.einsum("qhd,khd->hqk", q_heads, k_heads, preferred_element_type=jnp.float32)
            * score_scale
        )
        scores = jnp.where(allowed, scores, masked_score)
        prob_rows = jnp.exp(scores - log_sums[head_span][:, :, None])
        grad_prob = jnp.einsum("qhd,khd->hqk", g_heads, v_heads, preferred_element_type=jnp.float32)
        row_delta = jnp.sum(prob_rows * grad_prob, axis=-1)
        grad_score = (prob_rows * (grad_prob - row_delta[:, :, None])).astype(jnp.bfloat16)
        grad_q_parts.append(
            jnp.einsum("hqk,khd->qhd", grad_score, k_heads, preferred_element_type=jnp.float32)
            * score_scale
        )
        delta_parts.append(row_delta)
        grad_k_parts.append(
            jnp.einsum("hqk,qhd->khd", grad_score, q_heads, preferred_element_type=jnp.float32)
            * score_scale
        )
        grad_v_parts.append(
            jnp.einsum(
                "hqk,qhd->khd",
                prob_rows.astype(jnp.bfloat16),
                g_heads,
                preferred_element_type=jnp.float32,
            )
        )
    return (
        join_heads(grad_q_parts),
        jnp.concatenate(delta_parts, axis=0),
        join_heads(grad_k_parts),
        join_heads(grad_v_parts),
    )


def project(flat_bf, w_attn, vector, seq_here):
    query_rows = (matmul(flat_bf, w_attn[0]) + vector[0]).astype(jnp.bfloat16)
    key_rows = matmul(flat_bf, w_attn[1]).astype(jnp.bfloat16)
    value_rows = (matmul(flat_bf, w_attn[2]) + vector[1]).astype(jnp.bfloat16)
    return (
        query_rows.reshape(seq_here, -1, D),
        key_rows.reshape(seq_here, -1, D),
        value_rows.reshape(seq_here, -1, D),
    )


def dense_part(flat_rows, heads_bf, w_out, w_in, w_down, vector):
    branch = matmul(heads_bf, w_out) + vector[2]
    first_norm = layer_norm(flat_rows + branch, vector[4], vector[5])
    first_bf = first_norm.astype(jnp.bfloat16)
    inner_pre = matmul(first_bf, w_in) + vector[8:].reshape(-1)
    activated = gelu_exact(inner_pre).astype(jnp.bfloat16)
    feed_out = matmul(activated, w_down) + vector[3]
    second_sum = first_norm + feed_out
    output = layer_norm(second_sum, vector[6], vector[7])
    return (branch, first_norm, first_bf, inner_pre, activated, feed_out, second_sum, output)


def body(
    hidden_in,
    block_of,
    lengths,
    attn_latent,
    ffn_in_latent,
    ffn_out_latent,
    student_vec,
    teacher_attn,
    teacher_ffn_in,
    teacher_ffn_out,
    teacher_vec,
):
    seq_here, rows_here = (hidden_in.shape[0], hidden_in.shape[1])
    token_count = seq_here * rows_here
    ctx_index = lax.axis_index("ctx")
    shard_index = lax.axis_index("shard")
    key_pos = positions_of(block_of)
    query_pos = lax.dynamic_slice_in_dim(key_pos, ctx_index * rows_here, rows_here)
    own_lengths = lax.dynamic_slice_in_dim(lengths, shard_index * seq_here, seq_here)
    valid_rows = (
        (query_pos[None, :] < own_lengths[:, None]).astype(jnp.float32).reshape(token_count, 1)
    )
    valid_count = jnp.sum(lengths.astype(jnp.float32))
    loss_scale = valid_count * D
    attn_gain = jnp.asarray(attn_gains, dtype=jnp.float32)[:, None, None]
    full_attn, full_in, full_out = (
        lax.all_gather(attn_latent, "shard", axis=1, tiled=True),
        lax.all_gather(ffn_in_latent, "shard", axis=0, tiled=True),
        lax.all_gather(ffn_out_latent, "shard", axis=0, tiled=True),
    )
    bin_attn = binarize(full_attn, jnp.sum(jnp.abs(full_attn), axis=1, keepdims=True), attn_gain, D)
    bin_in = binarize(full_in, jnp.sum(jnp.abs(full_in), axis=0, keepdims=True), 1.0, D)
    bin_out = binarize(full_out, jnp.sum(jnp.abs(full_out), axis=0, keepdims=True), 1.0, FF)
    teach_attn, teach_in, teach_out = (
        lax.all_gather(teacher_attn, "shard", axis=1, tiled=True),
        lax.all_gather(teacher_ffn_in, "shard", axis=0, tiled=True),
        lax.all_gather(teacher_ffn_out, "shard", axis=0, tiled=True),
    )
    flat_bf = hidden_in.reshape(token_count, D)
    flat_rows = flat_bf.astype(jnp.float32)
    s_query, s_key, s_value = project(flat_bf, bin_attn, student_vec, seq_here)
    t_query, t_key, t_value = project(flat_bf, teach_attn, teacher_vec, seq_here)
    key_all, value_all, t_key_all, t_value_all = (
        lax.all_gather(s_key, "ctx", axis=1, tiled=True),
        lax.all_gather(s_value, "ctx", axis=1, tiled=True),
        lax.all_gather(t_key, "ctx", axis=1, tiled=True),
        lax.all_gather(t_value, "ctx", axis=1, tiled=True),
    )

    def forward_seq(seq_item):
        return attend_forward(seq_item[0], seq_item[1], seq_item[2], query_pos, key_pos)

    t_heads = lax.map(forward_seq, (t_query, t_key_all, t_value_all))[0]
    t_parts = dense_part(
        flat_rows,
        t_heads.reshape(token_count, D).astype(jnp.bfloat16),
        teach_attn[3],
        teach_in,
        teach_out,
        teacher_vec,
    )
    target = t_parts[7]
    s_heads, s_lse = lax.map(forward_seq, (s_query, key_all, value_all))
    heads_bf = s_heads.reshape(token_count, D).astype(jnp.bfloat16)
    branch, first_norm, first_bf, inner_pre, activated, feed_out, second_sum, output = dense_part(
        flat_rows, heads_bf, bin_attn[3], bin_in, bin_out, student_vec
    )
    mismatch = output - target
    grad_output = valid_rows * mismatch / loss_scale
    second_back = jax.vjp(layer_norm, second_sum, student_vec[6], student_vec[7])[1]
    grad_second, grad_g2, grad_c2 = second_back(grad_output)
    grad_b2 = jnp.sum(grad_second, axis=0)
    feed_bf = grad_second.astype(jnp.bfloat16)
    grad_down = left_product(activated, feed_bf)
    grad_act = right_product(feed_bf, bin_out)
    grad_inner = jax.vjp(gelu_exact, inner_pre)[1](grad_act)[0]
    grad_b1 = jnp.sum(grad_inner, axis=0)
    inner_bf = grad_inner.astype(jnp.bfloat16)
    grad_in = left_product(first_bf, inner_bf)
    grad_first = grad_second + right_product(inner_bf, bin_in)
    first_back = jax.vjp(layer_norm, flat_rows + branch, student_vec[4], student_vec[5])[1]
    grad_res, grad_g1, grad_c1 = first_back(grad_first)
    grad_bo = jnp.sum(grad_res, axis=0)
    branch_bf = grad_res.astype(jnp.bfloat16)
    grad_wo = left_product(heads_bf, branch_bf)
    grad_heads = (
        right_product(branch_bf, bin_attn[3]).astype(jnp.bfloat16).reshape(seq_here, rows_here, D)
    )

    def back_seq(seq_item):
        return attend_query_back(
            seq_item[0], seq_item[1], seq_item[2], seq_item[3], seq_item[4], query_pos, key_pos
        )

    grad_query, row_deltas, key_part, value_part = lax.map(
        back_seq, (s_query, key_all, value_all, grad_heads, s_lse)
    )
    grad_key, grad_value = (
        lax.psum_scatter(
            key_part.astype(jnp.bfloat16), "ctx", scatter_dimension=1, tiled=True
        ).astype(jnp.float32),
        lax.psum_scatter(
            value_part.astype(jnp.bfloat16), "ctx", scatter_dimension=1, tiled=True
        ).astype(jnp.float32),
    )
    grad_query = grad_query.reshape(token_count, D)
    grad_key = grad_key.reshape(token_count, D)
    grad_value = grad_value.reshape(token_count, D)
    grad_bq = jnp.sum(grad_query, axis=0)
    grad_bv = jnp.sum(grad_value, axis=0)
    query_bf = grad_query.astype(jnp.bfloat16)
    key_bf = grad_key.astype(jnp.bfloat16)
    value_bf = grad_value.astype(jnp.bfloat16)
    grad_attn = jnp.stack(
        [
            left_product(flat_bf, query_bf),
            left_product(flat_bf, key_bf),
            left_product(flat_bf, value_bf),
            grad_wo,
        ]
    )
    grad_flat = (
        grad_res
        + right_product(query_bf, bin_attn[0])
        + right_product(key_bf, bin_attn[1])
        + right_product(value_bf, bin_attn[2])
    )
    red_attn, red_in, red_down = (
        lax.psum_scatter(
            grad_attn.astype(jnp.bfloat16), "shard", scatter_dimension=1, tiled=True
        ).astype(jnp.float32),
        lax.psum_scatter(
            grad_in.astype(jnp.bfloat16), "shard", scatter_dimension=0, tiled=True
        ).astype(jnp.float32),
        lax.psum_scatter(
            grad_down.astype(jnp.bfloat16), "shard", scatter_dimension=0, tiled=True
        ).astype(jnp.float32),
    )
    red_attn, red_in, red_down = (
        lax.psum(red_attn.astype(jnp.bfloat16), "ctx").astype(jnp.float32),
        lax.psum(red_in.astype(jnp.bfloat16), "ctx").astype(jnp.float32),
        lax.psum(red_down.astype(jnp.bfloat16), "ctx").astype(jnp.float32),
    )
    keep_attn = (jnp.abs(attn_latent) <= 1.0).astype(jnp.float32)
    keep_in = (jnp.abs(ffn_in_latent) <= 1.0).astype(jnp.float32)
    keep_out = (jnp.abs(ffn_out_latent) <= 1.0).astype(jnp.float32)
    vec_grad = jnp.concatenate(
        [
            jnp.stack([grad_bq, grad_bv, grad_bo, grad_b2, grad_g1, grad_c1, grad_g2, grad_c2]),
            grad_b1.reshape(-1, D),
        ],
        axis=0,
    )
    square_sums = jnp.stack(
        [
            0.5 * jnp.sum(valid_rows * mismatch * mismatch),
            jnp.sum(valid_rows * branch * branch),
            jnp.sum(valid_rows * feed_out * feed_out),
            jnp.sum(valid_rows * second_sum * second_sum),
        ]
    )
    vec_total, sum_total = lax.psum((vec_grad, square_sums), ("ctx", "shard"))
    statistics = jnp.concatenate(
        [sum_total[0:1] / loss_scale, jnp.sqrt(sum_total[1:] / loss_scale)]
    )
    return (
        output.reshape(seq_here, rows_here, D).astype(jnp.bfloat16),
        statistics,
        grad_flat.reshape(seq_here, rows_here, D),
        red_attn * keep_attn,
        red_in * keep_in,
        red_down * keep_out,
        vec_total[1:],
        vec_total[0],
    )


def solution(mesh):
    in_specs = (
        P("shard", "ctx", None),
        P(),
        P(),
        P(None, "shard", None),
        P("shard", None),
        P("shard", None),
        P(),
        P(None, "shard", None),
        P("shard", None),
        P("shard", None),
        P(),
    )
    out_specs = (
        P("shard", "ctx", None),
        P(),
        P("shard", "ctx", None),
        P(None, "shard", None),
        P("shard", None),
        P("shard", None),
        P(),
        P(),
    )
    return jax.shard_map(body, mesh=mesh, in_specs=in_specs, out_specs=out_specs, check_vma=False)
```

profile of v0, /device:TPU:0, one launch (start us, length us, event | category | flops | bytes accessed | tf_op | source)
XLA Modules:
  0.0 1617.4 jit_solution(1807778586871363878)
XLA Ops:
  9.4 92.4 %all-gather.21.cloned.1.call-done = bf16[4,768,768]{2,1,0:T(8,128)(2,1)} async-done(((bf16[4,192,768]{2,1,0:T(8,128)(2,1)}), bf16[4,768,768]{2,1,0:T(8,128)(2,1)}) %all-gather.21.cloned.1.call-update) | async-done | bytes 4718608 | tf_op jit(solution)/shard_map/all_gather | solution.py:199
  114.1 2.6 fusion.60
  116.7 151.8 %all-gather.11.cloned.1.call-done = f32[4,768,768]{2,1,0:T(8,128)} async-done(((f32[4,192,768]{2,1,0:T(8,128)}), f32[4,768,768]{2,1,0:T(8,128)}) %all-gather.11.cloned.1.call-update) | async-done | bytes 9437200 | tf_op jit(solution)/shard_map/all_gather | solution.py:191
  268.6 4.5 abs_reduce_fusion.2
  274.9 3.1 multiply_convert_fusion.5
  282.2 19.9 %all-gather.23.cloned.1.call-done = bf16[2,1024,768]{1,2,0:T(8,128)(2,1)} async-done(((bf16[2,128,768]{1,2,0:T(8,128)(2,1)}), bf16[2,1024,768]{1,2,0:T(8,128)(2,1)}) %all-gather.23.cloned.1.call-update) | async-done | bytes 3145744 | tf_op jit(solution)/shard_map/all_gather | solution.py:211
  302.1 35.2 %all-gather.25.cloned.1.call-done = bf16[2,1024,768]{1,2,0:T(8,128)(2,1)} async-done(((bf16[2,128,768]{1,2,0:T(8,128)(2,1)}), bf16[2,1024,768]{1,2,0:T(8,128)(2,1)}) %all-gather.25.cloned.1.call-update) | async-done | bytes 3145744 | tf_op jit(solution)/shard_map/all_gather | solution.py:210
  338.0 20.3 %while.40 = (s32[]{:T(128)}, bf16[2,128,768]{2,1,0:T(8,128)(2,1)}, bf16[2,1024,768]{1,2,0:T(8,128)(2,1)}, s32[128]{0:T(128)S(1)}, bf16[2,128,768]{2,1,0:T(8,128)...) while((s32[]{:T(128)}, bf16[2,128,768]{2,1,0:T(8,128)(2,1)}, ...), condition=%wide.region_22.23_spmd.clone, body=%wide.region_15.22_spmd.clone.sunk | while | flops 414383616 | bytes 42658548 | solution.py:217
  363.6 64.5 %all-gather.27.cloned.1.call-done = bf16[768,3072]{1,0:T(8,128)(2,1)} async-done(((bf16[192,3072]{1,0:T(8,128)(2,1)}), bf16[768,3072]{1,0:T(8,128)(2,1)}) %all-gather.27.cloned.1.call-update) | async-done | bytes 4718608 | tf_op jit(solution)/shard_map/all_gather | solution.py:200
  428.1 89.4 %all-gather.29.cloned.1.call-done = bf16[3072,768]{1,0:T(8,128)(2,1)} async-done(((bf16[768,768]{1,0:T(8,128)(2,1)}), bf16[3072,768]{1,0:T(8,128)(2,1)}) %all-gather.29.cloned.1.call-update) | async-done | bytes 4718608 | tf_op jit(solution)/shard_map/all_gather | solution.py:201
  517.5 13.0 fusion.146
  533.3 150.9 %all-gather.19.cloned.1.call-done = f32[3072,768]{1,0:T(8,128)} async-done(((f32[768,768]{1,0:T(8,128)}), f32[3072,768]{1,0:T(8,128)}) %all-gather.19.cloned.1.call-update) | async-done | bytes 9437200 | tf_op jit(solution)/shard_map/all_gather | solution.py:193
  684.3 4.5 abs_reduce_fusion
  689.4 161.5 %all-gather.17.cloned.1.call-done = f32[768,3072]{1,0:T(8,128)} async-done(((f32[192,3072]{1,0:T(8,128)}), f32[768,3072]{1,0:T(8,128)}) %all-gather.17.cloned.1.call-update) | async-done | bytes 9437200 | tf_op jit(solution)/shard_map/all_gather | solution.py:192
  850.8 4.5 abs_reduce_fusion.1
  855.9 28.4 %all-gather.13.cloned.1.call-done = bf16[2,1024,768]{1,2,0:T(8,128)(2,1)} async-done(((bf16[2,128,768]{1,2,0:T(8,128)(2,1)}), bf16[2,1024,768]{1,2,0:T(8,128)(2,1)}) %all-gather.13.cloned.1.call-update) | async-done | bytes 3145744 | tf_op jit(solution)/shard_map/all_gather | solution.py:209
  884.3 35.5 %all-gather.15.cloned.1.call-done = bf16[2,1024,768]{1,2,0:T(8,128)(2,1)} async-done(((bf16[2,128,768]{1,2,0:T(8,128)(2,1)}), bf16[2,1024,768]{1,2,0:T(8,128)(2,1)}) %all-gather.15.cloned.1.call-update) | async-done | bytes 3145744 | tf_op jit(solution)/shard_map/all_gather | solution.py:208
  920.7 22.6 %while.39 = (s32[]{:T(128)}, bf16[2,128,768]{2,1,0:T(8,128)(2,1)}, f32[2,12,128]{2,1,0:T(8,128)}, bf16[2,1024,768]{1,2,0:T(8,128)(2,1)}, s32[128]{0:T(128)S(1)},...) while((s32[]{:T(128)}, bf16[2,128,768]{2,1,0:T(8,128)(2,1)}, ...), condition=%wide.region_8.9_spmd.clone, body=%wide.region_1.8_spmd.clone.sunk | while | flops 414386688 | bytes 41334212 | solution.py:227
  945.8 12.8 multiply_convert_fusion.6
  958.8 3.7 fusion.126
  965.5 11.6 fusion.149
  977.1 4.3 multiply_reduce_fusion.4
  984.6 80.0 %while.41 = (s32[]{:T(128)}, f32[2,128,768]{1,2,0:T(8,128)}, bf16[2,1024,768]{2,1,0:T(8,128)(2,1)}, bf16[2,1024,768]{2,1,0:T(8,128)(2,1)}, bf16[2,1024,768]{1,2,...) while((s32[]{:T(128)}, f32[2,128,768]{1,2,0:T(8,128)}, ...), condition=%wide.region_41.42_spmd.clone, body=%wide.region_37.41_spmd.clone.sunk | while | flops 1032224256 | bytes 197981808 | solution.py:259
  985.0 3.6 dynamic-slice_bitcast_fusion.16
  1004.9 2.6 copy.129
  1007.5 2.8 constant_dynamic-update-slice_fusion.11
  1017.1 2.6 copy.128
  1019.7 2.8 constant_dynamic-update-slice_fusion.10
  1024.8 3.6 dynamic-slice_bitcast_fusion.16
  1044.7 2.6 copy.129
  1047.3 2.8 constant_dynamic-update-slice_fusion.11
  1056.9 2.6 copy.128
  1059.5 2.8 constant_dynamic-update-slice_fusion.10
  1068.7 42.3 %reduce-scatter.5.cloned.1.call-done = bf16[2,128,768]{2,1,0:T(8,128)(2,1)} async-done(((bf16[2,1024,768]{2,1,0:T(8,128)(2,1)}), bf16[2,128,768]{2,1,0:T(8,128)(2,1)}) %reduce-scatter.5.cloned.1.call-update) | async-done | bytes 393232 | tf_op jit(solution)/shard_map/reduce_scatter | solution.py:263
  1113.5 47.4 %reduce-scatter.7.cloned.1.call-done = bf16[2,128,768]{2,1,0:T(8,128)(2,1)} async-done(((bf16[2,1024,768]{2,1,0:T(8,128)(2,1)}), bf16[2,128,768]{2,1,0:T(8,128)(2,1)}) %reduce-scatter.7.cloned.1.call-update) | async-done | bytes 393232 | tf_op jit(solution)/shard_map/reduce_scatter | solution.py:266
  1162.4 3.7 pad_maximum_fusion
  1166.1 8.6 copy.68
  1175.8 5.3 convolution_convert_fusion
  1182.3 5.1 convolution_convert_fusion.1
  1189.4 157.5 %all-reduce.6.cloned.1.call-done = bf16[4,768,768]{2,0,1:T(4,128)(2,1)} async-done(((bf16[4,768,768]{2,0,1:T(4,128)(2,1)}), bf16[4,768,768]{2,0,1:T(4,128)(2,1)}) %all-reduce.6.cloned.1.call-update) | async-done | bytes 4718608
  1346.8 2.7 constant_dynamic-slice_fusion.5
  1349.5 83.7 %reduce-scatter.11.cloned.1.call-done = bf16[768,768]{1,0:T(8,128)(2,1)} async-done(((bf16[3072,768]{1,0:T(8,128)(2,1)}), bf16[768,768]{1,0:T(8,128)(2,1)}) %reduce-scatter.11.cloned.1.call-update) | async-done | bytes 1179664 | tf_op jit(solution)/shard_map/reduce_scatter | solution.py:299
  1433.3 88.0 %reduce-scatter.9.cloned.1.call-done = bf16[192,3072]{1,0:T(8,128)(2,1)} async-done(((bf16[768,3072]{1,0:T(8,128)(2,1)}), bf16[192,3072]{1,0:T(8,128)(2,1)}) %reduce-scatter.9.cloned.1.call-update) | async-done | bytes 1179664 | tf_op jit(solution)/shard_map/reduce_scatter | solution.py:296
  1525.7 2.7 convolution_add_fusion.6
  1528.4 41.8 %all-reduce.1 = (f32[4]{0:T(128)S(1)}, f32[12,768]{1,0:T(8,128)S(1)}) all-reduce(f32[4]{0:T(128)S(1)} %pad_maximum_fusion.1, f32[12,768]{1,0:T(8,128)S(1)} %concatenate.25), channel_id=1, replica_groups=mesh['ctx'=8,'shard'=4] {'ctx','shard'}, use_global_device_ids=true, to_apply=%region_31.32 | all-reduce | flops 9220 | bytes 73760 | tf_op jit(solution)/shard_map/psum | solution.py:326
  1574.3 2.7 convolution_add_fusion.4
  1577.0 23.8 %all-reduce.8.cloned.1.call-done = (bf16[4,192,768]{2,0,1:T(4,128)(2,1)}, bf16[192,3072]{1,0:T(8,128)(2,1)}, bf16[768,768]{1,0:T(8,128)(2,1)}) async-done(((bf16[4,192,768]{2,0,1:T(4,128)(2,1)}, bf16[192,3072]{1,0:T(8,128)(2,1)}, bf16[768,768]{1,0:T(8,128)(2,1)}), (bf16[4,192,768]{2,0,1:T(4,128)(2,1)}, bf16[192,3072]{1,0:T(8,128)(2,1)}, bf16[768,768]{1,0:T(8,128)(2,1)})) %all-reduce.8.cloned.1.call-update) | async-done | bytes 3538960 | tf_op jit(solution)/shard_map/psum | solution.py:304
  1600.8 3.4 convert_select_fusion.2
  (583 shorter events, 156.8 us)
Async XLA Ops:
  7.2 94.6 %copy-start.34 = (bf16[2,128,768]{2,1,0:T(8,128)(2,1)S(1)}, bf16[2,128,768]{2,1,0:T(8,128)(2,1)}, u32[]{:S(2)}) copy-start(bf16[2,128,768]{2,1,0:T(8,128)(2,1)} %param.18) | copy-start | bytes 1179652
  7.2 94.5 %all-gather.21.cloned.1.call-start = ((), (), s32[]{:S(2)}) async-start(), calls=%async_computation.9 | async-start | bytes 5898240 | tf_op jit(solution)/shard_map/all_gather | solution.py:199
  7.9 260.6 %all-gather.11.cloned.1.call-start = ((), (), s32[]{:S(2)}) async-start(), calls=%async_computation.4 | async-start | bytes 11796480 | tf_op jit(solution)/shard_map/all_gather | solution.py:191
  8.7 293.4 %all-gather.23.cloned.1.call-start = ((), (), s32[]{:S(2)}) async-start(), calls=%async_computation.10 | async-start | bytes 3538944 | tf_op jit(solution)/shard_map/all_gather | solution.py:211
  104.4 232.8 %all-gather.25.cloned.1.call-start = ((), (), s32[]{:S(2)}) async-start(), calls=%async_computation.11 | async-start | bytes 3538944 | tf_op jit(solution)/shard_map/all_gather | solution.py:210
  107.2 320.9 %all-gather.27.cloned.1.call-start = ((), (), s32[]{:S(2)}) async-start(), calls=%async_computation.12 | async-start | bytes 5898240 | tf_op jit(solution)/shard_map/all_gather | solution.py:200
  107.8 409.6 %all-gather.29.cloned.1.call-start = ((), (), s32[]{:S(2)}) async-start(), calls=%async_computation.13 | async-start | bytes 5898240 | tf_op jit(solution)/shard_map/all_gather | solution.py:201
  108.4 575.9 %all-gather.19.cloned.1.call-start = ((), (), s32[]{:S(2)}) async-start(), calls=%async_computation.8 | async-start | bytes 11796480 | tf_op jit(solution)/shard_map/all_gather | solution.py:193
  109.2 741.7 %all-gather.17.cloned.1.call-start = ((), (), s32[]{:S(2)}) async-start(), calls=%async_computation.7 | async-start | bytes 11796480 | tf_op jit(solution)/shard_map/all_gather | solution.py:192
  109.9 774.4 %all-gather.13.cloned.1.call-start = ((), (), s32[]{:S(2)}) async-start(), calls=%async_computation.5 | async-start | bytes 3538944 | tf_op jit(solution)/shard_map/all_gather | solution.py:209
  113.5 868.0 %copy-start.55 = (f32[768]{0:T(1024)}, f32[768]{0:T(1024)S(1)}, u32[]{:S(2)}) copy-start(f32[768]{0:T(1024)S(1)} %get-tuple-element.337) | copy-start | bytes 9220
  116.7 156.3 %copy-start.101 = (f32[4]{0:T(128)S(1)}, f32[4]{0:T(128)}, u32[]{:S(2)}) copy-start(f32[4]{0:T(128)} %constant.192) | copy-start | bytes 52
  281.6 638.2 %all-gather.15.cloned.1.call-start = ((), (), s32[]{:S(2)}) async-start(), calls=%async_computation.6 | async-start | bytes 3538944 | tf_op jit(solution)/shard_map/all_gather | solution.py:208
  358.3 159.1 %copy-start.85 = (f32[3072]{0:T(1024)S(1)}, f32[3072]{0:T(1024)}, u32[]{:S(2)}) copy-start(f32[3072]{0:T(1024)} %add.353) | copy-start | bytes 36868
  358.3 159.1 %copy-start.94 = (f32[768]{0:T(1024)S(1)}, f32[768]{0:T(1024)}, u32[]{:S(2)}) copy-start(f32[768]{0:T(1024)} %get-tuple-element.327) | copy-start | bytes 9220
  358.3 159.1 %copy-start.95 = (f32[768]{0:T(1024)S(1)}, f32[768]{0:T(1024)}, u32[]{:S(2)}) copy-start(f32[768]{0:T(1024)} %get-tuple-element.328) | copy-start | bytes 9220
  358.3 159.1 %copy-start.96 = (f32[768]{0:T(1024)S(1)}, f32[768]{0:T(1024)}, u32[]{:S(2)}) copy-start(f32[768]{0:T(1024)} %get-tuple-element.329) | copy-start | bytes 9220
  361.3 749.8 %reduce-scatter.5.cloned.1.call-start = ((), (), s32[]{:S(2)}) async-start(), calls=%async_computation.14 | async-start | bytes 3538944 | tf_op jit(solution)/shard_map/reduce_scatter | solution.py:263
  517.5 13.8 copy-start.97
  530.4 158.3 %copy-start.42 = (f32[256,768]{1,0:T(8,128)}, f32[256,768]{1,0:T(8,128)S(1)}, u32[]{:S(2)}) copy-start(f32[256,768]{1,0:T(8,128)S(1)} %get-tuple-element.475) | copy-start | bytes 2359300
  943.3 15.3 slice-start
  945.5 36.0 %copy-start.21 = (f32[256,768]{1,0:T(8,128)}, f32[256,768]{1,0:T(8,128)S(1)}, u32[]{:S(2)}) copy-start(f32[256,768]{1,0:T(8,128)S(1)} %get-tuple-element.409) | copy-start | bytes 2359300
  945.5 36.0 %copy-start.72 = (f32[256]{0:T(256)}, f32[256]{0:T(256)S(1)}, u32[]{:S(2)}) copy-start(f32[256]{0:T(256)S(1)} %broadcast_multiply_fusion.6) | copy-start | bytes 3076
  945.7 35.8 %copy-start.81 = (f32[256]{0:T(256)}, f32[256]{0:T(256)S(1)}, u32[]{:S(2)}) copy-start(f32[256]{0:T(256)S(1)} %fusion.85) | copy-start | bytes 3076
  945.8 12.8 slice-start.1
  945.8 12.8 slice-start.2
  945.8 12.8 copy-start.93
  945.8 12.8 copy-start.100
  962.8 14.3 slice-start.3
  965.5 11.7 copy-start.30
  965.5 11.6 copy-start.90
  965.5 11.6 slice-start.4
  965.5 11.6 slice-start.5
  985.0 10.2 copy-start.63
  1024.8 10.2 copy-start.63
  1064.6 96.3 %reduce-scatter.7.cloned.1.call-start = ((), (), s32[]{:S(2)}) async-start(), calls=%async_computation.15 | async-start | bytes 3538944 | tf_op jit(solution)/shard_map/reduce_scatter | solution.py:266
  1065.2 281.6 %all-reduce.6.cloned.1.call-start = ((), (), s32[]{:S(2)}) async-start(), calls=%async_computation.18 | async-start | bytes 9437184
  1174.7 258.6 %reduce-scatter.11.cloned.1.call-start = ((), (), s32[]{:S(2)}) async-start(), calls=%async_computation.17 | async-start | bytes 5898240 | tf_op jit(solution)/shard_map/reduce_scatter | solution.py:299
  1181.2 340.0 %reduce-scatter.9.cloned.1.call-start = ((), (), s32[]{:S(2)}) async-start(), calls=%async_computation.16 | async-start | bytes 5898240 | tf_op jit(solution)/shard_map/reduce_scatter | solution.py:296
  1187.5 413.3 %all-reduce.8.cloned.1.call-start = ((), (), s32[]{:S(2)}) async-start(), calls=%async_computation.19 | async-start | bytes 7077888 | tf_op jit(solution)/shard_map/psum | solution.py:304
  1349.5 173.4 %copy-start.99 = (f32[768]{0:T(1024)S(1)}, f32[768]{0:T(1024)}, u32[]{:S(2)}) copy-start(f32[768]{0:T(1024)} %get-tuple-element.318) | copy-start | bytes 9220
  1349.5 173.4 %copy-start.98 = (f32[768]{0:T(1024)S(1)}, f32[768]{0:T(1024)}, u32[]{:S(2)}) copy-start(f32[768]{0:T(1024)} %get-tuple-element.325) | copy-start | bytes 9220
  1349.5 173.4 %copy-start.84 = (f32[3072]{0:T(1024)S(1)}, f32[3072]{0:T(1024)}, u32[]{:S(2)}) copy-start(f32[3072]{0:T(1024)} %get-tuple-element.477) | copy-start | bytes 36868
  1349.5 173.4 %copy-start.80 = (f32[768]{0:T(1024)S(1)}, f32[768]{0:T(1024)}, u32[]{:S(2)}) copy-start(f32[768]{0:T(1024)} %get-tuple-element.323) | copy-start | bytes 9220
  1349.5 173.5 %copy-start.79 = (f32[768]{0:T(1024)S(1)}, f32[768]{0:T(1024)}, u32[]{:S(2)}) copy-start(f32[768]{0:T(1024)} %get-tuple-element.320) | copy-start | bytes 9220
  1349.5 176.0 %copy-start.37 = (bf16[2,128,768]{2,1,0:T(8,128)(2,1)S(1)}, bf16[2,128,768]{2,1,0:T(8,128)(2,1)}, u32[]{:S(2)}) copy-start(bf16[2,128,768]{2,1,0:T(8,128)(2,1)} %reduce-scatter.7.cloned.1.call-done) | copy-start | bytes 1179652
  1521.3 50.9 %copy-start.47 = (bf16[2,128,768]{2,1,0:T(8,128)(2,1)S(1)}, bf16[2,128,768]{2,1,0:T(8,128)(2,1)}, u32[]{:S(2)}) copy-start(bf16[2,128,768]{2,1,0:T(8,128)(2,1)} %reduce-scatter.5.cloned.1.call-done) | copy-start | bytes 1179652
  1572.2 28.6 %copy-start.27 = (f32[4,192,768]{2,1,0:T(8,128)S(1)}, f32[4,192,768]{2,1,0:T(8,128)}, u32[]{:S(2)}) copy-start(f32[4,192,768]{2,1,0:T(8,128)} %param.21) | copy-start | bytes 7077892
  (122 other events, 315.1 us)
Sparse Core Ops, SparseCore 0:
  9.6 92.0 all-gather.20
  103.3 165.2 all-gather.10
  271.0 30.9 all-gather.22
  304.4 32.8 all-gather.24
  338.6 89.4 all-gather.26
  429.5 87.8 all-gather.28
  519.0 165.2 all-gather.18
  685.8 164.9 all-gather.16
  853.3 30.9 all-gather.12
  886.6 32.8 all-gather.14
  1064.8 46.2 reduce-scatter.4
  1114.6 46.2 reduce-scatter.6
  1174.8 171.9 all-reduce.5
  1349.0 84.2 reduce-scatter.10
  1435.4 85.7 reduce-scatter.8
  1525.3 75.4 all-reduce.7
where the time goes:
time: 1620 us
  waiting for transfers between devices  1280 us (79%)
  matrix products  118 us (7%)
  local copies, waits for them, and re-layouts  99.5 us (6%)
  other arithmetic  60.8 us (4%)
  blocking collectives  41.8 us (3%)
  between operations  17.2 us (1%)
    unnamed x17, waiting for transfers between devices  162 us
    all_gather x1, waiting for transfers between devices, body(): lax.all_gather(ffn_in_latent, 'shard', axis=0, tiled=True)  161 us
    all_gather x1, waiting for transfers between devices, body(): lax.all_gather(attn_latent, 'shard', axis=1, tiled=True)  152 us
    all_gather x1, waiting for transfers between devices, body(): lax.all_gather(ffn_out_latent, 'shard', axis=0, tiled=True)  151 us
    all_gather x1, waiting for transfers between devices, body(): lax.all_gather(teacher_attn, 'shard', axis=1, tiled=True)  92.4 us
    all_gather x1, waiting for transfers between devices, body(): lax.all_gather(teacher_ffn_out, 'shard', axis=0, tiled=True)  89.4 us
    reduce_scatter x1, waiting for transfers between devices, body(): lax.psum_scatter(grad_in.astype(jnp.bfloat16), 'shard', scatter_dimension...  88 us
    reduce_scatter x1, waiting for transfers between devices, body(): lax.psum_scatter(grad_down.astype(jnp.bfloat16), 'shard', scatter_dimensi...  83.7 us
  transfers between devices with their start and end apart: 16, of which 16 were waited for; matrix products, arithmetic and copies ran while one was open for 6% of the time, Pallas kernels for 0%

commit v1 on v0

v1 whole, which is shorter than its diff:
```python
import functools

import jax
import jax.numpy as jnp
from jax import lax
from jax.experimental import pallas as pl
from jax.experimental.pallas import tpu as pltpu
from jax.sharding import PartitionSpec as P

D = 768
HEADS = 12
HEAD_DIM = 64
FF = 3072
BLK = 64

CHIPS = 4
CORES = 2
GROUP = CHIPS * CORES
COLS = D // CHIPS
HEADS_HERE = HEADS // CHIPS
UNITS = FF // CHIPS

norm_eps = 1e-05
attn_gains = (2.0, 2.0, 1.0, 4.0)
masked_score = -1e30
score_scale = HEAD_DIM ** (-0.5)
bf16 = jnp.bfloat16
f32 = jnp.float32


def dot(left_side, right_side):
    return jnp.dot(left_side, right_side, preferred_element_type=f32)


def dot_left(left_side, right_side):
    return lax.dot_general(
        left_side, right_side, (((0,), (0,)), ((), ())), preferred_element_type=f32
    )


def dot_right(left_side, right_side):
    return lax.dot_general(
        left_side, right_side, (((1,), (1,)), ((), ())), preferred_element_type=f32
    )


def layer_norm(values, gain, shift):
    middle = jnp.mean(values, axis=-1, keepdims=True)
    centred = values - middle
    spread = jnp.mean(centred * centred, axis=-1, keepdims=True)
    return centred * lax.rsqrt(spread + norm_eps) * gain + shift


def layer_norm_back(values, gain, grad_out):
    middle = jnp.mean(values, axis=-1, keepdims=True)
    centred = values - middle
    spread = jnp.mean(centred * centred, axis=-1, keepdims=True)
    inverse = lax.rsqrt(spread + norm_eps)
    normal = centred * inverse
    scaled = grad_out * gain
    grad_in = (
        scaled
        - jnp.mean(scaled, axis=-1, keepdims=True)
        - normal * jnp.mean(scaled * normal, axis=-1, keepdims=True)
    ) * inverse
    return grad_in, jnp.sum(grad_out * normal, axis=0), jnp.sum(grad_out, axis=0)


def normal_cdf(values):
    return 0.5 * (1.0 + lax.erf(values * 0.7071067811865476))


def tree_sum(items):
    while len(items) > 1:
        items = [items[i] + items[i + 1] for i in range(0, len(items), 2)]
    return items[0]


def attend_kernel(q_ref, k_ref, v_ref, pq_ref, pk_ref, o_ref, lse_ref, *, tile):
    tiles = q_ref.shape[0] // tile
    for head in range(HEADS_HERE):
        span = slice(head * HEAD_DIM, (head + 1) * HEAD_DIM)
        k_head = k_ref[:, span]
        v_turned = v_ref[:, span].T

        def step(t, carry):
            rows = pl.ds(pl.multiple_of(t * tile, tile), tile)
            scores = dot_right(k_head, q_ref[rows, span]) * score_scale
            allowed = pq_ref[:, rows] >= pk_ref[...]
            scores = jnp.where(allowed, scores, masked_score)
            peak = jnp.max(scores, axis=0, keepdims=True)
            powers = jnp.exp(scores - peak)
            total = jnp.sum(powers, axis=0, keepdims=True)
            mixed = dot(v_turned, (powers / total).astype(bf16))
            o_ref[rows, span] = mixed.T.astype(bf16)
            lse_ref[head : head + 1, rows] = peak + jnp.log(total)
            return carry

        lax.fori_loop(0, tiles, step, 0)


def attend(query, key, value, pos_q, pos_k, tile=256):
    return pl.pallas_call(
        functools.partial(attend_kernel, tile=tile),
        out_shape=(
            jax.ShapeDtypeStruct(query.shape, bf16),
            jax.ShapeDtypeStruct((HEADS_HERE, query.shape[0]), f32),
        ),
        name="attend",
    )(query, key, value, pos_q, pos_k)


def attend_back_kernel(
    q_ref, k_ref, v_ref, g_ref, lse_ref, pq_ref, pk_ref, gq_ref, gk_ref, gv_ref, ak_ref, av_ref, *, tile
):
    tiles = q_ref.shape[0] // tile
    for head in range(HEADS_HERE):
        span = slice(head * HEAD_DIM, (head + 1) * HEAD_DIM)
        k_head = k_ref[:, span]
        v_head = v_ref[:, span]
        k_turned = k_head.T
        ak_ref[...] = jnp.zeros_like(ak_ref)
        av_ref[...] = jnp.zeros_like(av_ref)

        def step(t, carry):
            rows = pl.ds(pl.multiple_of(t * tile, tile), tile)
            q_tile = q_ref[rows, span]
            g_tile = g_ref[rows, span]
            scores = dot_right(k_head, q_tile) * score_scale
            allowed = pq_ref[:, rows] >= pk_ref[...]
            scores = jnp.where(allowed, scores, masked_score)
            probs = jnp.exp(scores - lse_ref[head : head + 1, rows])
            grad_probs = dot_right(v_head, g_tile)
            delta = jnp.sum(probs * grad_probs, axis=0, keepdims=True)
            grad_scores = (probs * (grad_probs - delta)).astype(bf16)
            gq_ref[rows, span] = dot(k_turned, grad_scores).T * score_scale
            ak_ref[...] += dot(grad_scores, q_tile)
            av_ref[...] += dot(probs.astype(bf16), g_tile)
            return carry

        lax.fori_loop(0, tiles, step, 0)
        gk_ref[:, span] = ak_ref[...] * score_scale
        gv_ref[:, span] = av_ref[...]


def attend_back(query, key, value, grad_rows, lse, pos_q, pos_k, tile=256):
    return pl.pallas_call(
        functools.partial(attend_back_kernel, tile=tile),
        out_shape=(
            jax.ShapeDtypeStruct(query.shape, f32),
            jax.ShapeDtypeStruct(key.shape, f32),
            jax.ShapeDtypeStruct(value.shape, f32),
        ),
        scratch_shapes=[
            pltpu.VMEM((key.shape[0], HEAD_DIM), f32),
            pltpu.VMEM((key.shape[0], HEAD_DIM), f32),
        ],
        name="attend_back",
    )(query, key, value, grad_rows, lse, pos_q, pos_k)


def body(
    n_ctx,
    n_shard,
    hidden_in,
    block_of,
    lengths,
    attn_latent,
    ffn_in_latent,
    ffn_out_latent,
    student_vec,
    teacher_attn,
    teacher_ffn_in,
    teacher_ffn_out,
    teacher_vec,
):
    seqs, rows, _ = hidden_in.shape
    rest = n_ctx // GROUP
    own = seqs * rows
    ctx = lax.axis_index("ctx")
    z = lax.axis_index("shard")
    k = ctx % CORES
    j = (ctx // CORES) % CHIPS
    r = ctx // GROUP
    units_z = FF // n_shard // CHIPS

    def over_chips(piece, mask):
        return lax.ppermute(piece, "ctx", [(a, a ^ (mask * CORES)) for a in range(n_ctx)])

    def over_cores(piece):
        return lax.ppermute(piece, "ctx", [(a, a ^ 1) for a in range(n_ctx)])

    def over_rest(piece, mask):
        return lax.ppermute(piece, "ctx", [(a, a ^ (mask * GROUP)) for a in range(n_ctx)])

    def over_z(piece, mask):
        return lax.ppermute(piece, "shard", [(a, a ^ mask) for a in range(n_shard)])

    def index(array, place, axis=0):
        return lax.dynamic_index_in_dim(array, place, axis, keepdims=False)

    def reorder(array, place, axis=0):
        return jnp.take(array, jnp.arange(array.shape[axis]) ^ place, axis=axis)

    def gather_z(piece):
        pieces = jnp.stack([piece] + [over_z(piece, m) for m in range(1, n_shard)])
        both = jnp.stack([pieces, over_cores(pieces)], axis=1)
        both = reorder(reorder(both, z, 0), k, 1)
        return both.reshape(n_shard * CORES * piece.shape[0], piece.shape[1])

    def gather_chips(piece):
        return [piece] + [over_chips(piece, m) for m in range(1, CHIPS)]

    def scatter_z(partial):
        part_rows = partial.shape[0] // (n_shard * CORES)
        view = partial.reshape(n_shard, CORES, part_rows, partial.shape[1])
        mine = index(view, k, 1) + over_cores(index(view, 1 - k, 1).astype(bf16)).astype(f32)
        total = tree_sum(
            [index(mine, z)]
            + [over_z(index(mine, z ^ m).astype(bf16), m).astype(f32) for m in range(1, n_shard)]
        )
        if rest > 1:
            total = tree_sum(
                [total]
                + [over_rest(total.astype(bf16), m).astype(f32) for m in range(1, rest)]
            )
        return total.astype(bf16)

    def gather_plane(piece):
        pieces = jnp.stack(gather_chips(piece))
        both = jnp.stack([pieces, over_cores(pieces)], axis=1)
        return reorder(reorder(both, j, 0), k, 1)

    def total_all(values):
        values = values + over_cores(values)
        values = tree_sum(gather_chips(values))
        if rest > 1:
            values = tree_sum([values] + [over_rest(values, m) for m in range(1, rest)])
        return tree_sum([values] + [over_z(values, m) for m in range(1, n_shard)])

    def places_of(chip):
        starts = jnp.stack([(chip * CORES + k) * rows, (chip * CORES + 1 - k) * rows])
        layout = (starts[:, None] + jnp.arange(rows, dtype=jnp.int32)[None, :]).reshape(own)
        hot = (layout[:, None] // BLK) == jnp.arange(block_of.shape[0], dtype=jnp.int32)[None, :]
        return jnp.sum(jnp.where(hot, block_of[None, :], 0), axis=1) * BLK + layout % BLK

    pos_q = jnp.concatenate([places_of(r * CHIPS + (j ^ m)) for m in range(CHIPS)])
    pos_k = jnp.concatenate(
        [places_of((r ^ n) * CHIPS + (j ^ m)) for n in range(rest) for m in range(CHIPS)]
    )
    pos_q_row = pos_q[None, :]
    pos_k_col = pos_k[:, None]

    mine_in = jnp.concatenate([index(hidden_in, k), over_cores(index(hidden_in, 1 - k))])
    own_rows = mine_in.astype(f32)
    own_length = index(lengths, z * seqs + k)
    valid = (pos_q[:own] < own_length).astype(f32)[:, None]
    count = jnp.sum(lengths.astype(f32))
    loss_scale = count * D

    x_all = jnp.concatenate(gather_chips(mine_in))

    def pieces_of(attn, w_in, w_down):
        half = attn.shape[1] // CORES
        mine = lax.dynamic_slice_in_dim(attn, k * half, half, 1)
        qkv = index(mine[:3].reshape(3, half, CHIPS, COLS), j, 2)
        qkv = jnp.concatenate([qkv[0], qkv[1], qkv[2]], axis=1)
        few = attn.shape[1] // GROUP
        out = lax.dynamic_slice_in_dim(attn[3], (j * CORES + k) * few, few, 0)
        inner = lax.dynamic_slice_in_dim(w_in, k * half, half, 0)
        inner = index(inner.reshape(half, n_shard, CHIPS, units_z), j, 2).reshape(half, UNITS)
        down = lax.dynamic_slice_in_dim(
            w_down, (j * CORES + k) * (units_z // CORES), units_z // CORES, 0
        )
        return qkv, out, inner, down

    def gather_out(piece):
        pieces = jnp.stack([piece] + [over_z(piece, m) for m in range(1, n_shard)])
        chips = jnp.stack(gather_chips(pieces), axis=1)
        both = jnp.stack([chips, over_cores(chips)], axis=2)
        both = reorder(reorder(reorder(both, z, 0), j, 1), k, 2)
        return reorder(both.reshape(CHIPS, COLS, D), j, 0).reshape(D, D)

    def weights_of(pieces):
        qkv, out, inner, down = pieces
        return gather_z(qkv), gather_out(out), gather_z(inner), gather_z(down)

    t_weights = weights_of(pieces_of(teacher_attn, teacher_ffn_in, teacher_ffn_out))

    sums = jnp.concatenate(
        [
            jnp.sum(jnp.abs(attn_latent), axis=1).reshape(-1),
            jnp.sum(jnp.abs(ffn_in_latent), axis=0),
            jnp.sum(jnp.abs(ffn_out_latent), axis=0),
        ]
    )
    sums = tree_sum([sums] + [over_z(sums, m) for m in range(1, n_shard)])
    gains = jnp.asarray(attn_gains, dtype=f32)[:, None, None]
    scale_attn = gains * (sums[: 4 * D].reshape(4, 1, D) / D)
    scale_in = sums[4 * D : 4 * D + FF][None] / D
    scale_down = sums[4 * D + FF :][None] / FF
    s_weights = weights_of(
        pieces_of(
            (scale_attn * jnp.sign(attn_latent) * D ** (-0.5)).astype(bf16),
            (scale_in * jnp.sign(ffn_in_latent) * D ** (-0.5)).astype(bf16),
            (scale_down * jnp.sign(ffn_out_latent) * FF ** (-0.5)).astype(bf16),
        )
    )

    def chunk_cols(vector):
        return index(vector.reshape(CHIPS, COLS), j)

    def rest_gather(values):
        if rest == 1:
            return values
        return jnp.concatenate([values] + [over_rest(values, m) for m in range(1, rest)])

    def rest_scatter(partial):
        if rest == 1:
            return partial
        view = partial.reshape(rest, -1, partial.shape[1])
        return tree_sum(
            [view[0]] + [over_rest(view[m].astype(bf16), m).astype(f32) for m in range(1, rest)]
        )

    def scatter_chips(pieces):
        return tree_sum(
            [pieces[0]]
            + [over_chips(pieces[m].astype(bf16), m).astype(f32) for m in range(1, CHIPS)]
        )

    def forward(weights, vector):
        w_qkv, w_out, w_in, w_down = weights
        bias = jnp.concatenate(
            [chunk_cols(vector[0]), jnp.zeros((COLS,), f32), chunk_cols(vector[1])]
        )
        qkv = (dot(x_all, w_qkv) + bias).astype(bf16)
        query = qkv[:, :COLS]
        key = rest_gather(qkv[:, COLS : 2 * COLS])
        value = rest_gather(qkv[:, 2 * COLS :])
        heads, lse = attend(query, key, value, pos_q_row, pos_k_col)
        pieces = heads.reshape(CHIPS, own, COLS)
        heads_own = jnp.concatenate(
            [pieces[0]] + [over_chips(pieces[m], m) for m in range(1, CHIPS)], axis=1
        )
        branch = dot(heads_own, w_out) + vector[2]
        residual = own_rows + branch
        first = layer_norm(residual, vector[4], vector[5])
        firsts = gather_chips(first.astype(bf16))
        b1 = index(vector[8:].reshape(n_shard, CHIPS, units_z), j, 1).reshape(UNITS)
        inners, acts, parts = [], [], []
        for piece in firsts:
            inner = dot(piece, w_in) + b1
            act = (inner * normal_cdf(inner)).astype(bf16)
            inners.append(inner)
            acts.append(act)
            parts.append(dot(act, w_down))
        feed = scatter_chips(parts) + vector[3]
        second = first + feed
        out = layer_norm(second, vector[6], vector[7])
        return dict(
            query=query,
            key=key,
            value=value,
            lse=lse,
            heads_own=heads_own,
            branch=branch,
            residual=residual,
            first=first,
            firsts=firsts,
            inners=inners,
            acts=acts,
            feed=feed,
            second=second,
            out=out,
        )

    target = forward(t_weights, teacher_vec)["out"]
    s = forward(s_weights, student_vec)
    w_qkv, w_out, w_in, w_down = s_weights
    out = s["out"]
    mismatch = out - target
    grad_second, grad_g2, grad_c2 = layer_norm_back(
        s["second"], student_vec[6], valid * mismatch / loss_scale
    )
    grad_b2 = jnp.sum(grad_second, axis=0)
    feeds = gather_chips(grad_second.astype(bf16))
    grad_inners, parts, grad_b1 = [], [], 0.0
    for feed, inner in zip(feeds, s["inners"]):
        slope = normal_cdf(inner) + inner * jnp.exp(-0.5 * inner * inner) * 0.3989422804014327
        grad_inner = dot_right(feed, w_down) * slope
        grad_b1 = grad_b1 + jnp.sum(grad_inner, axis=0)
        grad_inner = grad_inner.astype(bf16)
        grad_inners.append(grad_inner)
        parts.append(dot_right(grad_inner, w_in))
    grad_first = grad_second + scatter_chips(parts)
    grad_res, grad_g1, grad_c1 = layer_norm_back(s["residual"], student_vec[4], grad_first)
    grad_bo = jnp.sum(grad_res, axis=0)
    grad_branch = grad_res.astype(bf16)
    grad_heads_own = dot_right(grad_branch, w_out).astype(bf16)
    grad_heads = jnp.concatenate(
        [grad_heads_own[:, :COLS]]
        + [
            over_chips(grad_heads_own[:, m * COLS : (m + 1) * COLS], m)
            for m in range(1, CHIPS)
        ]
    )
    grad_query, grad_key, grad_value = attend_back(
        s["query"], s["key"], s["value"], grad_heads, s["lse"], pos_q_row, pos_k_col
    )
    grad_key, grad_value = rest_scatter(grad_key), rest_scatter(grad_value)
    grad_bq = jnp.sum(grad_query, axis=0)
    grad_bv = jnp.sum(grad_value, axis=0)
    grad_qkv = jnp.concatenate([grad_query, grad_key, grad_value], axis=1).astype(bf16)
    parts = dot_right(grad_qkv, w_qkv).reshape(CHIPS, own, D)
    grad_own = grad_res + scatter_chips([parts[m] for m in range(CHIPS)])

    acts = jnp.concatenate(s["acts"])
    down_grad = gather_plane(scatter_z(dot_left(acts, jnp.concatenate(feeds))))
    down_grad = down_grad.reshape(ffn_out_latent.shape)
    in_grad = scatter_z(dot_left(jnp.concatenate(s["firsts"]), jnp.concatenate(grad_inners)))
    in_grad = gather_plane(in_grad).reshape(CHIPS, ffn_in_latent.shape[0], n_shard, units_z)
    in_grad = in_grad.transpose(1, 2, 0, 3).reshape(ffn_in_latent.shape)
    rel_cols = reorder(grad_branch.reshape(own, CHIPS, COLS), j, 1)
    out_parts = reorder(
        dot_left(s["heads_own"], rel_cols.reshape(own, D)).reshape(CHIPS, COLS, D), j, 0
    ).reshape(D, CHIPS, COLS)
    out_grad = scatter_z(scatter_chips([out_parts[:, m] for m in range(CHIPS)]))
    qkv_grad = scatter_z(dot_left(x_all, grad_qkv))

    def columns(piece):
        full = gather_plane(piece)
        return full.reshape(CHIPS, attn_latent.shape[1], -1)

    out_grad = columns(out_grad).transpose(1, 0, 2).reshape(1, -1, D)
    qkv_grad = columns(qkv_grad).reshape(CHIPS, -1, 3, COLS).transpose(2, 1, 0, 3)
    attn_grad = jnp.concatenate([qkv_grad.reshape(3, -1, D), out_grad])

    def keep(latent, grad):
        return jnp.where(jnp.abs(latent) <= 1.0, grad.astype(f32), 0.0)

    def spread(chunk):
        hot = (jnp.arange(CHIPS) == j).astype(f32)[:, None]
        return (hot * chunk[None]).reshape(D)

    hot = (jnp.arange(CHIPS) == j).astype(f32)[None, :, None]
    b1_rows = (grad_b1.reshape(n_shard, 1, units_z) * hot).reshape(FF // D, D)
    stats = jnp.stack(
        [
            0.5 * jnp.sum(valid * mismatch * mismatch),
            jnp.sum(valid * s["branch"] * s["branch"]),
            jnp.sum(valid * s["feed"] * s["feed"]),
            jnp.sum(valid * s["second"] * s["second"]),
        ]
    )
    early = jnp.concatenate(
        [
            jnp.stack([grad_bo, grad_b2, grad_g1, grad_c1, grad_g2, grad_c2]),
            b1_rows,
            jnp.pad(stats, (0, D - 4))[None],
        ]
    )
    early = total_all(early)
    late = total_all(jnp.stack([spread(grad_bq), spread(grad_bv)]))
    stats = early[-1, :4]
    statistics = jnp.concatenate([stats[:1] / loss_scale, jnp.sqrt(stats[1:] / loss_scale)])

    def to_owners(values):
        here, there = values[:rows], over_cores(values[rows:])
        return jnp.where(k == 0, jnp.stack([here, there]), jnp.stack([there, here]))

    return (
        to_owners(out.astype(bf16)),
        statistics,
        to_owners(grad_own),
        keep(attn_latent, attn_grad),
        keep(ffn_in_latent, in_grad),
        keep(ffn_out_latent, down_grad),
        jnp.concatenate([late[1:], early[:-1]]),
        late[0],
    )


def solution(mesh):
    n_ctx, n_shard = mesh.shape["ctx"], mesh.shape["shard"]
    in_specs = (
        P("shard", "ctx", None),
        P(),
        P(),
        P(None, "shard", None),
        P("shard", None),
        P("shard", None),
        P(),
        P(None, "shard", None),
        P("shard", None),
        P("shard", None),
        P(),
    )
    out_specs = (
        P("shard", "ctx", None),
        P(),
        P("shard", "ctx", None),
        P(None, "shard", None),
        P("shard", None),
        P("shard", None),
        P(),
        P(),
    )
    return jax.shard_map(
        functools.partial(body, n_ctx, n_shard),
        mesh=mesh,
        in_specs=in_specs,
        out_specs=out_specs,
        check_vma=False,
    )
```

time: 1620 us -> 688 us (0.42)
  waiting for transfers between devices: 1280 us -> 123 us
  starting transfers between devices: 1.51 us -> 128 us
  local copies, waits for them, and re-layouts: 99.5 us -> 183 us
  other arithmetic: 60.8 us -> 131 us
  matrix products: 118 us -> 59.2 us
  Pallas kernels: 0 us -> 49.4 us
  blocking collectives: 41.8 us -> 0 us
    all_gather x10 -> x0, waiting for transfers between devices: 829 us -> none  [the longest x1 161 us: body(): lax.all_gather(ffn_in_latent, 'shard', axis=0, tiled=True)]
    reduce_scatter x4 -> x0, waiting for transfers between devices: 261 us -> none  [the longest x1 88 us: body(): lax.psum_scatter(grad_in.astype(jnp.bfloat16), 'shard', scatter_dimension...]
    unnamed x17 -> x0, waiting for transfers between devices: 162 us -> none
    ppermute x0 -> x126, starting transfers between devices: none -> 128 us  [the longest x60 67.2 us: over_chips(): lax.ppermute(piece, 'ctx', [(a, a ^ mask * CORES) for a in range(n_ctx)])]
    ppermute x0 -> x126, waiting for transfers between devices: none -> 123 us  [the longest x60 64.9 us: over_chips(): lax.ppermute(piece, 'ctx', [(a, a ^ mask * CORES) for a in range(n_ctx)])]
    dot_general x77 -> x30, matrix products: 118 us -> 59.2 us  [the longest x16 33.6 us: dot(): return jnp.dot(left_side, right_side, preferred_element_type=f32)]
    gather x0 -> x32, local copies, waits for them, and re-layouts: none -> 51.2 us  [reorder(): return jnp.take(array, jnp.arange(array.shape[axis]) ^ place, axis=axis)]
    pallas_call x0 -> x3, Pallas kernels: none -> 49.4 us  [the longest x2 30 us: attend(): pl.pallas_call(functools.partial(attend_kernel, tile=tile), out_shape=(ja...]
  transfers between devices with their start and end apart: 16 -> 126, of which waited for: 16 -> 41; matrix products, arithmetic and copies ran while one was open for 6% -> 49% of each run, Pallas kernels for 0% -> 7%
where the time goes in v1:
time: 688 us; the launch traced here: 679 us
  local copies, waits for them, and re-layouts  183 us (27%)
  other arithmetic  131 us (19%)
  starting transfers between devices  128 us (19%)
  waiting for transfers between devices  123 us (18%)
  matrix products  59.2 us (9%)
  Pallas kernels  49.4 us (7%)
    ppermute x60, starting transfers between devices, over_chips(): lax.ppermute(piece, 'ctx', [(a, a ^ mask * CORES) for a in range(n_ctx)])  67.2 us
    ppermute x60, waiting for transfers between devices, over_chips(): lax.ppermute(piece, 'ctx', [(a, a ^ mask * CORES) for a in range(n_ctx)])  64.9 us
    ppermute x45, starting transfers between devices, over_z(): return lax.ppermute(piece, 'shard', [(a, a ^ mask) for a in range(n_shard)])  58.9 us
    ppermute x45, waiting for transfers between devices, over_z(): return lax.ppermute(piece, 'shard', [(a, a ^ mask) for a in range(n_shard)])  57.9 us
    gather x32, local copies, waits for them, and re-layouts, reorder(): return jnp.take(array, jnp.arange(array.shape[axis]) ^ place, axis=axis)  51.2 us
    dot_general x16, matrix products, dot(): return jnp.dot(left_side, right_side, preferred_element_type=f32)  33.6 us
    pallas_call x2, Pallas kernels, attend(): pl.pallas_call(functools.partial(attend_kernel, tile=tile), out_shape=(ja...  30 us
    select_n x19, other arithmetic, reorder(): return jnp.take(array, jnp.arange(array.shape[axis]) ^ place, axis=axis)  23 us
  transfers between devices with their start and end apart: 126, of which 41 were waited for; matrix products, arithmetic and copies ran while one was open for 49% of the time, Pallas kernels for 7%

profile of v1, /device:TPU:0, one launch (start us, length us, event | category | flops | bytes accessed | tf_op | source)
XLA Modules:
  0.0 679.2 jit_solution(12161893636038045708)
XLA Ops:
  8.2 4.0 collective-permute-start.5
  16.9 2.9 collective-permute-start.45
  64.5 2.9 reshape.830
  97.6 2.9 collective-permute-start.38
  102.9 5.7 collective-permute-done.15
  115.4 12.9 %collective-permute-done.8 = bf16[96,576]{1,0:T(8,128)(2,1)S(1)} collective-permute-done((bf16[96,576]{1,0:T(8,128)(2,1)S(1)}, bf16[96,576]{1,0:T(8,128)(2,1)S(1)}, u32[]{:S(2)}, u32[]{:S(2)}) %collective-permute-start.8) | collective-permute-done | bytes 110624 | tf_op jit(solution)/shard_map/ppermute | solution.py:197
  139.0 11.0 %collective-permute-done.51 = bf16[96,768]{1,0:T(8,128)(2,1)S(1)} collective-permute-done((bf16[96,768]{1,0:T(8,128)(2,1)S(1)}, bf16[96,768]{1,0:T(8,128)(2,1)S(1)}, u32[]{:S(2)}, u32[]{:S(2)}) %collective-permute-start.51) | collective-permute-done | bytes 147488 | tf_op jit(solution)/shard_map/ppermute | solution.py:197
  158.6 5.5 collective-permute-done.22
  176.7 3.3 collective-permute-done.19
  198.1 3.5 collective-permute-done.3
  205.5 14.9 %attend.2 = (bf16[1024,192]{1,0:T(8,128)(2,1)}, f32[3,1024]{1,0:T(4,128)}) custom-call(bf16[1024,192]{1,0:T(8,128)(2,1)} %get-tuple-element.89.q_ref, bf16[1024,192]{1,0:T(8,128)(2,1)} %get-tuple-element.88.k_ref, bf16[1024,192]{1,0:T(8,128)(2,1)} %get-tuple-element.87.v_ref, s32[1,1024]{1,0:T(1,128)} %bitcast.531, s32[1024,1]{1,0:T(8,128)} %copy.198.pk_ref), custom_call_target="tpu_custom_call" | custom-call | tf_op jit(solution)/shard_map/attend/pallas_call | solution.py:103
  228.7 15.2 %attend.3 = (bf16[1024,192]{1,0:T(8,128)(2,1)}, f32[3,1024]{1,0:T(4,128)}) custom-call(bf16[1024,192]{1,0:T(8,128)(2,1)} %get-tuple-element.86.q_ref, bf16[1024,192]{1,0:T(8,128)(2,1)} %get-tuple-element.85.k_ref, bf16[1024,192]{1,0:T(8,128)(2,1)} %get-tuple-element.84.v_ref, s32[1,1024]{1,0:T(1,128)} %bitcast.532, s32[1024,1]{1,0:T(8,128)} %copy.198.pk_ref), custom_call_target="tpu_custom_call" | custom-call | tf_op jit(solution)/shard_map/attend/pallas_call | solution.py:103
  246.5 3.4 collective-permute-done.11
  265.7 2.9 gather_fusion.10
  268.6 3.6 broadcast_select_fusion.4
  274.9 3.0 gather_fusion.23
  291.4 2.9 gather_fusion.6
  294.3 3.0 broadcast_select_fusion.9
  297.3 3.0 gather_fusion.17
  301.9 2.9 select_bitcast_fusion.3
  310.2 2.9 gather_fusion.8
  321.1 2.9 gather_fusion.9
  337.2 3.5 fusion.56
  344.6 3.4 convolution_convert_fusion.4
  348.1 7.6 %collective-permute-done.60 = bf16[256,768]{1,0:T(8,128)(2,1)} collective-permute-done((bf16[256,768]{1,0:T(8,128)(2,1)}, bf16[256,768]{1,0:T(8,128)(2,1)}, u32[]{:S(2)}, u32[]{:S(2)}) %collective-permute-start.60) | collective-permute-done | bytes 393248 | tf_op jit(solution)/shard_map/ppermute | solution.py:188
  355.7 3.4 convolution_convert_fusion.5
  359.1 3.4 convolution_convert_fusion.6
  362.5 4.1 collective-permute-done.29
  367.2 2.8 multiply_convert_fusion.7
  385.3 6.5 collective-permute-done.30
  391.9 7.5 %collective-permute-done.34 = bf16[256,768]{1,0:T(8,128)(2,1)S(1)} collective-permute-done((bf16[256,768]{1,0:T(8,128)(2,1)S(1)}, bf16[256,768]{1,0:T(8,128)(2,1)S(1)}, u32[]{:S(2)}, u32[]{:S(2)}) %collective-permute-start.34) | collective-permute-done | bytes 393248 | tf_op jit(solution)/shard_map/ppermute | solution.py:188
  433.5 3.0 fusion.15
  438.7 3.0 fusion
  455.8 3.6 gather.46
  459.5 2.9 fusion.160
  473.4 19.3 %attend_back.1 = (f32[1024,192]{1,0:T(8,128)}, f32[1024,192]{1,0:T(8,128)}, f32[1024,192]{1,0:T(8,128)}) custom-call(bf16[1024,192]{1,0:T(8,128)(2,1)} %get-tuple-element.89.q_ref, bf16[1024,192]{1,0:T(8,128)(2,1)} %get-tuple-element.88.k_ref, bf16[1024,192]{1,0:T(8,128)(2,1)} %get-tuple-element.87.v_ref, bf16[1024,192]{1,0:T(8,128)(2,1)} %pad_maximum_fusion.20.g_ref, ...), custom_call_target="tpu_custom_call" | custom-call | tf_op jit(solution)/shard_map/attend_back/pallas_call | solution.py:147
  492.8 3.6 fusion.172
  528.1 3.3 collective-permute-done.92
  532.4 3.0 reshape.838
  554.8 6.7 collective-permute-done.105
  576.8 4.7 collective-permute-done.116
  613.9 4.3 collective-permute-done.86
  627.4 2.9 collective-permute-done.88
  645.8 3.6 reshape.844
  649.5 3.7 copy.235
  653.2 4.9 reshape.842
  658.1 3.6 compare_select_fusion
  675.6 3.1 convert_select_fusion
  (826 shorter events, 436.6 us)
Async XLA Ops:
  8.2 73.4 %collective-permute-start.5 = (f32[6912]{0:T(1024)}, f32[6912]{0:T(1024)}, u32[]{:S(2)}, u32[]{:S(2)}) collective-permute-start(f32[6912]{0:T(1024)} %pad_maximum_fusion.35), channel_id=1, source_target_pairs={{0,2},{1,3},{2,0},{3,1},{4,6},{5,7},{6,4},{7,5},{8,10},{9,11},{10,... | collective-permute-start | bytes 82952 | tf_op jit(solution)/shard_map/ppermute | solution.py:197
  12.2 70.6 %collective-permute-start.6 = (f32[6912]{0:T(1024)}, f32[6912]{0:T(1024)}, u32[]{:S(2)}, u32[]{:S(2)}) collective-permute-start(f32[6912]{0:T(1024)} %pad_maximum_fusion.35), channel_id=1, source_target_pairs={{0,3},{1,2},{2,1},{3,0},{4,7},{5,6},{6,5},{7,4},{8,11},{9,10},{10,... | collective-permute-start | bytes 82952 | tf_op jit(solution)/shard_map/ppermute | solution.py:197
  13.6 71.1 %collective-permute-start.4 = (f32[6912]{0:T(1024)}, f32[6912]{0:T(1024)}, u32[]{:S(2)}, u32[]{:S(2)}) collective-permute-start(f32[6912]{0:T(1024)} %pad_maximum_fusion.35), channel_id=1, source_target_pairs={{0,1},{1,0},{2,3},{3,2},{4,5},{5,4},{6,7},{7,6},{8,9},{9,8},{10,11... | collective-permute-start | bytes 82952 | tf_op jit(solution)/shard_map/ppermute | solution.py:197
  16.9 80.4 %collective-permute-start.45 = (bf16[24,768]{1,0:T(8,128)(2,1)}, bf16[24,768]{1,0:T(8,128)(2,1)}, u32[]{:S(2)}, u32[]{:S(2)}) collective-permute-start(bf16[24,768]{1,0:T(8,128)(2,1)} %fusion.245), channel_id=1, source_target_pairs={{0,3},{1,2},{2,1},{3,0},{4,7},{5,6},{6,5},{7,4},{8,11},{9,10},{10,... | collective-permute-start | bytes 110600 | tf_op jit(solution)/shard_map/ppermute | solution.py:197
  19.8 77.8 %collective-permute-start.44 = (bf16[24,768]{1,0:T(8,128)(2,1)}, bf16[24,768]{1,0:T(8,128)(2,1)}, u32[]{:S(2)}, u32[]{:S(2)}) collective-permute-start(bf16[24,768]{1,0:T(8,128)(2,1)} %fusion.245), channel_id=1, source_target_pairs={{0,2},{1,3},{2,0},{3,1},{4,6},{5,7},{6,4},{7,5},{8,10},{9,11},{10,... | collective-permute-start | bytes 110600 | tf_op jit(solution)/shard_map/ppermute | solution.py:197
  82.8 28.2 %collective-permute-start.37 = (bf16[96,576]{1,0:T(8,128)(2,1)}, bf16[96,576]{1,0:T(8,128)(2,1)}, u32[]{:S(2)}, u32[]{:S(2)}) collective-permute-start(bf16[96,576]{1,0:T(8,128)(2,1)} %pad_maximum_fusion.33), channel_id=1, source_target_pairs={{0,2},{1,3},{2,0},{3,1},{4,6},{5,7},{6,4},{7,5},{8,10},{9,11},{10,... | collective-permute-start | bytes 331784 | tf_op jit(solution)/shard_map/ppermute | solution.py:197
  108.6 25.6 %collective-permute-start.55 = (bf16[96,768]{1,0:T(8,128)(2,1)S(1)}, bf16[96,768]{1,0:T(8,128)(2,1)S(1)}, u32[]{:S(2)}, u32[]{:S(2)}) collective-permute-start(bf16[96,768]{1,0:T(8,128)(2,1)S(1)} %copy-done.69), channel_id=1, source_target_pairs={{0,2},{1,3},{2,0},{3,1},{4,6},{5,7},{6,4},{7,5},{8,10},{9,11},{10,... | collective-permute-start | bytes 442376 | tf_op jit(solution)/shard_map/ppermute | solution.py:197
  108.6 27.9 %collective-permute-start.54 = (bf16[96,768]{1,0:T(8,128)(2,1)S(1)}, bf16[96,768]{1,0:T(8,128)(2,1)S(1)}, u32[]{:S(2)}, u32[]{:S(2)}) collective-permute-start(bf16[96,768]{1,0:T(8,128)(2,1)S(1)} %copy-done.69), channel_id=1, source_target_pairs={{0,1},{1,0},{2,3},{3,2},{4,5},{5,4},{6,7},{7,6},{8,9},{9,8},{10,11... | collective-permute-start | bytes 442376 | tf_op jit(solution)/shard_map/ppermute | solution.py:197
  130.6 19.4 %collective-permute-start.51 = (bf16[96,768]{1,0:T(8,128)(2,1)S(1)}, bf16[96,768]{1,0:T(8,128)(2,1)S(1)}, u32[]{:S(2)}, u32[]{:S(2)}) collective-permute-start(bf16[96,768]{1,0:T(8,128)(2,1)S(1)} %copy-done.70), channel_id=1, source_target_pairs={{0,2},{1,3},{2,0},{3,1},{4,6},{5,7},{6,4},{7,5},{8,10},{9,11},{10,... | collective-permute-start | bytes 442376 | tf_op jit(solution)/shard_map/ppermute | solution.py:197
  130.6 19.4 %collective-permute-start.50 = (bf16[96,768]{1,0:T(8,128)(2,1)S(1)}, bf16[96,768]{1,0:T(8,128)(2,1)S(1)}, u32[]{:S(2)}, u32[]{:S(2)}) collective-permute-start(bf16[96,768]{1,0:T(8,128)(2,1)S(1)} %copy-done.70), channel_id=1, source_target_pairs={{0,1},{1,0},{2,3},{3,2},{4,5},{5,4},{6,7},{7,6},{8,9},{9,8},{10,11... | collective-permute-start | bytes 442376 | tf_op jit(solution)/shard_map/ppermute | solution.py:197
  134.2 19.6 %collective-permute-start.56 = (bf16[96,768]{1,0:T(8,128)(2,1)S(1)}, bf16[96,768]{1,0:T(8,128)(2,1)S(1)}, u32[]{:S(2)}, u32[]{:S(2)}) collective-permute-start(bf16[96,768]{1,0:T(8,128)(2,1)S(1)} %copy-done.69), channel_id=1, source_target_pairs={{0,3},{1,2},{2,1},{3,0},{4,7},{5,6},{6,5},{7,4},{8,11},{9,10},{10,... | collective-permute-start | bytes 442376 | tf_op jit(solution)/shard_map/ppermute | solution.py:197
  137.4 19.8 %collective-permute-start.23 = (bf16[96,768]{1,0:T(8,128)(2,1)S(1)}, bf16[96,768]{1,0:T(8,128)(2,1)S(1)}, u32[]{:S(2)}, u32[]{:S(2)}) collective-permute-start(bf16[96,768]{1,0:T(8,128)(2,1)S(1)} %reshape.822), channel_id=1, source_target_pairs={{0,3},{1,2},{2,1},{3,0},{4,7},{5,6},{6,5},{7,4},{8,11},{9,10},{10,... | collective-permute-start | bytes 442376 | tf_op jit(solution)/shard_map/ppermute | solution.py:197
  176.1 74.9 %collective-permute-start.57 = (bf16[4,96,768]{2,1,0:T(8,128)(2,1)}, bf16[4,96,768]{2,1,0:T(8,128)(2,1)}, u32[]{:S(2)}, u32[]{:S(2)}) collective-permute-start(bf16[4,96,768]{2,1,0:T(8,128)(2,1)} %get-tuple-element.128), channel_id=1, source_target_pairs={{0,4},{4,0},{8,12},{12,8},{16,20},{20,16},{24,28},{28,24},{1,5},{5... | collective-permute-start | bytes 1769480 | tf_op jit(solution)/shard_map/ppermute | solution.py:191
  176.7 76.7 %collective-permute-start.53 = (bf16[4,96,768]{2,1,0:T(8,128)(2,1)}, bf16[4,96,768]{2,1,0:T(8,128)(2,1)}, u32[]{:S(2)}, u32[]{:S(2)}) collective-permute-start(bf16[4,96,768]{2,1,0:T(8,128)(2,1)} %get-tuple-element.121), channel_id=1, source_target_pairs={{0,4},{4,0},{8,12},{12,8},{16,20},{20,16},{24,28},{28,24},{1,5},{5... | collective-permute-start | bytes 1769480 | tf_op jit(solution)/shard_map/ppermute | solution.py:191
  194.4 61.5 %collective-permute-start.28 = (bf16[4,96,768]{2,1,0:T(8,128)(2,1)}, bf16[4,96,768]{2,1,0:T(8,128)(2,1)}, u32[]{:S(2)}, u32[]{:S(2)}) collective-permute-start(bf16[4,96,768]{2,1,0:T(8,128)(2,1)} %get-tuple-element.130), channel_id=1, source_target_pairs={{0,4},{4,0},{8,12},{12,8},{16,20},{20,16},{24,28},{28,24},{1,5},{5... | collective-permute-start | bytes 1769480 | tf_op jit(solution)/shard_map/ppermute | solution.py:191
  221.5 22.4 %collective-permute-start.13 = (bf16[256,192]{1,0:T(8,128)(2,1)S(1)}, bf16[256,192]{1,0:T(8,128)(2,1)S(1)}, u32[]{:S(2)}, u32[]{:S(2)}) collective-permute-start(bf16[256,192]{1,0:T(8,128)(2,1)S(1)} %get-tuple-element.143), channel_id=1, source_target_pairs={{0,24},{4,28},{8,16},{12,20},{16,8},{20,12},{24,0},{28,4},{1,25},{... | collective-permute-start | bytes 294920 | tf_op jit(solution)/shard_map/ppermute | solution.py:188
  223.0 21.0 %collective-permute-start.12 = (bf16[256,192]{1,0:T(8,128)(2,1)S(1)}, bf16[256,192]{1,0:T(8,128)(2,1)S(1)}, u32[]{:S(2)}, u32[]{:S(2)}) collective-permute-start(bf16[256,192]{1,0:T(8,128)(2,1)S(1)} %get-tuple-element.144), channel_id=1, source_target_pairs={{0,16},{4,20},{8,24},{12,28},{16,0},{20,4},{24,8},{28,12},{1,17},{... | collective-permute-start | bytes 294920 | tf_op jit(solution)/shard_map/ppermute | solution.py:188
  249.9 34.1 %collective-permute-start.49 = (bf16[4,4,24,768]{3,2,1,0:T(8,128)(2,1)}, bf16[4,4,24,768]{3,2,1,0:T(8,128)(2,1)}, u32[]{:S(2)}, u32[]{:S(2)}) collective-permute-start(bf16[4,4,24,768]{3,2,1,0:T(8,128)(2,1)} %get-tuple-element.126), channel_id=1, source_target_pairs={{0,4},{4,0},{8,12},{12,8},{16,20},{20,16},{24,28},{28,24},{1,5},{5... | collective-permute-start | bytes 1769480 | tf_op jit(solution)/shard_map/ppermute | solution.py:191
  251.0 38.1 %collective-permute-start.20 = (bf16[4,4,24,768]{3,2,1,0:T(8,128)(2,1)}, bf16[4,4,24,768]{3,2,1,0:T(8,128)(2,1)}, u32[]{:S(2)}, u32[]{:S(2)}) collective-permute-start(bf16[4,4,24,768]{3,2,1,0:T(8,128)(2,1)} %get-tuple-element.137), channel_id=1, source_target_pairs={{0,4},{4,0},{8,12},{12,8},{16,20},{20,16},{24,28},{28,24},{1,5},{5... | collective-permute-start | bytes 1769480 | tf_op jit(solution)/shard_map/ppermute | solution.py:191
  253.4 72.2 %collective-permute-start.42 = (bf16[256,192]{1,0:T(8,128)(2,1)}, bf16[256,192]{1,0:T(8,128)(2,1)}, u32[]{:S(2)}, u32[]{:S(2)}) collective-permute-start(bf16[256,192]{1,0:T(8,128)(2,1)} %get-tuple-element.139), channel_id=1, source_target_pairs={{0,24},{4,28},{8,16},{12,20},{16,8},{20,12},{24,0},{28,4},{1,25},{... | collective-permute-start | bytes 294920 | tf_op jit(solution)/shard_map/ppermute | solution.py:188
  255.9 69.7 %collective-permute-start.41 = (bf16[256,192]{1,0:T(8,128)(2,1)}, bf16[256,192]{1,0:T(8,128)(2,1)}, u32[]{:S(2)}, u32[]{:S(2)}) collective-permute-start(bf16[256,192]{1,0:T(8,128)(2,1)} %get-tuple-element.140), channel_id=1, source_target_pairs={{0,16},{4,20},{8,24},{12,28},{16,0},{20,4},{24,8},{28,12},{1,17},{... | collective-permute-start | bytes 294920 | tf_op jit(solution)/shard_map/ppermute | solution.py:188
  261.8 63.8 %collective-permute-start.40 = (bf16[256,192]{1,0:T(8,128)(2,1)}, bf16[256,192]{1,0:T(8,128)(2,1)}, u32[]{:S(2)}, u32[]{:S(2)}) collective-permute-start(bf16[256,192]{1,0:T(8,128)(2,1)} %get-tuple-element.141), channel_id=1, source_target_pairs={{0,8},{4,12},{8,0},{12,4},{16,24},{20,28},{24,16},{28,20},{1,9},{5... | collective-permute-start | bytes 294920 | tf_op jit(solution)/shard_map/ppermute | solution.py:188
  329.4 26.2 %collective-permute-start.60 = (bf16[256,768]{1,0:T(8,128)(2,1)}, bf16[256,768]{1,0:T(8,128)(2,1)}, u32[]{:S(2)}, u32[]{:S(2)}) collective-permute-start(bf16[256,768]{1,0:T(8,128)(2,1)} %fusion.60), channel_id=1, source_target_pairs={{0,16},{4,20},{8,24},{12,28},{16,0},{20,4},{24,8},{28,12},{1,17},{... | collective-permute-start | bytes 1179656 | tf_op jit(solution)/shard_map/ppermute | solution.py:188
  331.0 28.1 %collective-permute-start.58 = (bf16[256,768]{1,0:T(8,128)(2,1)}, bf16[256,768]{1,0:T(8,128)(2,1)}, u32[]{:S(2)}, u32[]{:S(2)}) collective-permute-start(bf16[256,768]{1,0:T(8,128)(2,1)} %fusion.60), channel_id=1, source_target_pairs={{0,8},{4,12},{8,0},{12,4},{16,24},{20,28},{24,16},{28,20},{1,9},{5... | collective-permute-start | bytes 1179656 | tf_op jit(solution)/shard_map/ppermute | solution.py:188
  335.2 39.8 %collective-permute-start.33 = (bf16[256,768]{1,0:T(8,128)(2,1)}, bf16[256,768]{1,0:T(8,128)(2,1)}, u32[]{:S(2)}, u32[]{:S(2)}) collective-permute-start(bf16[256,768]{1,0:T(8,128)(2,1)} %fusion.58), channel_id=1, source_target_pairs={{0,24},{4,28},{8,16},{12,20},{16,8},{20,12},{24,0},{28,4},{1,25},{... | collective-permute-start | bytes 1179656 | tf_op jit(solution)/shard_map/ppermute | solution.py:188
  335.6 34.8 %collective-permute-start.31 = (bf16[256,768]{1,0:T(8,128)(2,1)}, bf16[256,768]{1,0:T(8,128)(2,1)}, u32[]{:S(2)}, u32[]{:S(2)}) collective-permute-start(bf16[256,768]{1,0:T(8,128)(2,1)} %fusion.58), channel_id=1, source_target_pairs={{0,16},{4,20},{8,24},{12,28},{16,0},{20,4},{24,8},{28,12},{1,17},{... | collective-permute-start | bytes 1179656 | tf_op jit(solution)/shard_map/ppermute | solution.py:188
  343.1 23.5 %collective-permute-start.29 = (bf16[256,768]{1,0:T(8,128)(2,1)}, bf16[256,768]{1,0:T(8,128)(2,1)}, u32[]{:S(2)}, u32[]{:S(2)}) collective-permute-start(bf16[256,768]{1,0:T(8,128)(2,1)} %fusion.58), channel_id=1, source_target_pairs={{0,8},{4,12},{8,0},{12,4},{16,24},{20,28},{24,16},{28,20},{1,9},{5... | collective-permute-start | bytes 1179656 | tf_op jit(solution)/shard_map/ppermute | solution.py:188
  355.7 23.8 %collective-permute-start.63 = (bf16[256,768]{1,0:T(8,128)(2,1)}, bf16[256,768]{1,0:T(8,128)(2,1)}, u32[]{:S(2)}, u32[]{:S(2)}) collective-permute-start(bf16[256,768]{1,0:T(8,128)(2,1)} %convolution_convert_fusion.4), channel_id=1, source_target_pairs={{0,24},{4,28},{8,16},{12,20},{16,8},{20,12},{24,0},{28,4},{1,25},{... | collective-permute-start | bytes 1179656 | tf_op jit(solution)/shard_map/ppermute | solution.py:188
  359.1 23.6 %collective-permute-start.61 = (bf16[256,768]{1,0:T(8,128)(2,1)}, bf16[256,768]{1,0:T(8,128)(2,1)}, u32[]{:S(2)}, u32[]{:S(2)}) collective-permute-start(bf16[256,768]{1,0:T(8,128)(2,1)} %convolution_convert_fusion.5), channel_id=1, source_target_pairs={{0,16},{4,20},{8,24},{12,28},{16,0},{20,4},{24,8},{28,12},{1,17},{... | collective-permute-start | bytes 1179656 | tf_op jit(solution)/shard_map/ppermute | solution.py:188
  370.5 21.4 %collective-permute-start.30 = (bf16[256,768]{1,0:T(8,128)(2,1)S(1)}, bf16[256,768]{1,0:T(8,128)(2,1)S(1)}, u32[]{:S(2)}, u32[]{:S(2)}) collective-permute-start(bf16[256,768]{1,0:T(8,128)(2,1)S(1)} %convolution_convert_fusion.9), channel_id=1, source_target_pairs={{0,8},{4,12},{8,0},{12,4},{16,24},{20,28},{24,16},{28,20},{1,9},{5... | collective-permute-start | bytes 1179656 | tf_op jit(solution)/shard_map/ppermute | solution.py:188
  379.4 20.0 %collective-permute-start.34 = (bf16[256,768]{1,0:T(8,128)(2,1)S(1)}, bf16[256,768]{1,0:T(8,128)(2,1)S(1)}, u32[]{:S(2)}, u32[]{:S(2)}) collective-permute-start(bf16[256,768]{1,0:T(8,128)(2,1)S(1)} %convolution_convert_fusion.7), channel_id=1, source_target_pairs={{0,24},{4,28},{8,16},{12,20},{16,8},{20,12},{24,0},{28,4},{1,25},{... | collective-permute-start | bytes 1179656 | tf_op jit(solution)/shard_map/ppermute | solution.py:188
  407.4 20.7 %collective-permute-start.64 = (bf16[256,768]{1,0:T(8,128)(2,1)}, bf16[256,768]{1,0:T(8,128)(2,1)}, u32[]{:S(2)}, u32[]{:S(2)}) collective-permute-start(bf16[256,768]{1,0:T(8,128)(2,1)} %convert_element_type.393), channel_id=1, source_target_pairs={{0,8},{4,12},{8,0},{12,4},{16,24},{20,28},{24,16},{28,20},{1,9},{5... | collective-permute-start | bytes 1179656 | tf_op jit(solution)/shard_map/ppermute | solution.py:188
  421.6 21.7 %collective-permute-start.69 = (bf16[256,768]{1,0:T(8,128)(2,1)}, bf16[256,768]{1,0:T(8,128)(2,1)}, u32[]{:S(2)}, u32[]{:S(2)}) collective-permute-start(bf16[256,768]{1,0:T(8,128)(2,1)} %convolution_convert_fusion.1), channel_id=1, source_target_pairs={{0,24},{4,28},{8,16},{12,20},{16,8},{20,12},{24,0},{28,4},{1,25},{... | collective-permute-start | bytes 1179656 | tf_op jit(solution)/shard_map/ppermute | solution.py:188
  437.6 80.7 %collective-permute-start.111 = (bf16[4,96,768]{2,1,0:T(8,128)(2,1)}, bf16[4,96,768]{2,1,0:T(8,128)(2,1)}, u32[]{:S(2)}, u32[]{:S(2)}) collective-permute-start(bf16[4,96,768]{2,1,0:T(8,128)(2,1)} %fusion.62), channel_id=1, source_target_pairs={{0,4},{4,0},{8,12},{12,8},{16,20},{20,16},{24,28},{28,24},{1,5},{5... | collective-permute-start | bytes 1769480 | tf_op jit(solution)/shard_map/ppermute | solution.py:191
  442.7 78.9 %collective-permute-start.103 = (bf16[4,96,768]{2,1,0:T(8,128)(2,1)}, bf16[4,96,768]{2,1,0:T(8,128)(2,1)}, u32[]{:S(2)}, u32[]{:S(2)}) collective-permute-start(bf16[4,96,768]{2,1,0:T(8,128)(2,1)} %fusion.61), channel_id=1, source_target_pairs={{0,4},{4,0},{8,12},{12,8},{16,20},{20,16},{24,28},{28,24},{1,5},{5... | collective-permute-start | bytes 1769480 | tf_op jit(solution)/shard_map/ppermute | solution.py:191
  448.7 22.8 %collective-permute-start.79 = (bf16[256,192]{1,0:T(8,128)(2,1)}, bf16[256,192]{1,0:T(8,128)(2,1)S(1)}, u32[]{:S(2)}, u32[]{:S(2)}) collective-permute-start(bf16[256,192]{1,0:T(8,128)(2,1)} %get-tuple-element.156), channel_id=1, source_target_pairs={{0,24},{4,28},{8,16},{12,20},{16,8},{20,12},{24,0},{28,4},{1,25},{... | collective-permute-start | bytes 294920 | tf_op jit(solution)/shard_map/ppermute | solution.py:188
  450.2 21.3 %collective-permute-start.78 = (bf16[256,192]{1,0:T(8,128)(2,1)}, bf16[256,192]{1,0:T(8,128)(2,1)}, u32[]{:S(2)}, u32[]{:S(2)}) collective-permute-start(bf16[256,192]{1,0:T(8,128)(2,1)} %get-tuple-element.157), channel_id=1, source_target_pairs={{0,16},{4,20},{8,24},{12,28},{16,0},{20,4},{24,8},{28,12},{1,17},{... | collective-permute-start | bytes 294920 | tf_op jit(solution)/shard_map/ppermute | solution.py:188
  451.3 20.2 %collective-permute-start.77 = (bf16[256,192]{1,0:T(8,128)(2,1)S(1)}, bf16[256,192]{1,0:T(8,128)(2,1)}, u32[]{:S(2)}, u32[]{:S(2)}) collective-permute-start(bf16[256,192]{1,0:T(8,128)(2,1)S(1)} %get-tuple-element.158), channel_id=1, source_target_pairs={{0,8},{4,12},{8,0},{12,4},{16,24},{20,28},{24,16},{28,20},{1,9},{5... | collective-permute-start | bytes 294920 | tf_op jit(solution)/shard_map/ppermute | solution.py:188
  518.3 52.5 %collective-permute-start.80 = (bf16[256,768]{1,0:T(8,128)(2,1)}, bf16[256,768]{1,0:T(8,128)(2,1)}, u32[]{:S(2)}, u32[]{:S(2)}) collective-permute-start(bf16[256,768]{1,0:T(8,128)(2,1)} %get-tuple-element.81), channel_id=1, source_target_pairs={{0,8},{4,12},{8,0},{12,4},{16,24},{20,28},{24,16},{28,20},{1,9},{5... | collective-permute-start | bytes 1179656 | tf_op jit(solution)/shard_map/ppermute | solution.py:188
  521.6 23.1 %collective-permute-start.112 = (bf16[96,768]{1,0:T(8,128)(2,1)}, bf16[96,768]{1,0:T(8,128)(2,1)}, u32[]{:S(2)}, u32[]{:S(2)}) collective-permute-start(bf16[96,768]{1,0:T(8,128)(2,1)} %get-tuple-element.90), channel_id=1, source_target_pairs={{0,1},{1,0},{2,3},{3,2},{4,5},{5,4},{6,7},{7,6},{8,9},{9,8},{10,11... | collective-permute-start | bytes 442376 | tf_op jit(solution)/shard_map/ppermute | solution.py:197
  525.8 21.1 %collective-permute-start.114 = (bf16[96,768]{1,0:T(8,128)(2,1)}, bf16[96,768]{1,0:T(8,128)(2,1)}, u32[]{:S(2)}, u32[]{:S(2)}) collective-permute-start(bf16[96,768]{1,0:T(8,128)(2,1)} %get-tuple-element.91), channel_id=1, source_target_pairs={{0,3},{1,2},{2,1},{3,0},{4,7},{5,6},{6,5},{7,4},{8,11},{9,10},{10,... | collective-permute-start | bytes 442376 | tf_op jit(solution)/shard_map/ppermute | solution.py:197
  528.1 19.9 %collective-permute-start.113 = (bf16[96,768]{1,0:T(8,128)(2,1)}, bf16[96,768]{1,0:T(8,128)(2,1)}, u32[]{:S(2)}, u32[]{:S(2)}) collective-permute-start(bf16[96,768]{1,0:T(8,128)(2,1)} %get-tuple-element.92), channel_id=1, source_target_pairs={{0,2},{1,3},{2,0},{3,1},{4,6},{5,7},{6,4},{7,5},{8,10},{9,11},{10,... | collective-permute-start | bytes 442376 | tf_op jit(solution)/shard_map/ppermute | solution.py:197
  550.4 21.3 %collective-permute-start.82 = (bf16[256,768]{1,0:T(8,128)(2,1)S(1)}, bf16[256,768]{1,0:T(8,128)(2,1)S(1)}, u32[]{:S(2)}, u32[]{:S(2)}) collective-permute-start(bf16[256,768]{1,0:T(8,128)(2,1)S(1)} %copy-done.51), channel_id=1, source_target_pairs={{0,24},{4,28},{8,16},{12,20},{16,8},{20,12},{24,0},{28,4},{1,25},{... | collective-permute-start | bytes 1179656 | tf_op jit(solution)/shard_map/ppermute | solution.py:188
  567.4 27.7 %collective-permute-start.84 = (bf16[4,96,576]{2,1,0:T(8,128)(2,1)}, bf16[4,96,576]{2,1,0:T(8,128)(2,1)}, u32[]{:S(2)}, u32[]{:S(2)}) collective-permute-start(bf16[4,96,576]{2,1,0:T(8,128)(2,1)} %fusion.64), channel_id=1, source_target_pairs={{0,4},{4,0},{8,12},{12,8},{16,20},{20,16},{24,28},{28,24},{1,5},{5... | collective-permute-start | bytes 1327112 | tf_op jit(solution)/shard_map/ppermute | solution.py:191
  589.6 42.8 %collective-permute-start.83 = (f32[128,768]{1,0:T(8,128)}, f32[128,768]{1,0:T(8,128)}, u32[]{:S(2)}, u32[]{:S(2)}) collective-permute-start(f32[128,768]{1,0:T(8,128)} %get-tuple-element.105), channel_id=1, source_target_pairs={{0,4},{4,0},{8,12},{12,8},{16,20},{20,16},{24,28},{28,24},{1,5},{5... | collective-permute-start | bytes 1179656 | tf_op jit(solution)/shard_map/ppermute | solution.py:191
  590.7 43.8 %collective-permute-start.118 = (bf16[4,96,768]{2,1,0:T(8,128)(2,1)S(1)}, bf16[4,96,768]{2,1,0:T(8,128)(2,1)}, u32[]{:S(2)}, u32[]{:S(2)}) collective-permute-start(bf16[4,96,768]{2,1,0:T(8,128)(2,1)S(1)} %get-tuple-element.117), channel_id=1, source_target_pairs={{0,4},{4,0},{8,12},{12,8},{16,20},{20,16},{24,28},{28,24},{1,5},{5... | collective-permute-start | bytes 1769480 | tf_op jit(solution)/shard_map/ppermute | solution.py:191
  612.2 24.3 %collective-permute-start.110 = (bf16[4,96,768]{2,1,0:T(8,128)(2,1)S(1)}, bf16[4,96,768]{2,1,0:T(8,128)(2,1)}, u32[]{:S(2)}, u32[]{:S(2)}) collective-permute-start(bf16[4,96,768]{2,1,0:T(8,128)(2,1)S(1)} %get-tuple-element.119), channel_id=1, source_target_pairs={{0,4},{4,0},{8,12},{12,8},{16,20},{20,16},{24,28},{28,24},{1,5},{5... | collective-permute-start | bytes 1769480 | tf_op jit(solution)/shard_map/ppermute | solution.py:191
  632.4 32.7 %collective-permute-start.91 = (bf16[4,96,576]{2,1,0:T(8,128)(2,1)}, bf16[4,96,576]{2,1,0:T(8,128)(2,1)}, u32[]{:S(2)}, u32[]{:S(2)}) collective-permute-start(bf16[4,96,576]{2,1,0:T(8,128)(2,1)} %get-tuple-element.147), channel_id=1, source_target_pairs={{0,4},{4,0},{8,12},{12,8},{16,20},{20,16},{24,28},{28,24},{1,5},{5... | collective-permute-start | bytes 1327112 | tf_op jit(solution)/shard_map/ppermute | solution.py:191
  (221 other events, 1847.5 us)

commit v2 on v1

v2 whole, which is shorter than its diff:
```python
import functools

import jax
import jax.numpy as jnp
from jax import lax
from jax.experimental import pallas as pl
from jax.experimental.pallas import tpu as pltpu
from jax.sharding import PartitionSpec as P

D = 768
HEADS = 12
HEAD_DIM = 64
FF = 3072
BLK = 64

CHIPS = 4
CORES = 2
GROUP = CHIPS * CORES
COLS = D // CHIPS
HEADS_HERE = HEADS // CHIPS
UNITS = FF // CHIPS
HALF = UNITS // CORES
QKV = 3 * COLS

norm_eps = 1e-05
attn_gains = (2.0, 2.0, 1.0, 4.0)
masked_score = -1e30
score_scale = HEAD_DIM ** (-0.5)
bf16 = jnp.bfloat16
f32 = jnp.float32

IZ, IK, IJ, IR = 0, 1, 2, 3
ROW_BO, ROW_B2, ROW_G1, ROW_C1, ROW_G2, ROW_C2, ROW_STATS, ROW_B1, ROW_QV = range(9)
VEC_ROWS = 16

SMEM_SPEC = pl.BlockSpec(memory_space=pltpu.SMEM)
VMEM_SPEC = pl.BlockSpec(memory_space=pltpu.VMEM)


def dot(left_side, right_side):
    return jnp.dot(left_side, right_side, preferred_element_type=f32)


def dot_left(left_side, right_side):
    return lax.dot_general(
        left_side, right_side, (((0,), (0,)), ((), ())), preferred_element_type=f32
    )


def dot_right(left_side, right_side):
    return lax.dot_general(
        left_side, right_side, (((1,), (1,)), ((), ())), preferred_element_type=f32
    )


def normal_cdf(values):
    return 0.5 * (1.0 + lax.erf(values * 0.7071067811865476))


def tree_sum(items):
    items = list(items)
    while len(items) > 1:
        items = [items[i] + items[i + 1] for i in range(0, len(items), 2)]
    return items[0]


def aligned(start, size):
    return pl.ds(pl.multiple_of(start, size), size)


def shape(dims, kind=bf16):
    return jax.ShapeDtypeStruct(dims, kind)


def call(kernel, name, outs, scalars, arrays, scratch=()):
    return pl.pallas_call(
        kernel,
        out_shape=outs,
        in_specs=[SMEM_SPEC] * len(scalars) + [VMEM_SPEC] * len(arrays),
        out_specs=jax.tree.map(lambda _: VMEM_SPEC, outs),
        scratch_shapes=list(scratch),
        name=name,
    )(*scalars, *arrays)


def pick(place, options):
    value = options[0]
    for number, option in enumerate(options[1:], 1):
        value = jnp.where(place == number, option, value)
    return value


def sums_kernel(attn_ref, in_ref, out_ref, sums_ref):
    @pl.when(pl.program_id(0) == 0)
    def _():
        sums_ref[...] = jnp.zeros_like(sums_ref)

    for number in range(4):
        sums_ref[number : number + 1, :] += jnp.sum(
            jnp.abs(attn_ref[number]), axis=0, keepdims=True
        )
    for number in range(FF // D):
        sums_ref[4 + number : 5 + number, :] += jnp.sum(
            jnp.abs(in_ref[:, number * D : (number + 1) * D]), axis=0, keepdims=True
        )
    last = 4 + FF // D
    sums_ref[last : last + 1, :] += jnp.sum(jnp.abs(out_ref[...]), axis=0, keepdims=True)


def column_sums(attn, w_in, w_down, steps=4):
    return pl.pallas_call(
        sums_kernel,
        out_shape=shape((16, D), f32),
        grid=(steps,),
        in_specs=[
            pl.BlockSpec((4, attn.shape[1] // steps, D), lambda i: (0, i, 0)),
            pl.BlockSpec((w_in.shape[0] // steps, FF), lambda i: (i, 0)),
            pl.BlockSpec((w_down.shape[0] // steps, D), lambda i: (i, 0)),
        ],
        out_specs=pl.BlockSpec((16, D), lambda i: (0, 0)),
        name="column_sums",
    )(attn, w_in, w_down)


def sign_of(values):
    return jnp.where(values > 0, 1.0, jnp.where(values < 0, -1.0, 0.0))


def choose(size, count, start):
    place = lax.broadcasted_iota(jnp.int32, (size, count), 0)
    goal = lax.broadcasted_iota(jnp.int32, (size, count), 1) + start
    return jnp.where(place == goal, 1.0, 0.0).astype(bf16)


def pieces_kernel(n_shard, student, ids_ref, *refs):
    if student:
        attn_ref, in_ref, down_ref, sums_ref, early_ref, late_ref = refs
    else:
        attn_ref, in_ref, down_ref, early_ref, late_ref = refs
    k, j = ids_ref[IK], ids_ref[IJ]
    units = FF // n_shard
    few = units // GROUP
    rows_z = in_ref.shape[0]

    def binary(values, row, gain, fan_in):
        if not student:
            return values
        scale = gain * (sums_ref[row : row + 1, :] / fan_in) * fan_in ** (-0.5)
        return (sign_of(values) * scale).astype(bf16)

    chosen = choose(D, COLS, j * COLS)
    for number in range(4):
        full = binary(attn_ref[number], number, attn_gains[number], D)
        early_ref[:, number * COLS : (number + 1) * COLS] = dot(full, chosen).astype(bf16)
    chosen = choose(units, few, (j * CORES + k) * few)
    for number in range(FF // D):
        full = binary(in_ref[:, number * D : (number + 1) * D], 4 + number, 1.0, D)
        for part in range(D // units):
            place = (number * (D // units) + part) * few
            late_ref[0:rows_z, place : place + few] = dot(
                full[:, part * units : (part + 1) * units], chosen
            ).astype(bf16)
    full = binary(down_ref[...], 4 + FF // D, 1.0, FF)
    late_ref[rows_z : rows_z + few, :] = full[:, :HALF]
    late_ref[rows_z + few : rows_z + 2 * few, :] = full[:, HALF:]


def weight_pieces(n_shard, ids, attn, w_in, w_down, sums=None):
    half = attn.shape[1] // CORES
    few = FF // n_shard // GROUP
    rows_z = w_in.shape[0]
    specs = [
        pl.BlockSpec((4, half, D), lambda i, ids: (0, ids[IK], 0)),
        pl.BlockSpec((rows_z, FF), lambda i, ids: (0, 0)),
        pl.BlockSpec((few, D), lambda i, ids: (CORES * ids[IJ] + ids[IK], 0)),
    ]
    args = [attn, w_in, w_down]
    if sums is not None:
        specs.append(pl.BlockSpec((16, D), lambda i, ids: (0, 0)))
        args.append(sums)
    return pl.pallas_call(
        functools.partial(pieces_kernel, n_shard, sums is not None),
        out_shape=(shape((half, D)), shape((rows_z + 2 * few, HALF))),
        grid_spec=pltpu.PrefetchScalarGridSpec(
            num_scalar_prefetch=1,
            grid=(1,),
            in_specs=specs,
            out_specs=(
                pl.BlockSpec((half, D), lambda i, ids: (0, 0)),
                pl.BlockSpec((rows_z + 2 * few, HALF), lambda i, ids: (0, 0)),
            ),
        ),
        name="student_pieces" if sums is not None else "teacher_pieces",
    )(ids, *args)


def early_kernel(n_shard, ids_ref, *refs):
    t_refs, s_refs = refs[:n_shard], refs[n_shard : 2 * n_shard]
    qkv_ref, out_ref = refs[2 * n_shard :]
    z = ids_ref[IZ]
    half = t_refs[0].shape[0]
    span = n_shard * half
    for model, group in enumerate((t_refs, s_refs)):
        for mask, ref in enumerate(group):
            place = z ^ mask
            rows = pl.ds(pl.multiple_of(model * span + place * half, half), half)
            qkv_ref[rows, :] = ref[:, :QKV]
            fold = n_shard // 2
            low = pl.ds(
                pl.multiple_of(model * (span // 2) + lax.rem(place, fold) * half, half), half
            )

            @pl.when(place < fold)
            def _():
                out_ref[low, 0:COLS] = ref[:, QKV:]

            @pl.when(place >= fold)
            def _():
                out_ref[low, COLS:] = ref[:, QKV:]


def out_weight_kernel(n_shard, ids_ref, *refs):
    z, k, j = ids_ref[IZ], ids_ref[IK], ids_ref[IJ]
    t_ref, s_ref = refs[2 * CHIPS :]
    half = D // n_shard // CORES
    span = n_shard * half // 2
    for core in range(CORES):
        for mask in range(CHIPS):
            ref = refs[core * CHIPS + mask]
            for model, goal in enumerate((t_ref, s_ref)):
                for place in range(n_shard):
                    fold = n_shard // 2
                    low = model * span + (place % fold) * half
                    lanes = slice(0, COLS) if place < fold else slice(COLS, 2 * COLS)
                    rows = pl.ds(
                        pl.multiple_of((place * CORES + (k ^ core)) * half, half), half
                    )
                    goal[j ^ mask, rows, :] = ref[low : low + half, lanes]


def late_kernel(n_shard, ids_ref, *refs):
    z, k, j = ids_ref[IZ], ids_ref[IK], ids_ref[IJ]
    vec_ref, in_ref, down_ref, b1_ref = refs[CORES * n_shard :]
    units = FF // n_shard
    few = units // GROUP
    rows_z = D // n_shard
    for core in range(CORES):
        lanes = aligned((k ^ core) * HALF, HALF)
        for mask in range(n_shard):
            ref = refs[core * n_shard + mask]
            place = z ^ mask
            in_ref[aligned(place * rows_z, rows_z), lanes] = ref[0:rows_z, :]
            rows = pl.ds(pl.multiple_of((k ^ core) * HALF + place * few, few), few)
            down_ref[rows, 0:HALF] = ref[rows_z : rows_z + few, :]
            down_ref[rows, HALF:] = ref[rows_z + few : rows_z + 2 * few, :]
    for core in range(CORES):
        for place in range(n_shard):
            options = []
            for chip in range(CHIPS):
                start = place * units + (chip * CORES + core) * few
                row, lane = 8 + start // D, start % D
                options.append(vec_ref[row : row + 1, lane : lane + few])
            goal = core * HALF + place * few
            b1_ref[0:1, goal : goal + few] = pick(j, options)


def places_kernel(rest, ids_ref, block_ref, lengths_ref, row_ref, col_ref, valid_ref, *, seqs, rows):
    z, k, j, r = ids_ref[IZ], ids_ref[IK], ids_ref[IJ], ids_ref[IR]
    length = lengths_ref[z * seqs + k]
    per = rows // BLK
    number = 0
    for far in range(rest):
        for mask in range(CHIPS):
            for half in range(CORES):
                for part in range(per):
                    block = ((((r ^ far) * CHIPS + (j ^ mask)) * CORES + (k ^ half)) * per) + part
                    base = block_ref[block] * BLK
                    goal = slice(number * BLK, (number + 1) * BLK)
                    col = base + lax.broadcasted_iota(jnp.int32, (BLK, 1), 0)
                    col_ref[goal, :] = col
                    if far == 0:
                        row_ref[:, goal] = base + lax.broadcasted_iota(jnp.int32, (1, BLK), 1)
                    if far == 0 and mask == 0:
                        valid_ref[goal, :] = jnp.where(col < length, 1.0, 0.0)
                    number += 1


def input_kernel(ids_ref, *refs):
    k = ids_ref[IK]
    own_ref, send_ref = refs[CHIPS:]
    rows = refs[0].shape[1]
    for mask in range(CHIPS):
        goal = slice(mask * rows, (mask + 1) * rows)
        own_ref[goal, :] = refs[mask][k]
        send_ref[goal, :] = refs[mask][1 - k]


def qkv_kernel(n_shard, model, ids_ref, own_ref, oth_ref, half_ref, peer_ref, vec_ref, *outs):
    k, j = ids_ref[IK], ids_ref[IJ]
    q_ref, k_ref, v_ref, w_ref = outs
    half = D // n_shard // CORES
    base = model * n_shard * half
    for core, ref in enumerate((half_ref, peer_ref)):
        for place in range(n_shard):
            rows = pl.ds(pl.multiple_of((place * CORES + (k ^ core)) * half, half), half)
            w_ref[rows, :] = ref[base + place * half : base + (place + 1) * half, :]
    weight = w_ref[...]
    chips = [slice(chip * COLS, (chip + 1) * COLS) for chip in range(CHIPS)]
    q_bias = pick(j, [vec_ref[0:1, chip] for chip in chips])
    v_bias = pick(j, [vec_ref[1:2, chip] for chip in chips])
    rows = own_ref.shape[0] // CHIPS
    for core, ref in enumerate((own_ref, oth_ref)):
        for mask in range(CHIPS):
            result = dot(ref[mask * rows : (mask + 1) * rows, :], weight)
            goal = slice((mask * CORES + core) * rows, (mask * CORES + core + 1) * rows)
            q_ref[goal, :] = (result[:, :COLS] + q_bias).astype(bf16)
            k_ref[goal, :] = result[:, COLS : 2 * COLS].astype(bf16)
            v_ref[goal, :] = (result[:, 2 * COLS :] + v_bias).astype(bf16)


def attend_kernel(q_ref, k_ref, v_ref, pq_ref, pk_ref, *outs, tile):
    o_refs, lse_ref = outs[:CHIPS], outs[CHIPS]
    own = q_ref.shape[0] // CHIPS
    for head in range(HEADS_HERE):
        span = slice(head * HEAD_DIM, (head + 1) * HEAD_DIM)
        k_head = k_ref[:, span]
        v_turned = v_ref[:, span].T
        for t in range(q_ref.shape[0] // tile):
            rows = slice(t * tile, (t + 1) * tile)
            scores = dot_right(k_head, q_ref[rows, span]) * score_scale
            allowed = pq_ref[:, rows] >= pk_ref[...]
            scores = jnp.where(allowed, scores, masked_score)
            peak = jnp.max(scores, axis=0, keepdims=True)
            powers = jnp.exp(scores - peak)
            total = jnp.sum(powers, axis=0, keepdims=True)
            mixed = dot(v_turned, powers.astype(bf16)) / total
            low = t * tile % own
            o_refs[t * tile // own][low : low + tile, span] = mixed.T.astype(bf16)
            lse_ref[head : head + 1, rows] = peak + jnp.log(total)


def norm_parts(values):
    middle = jnp.mean(values, axis=-1, keepdims=True)
    centred = values - middle
    spread = jnp.mean(centred * centred, axis=-1, keepdims=True)
    inverse = lax.rsqrt(spread + norm_eps)
    return centred * inverse, inverse


def norm_back(values, gain, grad_out):
    normal, inverse = norm_parts(values)
    scaled = grad_out * gain
    grad_in = (
        scaled
        - jnp.mean(scaled, axis=-1, keepdims=True)
        - normal * jnp.mean(scaled * normal, axis=-1, keepdims=True)
    ) * inverse
    return grad_in, normal


def column_total(values):
    return jnp.sum(values, axis=0, keepdims=True)


def branch_kernel(student, ids_ref, *refs):
    j = ids_ref[IJ]
    h_refs, (w_ref, own_ref, oth_ref, vec_ref, valid_ref) = refs[:CHIPS], refs[CHIPS : CHIPS + 5]
    outs = refs[CHIPS + 5 :]
    first_ref, sent_ref = outs[:2]
    rows = own_ref.shape[0] // CHIPS
    if student:
        residual_ref, sums_ref = outs[2:]
        sums_ref[...] = jnp.zeros_like(sums_ref)
    for core, x_ref in enumerate((own_ref, oth_ref)):
        goal = slice(core * rows, (core + 1) * rows)
        parts = []
        for chip in range(CHIPS):
            parts.append(
                tree_sum(
                    dot(
                        h_refs[mask][goal, :],
                        w_ref[chip, aligned((j ^ mask) * COLS, COLS), :],
                    )
                    for mask in range(CHIPS)
                )
            )
        branch = jnp.concatenate(parts, axis=1) + vec_ref[2:3, :]
        residual = x_ref[0:rows, :].astype(f32) + branch
        normal, _ = norm_parts(residual)
        first = normal * vec_ref[4:5, :] + vec_ref[5:6, :]
        first_ref[goal, :] = first
        sent_ref[goal, :] = first.astype(bf16)
        if student:
            residual_ref[goal, :] = residual
            sums_ref[0:1, :] += column_total(valid_ref[goal, :] * branch * branch)


def feed_kernel(student, piece_ref, in_ref, down_ref, b1_ref, part_ref, *outs):
    inner = dot(piece_ref[...], in_ref[...]) + b1_ref[0:1, :]
    act = (inner * normal_cdf(inner)).astype(bf16)
    if student:
        outs[0][...] = inner
        outs[1][...] = act
    part_ref[...] = dot(act, down_ref[...]).astype(part_ref.dtype)


def target_kernel(*refs):
    parts, (first_ref, vec_ref, target_ref) = refs[:CHIPS], refs[CHIPS:]
    feed = tree_sum(ref[...].astype(f32) for ref in parts) + vec_ref[3:4, :]
    normal, _ = norm_parts(first_ref[...] + feed)
    target_ref[...] = normal * vec_ref[6:7, :] + vec_ref[7:8, :]


def loss_kernel(lengths_ref, *refs):
    parts, rest = refs[:CHIPS], refs[CHIPS:]
    first_ref, vec_ref, target_ref, valid_ref, out_ref, grad_ref, sent_ref, sums_ref = rest
    count = lengths_ref[0]
    for number in range(1, lengths_ref.shape[0]):
        count = count + lengths_ref[number]
    share = 1.0 / (count.astype(f32) * D)
    feed = tree_sum(ref[...].astype(f32) for ref in parts) + vec_ref[3:4, :]
    second = first_ref[...] + feed
    normal, inverse = norm_parts(second)
    out = normal * vec_ref[6:7, :] + vec_ref[7:8, :]
    out_ref[...] = out.astype(bf16)
    valid = valid_ref[...]
    mismatch = valid * (out - target_ref[...])
    grad_out = mismatch * share
    scaled = grad_out * vec_ref[6:7, :]
    grad = (
        scaled
        - jnp.mean(scaled, axis=-1, keepdims=True)
        - normal * jnp.mean(scaled * normal, axis=-1, keepdims=True)
    ) * inverse
    grad_ref[...] = grad
    sent_ref[...] = grad.astype(bf16)
    sums_ref[...] = jnp.concatenate(
        [
            column_total(grad),
            column_total(grad_out * normal),
            column_total(grad_out),
            0.5 * column_total(mismatch * mismatch),
            column_total(valid * feed * feed),
            column_total(valid * second * second),
            jnp.zeros((2, D), f32),
        ]
    )


def feed_back_kernel(piece_ref, inner_ref, in_ref, down_ref, part_ref, grad_ref, sum_ref):
    inner = inner_ref[...]
    slope = normal_cdf(inner) + inner * jnp.exp(-0.5 * inner * inner) * 0.3989422804014327
    grad = dot_right(piece_ref[...], down_ref[...]) * slope
    sum_ref[...] = jnp.broadcast_to(column_total(grad), sum_ref.shape)
    grad = grad.astype(bf16)
    grad_ref[...] = grad
    part_ref[...] = dot_right(grad, in_ref[...]).astype(part_ref.dtype)


def branch_back_kernel(ids_ref, *refs):
    j = ids_ref[IJ]
    parts, rest = refs[:CHIPS], refs[CHIPS:]
    second_ref, residual_ref, vec_ref, w_ref = rest[:4]
    grad_ref, sent_ref = rest[4:6]
    h_refs, (sums_ref,) = rest[6 : 6 + CHIPS], rest[6 + CHIPS :]
    grad_first = second_ref[...] + tree_sum(ref[...].astype(f32) for ref in parts)
    grad, normal = norm_back(residual_ref[...], vec_ref[4:5, :], grad_first)
    grad_ref[...] = grad
    sums_ref[...] = jnp.concatenate(
        [
            column_total(grad),
            column_total(grad_first * normal),
            column_total(grad_first),
            jnp.zeros((5, D), f32),
        ]
    )
    grad = grad.astype(bf16)
    sent_ref[...] = grad
    chips = [grad[:, chip * COLS : (chip + 1) * COLS] for chip in range(CHIPS)]
    for mask in range(CHIPS):
        rows = aligned((j ^ mask) * COLS, COLS)
        h_refs[mask][...] = tree_sum(
            dot_right(chips[chip], w_ref[chip, rows, :]) for chip in range(CHIPS)
        ).astype(bf16)


def attend_back_kernel(*refs, tile):
    q_ref, k_ref, v_ref = refs[:3]
    g_refs = refs[3 : 3 + CHIPS]
    lse_ref, pq_ref, pk_ref, gq_ref, gk_ref, gv_ref, sums_ref, ak_ref, av_ref = refs[3 + CHIPS :]
    own = q_ref.shape[0] // CHIPS
    sums_ref[...] = jnp.zeros_like(sums_ref)
    for head in range(HEADS_HERE):
        span = slice(head * HEAD_DIM, (head + 1) * HEAD_DIM)
        k_head = k_ref[:, span]
        v_head = v_ref[:, span]
        k_turned = k_head.T
        for t in range(q_ref.shape[0] // tile):
            rows = slice(t * tile, (t + 1) * tile)
            low = t * tile % own
            q_tile = q_ref[rows, span]
            g_tile = g_refs[t * tile // own][low : low + tile, span]
            scores = dot_right(k_head, q_tile) * score_scale
            allowed = pq_ref[:, rows] >= pk_ref[...]
            scores = jnp.where(allowed, scores, masked_score)
            probs = jnp.exp(scores - lse_ref[head : head + 1, rows])
            grad_probs = dot_right(v_head, g_tile)
            delta = jnp.sum(probs * grad_probs, axis=0, keepdims=True)
            grad_scores = (probs * (grad_probs - delta)).astype(bf16)
            grad_query = dot(k_turned, grad_scores).T * score_scale
            gq_ref[rows, span] = grad_query.astype(bf16)
            sums_ref[0:1, span] += column_total(grad_query)
            if t == 0:
                ak_ref[...] = dot(grad_scores, q_tile)
                av_ref[...] = dot(probs.astype(bf16), g_tile)
            else:
                ak_ref[...] += dot(grad_scores, q_tile)
                av_ref[...] += dot(probs.astype(bf16), g_tile)
        gk_ref[:, span] = (ak_ref[...] * score_scale).astype(gk_ref.dtype)
        gv_ref[:, span] = av_ref[...].astype(gv_ref.dtype)
        sums_ref[1:2, span] = column_total(av_ref[...])


def qkv_back_kernel(gq_ref, gk_ref, gv_ref, w_ref, *part_refs):
    own = gq_ref.shape[0] // CHIPS
    for mask in range(CHIPS):
        rows = slice(mask * own, (mask + 1) * own)
        part_refs[mask][...] = (
            dot_right(gq_ref[rows, :], w_ref[:, :COLS])
            + dot_right(gk_ref[rows, :], w_ref[:, COLS : 2 * COLS])
            + dot_right(gv_ref[rows, :], w_ref[:, 2 * COLS :])
        ).astype(part_refs[mask].dtype)


def hidden_kernel(res_ref, *refs):
    parts, (own_ref, send_ref) = refs[:CHIPS], refs[CHIPS:]
    total = res_ref[...] + tree_sum(ref[...].astype(f32) for ref in parts)
    rows = own_ref.shape[0]
    own_ref[...] = total[:rows, :]
    send_ref[...] = total[rows:, :]


def late_grad_kernel(n_shard, ids_ref, *refs):
    k = ids_ref[IK]
    acts, feeds, firsts, inners = (refs[i * CHIPS : (i + 1) * CHIPS] for i in range(4))
    own_ref, send_ref, down_ref, in_ref = refs[4 * CHIPS :]
    down_ref[...] = tree_sum(dot_left(a[...], g[...]) for a, g in zip(acts, feeds))
    in_ref[...] = tree_sum(dot_left(a[...], g[...]) for a, g in zip(firsts, inners))
    few = FF // n_shard // GROUP
    rows_z = D // n_shard
    each = rows_z + 2 * few
    for goal_ref, half in ((own_ref, k), (send_ref, 1 - k)):
        lanes = aligned(half * HALF, HALF)
        for place in range(n_shard):
            base = place * each
            kind = goal_ref.dtype
            goal_ref[base : base + rows_z, :] = in_ref[
                place * rows_z : (place + 1) * rows_z, lanes
            ].astype(kind)
            rows = pl.ds(pl.multiple_of(half * HALF + place * few, few), few)
            goal_ref[base + rows_z : base + rows_z + few, :] = down_ref[rows, :HALF].astype(kind)
            goal_ref[base + rows_z + few : base + each, :] = down_ref[rows, HALF:].astype(kind)


def split_z_kernel(n_shard, ids_ref, own_ref, got_ref, *outs):
    z = ids_ref[IZ]
    each = outs[0].shape[0]
    for mask in range(n_shard):
        rows = aligned((z ^ mask) * each, each)
        outs[mask][...] = (own_ref[rows, :] + got_ref[rows, :].astype(f32)).astype(
            outs[mask].dtype
        )


def sum_kernel(*refs):
    refs[-1][...] = tree_sum(ref[...].astype(f32) for ref in refs[:-1]).astype(bf16)


def late_final_kernel(n_shard, ids_ref, *refs):
    k, j = ids_ref[IK], ids_ref[IJ]
    pieces = refs[:GROUP]
    in_latent_ref, down_latent_ref, in_ref, down_ref, all_ref = refs[GROUP:]
    few = FF // n_shard // GROUP
    rows_z = D // n_shard
    for core in range(CORES):
        for mask in range(CHIPS):
            ref = pieces[core * CHIPS + mask]
            all_ref[(j ^ mask) * CORES + (k ^ core)] = ref[...]
    for number in range(GROUP):
        for place in range(n_shard):
            goal = (place * GROUP + number) * few
            lanes = slice(goal, goal + few)
            grad = all_ref[number, 0:rows_z, place * few : (place + 1) * few].astype(f32)
            keep = jnp.abs(in_latent_ref[:, lanes]) <= 1.0
            in_ref[:, lanes] = jnp.where(keep, grad, 0.0)
        rows = slice(number * few, (number + 1) * few)
        for part in range(2):
            lanes = slice(part * HALF, (part + 1) * HALF)
            low = rows_z + part * few
            grad = all_ref[number, low : low + few, :].astype(f32)
            keep = jnp.abs(down_latent_ref[rows, lanes]) <= 1.0
            down_ref[rows, lanes] = jnp.where(keep, grad, 0.0)


def out_grad_kernel(n_shard, ids_ref, *refs):
    j = ids_ref[IJ]
    h_refs, grad_ref = refs[:CHIPS], refs[CHIPS]
    outs, (cols_ref, full_ref) = refs[CHIPS + 1 : CHIPS + 1 + CHIPS], refs[CHIPS + 1 + CHIPS :]
    half = D // n_shard // CORES
    for chip in range(CHIPS):
        cols_ref[chip] = grad_ref[:, chip * COLS : (chip + 1) * COLS]
    for goal in range(CHIPS):
        cols = cols_ref[j ^ goal]
        for mask in range(CHIPS):
            full_ref[aligned((j ^ mask) * COLS, COLS), :] = dot_left(h_refs[mask][...], cols)
        for core in range(CORES):
            for place in range(n_shard):
                low = (place * CORES + core) * half
                outs[goal][place * half : (place + 1) * half, core * COLS : (core + 1) * COLS] = (
                    full_ref[low : low + half, :].astype(outs[goal].dtype)
                )


def split_hi_lo(values):
    high = values.astype(bf16)
    low = (values - high.astype(f32)).astype(bf16)
    return high, low


def early_grad_kernel(n_shard, ids_ref, *refs):
    k = ids_ref[IK]
    own_x, oth_x, gq_ref, gk_ref, gv_ref = refs[:5]
    outs, refs = refs[5 : 5 + CHIPS], refs[5 + CHIPS :]
    branch_sums, loss_sums, res_sums = refs[:3]
    b1_sums, refs = refs[3 : 3 + CHIPS], refs[3 + CHIPS :]
    qv_sums, own_ref, vec_ref, send_ref, full_ref = refs
    half = D // n_shard // CORES
    rows = own_x.shape[0] // CHIPS
    for number, g_ref in enumerate((gq_ref, gk_ref, gv_ref)):
        parts = []
        for core, x_ref in enumerate((own_x, oth_x)):
            for mask in range(CHIPS):
                goal = slice((mask * CORES + core) * rows, (mask * CORES + core + 1) * rows)
                parts.append(dot_left(x_ref[mask * rows : (mask + 1) * rows, :], g_ref[goal, :]))
        full_ref[:, number * COLS : (number + 1) * COLS] = tree_sum(parts)
    total = tree_sum(ref[...].astype(f32) for ref in outs)
    for place in range(n_shard):
        for core in range(CORES):
            low = (place * CORES + core) * half
            full_ref[low : low + half, QKV:] = total[
                place * half : (place + 1) * half, core * COLS : (core + 1) * COLS
            ]
    for place in range(n_shard):
        goal = slice(place * half, (place + 1) * half)
        mine = pl.ds(pl.multiple_of((place * CORES + k) * half, half), half)
        theirs = pl.ds(pl.multiple_of((place * CORES + 1 - k) * half, half), half)
        own_ref[goal, :] = full_ref[mine, :]
        send_ref[goal, :] = full_ref[theirs, :].astype(bf16)
    lane = lax.broadcasted_iota(jnp.int32, (1, D), 1)
    stats = jnp.zeros((1, D), f32)
    for number, row in enumerate(
        (loss_sums[3:4, :], branch_sums[0:1, :], loss_sums[4:5, :], loss_sums[5:6, :])
    ):
        stats = stats + jnp.where(lane == number, jnp.sum(row, axis=1, keepdims=True), 0.0)
    table = jnp.concatenate(
        [
            res_sums[0:1, :],
            loss_sums[0:1, :],
            res_sums[1:3, :],
            loss_sums[1:3, :],
            stats,
            tree_sum(ref[0:1, :] for ref in b1_sums),
            jnp.concatenate(
                [qv_sums[0:1, :], qv_sums[1:2, :], jnp.zeros((1, D - 2 * COLS), f32)], axis=1
            ),
            jnp.zeros((VEC_ROWS - 9, D), f32),
        ]
    )
    high, low = split_hi_lo(table)
    base = n_shard * half
    send_ref[base : base + VEC_ROWS, :] = high
    send_ref[base + VEC_ROWS : base + 2 * VEC_ROWS, :] = low
    vec_ref[...] = high.astype(f32) + low.astype(f32)


def early_split_kernel(n_shard, ids_ref, own_ref, vec_ref, got_ref, *outs):
    z = ids_ref[IZ]
    half = D // n_shard // CORES
    base = n_shard * half
    table = vec_ref[...] + (
        got_ref[base : base + VEC_ROWS, :].astype(f32)
        + got_ref[base + VEC_ROWS : base + 2 * VEC_ROWS, :].astype(f32)
    )
    high, low = split_hi_lo(table)
    for mask in range(n_shard):
        rows = aligned((z ^ mask) * half, half)
        kind = outs[mask].dtype
        outs[mask][0:half, :] = (own_ref[rows, :] + got_ref[rows, :].astype(f32)).astype(kind)
        outs[mask][half : half + VEC_ROWS, :] = high.astype(kind)
        outs[mask][half + VEC_ROWS : half + 2 * VEC_ROWS, :] = low.astype(kind)


def early_sum_kernel(*refs):
    ins, out_ref = refs[:-1], refs[-1]
    half = out_ref.shape[0] - 2 * VEC_ROWS
    out_ref[0:half, :] = tree_sum(ref[0:half, :].astype(f32) for ref in ins).astype(bf16)
    table = tree_sum(
        ref[half : half + VEC_ROWS, :].astype(f32)
        + ref[half + VEC_ROWS : half + 2 * VEC_ROWS, :].astype(f32)
        for ref in ins
    )
    high, low = split_hi_lo(table)
    out_ref[half : half + VEC_ROWS, :] = high
    out_ref[half + VEC_ROWS : half + 2 * VEC_ROWS, :] = low


def early_final_kernel(n_shard, ids_ref, lengths_ref, *refs):
    k, j = ids_ref[IK], ids_ref[IJ]
    pieces = refs[:GROUP]
    latent_ref, attn_ref, vec_ref, query_ref, stats_ref, all_ref, rows_ref, flat_ref = refs[GROUP:]
    half = D // n_shard // CORES
    few = FF // n_shard // GROUP
    units = FF // n_shard
    for core in range(CORES):
        for mask in range(CHIPS):
            ref = pieces[core * CHIPS + mask]
            all_ref[(j ^ mask) * CORES + (k ^ core)] = ref[0:half, :]
    for chip in range(CHIPS):
        for core in range(CORES):
            for number in range(4):
                lanes = slice(chip * COLS, (chip + 1) * COLS)
                rows = slice(core * half, (core + 1) * half)
                grad = all_ref[
                    chip * CORES + core, :, number * COLS : (number + 1) * COLS
                ].astype(f32)
                keep = jnp.abs(latent_ref[number, rows, lanes]) <= 1.0
                attn_ref[number, rows, lanes] = jnp.where(keep, grad, 0.0)
    tables = [
        pieces[mask][half : half + VEC_ROWS, :].astype(f32)
        + pieces[mask][half + VEC_ROWS : half + 2 * VEC_ROWS, :].astype(f32)
        for mask in range(CHIPS)
    ]
    total = tree_sum(tables)
    for mask in range(CHIPS):
        rows_ref[j ^ mask] = tables[mask]
    count = lengths_ref[0]
    for number in range(1, lengths_ref.shape[0]):
        count = count + lengths_ref[number]
    scale = count.astype(f32) * D
    stats = total[ROW_STATS : ROW_STATS + 1, 0:128] / scale
    lane = lax.broadcasted_iota(jnp.int32, (1, 128), 1)
    stats_ref[...] = jnp.where(lane == 0, stats, jnp.sqrt(stats))
    vec_ref[1:7, :] = total[0:6, :]
    for chip in range(CHIPS):
        lanes = slice(chip * COLS, (chip + 1) * COLS)
        query_ref[:, lanes] = rows_ref[chip, ROW_QV : ROW_QV + 1, 0:COLS]
        vec_ref[0:1, lanes] = rows_ref[chip, ROW_QV : ROW_QV + 1, COLS : 2 * COLS]
        for core in range(CORES):
            for place in range(n_shard):
                start = place * units + (chip * CORES + core) * few
                row, lane = 7 + start // D, start % D
                vec_ref[row : row + 1, lane : lane + few] = rows_ref[
                    chip, ROW_B1 : ROW_B1 + 1, core * HALF + place * few : core * HALF + (place + 1) * few
                ]


def owners_kernel(ids_ref, here_ref, there_ref, out_ref):
    k = ids_ref[IK]
    out_ref[k] = here_ref[...]
    out_ref[1 - k] = there_ref[...]


def body(
    n_ctx,
    n_shard,
    hidden_in,
    block_of,
    lengths,
    attn_latent,
    ffn_in_latent,
    ffn_out_latent,
    student_vec,
    teacher_attn,
    teacher_ffn_in,
    teacher_ffn_out,
    teacher_vec,
):
    seqs, rows, _ = hidden_in.shape
    rest = n_ctx // GROUP
    own = seqs * rows
    tokens = CHIPS * own
    keys = rest * tokens
    ctx = lax.axis_index("ctx")
    z = lax.axis_index("shard")
    ids = jnp.stack([z, ctx % CORES, (ctx // CORES) % CHIPS, ctx // GROUP]).astype(jnp.int32)
    half = D // n_shard // CORES
    few = FF // n_shard // GROUP
    rows_z = D // n_shard
    each = rows_z + 2 * few

    def over_chips(piece, mask):
        return lax.ppermute(piece, "ctx", [(a, a ^ (mask * CORES)) for a in range(n_ctx)])

    def over_cores(piece):
        return lax.ppermute(piece, "ctx", [(a, a ^ 1) for a in range(n_ctx)])

    def over_rest(piece, mask):
        return lax.ppermute(piece, "ctx", [(a, a ^ (mask * GROUP)) for a in range(n_ctx)])

    def over_z(piece, mask):
        return lax.ppermute(piece, "shard", [(a, a ^ mask) for a in range(n_shard)])

    def gather_z(piece):
        return [piece] + [over_z(piece, m) for m in range(1, n_shard)]

    def gather_chips(piece):
        return [piece] + [over_chips(piece, m) for m in range(1, CHIPS)]

    def exchange_chips(pieces):
        return [pieces[0]] + [over_chips(pieces[m], m) for m in range(1, CHIPS)]

    def exchange_z(pieces):
        return [pieces[0]] + [over_z(pieces[m], m) for m in range(1, n_shard)]

    def both_cores(pieces):
        return list(pieces) + [over_cores(piece) for piece in pieces]

    pos_row, pos_col, valid = call(
        functools.partial(places_kernel, rest, seqs=seqs, rows=rows),
        "places",
        (
            shape((1, tokens), jnp.int32),
            shape((keys, 1), jnp.int32),
            shape((own, 1), f32),
        ),
        (ids, block_of, lengths),
        (),
    )
    sums = column_sums(attn_latent, ffn_in_latent, ffn_out_latent)
    sums = tree_sum(gather_z(sums))
    x_own, x_send = call(
        input_kernel,
        "input",
        (shape((tokens // CORES, D)), shape((tokens // CORES, D))),
        (ids,),
        gather_chips(hidden_in),
    )
    x_oth = over_cores(x_send)

    t_early, t_late = weight_pieces(n_shard, ids, teacher_attn, teacher_ffn_in, teacher_ffn_out)
    s_early, s_late = weight_pieces(
        n_shard, ids, attn_latent, ffn_in_latent, ffn_out_latent, sums
    )
    qkv_half, out_half = call(
        functools.partial(early_kernel, n_shard),
        "early_weights",
        (shape((2 * n_shard * half, QKV)), shape((n_shard * half, 2 * COLS))),
        (ids,),
        gather_z(t_early) + gather_z(s_early),
    )
    qkv_peer = over_cores(qkv_half)
    t_out, s_out = call(
        functools.partial(out_weight_kernel, n_shard),
        "out_weights",
        (shape((CHIPS, D, COLS)), shape((CHIPS, D, COLS))),
        (ids,),
        both_cores(gather_chips(out_half)),
    )

    def late_weights(piece, vector):
        return call(
            functools.partial(late_kernel, n_shard),
            "late_weights",
            (shape((D, UNITS)), shape((UNITS, D)), shape((8, UNITS), f32)),
            (ids,),
            both_cores(gather_z(piece)) + [vector],
        )

    t_late = late_weights(t_late, teacher_vec)
    s_late = late_weights(s_late, student_vec)

    def rest_gather(values):
        if rest == 1:
            return values
        return jnp.concatenate([values] + [over_rest(values, m) for m in range(1, rest)])

    def rest_scatter(partial):
        if rest == 1:
            return partial
        view = partial.reshape(rest, tokens, partial.shape[1])
        return tree_sum(
            [view[0]] + [over_rest(view[m].astype(bf16), m).astype(f32) for m in range(1, rest)]
        ).astype(bf16)

    def rest_total(piece):
        if rest == 1:
            return piece
        return call(
            early_sum_kernel if piece.shape[1] == D else sum_kernel,
            "rest_sum",
            shape(piece.shape),
            (),
            [piece] + [over_rest(piece, m) for m in range(1, rest)],
        )

    def attention(model, vector):
        query, key, value, w_qkv = call(
            functools.partial(qkv_kernel, n_shard, model),
            "qkv",
            (
                shape((tokens, COLS)),
                shape((tokens, COLS)),
                shape((tokens, COLS)),
                shape((D, QKV)),
            ),
            (ids,),
            (x_own, x_oth, qkv_half, qkv_peer, vector),
        )
        key, value = rest_gather(key), rest_gather(value)
        *heads, lse = call(
            functools.partial(attend_kernel, tile=own),
            "attend",
            tuple([shape((own, COLS))] * CHIPS + [shape((HEADS_HERE, tokens), f32)]),
            (),
            (query, key, value, pos_row, pos_col),
        )
        return query, key, value, w_qkv, lse, exchange_chips(heads)

    def branch(student, heads, w_out, vector):
        outs = [shape((own, D), f32), shape((own, D))]
        if student:
            outs += [shape((own, D), f32), shape((8, D), f32)]
        return call(
            functools.partial(branch_kernel, student),
            "branch",
            tuple(outs),
            (ids,),
            (*heads, w_out, x_own, x_oth, vector, valid),
        )

    def feed(student, piece, mask, late):
        outs = [shape((own, D), f32 if mask == 0 else bf16)]
        if student:
            outs += [shape((own, UNITS), f32), shape((own, UNITS))]
        return call(
            functools.partial(feed_kernel, student), "feed", tuple(outs), (), (piece, *late)
        )

    t_heads = attention(0, teacher_vec)[-1]
    query, key, value, w_qkv, lse, heads = attention(1, student_vec)

    t_first, sent = branch(False, t_heads, t_out, teacher_vec)
    parts = [feed(False, p, m, t_late)[0] for m, p in enumerate(gather_chips(sent))]
    target = call(
        target_kernel,
        "target",
        shape((own, D), f32),
        (),
        (*exchange_chips(parts), t_first, teacher_vec),
    )

    first, sent, residual, branch_sums = branch(True, heads, s_out, student_vec)
    firsts = gather_chips(sent)
    w_in, w_down, _ = s_late
    fed = [feed(True, p, m, s_late) for m, p in enumerate(firsts)]
    parts, inners, acts = ([f[i] for f in fed] for i in range(3))
    out, grad_second, sent, loss_sums = call(
        loss_kernel,
        "loss",
        (shape((own, D)), shape((own, D), f32), shape((own, D)), shape((8, D), f32)),
        (lengths,),
        (*exchange_chips(parts), first, student_vec, target, valid),
    )

    feeds = gather_chips(sent)
    backs = [
        call(
            feed_back_kernel,
            "feed_back",
            (
                shape((own, D), f32 if m == 0 else bf16),
                shape((own, UNITS)),
                shape((8, UNITS), f32),
            ),
            (),
            (feeds[m], inners[m], w_in, w_down),
        )
        for m in range(CHIPS)
    ]
    parts, grad_inners, b1_sums = ([b[i] for b in backs] for i in range(3))
    grad_res, grad_branch, *rest_outs = call(
        branch_back_kernel,
        "branch_back",
        tuple(
            [shape((own, D), f32), shape((own, D))]
            + [shape((own, COLS))] * CHIPS
            + [shape((8, D), f32)]
        ),
        (ids,),
        (*exchange_chips(parts), grad_second, residual, student_vec, s_out),
    )
    grad_heads, res_sums = exchange_chips(rest_outs[:CHIPS]), rest_outs[CHIPS]

    kind = bf16 if rest == 1 else f32
    grad_query, grad_key, grad_value, qv_sums = call(
        functools.partial(attend_back_kernel, tile=own),
        "attend_back",
        (
            shape((tokens, COLS)),
            shape((keys, COLS), kind),
            shape((keys, COLS), kind),
            shape((8, COLS), f32),
        ),
        (),
        (query, key, value, *grad_heads, lse, pos_row, pos_col),
        (pltpu.VMEM((keys, HEAD_DIM), f32), pltpu.VMEM((keys, HEAD_DIM), f32)),
    )
    grad_key, grad_value = rest_scatter(grad_key), rest_scatter(grad_value)
    parts = call(
        qkv_back_kernel,
        "qkv_back",
        tuple(shape((own, D), f32 if m == 0 else bf16) for m in range(CHIPS)),
        (),
        (grad_query, grad_key, grad_value, w_qkv),
    )
    here, there = call(
        hidden_kernel,
        "hidden",
        (shape((rows, D), f32), shape((rows, D), f32)),
        (),
        (grad_res, *exchange_chips(parts)),
    )

    def to_owners(here, there):
        return call(
            owners_kernel,
            "owners",
            shape((CORES, *here.shape), here.dtype),
            (ids,),
            (here, over_cores(there)),
        )

    grad_hidden = to_owners(here, there)
    output = to_owners(out[:rows], out[rows:])

    mine, send = call(
        functools.partial(late_grad_kernel, n_shard),
        "late_grad",
        (shape((n_shard * each, HALF), f32), shape((n_shard * each, HALF))),
        (ids,),
        (*acts, *feeds, *firsts, *grad_inners),
        (pltpu.VMEM((UNITS, D), f32), pltpu.VMEM((D, UNITS), f32)),
    )
    pieces = call(
        functools.partial(split_z_kernel, n_shard),
        "late_split",
        tuple(shape((each, HALF), f32 if m == 0 else bf16) for m in range(n_shard)),
        (ids,),
        (mine, over_cores(send)),
    )
    piece = call(sum_kernel, "late_sum", shape((each, HALF)), (), exchange_z(pieces))
    in_grad, down_grad = call(
        functools.partial(late_final_kernel, n_shard),
        "late_final",
        (shape(ffn_in_latent.shape, f32), shape(ffn_out_latent.shape, f32)),
        (ids,),
        (*both_cores(gather_chips(rest_total(piece))), ffn_in_latent, ffn_out_latent),
        (pltpu.VMEM((GROUP, each, HALF), bf16),),
    )

    pieces = call(
        functools.partial(out_grad_kernel, n_shard),
        "out_grad",
        tuple(
            shape((n_shard * half, 2 * COLS), f32 if m == 0 else bf16) for m in range(CHIPS)
        ),
        (ids,),
        (*heads, grad_branch),
        (pltpu.VMEM((CHIPS, own, COLS), bf16), pltpu.VMEM((D, COLS), f32)),
    )
    mine, table, send = call(
        functools.partial(early_grad_kernel, n_shard),
        "early_grad",
        (
            shape((n_shard * half, D), f32),
            shape((VEC_ROWS, D), f32),
            shape((n_shard * half + 2 * VEC_ROWS, D)),
        ),
        (ids,),
        (
            x_own,
            x_oth,
            grad_query,
            grad_key,
            grad_value,
            *exchange_chips(pieces),
            branch_sums,
            loss_sums,
            res_sums,
            *b1_sums,
            qv_sums,
        ),
        (pltpu.VMEM((D, D), f32),),
    )
    pieces = call(
        functools.partial(early_split_kernel, n_shard),
        "early_split",
        tuple(
            shape((half + 2 * VEC_ROWS, D), f32 if m == 0 else bf16) for m in range(n_shard)
        ),
        (ids,),
        (mine, table, over_cores(send)),
    )
    piece = call(
        early_sum_kernel, "early_sum", shape((half + 2 * VEC_ROWS, D)), (), exchange_z(pieces)
    )
    attn_grad, vec_grad, query_grad, stats = call(
        functools.partial(early_final_kernel, n_shard),
        "early_final",
        (
            shape(attn_latent.shape, f32),
            shape((7 + FF // D, D), f32),
            shape((1, D), f32),
            shape((1, 128), f32),
        ),
        (ids, lengths),
        (*both_cores(gather_chips(rest_total(piece))), attn_latent),
        (
            pltpu.VMEM((GROUP, half, D), bf16),
            pltpu.VMEM((CHIPS, VEC_ROWS, D), f32),
            pltpu.VMEM((8, D), f32),
        ),
    )
    return (
        output,
        stats[0, :4],
        grad_hidden,
        attn_grad,
        in_grad,
        down_grad,
        vec_grad,
        query_grad[0],
    )


def solution(mesh):
    n_ctx, n_shard = mesh.shape["ctx"], mesh.shape["shard"]
    in_specs = (
        P("shard", "ctx", None),
        P(),
        P(),
        P(None, "shard", None),
        P("shard", None),
        P("shard", None),
        P(),
        P(None, "shard", None),
        P("shard", None),
        P("shard", None),
        P(),
    )
    out_specs = (
        P("shard", "ctx", None),
        P(),
        P("shard", "ctx", None),
        P(None, "shard", None),
        P("shard", None),
        P("shard", None),
        P(),
        P(),
    )
    return jax.shard_map(
        functools.partial(body, n_ctx, n_shard),
        mesh=mesh,
        in_specs=in_specs,
        out_specs=out_specs,
        check_vma=False,
    )
```

time: 688 us -> 476 us (0.69)
  the two profiles are of different devices: /device:TPU:0 before, /device:TPU:9 now
where the time goes in v2:
time: 476 us; the launch traced here: 470 us
  Pallas kernels  189 us (40%)
  waiting for transfers between devices  158 us (33%)
  starting transfers between devices  100 us (21%)
  local copies, waits for them, and re-layouts  18.7 us (4%)
    pallas_call x41, Pallas kernels, call(): pl.pallas_call(kernel, out_shape=outs, in_specs=[SMEM_SPEC] * len(scalars...  177 us
    ppermute x45, waiting for transfers between devices, over_chips(): lax.ppermute(piece, 'ctx', [(a, a ^ mask * CORES) for a in range(n_ctx)])  82.3 us
    ppermute x21, waiting for transfers between devices, over_z(): return lax.ppermute(piece, 'shard', [(a, a ^ mask) for a in range(n_shard)])  76 us
    ppermute x45, starting transfers between devices, over_chips(): lax.ppermute(piece, 'ctx', [(a, a ^ mask * CORES) for a in range(n_ctx)])  41 us
    ppermute x21, starting transfers between devices, over_z(): return lax.ppermute(piece, 'shard', [(a, a ^ mask) for a in range(n_shard)])  30.4 us
    ppermute x26, starting transfers between devices, over_cores(): return lax.ppermute(piece, 'ctx', [(a, a ^ 1) for a in range(n_ctx)])  28.7 us
    unnamed x176, local copies, waits for them, and re-layouts  13.5 us
  transfers between devices with their start and end apart: 92, of which 24 were waited for; matrix products, arithmetic and copies ran while one was open for 2% of the time, Pallas kernels for 37%

profile of v2, /device:TPU:9, one launch (start us, length us, event | category | flops | bytes accessed | tf_op | source)
XLA Modules:
  0.0 470.4 jit_solution(4083808867450317788)
XLA Ops:
  0.6 4.5 column_sums.1
  9.2 3.8 teacher_pieces.1
  19.3 4.6 student_pieces.1
  25.9 4.0 collective-permute-start.11
  30.6 11.2 %collective-permute-done.12.refs_7_ = bf16[96,768]{1,0:T(8,128)(2,1)S(1)} collective-permute-done((bf16[96,768]{1,0:T(8,128)(2,1)}, bf16[96,768]{1,0:T(8,128)(2,1)S(1)}, u32[]{:S(2)}, u32[]{:S(2)}) %collective-permute-start.12) | collective-permute-done | bytes 147488 | tf_op jit(solution)/shard_map/ppermute | solution.py:811
  41.8 15.9 %collective-permute-done.11.refs_6_ = bf16[96,768]{1,0:T(8,128)(2,1)S(1)} collective-permute-done((bf16[96,768]{1,0:T(8,128)(2,1)}, bf16[96,768]{1,0:T(8,128)(2,1)S(1)}, u32[]{:S(2)}, u32[]{:S(2)}) %collective-permute-start.11) | collective-permute-done | bytes 147488 | tf_op jit(solution)/shard_map/ppermute | solution.py:811
  66.8 4.9 %collective-permute-done.40.refs_1_ = bf16[384,384]{1,0:T(8,128)(2,1)S(1)} collective-permute-done((bf16[384,384]{1,0:T(8,128)(2,1)S(1)}, bf16[384,384]{1,0:T(8,128)(2,1)S(1)}, u32[]{:S(2)}, u32[]{:S(2)}) %collective-permute-start.40) | collective-permute-done | bytes 294944 | tf_op jit(solution)/shard_map/ppermute | solution.py:811
  85.6 7.2 %collective-permute-done.26.refs_3_ = bf16[384,384]{1,0:T(8,128)(2,1)} collective-permute-done((bf16[384,384]{1,0:T(8,128)(2,1)}, bf16[384,384]{1,0:T(8,128)(2,1)}, u32[]{:S(2)}, u32[]{:S(2)}) %collective-permute-start.26) | collective-permute-done | bytes 294944 | tf_op jit(solution)/shard_map/ppermute | solution.py:811
  100.7 5.4 %collective-permute-done.19.refs_3_ = bf16[384,384]{1,0:T(8,128)(2,1)S(1)} collective-permute-done((bf16[384,384]{1,0:T(8,128)(2,1)S(1)}, bf16[384,384]{1,0:T(8,128)(2,1)S(1)}, u32[]{:S(2)}, u32[]{:S(2)}) %collective-permute-start.19) | collective-permute-done | bytes 294944 | tf_op jit(solution)/shard_map/ppermute | solution.py:802
  106.1 4.1 collective-permute-start.23
  110.3 4.0 collective-permute-done.18.refs_2_
  119.4 4.6 qkv.3
  124.0 11.2 %attend.3 = (bf16[256,192]{1,0:T(8,128)(2,1)}, bf16[256,192]{1,0:T(8,128)(2,1)}, bf16[256,192]{1,0:T(8,128)(2,1)}, bf16[256,192]{1,0:T(8,128)(2,1)}, f32[3,1024]{1,0:T(4,128)}) custom-call(bf16[1024,192]{1,0:T(8,128)(2,1)} %get-tuple-element.144.q_ref, bf16[1024,192]{1,0:T(8,128)(2,1)} %get-tuple-element.145.k_ref, ...), custom_call_target="tpu_custom_call" | custom-call | tf_op jit(solution)/shard_map/attend/pallas_call | solution.py:76
  137.0 3.5 collective-permute-done.37.refs_1_
  142.1 3.7 out_weights.1
  145.8 4.6 qkv.2
  150.4 11.4 %attend.2 = (bf16[256,192]{1,0:T(8,128)(2,1)}, bf16[256,192]{1,0:T(8,128)(2,1)}, bf16[256,192]{1,0:T(8,128)(2,1)}, bf16[256,192]{1,0:T(8,128)(2,1)}, f32[3,1024]{1,0:T(4,128)}) custom-call(bf16[1024,192]{1,0:T(8,128)(2,1)} %get-tuple-element.122.q_ref.refs_0_, bf16[1024,192]{1,0:T(8,128)(2,1)} %get-tuple-element.123.k_ref.refs_1_, ...), custom_call_target="tpu_custom_call" | custom-call | tf_op jit(solution)/shard_map/attend/pallas_call | solution.py:76
  163.4 4.1 branch.3
  176.4 4.5 branch.2
  192.9 3.5 late_weights.2
  196.4 3.4 feed.14
  200.6 3.4 feed.13
  204.8 3.5 feed.9
  209.1 3.5 feed.10
  213.4 3.5 feed.11
  218.2 3.6 feed.12.refs_0_
  221.8 3.6 feed.8
  235.9 6.5 %collective-permute-done.36.refs_3_ = bf16[256,768]{1,0:T(8,128)(2,1)S(1)} collective-permute-done((bf16[256,768]{1,0:T(8,128)(2,1)}, bf16[256,768]{1,0:T(8,128)(2,1)S(1)}, u32[]{:S(2)}, u32[]{:S(2)}) %collective-permute-start.36) | collective-permute-done | bytes 393248 | tf_op jit(solution)/shard_map/ppermute | solution.py:802
  243.2 4.0 loss.1
  249.9 7.6 %collective-permute-done.58.piece_ref.refs_7_ = bf16[256,768]{1,0:T(8,128)(2,1)S(1)} collective-permute-done((bf16[256,768]{1,0:T(8,128)(2,1)}, bf16[256,768]{1,0:T(8,128)(2,1)S(1)}, u32[]{:S(2)}, u32[]{:S(2)}) %collective-permute-start.58) | collective-permute-done | bytes 393248 | tf_op jit(solution)/shard_map/ppermute | solution.py:802
  258.3 3.7 feed_back.7
  263.0 6.6 %collective-permute-done.56.piece_ref.refs_6_ = bf16[256,768]{1,0:T(8,128)(2,1)S(1)} collective-permute-done((bf16[256,768]{1,0:T(8,128)(2,1)}, bf16[256,768]{1,0:T(8,128)(2,1)S(1)}, u32[]{:S(2)}, u32[]{:S(2)}) %collective-permute-start.56) | collective-permute-done | bytes 393248 | tf_op jit(solution)/shard_map/ppermute | solution.py:802
  270.4 3.7 feed_back.6
  275.3 3.7 feed_back.5
  280.0 3.9 feed_back.4
  283.9 7.9 %late_grad.1 = (f32[1536,384]{1,0:T(8,128)}, bf16[1536,384]{1,0:T(8,128)(2,1)}) custom-call(s32[4]{0:T(128)} %pad_add_fusion.ids_ref, bf16[256,768]{1,0:T(8,128)(2,1)} %get-tuple-element.208.refs_0_, bf16[256,768]{1,0:T(8,128)(2,1)} %get-tuple-element.209.refs_1_, bf16[256,768]{1,0:T(8,128)(2,1)} %get-tuple-element.210.refs_2_, ...), custom_call_target="tpu_custom_call" | custom-call | tf_op jit(solution)/shard_map/late_grad/pallas_call | solution.py:76
  293.9 4.7 branch_back.1
  306.2 14.6 %collective-permute-done.61.refs_5_ = bf16[256,192]{1,0:T(8,128)(2,1)S(1)} collective-permute-done((bf16[256,192]{1,0:T(8,128)(2,1)}, bf16[256,192]{1,0:T(8,128)(2,1)S(1)}, u32[]{:S(2)}, u32[]{:S(2)}) %collective-permute-start.61) | collective-permute-done | bytes 98336 | tf_op jit(solution)/shard_map/ppermute | solution.py:802
  322.0 3.7 collective-permute-done.62.refs_6_
  326.3 14.8 %attend_back.1 = (bf16[1024,192]{1,0:T(8,128)(2,1)}, bf16[1024,192]{1,0:T(8,128)(2,1)}, bf16[1024,192]{1,0:T(8,128)(2,1)}, f32[8,192]{1,0:T(8,128)}) custom-call(bf16[1024,192]{1,0:T(8,128)(2,1)} %get-tuple-element.122.q_ref.refs_0_, bf16[1024,192]{1,0:T(8,128)(2,1)} %get-tuple-element.123.k_ref.refs_1_, bf16[1024,192]{1,0:T(8,128)(2,1)} %get-tuple-element.124.v_ref.refs_2_, ...), custom_call_target="tpu_custom_call" | custom-call | tf_op jit(solution)/shard_map/attend_back/pallas_call | solution.py:76
  342.1 6.5 %early_grad.1 = (f32[384,768]{1,0:T(8,128)}, f32[16,768]{1,0:T(8,128)}, bf16[416,768]{1,0:T(8,128)(2,1)}) custom-call(s32[4]{0:T(128)} %pad_add_fusion.ids_ref, bf16[512,768]{1,0:T(8,128)(2,1)} %get-tuple-element.117.own_ref.refs_5_.refs_0_, bf16[512,768]{1,0:T(8,128)(2,1)} %copy-done, bf16[1024,192]{1,0:T(8,128)(2,1)} %get-tuple-element.175.refs_2_.gq_ref, ...), custom_call_target="tpu_custom_call" | custom-call | tf_op jit(solution)/shard_map/early_grad/pallas_call | solution.py:76
  351.2 4.1 qkv_back.1
  369.3 5.6 %collective-permute-done.79.refs_3_ = bf16[256,768]{1,0:T(8,128)(2,1)S(1)} collective-permute-done((bf16[256,768]{1,0:T(8,128)(2,1)}, bf16[256,768]{1,0:T(8,128)(2,1)S(1)}, u32[]{:S(2)}, u32[]{:S(2)}) %collective-permute-start.79) | collective-permute-done | bytes 393248 | tf_op jit(solution)/shard_map/ppermute | solution.py:802
  389.2 32.9 %collective-permute-done.69.refs_3_ = bf16[128,768]{1,0:T(8,128)(2,1)S(1)} collective-permute-done((bf16[128,768]{1,0:T(8,128)(2,1)S(1)}, bf16[128,768]{1,0:T(8,128)(2,1)S(1)}, u32[]{:S(2)}, u32[]{:S(2)}) %collective-permute-start.69) | collective-permute-done | bytes 196640 | tf_op jit(solution)/shard_map/ppermute | solution.py:811
  434.1 9.9 %collective-permute-done.71.refs_2_ = bf16[128,768]{1,0:T(8,128)(2,1)S(1)} collective-permute-done((bf16[128,768]{1,0:T(8,128)(2,1)S(1)}, bf16[128,768]{1,0:T(8,128)(2,1)S(1)}, u32[]{:S(2)}, u32[]{:S(2)}) %collective-permute-start.71) | collective-permute-done | bytes 196640 | tf_op jit(solution)/shard_map/ppermute | solution.py:802
  445.2 5.2 %collective-permute-done.86.refs_2_ = bf16[384,384]{1,0:T(8,128)(2,1)S(1)} collective-permute-done((bf16[384,384]{1,0:T(8,128)(2,1)}, bf16[384,384]{1,0:T(8,128)(2,1)S(1)}, u32[]{:S(2)}, u32[]{:S(2)}) %collective-permute-start.86) | collective-permute-done | bytes 294944 | tf_op jit(solution)/shard_map/ppermute | solution.py:802
  455.5 4.3 early_final.1
  463.9 6.4 %late_final.1 = (f32[192,3072]{1,0:T(8,128)}, f32[768,768]{1,0:T(8,128)}) custom-call(s32[4]{0:T(128)} %pad_add_fusion.ids_ref, bf16[384,384]{1,0:T(8,128)(2,1)} %late_sum.1.refs_0_, bf16[384,384]{1,0:T(8,128)(2,1)} %copy-done.38, bf16[384,384]{1,0:T(8,128)(2,1)} %copy-done.37, bf16[384,384]{1,0:T(8,128)(2,1)} %copy-done.36, bf16[384,384]{1,0:T(8,128)(2,1)} %copy-done.39, ...), custom_call_target="tpu_custom_call" | custom-call | tf_op jit(solution)/shard_map/late_final/pallas_call | solution.py:76
  (363 shorter events, 163.5 us)
Async XLA Ops:
  16.6 45.1 %collective-permute-start.43 = (bf16[384,384]{1,0:T(8,128)(2,1)}, bf16[384,384]{1,0:T(8,128)(2,1)S(1)}, u32[]{:S(2)}, u32[]{:S(2)}) collective-permute-start(bf16[384,384]{1,0:T(8,128)(2,1)} %get-tuple-element.153.refs_0_), channel_id=1, source_target_pairs={{0,4},{4,0},{8,12},{12,8},{16,20},{20,16},{24,28},{28,24},{1,5},{5... | collective-permute-start | bytes 884744 | tf_op jit(solution)/shard_map/ppermute | solution.py:805
  25.2 37.8 %collective-permute-start.42 = (bf16[384,384]{1,0:T(8,128)(2,1)S(1)}, bf16[384,384]{1,0:T(8,128)(2,1)S(1)}, u32[]{:S(2)}, u32[]{:S(2)}) collective-permute-start(bf16[384,384]{1,0:T(8,128)(2,1)S(1)} %copy-done.54), channel_id=1, source_target_pairs={{0,3},{1,2},{2,1},{3,0},{4,7},{5,6},{6,5},{7,4},{8,11},{9,10},{10,... | collective-permute-start | bytes 884744 | tf_op jit(solution)/shard_map/ppermute | solution.py:811
  25.9 31.8 %collective-permute-start.11 = (bf16[96,768]{1,0:T(8,128)(2,1)}, bf16[96,768]{1,0:T(8,128)(2,1)S(1)}, u32[]{:S(2)}, u32[]{:S(2)}) collective-permute-start(bf16[96,768]{1,0:T(8,128)(2,1)} %get-tuple-element.120.refs_4_), channel_id=1, source_target_pairs={{0,2},{1,3},{2,0},{3,1},{4,6},{5,7},{6,4},{7,5},{8,10},{9,11},{10,... | collective-permute-start | bytes 442376 | tf_op jit(solution)/shard_map/ppermute | solution.py:811
  29.9 30.4 %collective-permute-start.10 = (bf16[96,768]{1,0:T(8,128)(2,1)}, bf16[96,768]{1,0:T(8,128)(2,1)S(1)}, u32[]{:S(2)}, u32[]{:S(2)}) collective-permute-start(bf16[96,768]{1,0:T(8,128)(2,1)} %get-tuple-element.120.refs_4_), channel_id=1, source_target_pairs={{0,1},{1,0},{2,3},{3,2},{4,5},{5,4},{6,7},{7,6},{8,9},{9,8},{10,11... | collective-permute-start | bytes 442376 | tf_op jit(solution)/shard_map/ppermute | solution.py:811
  41.8 22.2 %collective-permute-start.41 = (bf16[384,384]{1,0:T(8,128)(2,1)S(1)}, bf16[384,384]{1,0:T(8,128)(2,1)S(1)}, u32[]{:S(2)}, u32[]{:S(2)}) collective-permute-start(bf16[384,384]{1,0:T(8,128)(2,1)S(1)} %copy-done.54), channel_id=1, source_target_pairs={{0,2},{1,3},{2,0},{3,1},{4,6},{5,7},{6,4},{7,5},{8,10},{9,11},{10,... | collective-permute-start | bytes 884744 | tf_op jit(solution)/shard_map/ppermute | solution.py:811
  61.7 18.8 %collective-permute-start = (bf16[2,128,768]{2,1,0:T(8,128)(2,1)S(1)}, bf16[2,128,768]{2,1,0:T(8,128)(2,1)S(1)}, u32[]{:S(2)}, u32[]{:S(2)}) collective-permute-start(bf16[2,128,768]{2,1,0:T(8,128)(2,1)S(1)} %copy-done.22), channel_id=1, source_target_pairs={{0,8},{4,12},{8,0},{12,4},{16,24},{20,28},{24,16},{28,20},{1,9},{5... | collective-permute-start | bytes 1179656 | tf_op jit(solution)/shard_map/ppermute | solution.py:802
  62.9 18.6 %collective-permute-start.2 = (bf16[2,128,768]{2,1,0:T(8,128)(2,1)S(1)}, bf16[2,128,768]{2,1,0:T(8,128)(2,1)S(1)}, u32[]{:S(2)}, u32[]{:S(2)}) collective-permute-start(bf16[2,128,768]{2,1,0:T(8,128)(2,1)S(1)} %copy-done.22), channel_id=1, source_target_pairs={{0,24},{4,28},{8,16},{12,20},{16,8},{20,12},{24,0},{28,4},{1,25},{... | collective-permute-start | bytes 1179656 | tf_op jit(solution)/shard_map/ppermute | solution.py:802
  63.9 21.2 %collective-permute-start.27 = (bf16[384,384]{1,0:T(8,128)(2,1)}, bf16[384,384]{1,0:T(8,128)(2,1)S(1)}, u32[]{:S(2)}, u32[]{:S(2)}) collective-permute-start(bf16[384,384]{1,0:T(8,128)(2,1)} %get-tuple-element.135.refs_0_), channel_id=1, source_target_pairs={{0,4},{4,0},{8,12},{12,8},{16,20},{20,16},{24,28},{28,24},{1,5},{5... | collective-permute-start | bytes 884744 | tf_op jit(solution)/shard_map/ppermute | solution.py:805
  71.7 21.0 %collective-permute-start.26 = (bf16[384,384]{1,0:T(8,128)(2,1)}, bf16[384,384]{1,0:T(8,128)(2,1)}, u32[]{:S(2)}, u32[]{:S(2)}) collective-permute-start(bf16[384,384]{1,0:T(8,128)(2,1)} %get-tuple-element.135.refs_0_), channel_id=1, source_target_pairs={{0,3},{1,2},{2,1},{3,0},{4,7},{5,6},{6,5},{7,4},{8,11},{9,10},{10,... | collective-permute-start | bytes 884744 | tf_op jit(solution)/shard_map/ppermute | solution.py:811
  72.9 25.2 %collective-permute-start.25 = (bf16[384,384]{1,0:T(8,128)(2,1)}, bf16[384,384]{1,0:T(8,128)(2,1)}, u32[]{:S(2)}, u32[]{:S(2)}) collective-permute-start(bf16[384,384]{1,0:T(8,128)(2,1)} %get-tuple-element.135.refs_0_), channel_id=1, source_target_pairs={{0,2},{1,3},{2,0},{3,1},{4,6},{5,7},{6,4},{7,5},{8,10},{9,11},{10,... | collective-permute-start | bytes 884744 | tf_op jit(solution)/shard_map/ppermute | solution.py:811
  80.5 34.8 %collective-permute-start.13 = (bf16[768,576]{0,1:T(8,128)(2,1)S(1)}, bf16[768,576]{0,1:T(8,128)(2,1)S(1)}, u32[]{:S(2)}, u32[]{:S(2)}) collective-permute-start(bf16[768,576]{0,1:T(8,128)(2,1)S(1)} %copy.19), channel_id=1, source_target_pairs={{0,4},{4,0},{8,12},{12,8},{16,20},{20,16},{24,28},{28,24},{1,5},{5... | collective-permute-start | bytes 2654216 | tf_op jit(solution)/shard_map/ppermute | solution.py:805
  81.6 18.6 %collective-permute-start.24 = (bf16[384,384]{1,0:T(8,128)(2,1)}, bf16[384,384]{1,0:T(8,128)(2,1)}, u32[]{:S(2)}, u32[]{:S(2)}) collective-permute-start(bf16[384,384]{1,0:T(8,128)(2,1)} %get-tuple-element.135.refs_0_), channel_id=1, source_target_pairs={{0,1},{1,0},{2,3},{3,2},{4,5},{5,4},{6,7},{7,6},{8,9},{9,8},{10,11... | collective-permute-start | bytes 884744 | tf_op jit(solution)/shard_map/ppermute | solution.py:811
  85.1 30.3 %collective-permute-start.3 = (bf16[512,768]{1,0:T(8,128)(2,1)}, bf16[512,768]{1,0:T(8,128)(2,1)S(1)}, u32[]{:S(2)}, u32[]{:S(2)}) collective-permute-start(bf16[512,768]{1,0:T(8,128)(2,1)} %get-tuple-element.118), channel_id=1, source_target_pairs={{0,4},{4,0},{8,12},{12,8},{16,20},{20,16},{24,28},{28,24},{1,5},{5... | collective-permute-start | bytes 2359304 | tf_op jit(solution)/shard_map/ppermute | solution.py:805
  114.3 20.9 %collective-permute-start.22 = (bf16[384,384]{1,0:T(8,128)(2,1)}, bf16[384,384]{1,0:T(8,128)(2,1)}, u32[]{:S(2)}, u32[]{:S(2)}) collective-permute-start(bf16[384,384]{1,0:T(8,128)(2,1)} %collective-permute-done.18.refs_2_), channel_id=1, source_target_pairs={{0,4},{4,0},{8,12},{12,8},{16,20},{20,16},{24,28},{28,24},{1,5},{5... | collective-permute-start | bytes 884744 | tf_op jit(solution)/shard_map/ppermute | solution.py:805
  114.8 21.7 %collective-permute-start.21 = (bf16[384,384]{1,0:T(8,128)(2,1)}, bf16[384,384]{1,0:T(8,128)(2,1)S(1)}, u32[]{:S(2)}, u32[]{:S(2)}) collective-permute-start(bf16[384,384]{1,0:T(8,128)(2,1)} %collective-permute-done.17.refs_1_), channel_id=1, source_target_pairs={{0,4},{4,0},{8,12},{12,8},{16,20},{20,16},{24,28},{28,24},{1,5},{5... | collective-permute-start | bytes 884744 | tf_op jit(solution)/shard_map/ppermute | solution.py:805
  114.9 52.6 %collective-permute-start.46 = (bf16[384,384]{1,0:T(8,128)(2,1)}, bf16[384,384]{1,0:T(8,128)(2,1)}, u32[]{:S(2)}, u32[]{:S(2)}) collective-permute-start(bf16[384,384]{1,0:T(8,128)(2,1)} %copy-done.56), channel_id=1, source_target_pairs={{0,4},{4,0},{8,12},{12,8},{16,20},{20,16},{24,28},{28,24},{1,5},{5... | collective-permute-start | bytes 884744 | tf_op jit(solution)/shard_map/ppermute | solution.py:805
  115.3 53.4 %collective-permute-start.45 = (bf16[384,384]{1,0:T(8,128)(2,1)}, bf16[384,384]{1,0:T(8,128)(2,1)S(1)}, u32[]{:S(2)}, u32[]{:S(2)}) collective-permute-start(bf16[384,384]{1,0:T(8,128)(2,1)} %copy-done.57), channel_id=1, source_target_pairs={{0,4},{4,0},{8,12},{12,8},{16,20},{20,16},{24,28},{28,24},{1,5},{5... | collective-permute-start | bytes 884744 | tf_op jit(solution)/shard_map/ppermute | solution.py:805
  115.6 54.4 %collective-permute-start.44 = (bf16[384,384]{1,0:T(8,128)(2,1)}, bf16[384,384]{1,0:T(8,128)(2,1)S(1)}, u32[]{:S(2)}, u32[]{:S(2)}) collective-permute-start(bf16[384,384]{1,0:T(8,128)(2,1)} %copy-done.59), channel_id=1, source_target_pairs={{0,4},{4,0},{8,12},{12,8},{16,20},{20,16},{24,28},{28,24},{1,5},{5... | collective-permute-start | bytes 884744 | tf_op jit(solution)/shard_map/ppermute | solution.py:805
  136.5 25.3 %collective-permute-start.38 = (bf16[256,192]{1,0:T(8,128)(2,1)}, bf16[256,192]{1,0:T(8,128)(2,1)S(1)}, u32[]{:S(2)}, u32[]{:S(2)}) collective-permute-start(bf16[256,192]{1,0:T(8,128)(2,1)} %get-tuple-element.149), channel_id=1, source_target_pairs={{0,16},{4,20},{8,24},{12,28},{16,0},{20,4},{24,8},{28,12},{1,17},{... | collective-permute-start | bytes 294920 | tf_op jit(solution)/shard_map/ppermute | solution.py:802
  140.5 22.2 %collective-permute-start.39 = (bf16[256,192]{1,0:T(8,128)(2,1)}, bf16[256,192]{1,0:T(8,128)(2,1)S(1)}, u32[]{:S(2)}, u32[]{:S(2)}) collective-permute-start(bf16[256,192]{1,0:T(8,128)(2,1)} %get-tuple-element.150), channel_id=1, source_target_pairs={{0,24},{4,28},{8,16},{12,20},{16,8},{20,12},{24,0},{28,4},{1,25},{... | collective-permute-start | bytes 294920 | tf_op jit(solution)/shard_map/ppermute | solution.py:802
  168.7 18.4 %collective-permute-start.51 = (bf16[256,768]{1,0:T(8,128)(2,1)}, bf16[256,768]{1,0:T(8,128)(2,1)S(1)}, u32[]{:S(2)}, u32[]{:S(2)}) collective-permute-start(bf16[256,768]{1,0:T(8,128)(2,1)} %get-tuple-element.152.piece_ref), channel_id=1, source_target_pairs={{0,24},{4,28},{8,16},{12,20},{16,8},{20,12},{24,0},{28,4},{1,25},{... | collective-permute-start | bytes 1179656 | tf_op jit(solution)/shard_map/ppermute | solution.py:802
  170.0 21.6 %collective-permute-start.49 = (bf16[256,768]{1,0:T(8,128)(2,1)}, bf16[256,768]{1,0:T(8,128)(2,1)S(1)}, u32[]{:S(2)}, u32[]{:S(2)}) collective-permute-start(bf16[256,768]{1,0:T(8,128)(2,1)} %get-tuple-element.152.piece_ref), channel_id=1, source_target_pairs={{0,16},{4,20},{8,24},{12,28},{16,0},{20,4},{24,8},{28,12},{1,17},{... | collective-permute-start | bytes 1179656 | tf_op jit(solution)/shard_map/ppermute | solution.py:802
  180.9 18.9 %collective-permute-start.47 = (bf16[256,768]{1,0:T(8,128)(2,1)S(1)}, bf16[256,768]{1,0:T(8,128)(2,1)S(1)}, u32[]{:S(2)}, u32[]{:S(2)}) collective-permute-start(bf16[256,768]{1,0:T(8,128)(2,1)S(1)} %copy-done.14), channel_id=1, source_target_pairs={{0,8},{4,12},{8,0},{12,4},{16,24},{20,28},{24,16},{28,20},{1,9},{5... | collective-permute-start | bytes 1179656 | tf_op jit(solution)/shard_map/ppermute | solution.py:802
  182.0 22.1 %collective-permute-start.31 = (bf16[256,768]{1,0:T(8,128)(2,1)}, bf16[256,768]{1,0:T(8,128)(2,1)S(1)}, u32[]{:S(2)}, u32[]{:S(2)}) collective-permute-start(bf16[256,768]{1,0:T(8,128)(2,1)} %get-tuple-element.134.piece_ref.refs_8_), channel_id=1, source_target_pairs={{0,8},{4,12},{8,0},{12,4},{16,24},{20,28},{24,16},{28,20},{1,9},{5... | collective-permute-start | bytes 1179656 | tf_op jit(solution)/shard_map/ppermute | solution.py:802
  186.0 22.4 %collective-permute-start.33 = (bf16[256,768]{1,0:T(8,128)(2,1)S(1)}, bf16[256,768]{1,0:T(8,128)(2,1)S(1)}, u32[]{:S(2)}, u32[]{:S(2)}) collective-permute-start(bf16[256,768]{1,0:T(8,128)(2,1)S(1)} %copy-done.4), channel_id=1, source_target_pairs={{0,16},{4,20},{8,24},{12,28},{16,0},{20,4},{24,8},{28,12},{1,17},{... | collective-permute-start | bytes 1179656 | tf_op jit(solution)/shard_map/ppermute | solution.py:802
  187.1 25.5 %collective-permute-start.35 = (bf16[256,768]{1,0:T(8,128)(2,1)S(1)}, bf16[256,768]{1,0:T(8,128)(2,1)S(1)}, u32[]{:S(2)}, u32[]{:S(2)}) collective-permute-start(bf16[256,768]{1,0:T(8,128)(2,1)S(1)} %copy-done.4), channel_id=1, source_target_pairs={{0,24},{4,28},{8,16},{12,20},{16,8},{20,12},{24,0},{28,4},{1,25},{... | collective-permute-start | bytes 1179656 | tf_op jit(solution)/shard_map/ppermute | solution.py:802
  191.6 25.5 %collective-permute-start.52 = (bf16[256,768]{1,0:T(8,128)(2,1)}, bf16[256,768]{1,0:T(8,128)(2,1)S(1)}, u32[]{:S(2)}, u32[]{:S(2)}) collective-permute-start(bf16[256,768]{1,0:T(8,128)(2,1)} %feed.15), channel_id=1, source_target_pairs={{0,24},{4,28},{8,16},{12,20},{16,8},{20,12},{24,0},{28,4},{1,25},{... | collective-permute-start | bytes 1179656 | tf_op jit(solution)/shard_map/ppermute | solution.py:802
  199.8 26.7 %collective-permute-start.50 = (bf16[256,768]{1,0:T(8,128)(2,1)}, bf16[256,768]{1,0:T(8,128)(2,1)S(1)}, u32[]{:S(2)}, u32[]{:S(2)}) collective-permute-start(bf16[256,768]{1,0:T(8,128)(2,1)} %feed.14), channel_id=1, source_target_pairs={{0,16},{4,20},{8,24},{12,28},{16,0},{20,4},{24,8},{28,12},{1,17},{... | collective-permute-start | bytes 1179656 | tf_op jit(solution)/shard_map/ppermute | solution.py:802
  204.1 22.5 %collective-permute-start.48 = (bf16[256,768]{1,0:T(8,128)(2,1)}, bf16[256,768]{1,0:T(8,128)(2,1)S(1)}, u32[]{:S(2)}, u32[]{:S(2)}) collective-permute-start(bf16[256,768]{1,0:T(8,128)(2,1)} %feed.13), channel_id=1, source_target_pairs={{0,8},{4,12},{8,0},{12,4},{16,24},{20,28},{24,16},{28,20},{1,9},{5... | collective-permute-start | bytes 1179656 | tf_op jit(solution)/shard_map/ppermute | solution.py:802
  208.3 24.8 %collective-permute-start.32 = (bf16[256,768]{1,0:T(8,128)(2,1)}, bf16[256,768]{1,0:T(8,128)(2,1)S(1)}, u32[]{:S(2)}, u32[]{:S(2)}) collective-permute-start(bf16[256,768]{1,0:T(8,128)(2,1)} %get-tuple-element.140), channel_id=1, source_target_pairs={{0,8},{4,12},{8,0},{12,4},{16,24},{20,28},{24,16},{28,20},{1,9},{5... | collective-permute-start | bytes 1179656 | tf_op jit(solution)/shard_map/ppermute | solution.py:802
  212.6 23.3 %collective-permute-start.34 = (bf16[256,768]{1,0:T(8,128)(2,1)}, bf16[256,768]{1,0:T(8,128)(2,1)S(1)}, u32[]{:S(2)}, u32[]{:S(2)}) collective-permute-start(bf16[256,768]{1,0:T(8,128)(2,1)} %get-tuple-element.141), channel_id=1, source_target_pairs={{0,16},{4,20},{8,24},{12,28},{16,0},{20,4},{24,8},{28,12},{1,17},{... | collective-permute-start | bytes 1179656 | tf_op jit(solution)/shard_map/ppermute | solution.py:802
  217.1 25.3 %collective-permute-start.36 = (bf16[256,768]{1,0:T(8,128)(2,1)}, bf16[256,768]{1,0:T(8,128)(2,1)S(1)}, u32[]{:S(2)}, u32[]{:S(2)}) collective-permute-start(bf16[256,768]{1,0:T(8,128)(2,1)} %get-tuple-element.142), channel_id=1, source_target_pairs={{0,24},{4,28},{8,16},{12,20},{16,8},{20,12},{24,0},{28,4},{1,25},{... | collective-permute-start | bytes 1179656 | tf_op jit(solution)/shard_map/ppermute | solution.py:802
  248.3 21.4 %collective-permute-start.56 = (bf16[256,768]{1,0:T(8,128)(2,1)}, bf16[256,768]{1,0:T(8,128)(2,1)S(1)}, u32[]{:S(2)}, u32[]{:S(2)}) collective-permute-start(bf16[256,768]{1,0:T(8,128)(2,1)} %get-tuple-element.159.piece_ref.refs_4_), channel_id=1, source_target_pairs={{0,16},{4,20},{8,24},{12,28},{16,0},{20,4},{24,8},{28,12},{1,17},{... | collective-permute-start | bytes 1179656 | tf_op jit(solution)/shard_map/ppermute | solution.py:802
  248.8 25.7 %collective-permute-start.54 = (bf16[256,768]{1,0:T(8,128)(2,1)}, bf16[256,768]{1,0:T(8,128)(2,1)S(1)}, u32[]{:S(2)}, u32[]{:S(2)}) collective-permute-start(bf16[256,768]{1,0:T(8,128)(2,1)} %get-tuple-element.159.piece_ref.refs_4_), channel_id=1, source_target_pairs={{0,8},{4,12},{8,0},{12,4},{16,24},{20,28},{24,16},{28,20},{1,9},{5... | collective-permute-start | bytes 1179656 | tf_op jit(solution)/shard_map/ppermute | solution.py:802
  262.0 30.9 %collective-permute-start.59 = (bf16[256,768]{1,0:T(8,128)(2,1)}, bf16[256,768]{1,0:T(8,128)(2,1)S(1)}, u32[]{:S(2)}, u32[]{:S(2)}) collective-permute-start(bf16[256,768]{1,0:T(8,128)(2,1)} %get-tuple-element.167), channel_id=1, source_target_pairs={{0,24},{4,28},{8,16},{12,20},{16,8},{20,12},{24,0},{28,4},{1,25},{... | collective-permute-start | bytes 1179656 | tf_op jit(solution)/shard_map/ppermute | solution.py:802
  274.1 18.8 %collective-permute-start.57 = (bf16[256,768]{1,0:T(8,128)(2,1)}, bf16[256,768]{1,0:T(8,128)(2,1)S(1)}, u32[]{:S(2)}, u32[]{:S(2)}) collective-permute-start(bf16[256,768]{1,0:T(8,128)(2,1)} %get-tuple-element.165), channel_id=1, source_target_pairs={{0,16},{4,20},{8,24},{12,28},{16,0},{20,4},{24,8},{28,12},{1,17},{... | collective-permute-start | bytes 1179656 | tf_op jit(solution)/shard_map/ppermute | solution.py:802
  291.8 87.7 %collective-permute-start.81 = (bf16[1536,384]{1,0:T(8,128)(2,1)}, bf16[1536,384]{1,0:T(8,128)(2,1)S(1)}, u32[]{:S(2)}, u32[]{:S(2)}) collective-permute-start(bf16[1536,384]{1,0:T(8,128)(2,1)} %get-tuple-element.217), channel_id=1, source_target_pairs={{0,4},{4,0},{8,12},{12,8},{16,20},{20,16},{24,28},{28,24},{1,5},{5... | collective-permute-start | bytes 3538952 | tf_op jit(solution)/shard_map/ppermute | solution.py:805
  302.4 38.8 %collective-permute-start.63 = (bf16[384,384]{1,0:T(8,128)(2,1)}, bf16[384,384]{1,0:T(8,128)(2,1)S(1)}, u32[]{:S(2)}, u32[]{:S(2)}) collective-permute-start(bf16[384,384]{1,0:T(8,128)(2,1)} %get-tuple-element.180), channel_id=1, source_target_pairs={{0,8},{4,12},{8,0},{12,4},{16,24},{20,28},{24,16},{28,20},{1,9},{5... | collective-permute-start | bytes 884744 | tf_op jit(solution)/shard_map/ppermute | solution.py:802
  303.4 37.8 %collective-permute-start.64 = (bf16[384,384]{1,0:T(8,128)(2,1)}, bf16[384,384]{1,0:T(8,128)(2,1)S(1)}, u32[]{:S(2)}, u32[]{:S(2)}) collective-permute-start(bf16[384,384]{1,0:T(8,128)(2,1)} %get-tuple-element.181), channel_id=1, source_target_pairs={{0,16},{4,20},{8,24},{12,28},{16,0},{20,4},{24,8},{28,12},{1,17},{... | collective-permute-start | bytes 884744 | tf_op jit(solution)/shard_map/ppermute | solution.py:802
  303.9 37.3 %collective-permute-start.65 = (bf16[384,384]{1,0:T(8,128)(2,1)}, bf16[384,384]{1,0:T(8,128)(2,1)S(1)}, u32[]{:S(2)}, u32[]{:S(2)}) collective-permute-start(bf16[384,384]{1,0:T(8,128)(2,1)} %get-tuple-element.182), channel_id=1, source_target_pairs={{0,24},{4,28},{8,16},{12,20},{16,8},{20,12},{24,0},{28,4},{1,25},{... | collective-permute-start | bytes 884744 | tf_op jit(solution)/shard_map/ppermute | solution.py:802
  356.8 18.1 %collective-permute-start.79 = (bf16[256,768]{1,0:T(8,128)(2,1)}, bf16[256,768]{1,0:T(8,128)(2,1)S(1)}, u32[]{:S(2)}, u32[]{:S(2)}) collective-permute-start(bf16[256,768]{1,0:T(8,128)(2,1)} %get-tuple-element.204), channel_id=1, source_target_pairs={{0,24},{4,28},{8,16},{12,20},{16,8},{20,12},{24,0},{28,4},{1,25},{... | collective-permute-start | bytes 1179656 | tf_op jit(solution)/shard_map/ppermute | solution.py:802
  361.2 25.7 %collective-permute-start.67 = (bf16[128,768]{1,0:T(8,128)(2,1)}, bf16[128,768]{1,0:T(8,128)(2,1)S(1)}, u32[]{:S(2)}, u32[]{:S(2)}) collective-permute-start(bf16[128,768]{1,0:T(8,128)(2,1)} %get-tuple-element.195), channel_id=1, source_target_pairs={{0,1},{1,0},{2,3},{3,2},{4,5},{5,4},{6,7},{7,6},{8,9},{9,8},{10,11... | collective-permute-start | bytes 589832 | tf_op jit(solution)/shard_map/ppermute | solution.py:811
  366.2 21.1 %collective-permute-start.68 = (bf16[128,768]{1,0:T(8,128)(2,1)}, bf16[128,768]{1,0:T(8,128)(2,1)S(1)}, u32[]{:S(2)}, u32[]{:S(2)}) collective-permute-start(bf16[128,768]{1,0:T(8,128)(2,1)} %get-tuple-element.196), channel_id=1, source_target_pairs={{0,2},{1,3},{2,0},{3,1},{4,6},{5,7},{6,4},{7,5},{8,10},{9,11},{10,... | collective-permute-start | bytes 589832 | tf_op jit(solution)/shard_map/ppermute | solution.py:811
  378.3 53.7 %collective-permute-start.80 = (f32[128,768]{1,0:T(8,128)}, f32[128,768]{1,0:T(8,128)S(1)}, u32[]{:S(2)}, u32[]{:S(2)}) collective-permute-start(f32[128,768]{1,0:T(8,128)} %get-tuple-element.206), channel_id=1, source_target_pairs={{0,4},{4,0},{8,12},{12,8},{16,20},{20,16},{24,28},{28,24},{1,5},{5... | collective-permute-start | bytes 1179656 | tf_op jit(solution)/shard_map/ppermute | solution.py:805
  383.8 41.0 %collective-permute-start.82 = (bf16[384,384]{1,0:T(8,128)(2,1)}, bf16[384,384]{1,0:T(8,128)(2,1)S(1)}, u32[]{:S(2)}, u32[]{:S(2)}) collective-permute-start(bf16[384,384]{1,0:T(8,128)(2,1)} %get-tuple-element.219), channel_id=1, source_target_pairs={{0,1},{1,0},{2,3},{3,2},{4,5},{5,4},{6,7},{7,6},{8,9},{9,8},{10,11... | collective-permute-start | bytes 884744 | tf_op jit(solution)/shard_map/ppermute | solution.py:811
  386.0 39.5 %collective-permute-start.83 = (bf16[384,384]{1,0:T(8,128)(2,1)}, bf16[384,384]{1,0:T(8,128)(2,1)S(1)}, u32[]{:S(2)}, u32[]{:S(2)}) collective-permute-start(bf16[384,384]{1,0:T(8,128)(2,1)} %get-tuple-element.220), channel_id=1, source_target_pairs={{0,2},{1,3},{2,0},{3,1},{4,6},{5,7},{6,4},{7,5},{8,10},{9,11},{10,... | collective-permute-start | bytes 884744 | tf_op jit(solution)/shard_map/ppermute | solution.py:811
  386.9 39.9 %collective-permute-start.84 = (bf16[384,384]{1,0:T(8,128)(2,1)}, bf16[384,384]{1,0:T(8,128)(2,1)S(1)}, u32[]{:S(2)}, u32[]{:S(2)}) collective-permute-start(bf16[384,384]{1,0:T(8,128)(2,1)} %get-tuple-element.221), channel_id=1, source_target_pairs={{0,3},{1,2},{2,1},{3,0},{4,7},{5,6},{6,5},{7,4},{8,11},{9,10},{10,... | collective-permute-start | bytes 884744 | tf_op jit(solution)/shard_map/ppermute | solution.py:811
  387.3 34.7 %collective-permute-start.69 = (bf16[128,768]{1,0:T(8,128)(2,1)S(1)}, bf16[128,768]{1,0:T(8,128)(2,1)S(1)}, u32[]{:S(2)}, u32[]{:S(2)}) collective-permute-start(bf16[128,768]{1,0:T(8,128)(2,1)S(1)} %copy-done.86), channel_id=1, source_target_pairs={{0,3},{1,2},{2,1},{3,0},{4,7},{5,6},{6,5},{7,4},{8,11},{9,10},{10,... | collective-permute-start | bytes 589832 | tf_op jit(solution)/shard_map/ppermute | solution.py:811
  (132 other events, 1140.6 us)

commit v3 on v2

v3 whole, which is shorter than its diff:
```python
import functools

import jax
import jax.numpy as jnp
from jax import lax
from jax.experimental import pallas as pl
from jax.experimental.pallas import tpu as pltpu
from jax.sharding import Mesh
from jax.sharding import PartitionSpec as P

D = 768
HEADS = 12
HEAD_DIM = 64
FF = 3072
BLK = 64

CHIPS = 4
CORES = 2
GROUP = CHIPS * CORES
COLS = D // CHIPS
HEADS_HERE = HEADS // CHIPS
UNITS = FF // CHIPS
HALF = UNITS // CORES
QKV = 3 * COLS

norm_eps = 1e-05
attn_gains = (2.0, 2.0, 1.0, 4.0)
masked_score = -1e30
score_scale = HEAD_DIM ** (-0.5)
log2_e = 1.4426950408889634
bf16 = jnp.bfloat16
f32 = jnp.float32

IZ, IK, IJ, IR = 0, 1, 2, 3
ROW_BO, ROW_B2, ROW_G1, ROW_C1, ROW_G2, ROW_C2, ROW_STATS, ROW_B1, ROW_QV = range(9)
VEC_ROWS = 16

SMEM_SPEC = pl.BlockSpec(memory_space=pltpu.SMEM)
VMEM_SPEC = pl.BlockSpec(memory_space=pltpu.VMEM)


def dot(left_side, right_side):
    return jnp.dot(left_side, right_side, preferred_element_type=f32)


def dot_left(left_side, right_side):
    return lax.dot_general(
        left_side, right_side, (((0,), (0,)), ((), ())), preferred_element_type=f32
    )


def dot_right(left_side, right_side):
    return lax.dot_general(
        left_side, right_side, (((1,), (1,)), ((), ())), preferred_element_type=f32
    )


def normal_cdf(values):
    return 0.5 * (1.0 + lax.erf(values * 0.7071067811865476))


def tree_sum(items):
    items = list(items)
    while len(items) > 1:
        items = [items[i] + items[i + 1] for i in range(0, len(items), 2)]
    return items[0]


def aligned(start, size):
    return pl.ds(pl.multiple_of(start, size), size)


def shape(dims, kind=bf16):
    return jax.ShapeDtypeStruct(dims, kind)


def call(kernel, name, outs, scalars, arrays, scratch=(), limit=16):
    return pl.pallas_call(
        kernel,
        out_shape=outs,
        in_specs=[SMEM_SPEC] * len(scalars) + [VMEM_SPEC] * len(arrays),
        out_specs=jax.tree.map(lambda _: VMEM_SPEC, outs),
        scratch_shapes=list(scratch),
        compiler_params=pltpu.CompilerParams(vmem_limit_bytes=limit * 2**20),
        name=name,
    )(*scalars, *arrays)


def without_ids(kernel, ids_ref, *refs):
    kernel(*refs)


class Line:
    def __init__(self, ids):
        self.ids = ids

    def wait(self, *values):
        self.ids = lax.optimization_barrier((self.ids, *values))[0]

    def behind(self, *values):
        return lax.optimization_barrier((self.ids, *values))[1:]

    def __call__(self, kernel, name, outs, scalars, arrays, scratch=(), limit=16, bare=False):
        if bare:
            kernel = functools.partial(without_ids, kernel)
        result = call(kernel, name, outs, (self.ids, *scalars), arrays, scratch, limit)
        self.wait(jax.tree.leaves(result)[0])
        return result


def pick(place, options):
    value = options[0]
    for number, option in enumerate(options[1:], 1):
        value = jnp.where(place == number, option, value)
    return value


def sums_kernel(ids_ref, attn_ref, in_ref, out_ref, sums_ref):
    @pl.when(pl.program_id(0) == 0)
    def _():
        sums_ref[...] = jnp.zeros_like(sums_ref)

    for number in range(4):
        sums_ref[number : number + 1, :] += jnp.sum(
            jnp.abs(attn_ref[number]), axis=0, keepdims=True
        )
    for number in range(FF // D):
        sums_ref[4 + number : 5 + number, :] += jnp.sum(
            jnp.abs(in_ref[:, number * D : (number + 1) * D]), axis=0, keepdims=True
        )
    last = 4 + FF // D
    sums_ref[last : last + 1, :] += jnp.sum(jnp.abs(out_ref[...]), axis=0, keepdims=True)


def column_sums(ids, attn, w_in, w_down, steps=4):
    return pl.pallas_call(
        sums_kernel,
        out_shape=shape((16, D), f32),
        grid_spec=pltpu.PrefetchScalarGridSpec(
            num_scalar_prefetch=1,
            grid=(steps,),
            in_specs=[
                pl.BlockSpec((4, attn.shape[1] // steps, D), lambda i, ids: (0, i, 0)),
                pl.BlockSpec((w_in.shape[0] // steps, FF), lambda i, ids: (i, 0)),
                pl.BlockSpec((w_down.shape[0] // steps, D), lambda i, ids: (i, 0)),
            ],
            out_specs=pl.BlockSpec((16, D), lambda i, ids: (0, 0)),
        ),
        compiler_params=pltpu.CompilerParams(vmem_limit_bytes=16 * 2**20),
        name="column_sums",
    )(ids, attn, w_in, w_down)


def sign_of(values):
    return jnp.where(values > 0, 1.0, jnp.where(values < 0, -1.0, 0.0))


def choose(size, count, start):
    place = lax.broadcasted_iota(jnp.int32, (size, count), 0)
    goal = lax.broadcasted_iota(jnp.int32, (size, count), 1) + start
    return jnp.where(place == goal, 1.0, 0.0).astype(bf16)


def pieces_kernel(n_shard, student, ids_ref, attn_ref, in_ref, down_ref, early_ref, late_ref):
    k, j = ids_ref[IK], ids_ref[IJ]
    units = FF // n_shard
    few = units // GROUP
    rows_z = in_ref.shape[0]

    def travels(values):
        return sign_of(values).astype(bf16) if student else values

    chosen = choose(D, COLS, j * COLS)
    for number in range(4):
        early_ref[:, number * COLS : (number + 1) * COLS] = dot(
            travels(attn_ref[number]), chosen
        ).astype(bf16)
    chosen = choose(units, few, (j * CORES + k) * few)
    for place in range(n_shard):
        late_ref[0:rows_z, place * few : (place + 1) * few] = dot(
            travels(in_ref[:, place * units : (place + 1) * units]), chosen
        ).astype(bf16)
    full = travels(down_ref[...])
    late_ref[rows_z : rows_z + few, :] = full[:, :HALF]
    late_ref[rows_z + few : rows_z + 2 * few, :] = full[:, HALF:]


def weight_pieces(n_shard, student, ids, attn, w_in, w_down):
    half = attn.shape[1] // CORES
    few = FF // n_shard // GROUP
    rows_z = w_in.shape[0]
    return pl.pallas_call(
        functools.partial(pieces_kernel, n_shard, student),
        out_shape=(shape((half, D)), shape((rows_z + 2 * few, HALF))),
        grid_spec=pltpu.PrefetchScalarGridSpec(
            num_scalar_prefetch=1,
            grid=(1,),
            in_specs=[
                pl.BlockSpec((4, half, D), lambda i, ids: (0, ids[IK], 0)),
                pl.BlockSpec((rows_z, FF), lambda i, ids: (0, 0)),
                pl.BlockSpec((few, D), lambda i, ids: (CORES * ids[IJ] + ids[IK], 0)),
            ],
            out_specs=(
                pl.BlockSpec((half, D), lambda i, ids: (0, 0)),
                pl.BlockSpec((rows_z + 2 * few, HALF), lambda i, ids: (0, 0)),
            ),
        ),
        compiler_params=pltpu.CompilerParams(vmem_limit_bytes=24 * 2**20),
        name="student_pieces" if student else "teacher_pieces",
    )(ids, attn, w_in, w_down)


def scale_row(sums_ref, row, gain, fan_in):
    return gain * (sums_ref[row : row + 1, :] / fan_in) * fan_in ** (-0.5)


def scaled(values, scale):
    return (values.astype(f32) * scale).astype(bf16)


def early_kernel(n_shard, model, ids_ref, *refs):
    group, refs = refs[:n_shard], refs[n_shard:]
    qkv_ref, out_ref = refs[-2:]
    z = ids_ref[IZ]
    half = group[0].shape[0]
    fold = n_shard // 2
    base = model * fold * half
    if model:
        out_ref[0:base, :] = refs[0][...]
    for mask, ref in enumerate(group):
        place = z ^ mask
        qkv_ref[aligned(place * half, half), :] = ref[:, :QKV]
        low = pl.ds(pl.multiple_of(base + lax.rem(place, fold) * half, half), half)

        @pl.when(place < fold)
        def _():
            out_ref[low, 0:COLS] = ref[:, QKV:]

        @pl.when(place >= fold)
        def _():
            out_ref[low, COLS:] = ref[:, QKV:]


def out_weight_kernel(n_shard, ids_ref, *refs):
    k, j = ids_ref[IK], ids_ref[IJ]
    sums_ref, t_ref, s_ref, scale_ref = refs[2 * CHIPS :]
    scale = scale_row(sums_ref, 3, attn_gains[3], D)
    for chip in range(CHIPS):
        scale_ref[chip] = scale[:, chip * COLS : (chip + 1) * COLS]
    half = D // n_shard // CORES
    span = n_shard * half // 2
    for core in range(CORES):
        for mask in range(CHIPS):
            ref = refs[core * CHIPS + mask]
            for model, goal in enumerate((t_ref, s_ref)):
                for place in range(n_shard):
                    fold = n_shard // 2
                    low = model * span + (place % fold) * half
                    lanes = slice(0, COLS) if place < fold else slice(COLS, 2 * COLS)
                    rows = pl.ds(
                        pl.multiple_of((place * CORES + (k ^ core)) * half, half), half
                    )
                    piece = ref[low : low + half, lanes]
                    if model:
                        piece = scaled(piece, scale_ref[j ^ mask])
                    goal[j ^ mask, rows, :] = piece


def late_kernel(n_shard, student, ids_ref, all_ref, vec_ref, *refs):
    if student:
        sums_ref, in_ref, down_ref, b1_ref = refs
        down_scale = scale_row(sums_ref, 4 + FF // D, 1.0, FF)
    else:
        in_ref, down_ref, b1_ref = refs
    j = ids_ref[IJ]
    units = FF // n_shard
    few = units // GROUP
    rows_z = D // n_shard
    each = rows_z + 2 * few

    def mine(ref, row, core, place):
        options = []
        for chip in range(CHIPS):
            start = place * units + (chip * CORES + core) * few
            low, lane = row + start // D, start % D
            options.append(ref[low : low + 1, lane : lane + few])
        return pick(j, options)

    for core in range(CORES):
        lanes = slice(core * HALF, (core + 1) * HALF)
        if student:
            scale = jnp.concatenate(
                [mine(sums_ref, 4, core, place) for place in range(n_shard)], axis=1
            )
            scale = (scale / D) * D ** (-0.5)
        for place in range(n_shard):
            base = (place * CORES + core) * each
            piece = all_ref[base : base + rows_z, :]
            rows = slice(core * HALF + place * few, core * HALF + (place + 1) * few)
            left = all_ref[base + rows_z : base + rows_z + few, :]
            right = all_ref[base + rows_z + few : base + each, :]
            if student:
                piece = scaled(piece, scale)
                left = scaled(left, down_scale[:, :HALF])
                right = scaled(right, down_scale[:, HALF:])
            in_ref[place * rows_z : (place + 1) * rows_z, lanes] = piece
            down_ref[rows, 0:HALF] = left
            down_ref[rows, HALF:] = right
            b1_ref[0:1, rows] = mine(vec_ref, 8, core, place)


def places_kernel(rest, ids_ref, block_ref, lengths_ref, row_ref, col_ref, valid_ref, *, seqs, rows):
    z, k, j, r = ids_ref[IZ], ids_ref[IK], ids_ref[IJ], ids_ref[IR]
    length = lengths_ref[z * seqs + k]
    per = rows // BLK
    number = 0
    for far in range(rest):
        for mask in range(CHIPS):
            for half in range(CORES):
                for part in range(per):
                    block = ((((r ^ far) * CHIPS + (j ^ mask)) * CORES + (k ^ half)) * per) + part
                    base = block_ref[block] * BLK
                    goal = slice(number * BLK, (number + 1) * BLK)
                    col = base + lax.broadcasted_iota(jnp.int32, (BLK, 1), 0)
                    col_ref[goal, :] = col
                    if far == 0:
                        row_ref[:, goal] = base + lax.broadcasted_iota(jnp.int32, (1, BLK), 1)
                    if far == 0 and mask == 0:
                        valid_ref[goal, :] = jnp.where(col < length, 1.0, 0.0)
                    number += 1


def input_kernel(ids_ref, *refs):
    k = ids_ref[IK]
    own_ref, send_ref = refs[CHIPS:]
    rows = refs[0].shape[1]
    for mask in range(CHIPS):
        goal = slice(mask * rows, (mask + 1) * rows)
        own_ref[goal, :] = refs[mask][k]
        send_ref[goal, :] = refs[mask][1 - k]


def qkv_kernel(n_shard, student, ids_ref, own_ref, oth_ref, half_ref, peer_ref, vec_ref, *outs):
    k, j = ids_ref[IK], ids_ref[IJ]
    if student:
        sums_ref, outs = outs[0], outs[1:]
        scale = jnp.concatenate(
            [
                pick(
                    j,
                    [
                        scale_row(sums_ref, number, attn_gains[number], D)[
                            :, chip * COLS : (chip + 1) * COLS
                        ]
                        for chip in range(CHIPS)
                    ],
                )
                for number in range(3)
            ],
            axis=1,
        )
    q_ref, k_ref, v_ref, w_ref = outs
    half = D // n_shard // CORES
    for core, ref in enumerate((half_ref, peer_ref)):
        for place in range(n_shard):
            rows = pl.ds(pl.multiple_of((place * CORES + (k ^ core)) * half, half), half)
            piece = ref[place * half : (place + 1) * half, :]
            w_ref[rows, :] = scaled(piece, scale) if student else piece
    weight = w_ref[...]
    chips = [slice(chip * COLS, (chip + 1) * COLS) for chip in range(CHIPS)]
    q_bias = pick(j, [vec_ref[0:1, chip] for chip in chips])
    v_bias = pick(j, [vec_ref[1:2, chip] for chip in chips])
    rows = own_ref.shape[0] // CHIPS
    for core, ref in enumerate((own_ref, oth_ref)):
        for mask in range(CHIPS):
            result = dot(ref[mask * rows : (mask + 1) * rows, :], weight)
            goal = slice((mask * CORES + core) * rows, (mask * CORES + core + 1) * rows)
            sets = (
                (q_ref, result[:, :COLS] + q_bias),
                (k_ref, result[:, COLS : 2 * COLS]),
                (v_ref, result[:, 2 * COLS :] + v_bias),
            )
            for goal_ref, values in sets:
                for head in range(HEADS_HERE):
                    span = slice(head * HEAD_DIM, (head + 1) * HEAD_DIM)
                    goal_ref[head, goal, :] = values[:, span].astype(bf16)


def attend_kernel(q_ref, k_ref, v_ref, pq_ref, pk_ref, *outs, tile):
    o_refs, lse_ref, all_ref = outs[:CHIPS], outs[CHIPS], outs[CHIPS + 1]
    tokens = q_ref.shape[1]
    own = tokens // CHIPS

    def one_head(head, carry):
        k_head = k_ref[head]
        v_turned = v_ref[head].T
        for t in range(tokens // tile):
            rows = slice(t * tile, (t + 1) * tile)
            scores = dot_right(k_head, q_ref[head, rows, :]) * (score_scale * log2_e)
            allowed = pq_ref[:, rows] >= pk_ref[...]
            scores = jnp.where(allowed, scores, masked_score)
            peak = jnp.max(scores, axis=0, keepdims=True)
            powers = jnp.exp2(scores - peak)
            total = jnp.sum(powers, axis=0, keepdims=True)
            mixed = dot(v_turned, powers.astype(bf16)) / total
            all_ref[head, rows, :] = mixed.T.astype(bf16)
            lse_ref[head, :, rows] = peak + jnp.log2(total)
        return carry

    lax.fori_loop(0, HEADS_HERE, one_head, 0)
    for head in range(HEADS_HERE):
        span = slice(head * HEAD_DIM, (head + 1) * HEAD_DIM)
        for mask in range(CHIPS):
            o_refs[mask][:, span] = all_ref[head, mask * own : (mask + 1) * own, :]


def norm_parts(values):
    middle = jnp.mean(values, axis=-1, keepdims=True)
    centred = values - middle
    spread = jnp.mean(centred * centred, axis=-1, keepdims=True)
    inverse = lax.rsqrt(spread + norm_eps)
    return centred * inverse, inverse


def norm_back(values, gain, grad_out):
    normal, inverse = norm_parts(values)
    scaled = grad_out * gain
    grad_in = (
        scaled
        - jnp.mean(scaled, axis=-1, keepdims=True)
        - normal * jnp.mean(scaled * normal, axis=-1, keepdims=True)
    ) * inverse
    return grad_in, normal


def column_total(values):
    return jnp.sum(values, axis=0, keepdims=True)


def branch_kernel(student, ids_ref, *refs):
    j = ids_ref[IJ]
    h_refs, (w_ref, own_ref, oth_ref, vec_ref, valid_ref) = refs[:CHIPS], refs[CHIPS : CHIPS + 5]
    outs = refs[CHIPS + 5 :]
    first_ref, sent_ref = outs[:2]
    rows = own_ref.shape[0] // CHIPS
    if student:
        residual_ref, sums_ref = outs[2:]
        sums_ref[...] = jnp.zeros_like(sums_ref)
    for core, x_ref in enumerate((own_ref, oth_ref)):
        goal = slice(core * rows, (core + 1) * rows)
        parts = []
        for chip in range(CHIPS):
            parts.append(
                tree_sum(
                    dot(
                        h_refs[mask][goal, :],
                        w_ref[chip, aligned((j ^ mask) * COLS, COLS), :],
                    )
                    for mask in range(CHIPS)
                )
            )
        branch = jnp.concatenate(parts, axis=1) + vec_ref[2:3, :]
        residual = x_ref[0:rows, :].astype(f32) + branch
        normal, _ = norm_parts(residual)
        first = normal * vec_ref[4:5, :] + vec_ref[5:6, :]
        first_ref[goal, :] = first
        sent_ref[goal, :] = first.astype(bf16)
        if student:
            residual_ref[goal, :] = residual
            sums_ref[0:1, :] += column_total(valid_ref[goal, :] * branch * branch)


def feed_kernel(student, piece_ref, in_ref, down_ref, b1_ref, part_ref, *outs):
    inner = dot(piece_ref[...], in_ref[...]) + b1_ref[0:1, :]
    act = (inner * normal_cdf(inner)).astype(bf16)
    if student:
        outs[0][...] = inner
        outs[1][...] = act
    part_ref[...] = dot(act, down_ref[...]).astype(part_ref.dtype)


def target_kernel(*refs):
    parts, (first_ref, vec_ref, target_ref) = refs[:CHIPS], refs[CHIPS:]
    feed = tree_sum(ref[...].astype(f32) for ref in parts) + vec_ref[3:4, :]
    normal, _ = norm_parts(first_ref[...] + feed)
    target_ref[...] = normal * vec_ref[6:7, :] + vec_ref[7:8, :]


def loss_kernel(ids_ref, lengths_ref, *refs):
    parts, rest = refs[:CHIPS], refs[CHIPS:]
    first_ref, vec_ref, target_ref, valid_ref, out_ref, grad_ref, sent_ref, sums_ref = rest
    count = lengths_ref[0]
    for number in range(1, lengths_ref.shape[0]):
        count = count + lengths_ref[number]
    share = 1.0 / (count.astype(f32) * D)
    feed = tree_sum(ref[...].astype(f32) for ref in parts) + vec_ref[3:4, :]
    second = first_ref[...] + feed
    normal, inverse = norm_parts(second)
    out = normal * vec_ref[6:7, :] + vec_ref[7:8, :]
    out_ref[...] = out.astype(bf16)
    valid = valid_ref[...]
    mismatch = valid * (out - target_ref[...])
    grad_out = mismatch * share
    scaled = grad_out * vec_ref[6:7, :]
    grad = (
        scaled
        - jnp.mean(scaled, axis=-1, keepdims=True)
        - normal * jnp.mean(scaled * normal, axis=-1, keepdims=True)
    ) * inverse
    grad_ref[...] = grad
    sent_ref[...] = grad.astype(bf16)
    sums_ref[...] = jnp.concatenate(
        [
            column_total(grad),
            column_total(grad_out * normal),
            column_total(grad_out),
            0.5 * column_total(mismatch * mismatch),
            column_total(valid * feed * feed),
            column_total(valid * second * second),
            jnp.zeros((2, D), f32),
        ]
    )


def feed_back_kernel(piece_ref, inner_ref, in_ref, down_ref, part_ref, grad_ref, sum_ref):
    inner = inner_ref[...]
    slope = normal_cdf(inner) + inner * jnp.exp(-0.5 * inner * inner) * 0.3989422804014327
    grad = dot_right(piece_ref[...], down_ref[...]) * slope
    sum_ref[...] = jnp.broadcast_to(column_total(grad), sum_ref.shape)
    grad = grad.astype(bf16)
    grad_ref[...] = grad
    part_ref[...] = dot_right(grad, in_ref[...]).astype(part_ref.dtype)


def branch_back_kernel(ids_ref, *refs):
    j = ids_ref[IJ]
    parts, rest = refs[:CHIPS], refs[CHIPS:]
    second_ref, residual_ref, vec_ref, w_ref = rest[:4]
    grad_ref, sent_ref = rest[4:6]
    h_refs, (sums_ref,) = rest[6 : 6 + CHIPS], rest[6 + CHIPS :]
    grad_first = second_ref[...] + tree_sum(ref[...].astype(f32) for ref in parts)
    grad, normal = norm_back(residual_ref[...], vec_ref[4:5, :], grad_first)
    grad_ref[...] = grad
    sums_ref[...] = jnp.concatenate(
        [
            column_total(grad),
            column_total(grad_first * normal),
            column_total(grad_first),
            jnp.zeros((5, D), f32),
        ]
    )
    grad = grad.astype(bf16)
    sent_ref[...] = grad
    chips = [grad[:, chip * COLS : (chip + 1) * COLS] for chip in range(CHIPS)]
    for mask in range(CHIPS):
        rows = aligned((j ^ mask) * COLS, COLS)
        h_refs[mask][...] = tree_sum(
            dot_right(chips[chip], w_ref[chip, rows, :]) for chip in range(CHIPS)
        ).astype(bf16)


def attend_back_kernel(*refs, tile):
    q_ref, k_ref, v_ref = refs[:3]
    g_refs, refs = refs[3 : 3 + CHIPS], refs[3 + CHIPS :]
    lse_ref, pq_ref, pk_ref, gq_ref, gk_ref, gv_ref, sums_ref = refs[:7]
    g_all, aq_ref, ak_ref, av_ref = refs[7:]
    tokens = q_ref.shape[1]
    own = tokens // CHIPS
    for head in range(HEADS_HERE):
        span = slice(head * HEAD_DIM, (head + 1) * HEAD_DIM)
        for mask in range(CHIPS):
            g_all[head, mask * own : (mask + 1) * own, :] = g_refs[mask][:, span]

    def one_head(head, carry):
        k_head = k_ref[head]
        v_head = v_ref[head]
        k_turned = k_head.T
        for t in range(tokens // tile):
            rows = slice(t * tile, (t + 1) * tile)
            q_tile = q_ref[head, rows, :]
            g_tile = g_all[head, rows, :]
            scores = dot_right(k_head, q_tile) * (score_scale * log2_e)
            allowed = pq_ref[:, rows] >= pk_ref[...]
            scores = jnp.where(allowed, scores, masked_score)
            probs = jnp.exp2(scores - lse_ref[head, :, rows])
            grad_probs = dot_right(v_head, g_tile)
            delta = jnp.sum(probs * grad_probs, axis=0, keepdims=True)
            grad_scores = (probs * (grad_probs - delta)).astype(bf16)
            aq_ref[head, rows, :] = dot(k_turned, grad_scores).T * score_scale
            if t == 0:
                ak_ref[head] = dot(grad_scores, q_tile)
                av_ref[head] = dot(probs.astype(bf16), g_tile)
            else:
                ak_ref[head] += dot(grad_scores, q_tile)
                av_ref[head] += dot(probs.astype(bf16), g_tile)
        return carry

    lax.fori_loop(0, HEADS_HERE, one_head, 0)
    sums_ref[...] = jnp.zeros_like(sums_ref)
    for head in range(HEADS_HERE):
        span = slice(head * HEAD_DIM, (head + 1) * HEAD_DIM)
        grad_query = aq_ref[head]
        grad_value = av_ref[head]
        gq_ref[:, span] = grad_query.astype(bf16)
        gk_ref[:, span] = (ak_ref[head] * score_scale).astype(gk_ref.dtype)
        gv_ref[:, span] = grad_value.astype(gv_ref.dtype)
        sums_ref[0:1, span] = column_total(grad_query)
        sums_ref[1:2, span] = column_total(grad_value)


def qkv_back_kernel(gq_ref, gk_ref, gv_ref, w_ref, *part_refs):
    own = gq_ref.shape[0] // CHIPS
    for mask in range(CHIPS):
        rows = slice(mask * own, (mask + 1) * own)
        part_refs[mask][...] = (
            dot_right(gq_ref[rows, :], w_ref[:, :COLS])
            + dot_right(gk_ref[rows, :], w_ref[:, COLS : 2 * COLS])
            + dot_right(gv_ref[rows, :], w_ref[:, 2 * COLS :])
        ).astype(part_refs[mask].dtype)


def hidden_kernel(res_ref, *refs):
    parts, (own_ref, send_ref) = refs[:CHIPS], refs[CHIPS:]
    total = res_ref[...] + tree_sum(ref[...].astype(f32) for ref in parts)
    rows = own_ref.shape[0]
    own_ref[...] = total[:rows, :]
    send_ref[...] = total[rows:, :]


def late_grad_kernel(n_shard, *refs):
    acts, feeds, firsts, inners = (refs[i * CHIPS : (i + 1) * CHIPS] for i in range(4))
    all_ref, down_ref, in_ref = refs[4 * CHIPS :]
    down_ref[...] = tree_sum(dot_left(a[...], g[...]) for a, g in zip(acts, feeds)).astype(bf16)
    in_ref[...] = tree_sum(dot_left(a[...], g[...]) for a, g in zip(firsts, inners)).astype(bf16)
    few = FF // n_shard // GROUP
    rows_z = D // n_shard
    each = rows_z + 2 * few
    for core in range(CORES):
        lanes = slice(core * HALF, (core + 1) * HALF)
        for place in range(n_shard):
            base = (place * CORES + core) * each
            all_ref[base : base + rows_z, :] = in_ref[place * rows_z : (place + 1) * rows_z, lanes]
            rows = slice(core * HALF + place * few, core * HALF + (place + 1) * few)
            all_ref[base + rows_z : base + rows_z + few, :] = down_ref[rows, :HALF]
            all_ref[base + rows_z + few : base + each, :] = down_ref[rows, HALF:]


def late_final_kernel(n_shard, all_ref, in_latent_ref, down_latent_ref, in_ref, down_ref):
    few = FF // n_shard // GROUP
    rows_z = D // n_shard
    each = rows_z + 2 * few
    for number in range(GROUP):
        base = number * each
        for place in range(n_shard):
            goal = (place * GROUP + number) * few
            lanes = slice(goal, goal + few)
            grad = all_ref[base : base + rows_z, place * few : (place + 1) * few].astype(f32)
            keep = jnp.abs(in_latent_ref[:, lanes]) <= 1.0
            in_ref[:, lanes] = jnp.where(keep, grad, 0.0)
        rows = slice(number * few, (number + 1) * few)
        for part in range(2):
            lanes = slice(part * HALF, (part + 1) * HALF)
            low = base + rows_z + part * few
            grad = all_ref[low : low + few, :].astype(f32)
            keep = jnp.abs(down_latent_ref[rows, lanes]) <= 1.0
            down_ref[rows, lanes] = jnp.where(keep, grad, 0.0)


def out_grad_kernel(n_shard, ids_ref, *refs):
    j = ids_ref[IJ]
    h_refs, grad_ref = refs[:CHIPS], refs[CHIPS]
    outs, (cols_ref, full_ref) = refs[CHIPS + 1 : CHIPS + 1 + CHIPS], refs[CHIPS + 1 + CHIPS :]
    half = D // n_shard // CORES
    for chip in range(CHIPS):
        cols_ref[chip] = grad_ref[:, chip * COLS : (chip + 1) * COLS]
    for goal in range(CHIPS):
        cols = cols_ref[j ^ goal]
        for mask in range(CHIPS):
            full_ref[aligned((j ^ mask) * COLS, COLS), :] = dot_left(h_refs[mask][...], cols)
        for core in range(CORES):
            for place in range(n_shard):
                low = (place * CORES + core) * half
                outs[goal][place * half : (place + 1) * half, core * COLS : (core + 1) * COLS] = (
                    full_ref[low : low + half, :].astype(outs[goal].dtype)
                )


def split_hi_lo(values):
    high = values.astype(bf16)
    low = (values - high.astype(f32)).astype(bf16)
    return high, low


def early_grad_kernel(n_shard, ids_ref, *refs):
    k = ids_ref[IK]
    own_x, oth_x, gq_ref, gk_ref, gv_ref = refs[:5]
    outs, refs = refs[5 : 5 + CHIPS], refs[5 + CHIPS :]
    branch_sums, loss_sums, res_sums = refs[:3]
    b1_sums, refs = refs[3 : 3 + CHIPS], refs[3 + CHIPS :]
    qv_sums, own_ref, vec_ref, send_ref, full_ref = refs
    half = D // n_shard // CORES
    rows = own_x.shape[0] // CHIPS
    for number, g_ref in enumerate((gq_ref, gk_ref, gv_ref)):
        parts = []
        for core, x_ref in enumerate((own_x, oth_x)):
            for mask in range(CHIPS):
                goal = slice((mask * CORES + core) * rows, (mask * CORES + core + 1) * rows)
                parts.append(dot_left(x_ref[mask * rows : (mask + 1) * rows, :], g_ref[goal, :]))
        full_ref[:, number * COLS : (number + 1) * COLS] = tree_sum(parts)
    total = tree_sum(ref[...].astype(f32) for ref in outs)
    for place in range(n_shard):
        for core in range(CORES):
            low = (place * CORES + core) * half
            full_ref[low : low + half, QKV:] = total[
                place * half : (place + 1) * half, core * COLS : (core + 1) * COLS
            ]
    for place in range(n_shard):
        goal = slice(place * half, (place + 1) * half)
        mine = pl.ds(pl.multiple_of((place * CORES + k) * half, half), half)
        theirs = pl.ds(pl.multiple_of((place * CORES + 1 - k) * half, half), half)
        own_ref[goal, :] = full_ref[mine, :]
        send_ref[goal, :] = full_ref[theirs, :].astype(bf16)
    lane = lax.broadcasted_iota(jnp.int32, (1, D), 1)
    stats = jnp.zeros((1, D), f32)
    for number, row in enumerate(
        (loss_sums[3:4, :], branch_sums[0:1, :], loss_sums[4:5, :], loss_sums[5:6, :])
    ):
        stats = stats + jnp.where(lane == number, jnp.sum(row, axis=1, keepdims=True), 0.0)
    table = jnp.concatenate(
        [
            res_sums[0:1, :],
            loss_sums[0:1, :],
            res_sums[1:3, :],
            loss_sums[1:3, :],
            stats,
            tree_sum(ref[0:1, :] for ref in b1_sums),
            jnp.concatenate(
                [qv_sums[0:1, :], qv_sums[1:2, :], jnp.zeros((1, D - 2 * COLS), f32)], axis=1
            ),
            jnp.zeros((VEC_ROWS - 9, D), f32),
        ]
    )
    high, low = split_hi_lo(table)
    base = n_shard * half
    send_ref[base : base + VEC_ROWS, :] = high
    send_ref[base + VEC_ROWS : base + 2 * VEC_ROWS, :] = low
    vec_ref[...] = high.astype(f32) + low.astype(f32)


def early_split_kernel(n_shard, ids_ref, own_ref, vec_ref, got_ref, *outs):
    z = ids_ref[IZ]
    half = D // n_shard // CORES
    base = n_shard * half
    table = vec_ref[...] + (
        got_ref[base : base + VEC_ROWS, :].astype(f32)
        + got_ref[base + VEC_ROWS : base + 2 * VEC_ROWS, :].astype(f32)
    )
    high, low = split_hi_lo(table)
    for mask in range(n_shard):
        rows = aligned((z ^ mask) * half, half)
        kind = outs[mask].dtype
        outs[mask][0:half, :] = (own_ref[rows, :] + got_ref[rows, :].astype(f32)).astype(kind)
        outs[mask][half : half + VEC_ROWS, :] = high.astype(kind)
        outs[mask][half + VEC_ROWS : half + 2 * VEC_ROWS, :] = low.astype(kind)


def early_sum_kernel(*refs):
    ins, out_ref = refs[:-1], refs[-1]
    half = out_ref.shape[0] - 2 * VEC_ROWS
    out_ref[0:half, :] = tree_sum(ref[0:half, :].astype(f32) for ref in ins).astype(bf16)
    table = tree_sum(
        ref[half : half + VEC_ROWS, :].astype(f32)
        + ref[half + VEC_ROWS : half + 2 * VEC_ROWS, :].astype(f32)
        for ref in ins
    )
    high, low = split_hi_lo(table)
    out_ref[half : half + VEC_ROWS, :] = high
    out_ref[half + VEC_ROWS : half + 2 * VEC_ROWS, :] = low


def early_final_kernel(n_shard, ids_ref, lengths_ref, *refs):
    k, j = ids_ref[IK], ids_ref[IJ]
    pieces = refs[:GROUP]
    latent_ref, attn_ref, vec_ref, query_ref, stats_ref, all_ref, rows_ref, flat_ref = refs[GROUP:]
    half = D // n_shard // CORES
    few = FF // n_shard // GROUP
    units = FF // n_shard
    for core in range(CORES):
        for mask in range(CHIPS):
            ref = pieces[core * CHIPS + mask]
            all_ref[(j ^ mask) * CORES + (k ^ core)] = ref[0:half, :]
    for chip in range(CHIPS):
        for core in range(CORES):
            for number in range(4):
                lanes = slice(chip * COLS, (chip + 1) * COLS)
                rows = slice(core * half, (core + 1) * half)
                grad = all_ref[
                    chip * CORES + core, :, number * COLS : (number + 1) * COLS
                ].astype(f32)
                keep = jnp.abs(latent_ref[number, rows, lanes]) <= 1.0
                attn_ref[number, rows, lanes] = jnp.where(keep, grad, 0.0)
    tables = [
        pieces[mask][half : half + VEC_ROWS, :].astype(f32)
        + pieces[mask][half + VEC_ROWS : half + 2 * VEC_ROWS, :].astype(f32)
        for mask in range(CHIPS)
    ]
    total = tree_sum(tables)
    for mask in range(CHIPS):
        rows_ref[j ^ mask] = tables[mask]
    count = lengths_ref[0]
    for number in range(1, lengths_ref.shape[0]):
        count = count + lengths_ref[number]
    scale = count.astype(f32) * D
    stats = total[ROW_STATS : ROW_STATS + 1, 0:128] / scale
    lane = lax.broadcasted_iota(jnp.int32, (1, 128), 1)
    stats_ref[...] = jnp.where(lane == 0, stats, jnp.sqrt(stats))
    vec_ref[1:7, :] = total[0:6, :]
    for chip in range(CHIPS):
        lanes = slice(chip * COLS, (chip + 1) * COLS)
        query_ref[:, lanes] = rows_ref[chip, ROW_QV : ROW_QV + 1, 0:COLS]
        vec_ref[0:1, lanes] = rows_ref[chip, ROW_QV : ROW_QV + 1, COLS : 2 * COLS]
        for core in range(CORES):
            for place in range(n_shard):
                start = place * units + (chip * CORES + core) * few
                row, lane = 7 + start // D, start % D
                vec_ref[row : row + 1, lane : lane + few] = rows_ref[
                    chip, ROW_B1 : ROW_B1 + 1, core * HALF + place * few : core * HALF + (place + 1) * few
                ]


def owners_kernel(ids_ref, here_ref, there_ref, out_ref):
    k = ids_ref[IK]
    out_ref[k] = here_ref[...]
    out_ref[1 - k] = there_ref[...]


def body(
    hidden_in,
    block_of,
    lengths,
    attn_latent,
    ffn_in_latent,
    ffn_out_latent,
    student_vec,
    teacher_attn,
    teacher_ffn_in,
    teacher_ffn_out,
    teacher_vec,
):
    seqs, rows, _ = hidden_in.shape
    rest = lax.axis_size("rest")
    n_shard = lax.axis_size("shard")
    own = seqs * rows
    tokens = CHIPS * own
    keys = rest * tokens
    ids = jnp.stack([lax.axis_index(name) for name in ("shard", "core", "chip", "rest")])
    half = D // n_shard // CORES
    few = FF // n_shard // GROUP
    rows_z = D // n_shard
    each = rows_z + 2 * few
    line = Line(ids.astype(jnp.int32))

    def flip(piece, axis, mask):
        size = lax.axis_size(axis)
        return lax.ppermute(piece, axis, [(a, a ^ mask) for a in range(size)])

    def gather(piece, axis):
        return [piece] + [flip(piece, axis, m) for m in range(1, lax.axis_size(axis))]

    def exchange(pieces, axis):
        return [pieces[0]] + [flip(pieces[m], axis, m) for m in range(1, len(pieces))]

    def swap(piece):
        return flip(piece, "core", 1)

    t_early, t_late = weight_pieces(
        n_shard, False, line.ids, teacher_attn, teacher_ffn_in, teacher_ffn_out
    )
    line.wait(t_early)
    s_early, s_late = weight_pieces(
        n_shard, True, line.ids, attn_latent, ffn_in_latent, ffn_out_latent
    )
    line.wait(s_early)
    sums = column_sums(line.ids, attn_latent, ffn_in_latent, ffn_out_latent)
    line.wait(sums)
    pos_row, pos_col, valid = line(
        functools.partial(places_kernel, rest, seqs=seqs, rows=rows),
        "places",
        (
            shape((1, tokens), jnp.int32),
            shape((keys, 1), jnp.int32),
            shape((own, 1), f32),
        ),
        (block_of, lengths),
        (),
    )
    for mask in (1 << bit for bit in range(n_shard.bit_length() - 1)):
        sums = sums + flip(sums, "shard", mask)
    t_late = lax.all_gather(t_late, ("shard", "core"), axis=0, tiled=True)
    s_late = lax.all_gather(s_late, ("shard", "core"), axis=0, tiled=True)

    t_qkv_half, t_out_half = line(
        functools.partial(early_kernel, n_shard, 0),
        "early_weights",
        (shape((n_shard * half, QKV)), shape((n_shard * half // 2, 2 * COLS))),
        (),
        gather(t_early, "shard"),
    )
    x_own, x_send = line(
        input_kernel,
        "input",
        (shape((tokens // CORES, D)), shape((tokens // CORES, D))),
        (),
        gather(hidden_in, "chip"),
    )
    x_oth = swap(x_send)

    def rest_gather(values):
        if rest == 1:
            return values
        return jnp.concatenate(gather(values, "rest"), axis=1)

    def rest_scatter(partial):
        if rest == 1:
            return partial
        view = partial.reshape(rest, tokens, COLS)
        return tree_sum(
            [view[0]]
            + [flip(view[m].astype(bf16), "rest", m).astype(f32) for m in range(1, rest)]
        ).astype(bf16)

    def project(student, qkv_half, vector):
        heads = shape((HEADS_HERE, tokens, HEAD_DIM))
        query, key, value, w_qkv = line(
            functools.partial(qkv_kernel, n_shard, student),
            "qkv",
            (heads, heads, heads, shape((D, QKV))),
            (),
            [x_own, x_oth, qkv_half, swap(qkv_half), vector] + [sums] * student,
        )
        return query, rest_gather(key), rest_gather(value), w_qkv

    def attend(query, key, value):
        *heads, lse = line(
            functools.partial(attend_kernel, tile=own),
            "attend",
            tuple([shape((own, COLS))] * CHIPS + [shape((HEADS_HERE, 1, tokens), f32)]),
            (),
            (query, key, value, pos_row, pos_col),
            (pltpu.VMEM((HEADS_HERE, tokens, HEAD_DIM), bf16),),
            limit=20 if rest == 1 else 48,
            bare=True,
        )
        return exchange(heads, "chip"), lse

    def branch(student, heads, w_out, vector):
        outs = [shape((own, D), f32), shape((own, D))]
        if student:
            outs += [shape((own, D), f32), shape((8, D), f32)]
        return line(
            functools.partial(branch_kernel, student),
            "branch",
            tuple(outs),
            (),
            (*heads, w_out, x_own, x_oth, vector, valid),
        )

    def late_weights(student, gathered, vector):
        return line(
            functools.partial(late_kernel, n_shard, student),
            "late_weights",
            (shape((D, UNITS)), shape((UNITS, D)), shape((8, UNITS), f32)),
            (),
            [gathered, vector] + [sums] * student,
        )

    def feed(student, piece, mask, late):
        outs = [shape((own, D), f32 if mask == 0 else bf16)]
        if student:
            outs += [shape((own, UNITS), f32), shape((own, UNITS))]
        return line(
            functools.partial(feed_kernel, student),
            "feed",
            tuple(outs),
            (),
            (piece, *late),
            bare=True,
        )

    t_query, t_key, t_value, _ = project(False, t_qkv_half, teacher_vec)
    s_qkv_half, out_half = line(
        functools.partial(early_kernel, n_shard, 1),
        "early_weights",
        (shape((n_shard * half, QKV)), shape((n_shard * half, 2 * COLS))),
        (),
        gather(s_early, "shard") + [t_out_half],
    )
    t_heads, _ = attend(t_query, t_key, t_value)
    query, key, value, w_qkv = project(True, s_qkv_half, student_vec)
    out_all = list(line.behind(*gather(out_half, "chip")))
    t_out, s_out = line(
        functools.partial(out_weight_kernel, n_shard),
        "out_weights",
        (shape((CHIPS, D, COLS)), shape((CHIPS, D, COLS))),
        (),
        out_all + [swap(piece) for piece in out_all] + [sums],
        (pltpu.VMEM((CHIPS, 1, COLS), f32),),
    )
    t_first, t_sent = branch(False, t_heads, t_out, teacher_vec)
    t_firsts = gather(t_sent, "chip")
    heads, lse = attend(query, key, value)
    t_late = late_weights(False, t_late, teacher_vec)
    t_parts = [feed(False, t_firsts[0], 0, t_late)[0]]
    first, sent, residual, branch_sums = branch(True, heads, s_out, student_vec)
    firsts = gather(sent, "chip")
    t_parts += [feed(False, t_firsts[m], m, t_late)[0] for m in range(1, CHIPS)]
    t_parts = exchange(t_parts, "chip")
    s_late = late_weights(True, s_late, student_vec)
    w_in, w_down, _ = s_late
    fed = [feed(True, firsts[m], m, s_late) for m in range(CHIPS)]
    parts, inners, acts = ([f[i] for f in fed] for i in range(3))
    target = line(
        target_kernel,
        "target",
        shape((own, D), f32),
        (),
        (*t_parts, t_first, teacher_vec),
        bare=True,
    )
    out, grad_second, sent, loss_sums = line(
        loss_kernel,
        "loss",
        (shape((own, D)), shape((own, D), f32), shape((own, D)), shape((8, D), f32)),
        (lengths,),
        (*exchange(parts, "chip"), first, student_vec, target, valid),
    )

    feeds = gather(sent, "chip")

    def to_owners(here, there):
        return line(
            owners_kernel,
            "owners",
            shape((CORES, *here.shape), here.dtype),
            (),
            (here, swap(there)),
        )

    output = to_owners(out[:rows], out[rows:])
    backs = [
        line(
            feed_back_kernel,
            "feed_back",
            (
                shape((own, D), f32 if m == 0 else bf16),
                shape((own, UNITS)),
                shape((8, UNITS), f32),
            ),
            (),
            (feeds[m], inners[m], w_in, w_down),
            bare=True,
        )
        for m in range(CHIPS)
    ]
    parts, grad_inners, b1_sums = ([b[i] for b in backs] for i in range(3))
    late_grad = line(
        functools.partial(late_grad_kernel, n_shard),
        "late_grad",
        shape((n_shard * CORES * each, HALF)),
        (),
        (*acts, *feeds, *firsts, *grad_inners),
        (pltpu.VMEM((UNITS, D), bf16), pltpu.VMEM((D, UNITS), bf16)),
        limit=24,
        bare=True,
    )
    grad_res, grad_branch, *rest_outs = line(
        branch_back_kernel,
        "branch_back",
        tuple(
            [shape((own, D), f32), shape((own, D))]
            + [shape((own, COLS))] * CHIPS
            + [shape((8, D), f32)]
        ),
        (),
        (*exchange(parts, "chip"), grad_second, residual, student_vec, s_out),
    )
    grad_heads, res_sums = exchange(rest_outs[:CHIPS], "chip"), rest_outs[CHIPS]
    line.wait(*grad_heads)
    out_parts = line(
        functools.partial(out_grad_kernel, n_shard),
        "out_grad",
        tuple(
            shape((n_shard * half, 2 * COLS), f32 if m == 0 else bf16) for m in range(CHIPS)
        ),
        (),
        (*heads, grad_branch),
        (pltpu.VMEM((CHIPS, own, COLS), bf16), pltpu.VMEM((D, COLS), f32)),
    )
    late = lax.psum_scatter(late_grad, ("shard", "core"), scatter_dimension=0, tiled=True)
    (late,) = line.behind(late)
    if rest > 1:
        late = lax.psum(late, "rest")
    late = lax.all_gather(late, ("chip", "core"), axis=0, tiled=True)
    kind = bf16 if rest == 1 else f32
    grad_query, grad_key, grad_value, qv_sums = line(
        functools.partial(attend_back_kernel, tile=own),
        "attend_back",
        (
            shape((tokens, COLS)),
            shape((keys, COLS), kind),
            shape((keys, COLS), kind),
            shape((8, COLS), f32),
        ),
        (),
        (query, key, value, *grad_heads, lse, pos_row, pos_col),
        (
            pltpu.VMEM((HEADS_HERE, tokens, HEAD_DIM), bf16),
            pltpu.VMEM((HEADS_HERE, tokens, HEAD_DIM), f32),
            pltpu.VMEM((HEADS_HERE, keys, HEAD_DIM), f32),
            pltpu.VMEM((HEADS_HERE, keys, HEAD_DIM), f32),
        ),
        limit=28 if rest == 1 else 56,
        bare=True,
    )
    grad_key, grad_value = rest_scatter(grad_key), rest_scatter(grad_value)
    mine, table, send = line(
        functools.partial(early_grad_kernel, n_shard),
        "early_grad",
        (
            shape((n_shard * half, D), f32),
            shape((VEC_ROWS, D), f32),
            shape((n_shard * half + 2 * VEC_ROWS, D)),
        ),
        (),
        (
            x_own,
            x_oth,
            grad_query,
            grad_key,
            grad_value,
            *exchange(out_parts, "chip"),
            branch_sums,
            loss_sums,
            res_sums,
            *b1_sums,
            qv_sums,
        ),
        (pltpu.VMEM((D, D), f32),),
        limit=20,
    )
    parts = line(
        qkv_back_kernel,
        "qkv_back",
        tuple(shape((own, D), f32 if m == 0 else bf16) for m in range(CHIPS)),
        (),
        (grad_query, grad_key, grad_value, w_qkv),
        bare=True,
    )
    pieces = line(
        functools.partial(early_split_kernel, n_shard),
        "early_split",
        tuple(
            shape((half + 2 * VEC_ROWS, D), f32 if m == 0 else bf16) for m in range(n_shard)
        ),
        (),
        (mine, table, swap(send)),
    )
    here, there = line(
        hidden_kernel,
        "hidden",
        (shape((rows, D), f32), shape((rows, D), f32)),
        (),
        (grad_res, *exchange(parts, "chip")),
        bare=True,
    )
    early = line(
        early_sum_kernel,
        "early_sum",
        shape((half + 2 * VEC_ROWS, D)),
        (),
        exchange(pieces, "shard"),
        bare=True,
    )
    if rest > 1:
        early = line(
            early_sum_kernel, "rest_sum", shape(early.shape), (), gather(early, "rest"), bare=True
        )
    early = gather(early, "chip")
    grad_hidden = to_owners(here, there)
    in_grad, down_grad = line(
        functools.partial(late_final_kernel, n_shard),
        "late_final",
        (shape(ffn_in_latent.shape, f32), shape(ffn_out_latent.shape, f32)),
        (),
        (late, ffn_in_latent, ffn_out_latent),
        bare=True,
    )
    early = list(line.behind(*early))
    attn_grad, vec_grad, query_grad, stats = line(
        functools.partial(early_final_kernel, n_shard),
        "early_final",
        (
            shape(attn_latent.shape, f32),
            shape((7 + FF // D, D), f32),
            shape((1, D), f32),
            shape((1, 128), f32),
        ),
        (lengths,),
        (*early, *[swap(piece) for piece in early], attn_latent),
        (
            pltpu.VMEM((GROUP, half, D), bf16),
            pltpu.VMEM((CHIPS, VEC_ROWS, D), f32),
            pltpu.VMEM((8, D), f32),
        ),
    )
    return (
        output,
        stats[0, :4],
        grad_hidden,
        attn_grad,
        in_grad,
        down_grad,
        vec_grad,
        query_grad[0],
    )


def solution(mesh):
    n_ctx, n_shard = mesh.shape["ctx"], mesh.shape["shard"]
    places = mesh.devices.reshape(n_ctx // GROUP, CHIPS, CORES, n_shard)
    inner = Mesh(places, ("rest", "chip", "core", "shard"))
    ctx = ("rest", "chip", "core")
    in_specs = (
        P("shard", ctx, None),
        P(),
        P(),
        P(None, "shard", None),
        P("shard", None),
        P("shard", None),
        P(),
        P(None, "shard", None),
        P("shard", None),
        P("shard", None),
        P(),
    )
    out_specs = (
        P("shard", ctx, None),
        P(),
        P("shard", ctx, None),
        P(None, "shard", None),
        P("shard", None),
        P("shard", None),
        P(),
        P(),
    )
    return jax.shard_map(
        body, mesh=inner, in_specs=in_specs, out_specs=out_specs, check_vma=False
    )
```

time: 476 us -> 391 us (0.82)
  the two profiles are of different devices: /device:TPU:9 before, /device:TPU:0 now
where the time goes in v3:
time: 391 us; the launch traced here: 383 us
  waiting for transfers between devices  129 us (33%)
  Pallas kernels  108 us (28%)
  starting transfers between devices  78.4 us (20%)
  local copies, waits for them, and re-layouts  51.6 us (13%)
  between operations  15 us (4%)
    ppermute x67, waiting for transfers between devices, flip(): return lax.ppermute(piece, axis, [(a, a ^ mask) for a in range(size)])  129 us
    pallas_call x40, Pallas kernels, call(): pl.pallas_call(kernel, out_shape=outs, in_specs=[SMEM_SPEC] * len(scalars...  103 us
    ppermute x67, starting transfers between devices, flip(): return lax.ppermute(piece, axis, [(a, a ^ mask) for a in range(size)])  78.2 us
    unnamed x196, local copies, waits for them, and re-layouts  51.1 us
  transfers between devices with their start and end apart: 71, of which 29 were waited for; matrix products, arithmetic and copies ran while one was open for 0% of the time, Pallas kernels for 25%

profile of v3, /device:TPU:0, one launch (start us, length us, event | category | flops | bytes accessed | tf_op | source)
XLA Modules:
  0.0 383.4 jit_solution(3948529131818287387)
XLA Ops:
  11.3 2.0 teacher_pieces.1
  16.7 2.2 student_pieces.1
  19.0 3.0 collective-permute-start.4
  23.6 4.0 %collective-permute-start.2 = (bf16[96,768]{1,0:T(8,128)(2,1)S(1)}, bf16[96,768]{1,0:T(8,128)(2,1)S(1)}, u32[]{:S(2)}, u32[]{:S(2)}) collective-permute-start(bf16[96,768]{1,0:T(8,128)(2,1)S(1)} %get-tuple-element.165.refs_0_), channel_id=1, source_target_pairs={{0,3},{1,2},{2,1},{3,0},{4,7},{5,6},{6,5},{7,4},{8,11},{9,10},{10,... | collective-permute-start | bytes 442376 | tf_op jit(solution)/shard_map/ppermute | solution.py:865
  27.6 7.3 %collective-permute-done.2.refs_3_ = bf16[96,768]{1,0:T(8,128)(2,1)S(1)} collective-permute-done((bf16[96,768]{1,0:T(8,128)(2,1)S(1)}, bf16[96,768]{1,0:T(8,128)(2,1)S(1)}, u32[]{:S(2)}, u32[]{:S(2)}) %collective-permute-start.2) | collective-permute-done | bytes 147488 | tf_op jit(solution)/shard_map/ppermute | solution.py:865
  35.0 11.2 %collective-permute-start = (bf16[96,768]{1,0:T(8,128)(2,1)S(1)}, bf16[96,768]{1,0:T(8,128)(2,1)S(1)}, u32[]{:S(2)}, u32[]{:S(2)}) collective-permute-start(bf16[96,768]{1,0:T(8,128)(2,1)S(1)} %get-tuple-element.165.refs_0_), channel_id=1, source_target_pairs={{0,1},{1,0},{2,3},{3,2},{4,5},{5,4},{6,7},{7,6},{8,9},{9,8},{10,11... | collective-permute-start | bytes 442376 | tf_op jit(solution)/shard_map/ppermute | solution.py:865
  53.6 5.7 %collective-permute-done.refs_1_ = bf16[96,768]{1,0:T(8,128)(2,1)S(1)} collective-permute-done((bf16[96,768]{1,0:T(8,128)(2,1)S(1)}, bf16[96,768]{1,0:T(8,128)(2,1)S(1)}, u32[]{:S(2)}, u32[]{:S(2)}) %collective-permute-start) | collective-permute-done | bytes 147488 | tf_op jit(solution)/shard_map/ppermute | solution.py:865
  63.3 2.9 collective-permute-start.8
  66.2 2.2 qkv.2
  68.4 2.0 collective-permute-done.10.refs_3_
  70.4 12.9 %collective-permute-done.9.refs_2_ = bf16[96,768]{1,0:T(8,128)(2,1)S(1)} collective-permute-done((bf16[96,768]{1,0:T(8,128)(2,1)S(1)}, bf16[96,768]{1,0:T(8,128)(2,1)S(1)}, u32[]{:S(2)}, u32[]{:S(2)}) %collective-permute-start.9) | collective-permute-done | bytes 147488 | tf_op jit(solution)/shard_map/ppermute | solution.py:865
  84.4 2.6 collective-permute-start.16
  88.0 7.3 %collective-permute-done.12 = f32[16,768]{1,0:T(8,128)S(1)} collective-permute-done((f32[16,768]{1,0:T(8,128)S(1)}, f32[16,768]{1,0:T(8,128)S(1)}, u32[]{:S(2)}, u32[]{:S(2)}) %collective-permute-start.12) | collective-permute-done | bytes 49184 | tf_op jit(solution)/shard_map/ppermute | solution.py:865
  95.4 5.0 %collective-permute-done.13 = f32[16,768]{1,0:T(8,128)S(1)} collective-permute-done((f32[16,768]{1,0:T(8,128)S(1)}, f32[16,768]{1,0:T(8,128)S(1)}, u32[]{:S(2)}, u32[]{:S(2)}) %collective-permute-start.13) | collective-permute-done | bytes 49184 | tf_op jit(solution)/shard_map/ppermute | solution.py:865
  100.4 10.5 %attend.2 = (bf16[256,192]{1,0:T(8,128)(2,1)S(1)}, bf16[256,192]{1,0:T(8,128)(2,1)S(1)}, bf16[256,192]{1,0:T(8,128)(2,1)S(1)}, bf16[256,192]{1,0:T(8,128)(2,1)S(1)}, f32[3,1,1024]{2,1,0:T(1,128)}) custom-call(s32[4]{0:T(128)S(1)} %pad_add_fusion.ids_ref, bf16[3,1024,64]{2,1,0:T(8,128)(2,1)S(1)} %get-tuple-element.177.refs_0_, ...), custom_call_target="tpu_custom_call" | custom-call | tf_op jit(solution)/shard_map/attend/pallas_call | solution.py:78
  110.9 2.3 qkv.3
  121.7 3.1 collective-permute-done.22.refs_2_
  124.8 2.3 branch.2
  131.5 10.9 %attend.3 = (bf16[256,192]{1,0:T(8,128)(2,1)S(1)}, bf16[256,192]{1,0:T(8,128)(2,1)S(1)}, bf16[256,192]{1,0:T(8,128)(2,1)}, bf16[256,192]{1,0:T(8,128)(2,1)}, f32[3,1,1024]{2,1,0:T(1,128)S(1)}) custom-call(s32[4]{0:T(128)S(1)} %pad_add_fusion.ids_ref, bf16[3,1024,64]{2,1,0:T(8,128)(2,1)S(1)} %get-tuple-element.187.refs_0_, ...), custom_call_target="tpu_custom_call" | custom-call | tf_op jit(solution)/shard_map/attend/pallas_call | solution.py:78
  145.4 3.9 %collective-permute-done.24.refs_1_ = bf16[256,192]{1,0:T(8,128)(2,1)S(1)} collective-permute-done((bf16[256,192]{1,0:T(8,128)(2,1)S(1)}, bf16[256,192]{1,0:T(8,128)(2,1)S(1)}, u32[]{:S(2)}, u32[]{:S(2)}) %collective-permute-start.24) | collective-permute-done | bytes 98336 | tf_op jit(solution)/shard_map/ppermute | solution.py:865
  153.6 2.1 feed.8.refs_0_
  157.8 2.0 branch.3
  166.1 2.7 feed.10
  168.8 2.7 feed.11
  191.4 3.6 collective-permute-done.34.refs_2_
  195.0 3.1 collective-permute-done.33.refs_1_
  199.8 6.8 %collective-permute-done.36.refs_1_ = bf16[256,768]{1,0:T(8,128)(2,1)S(1)} collective-permute-done((bf16[256,768]{1,0:T(8,128)(2,1)S(1)}, bf16[256,768]{1,0:T(8,128)(2,1)S(1)}, u32[]{:S(2)}, u32[]{:S(2)}) %collective-permute-start.36) | collective-permute-done | bytes 393248 | tf_op jit(solution)/shard_map/ppermute | solution.py:865
  206.6 5.0 %collective-permute-done.38.refs_3_ = bf16[256,768]{1,0:T(8,128)(2,1)S(1)} collective-permute-done((bf16[256,768]{1,0:T(8,128)(2,1)S(1)}, bf16[256,768]{1,0:T(8,128)(2,1)S(1)}, u32[]{:S(2)}, u32[]{:S(2)}) %collective-permute-start.38) | collective-permute-done | bytes 393248 | tf_op jit(solution)/shard_map/ppermute | solution.py:865
  222.0 10.3 %collective-permute-done.40.refs_0_.refs_5_ = bf16[256,768]{1,0:T(8,128)(2,1)S(1)} collective-permute-done((bf16[256,768]{1,0:T(8,128)(2,1)S(1)}, bf16[256,768]{1,0:T(8,128)(2,1)S(1)}, u32[]{:S(2)}, u32[]{:S(2)}) %collective-permute-start.40) | collective-permute-done | bytes 393248 | tf_op jit(solution)/shard_map/ppermute | solution.py:865
  232.3 2.0 feed_back.5
  240.2 4.2 %late_grad.1 = bf16[3072,384]{1,0:T(8,128)(2,1)S(1)} custom-call(s32[4]{0:T(128)S(1)} %pad_add_fusion.ids_ref, bf16[256,768]{1,0:T(8,128)(2,1)S(1)} %get-tuple-element.253.refs_0_, bf16[256,768]{1,0:T(8,128)(2,1)S(1)} %get-tuple-element.254.refs_1_, bf16[256,768]{1,0:T(8,128)(2,1)S(1)} %get-tuple-element.255.refs_2_, ...), custom_call_target="tpu_custom_call" | custom-call | tf_op jit(solution)/shard_map/late_grad/pallas_call | solution.py:78
  247.0 2.5 collective-permute-start.43
  249.4 9.3 %collective-permute-done.45.refs_3_ = bf16[256,768]{1,0:T(8,128)(2,1)S(1)} collective-permute-done((bf16[256,768]{1,0:T(8,128)(2,1)}, bf16[256,768]{1,0:T(8,128)(2,1)S(1)}, u32[]{:S(2)}, u32[]{:S(2)}) %collective-permute-start.45) | collective-permute-done | bytes 393248 | tf_op jit(solution)/shard_map/ppermute | solution.py:865
  258.8 4.0 %collective-permute-done.44.refs_2_ = bf16[256,768]{1,0:T(8,128)(2,1)S(1)} collective-permute-done((bf16[256,768]{1,0:T(8,128)(2,1)}, bf16[256,768]{1,0:T(8,128)(2,1)S(1)}, u32[]{:S(2)}, u32[]{:S(2)}) %collective-permute-start.44) | collective-permute-done | bytes 393248 | tf_op jit(solution)/shard_map/ppermute | solution.py:865
  267.7 2.0 branch_back.1
  277.4 3.4 collective-permute-done.47.refs_5_
  282.1 2.1 out_grad.1
  299.7 13.8 %attend_back.1 = (bf16[1024,192]{1,0:T(8,128)(2,1)S(1)}, bf16[1024,192]{1,0:T(8,128)(2,1)S(1)}, bf16[1024,192]{1,0:T(8,128)(2,1)S(1)}, f32[8,192]{1,0:T(8,128)S(1)}) custom-call(s32[4]{0:T(128)S(1)} %pad_add_fusion.ids_ref, bf16[3,1024,64]{2,1,0:T(8,128)(2,1)S(1)} %copy-done.17, bf16[3,1024,64]{2,1,0:T(8,128)(2,1)S(1)} %copy-done.19, ...), custom_call_target="tpu_custom_call" | custom-call | tf_op jit(solution)/shard_map/attend_back/pallas_call | solution.py:78
  314.3 3.4 early_grad.1
  317.8 2.0 qkv_back.1
  324.1 7.8 %collective-permute-done.53.refs_2_ = bf16[256,768]{1,0:T(8,128)(2,1)S(1)} collective-permute-done((bf16[256,768]{1,0:T(8,128)(2,1)S(1)}, bf16[256,768]{1,0:T(8,128)(2,1)S(1)}, u32[]{:S(2)}, u32[]{:S(2)}) %collective-permute-start.53) | collective-permute-done | bytes 393248 | tf_op jit(solution)/shard_map/ppermute | solution.py:865
  331.8 8.1 %collective-permute-done.54.refs_3_ = bf16[256,768]{1,0:T(8,128)(2,1)S(1)} collective-permute-done((bf16[256,768]{1,0:T(8,128)(2,1)S(1)}, bf16[256,768]{1,0:T(8,128)(2,1)S(1)}, u32[]{:S(2)}, u32[]{:S(2)}) %collective-permute-start.54) | collective-permute-done | bytes 393248 | tf_op jit(solution)/shard_map/ppermute | solution.py:865
  340.9 2.3 collective-permute-start.57
  343.3 2.0 collective-permute-start.58
  345.3 6.3 %collective-permute-done.56.refs_1_ = bf16[128,768]{1,0:T(8,128)(2,1)S(1)} collective-permute-done((bf16[128,768]{1,0:T(8,128)(2,1)S(1)}, bf16[128,768]{1,0:T(8,128)(2,1)S(1)}, u32[]{:S(2)}, u32[]{:S(2)}) %collective-permute-start.56) | collective-permute-done | bytes 196640 | tf_op jit(solution)/shard_map/ppermute | solution.py:865
  351.6 6.5 %collective-permute-done.57.refs_2_ = bf16[128,768]{1,0:T(8,128)(2,1)S(1)} collective-permute-done((bf16[128,768]{1,0:T(8,128)(2,1)S(1)}, bf16[128,768]{1,0:T(8,128)(2,1)S(1)}, u32[]{:S(2)}, u32[]{:S(2)}) %collective-permute-start.57) | collective-permute-done | bytes 196640 | tf_op jit(solution)/shard_map/ppermute | solution.py:865
  367.1 3.6 late_final.1
  373.0 2.6 early_final.1
  (343 shorter events, 138.6 us)
Async XLA Ops:
  7.2 143.9 %all-gather.4.cloned.1.call-start = ((), (), s32[]{:S(2)}) async-start(), calls=%async_computation.1 | async-start | bytes 2654208 | tf_op jit(solution)/shard_map/all_gather | solution.py:899
  13.3 161.0 %all-gather.6.cloned.1.call-start = ((), (), s32[]{:S(2)}) async-start(), calls=%async_computation.2 | async-start | bytes 2654208 | tf_op jit(solution)/shard_map/all_gather | solution.py:900
  19.0 268.3 %reduce-scatter.2.cloned.1.call-start = ((), (), s32[]{:S(2)}) async-start(), calls=%async_computation.3 | async-start | bytes 2654208 | tf_op jit(solution)/shard_map/reduce_scatter | solution.py:1099
  19.0 41.0 %collective-permute-start.4 = (bf16[2,128,768]{2,1,0:T(8,128)(2,1)}, bf16[2,128,768]{2,1,0:T(8,128)(2,1)S(1)}, u32[]{:S(2)}, u32[]{:S(2)}) collective-permute-start(bf16[2,128,768]{2,1,0:T(8,128)(2,1)} %refs_0_.1), channel_id=1, source_target_pairs={{0,16},{8,24},{16,0},{24,8},{1,17},{9,25},{17,1},{25,9},{2,18},{10... | collective-permute-start | bytes 1179656 | tf_op jit(solution)/shard_map/ppermute | solution.py:865
  22.1 38.0 %collective-permute-start.3 = (bf16[2,128,768]{2,1,0:T(8,128)(2,1)}, bf16[2,128,768]{2,1,0:T(8,128)(2,1)S(1)}, u32[]{:S(2)}, u32[]{:S(2)}) collective-permute-start(bf16[2,128,768]{2,1,0:T(8,128)(2,1)} %refs_0_.1), channel_id=1, source_target_pairs={{0,8},{8,0},{16,24},{24,16},{1,9},{9,1},{17,25},{25,17},{2,10},{10... | collective-permute-start | bytes 1179656 | tf_op jit(solution)/shard_map/ppermute | solution.py:865
  23.6 36.5 %collective-permute-start.5 = (bf16[2,128,768]{2,1,0:T(8,128)(2,1)}, bf16[2,128,768]{2,1,0:T(8,128)(2,1)S(1)}, u32[]{:S(2)}, u32[]{:S(2)}) collective-permute-start(bf16[2,128,768]{2,1,0:T(8,128)(2,1)} %refs_0_.1), channel_id=1, source_target_pairs={{0,24},{8,16},{16,8},{24,0},{1,25},{9,17},{17,9},{25,1},{2,26},{10... | collective-permute-start | bytes 1179656 | tf_op jit(solution)/shard_map/ppermute | solution.py:865
  23.6 11.4 %collective-permute-start.2 = (bf16[96,768]{1,0:T(8,128)(2,1)S(1)}, bf16[96,768]{1,0:T(8,128)(2,1)S(1)}, u32[]{:S(2)}, u32[]{:S(2)}) collective-permute-start(bf16[96,768]{1,0:T(8,128)(2,1)S(1)} %get-tuple-element.165.refs_0_), channel_id=1, source_target_pairs={{0,3},{1,2},{2,1},{3,0},{4,7},{5,6},{6,5},{7,4},{8,11},{9,10},{10,... | collective-permute-start | bytes 442376 | tf_op jit(solution)/shard_map/ppermute | solution.py:865
  27.6 25.9 %collective-permute-start.1 = (bf16[96,768]{1,0:T(8,128)(2,1)S(1)}, bf16[96,768]{1,0:T(8,128)(2,1)S(1)}, u32[]{:S(2)}, u32[]{:S(2)}) collective-permute-start(bf16[96,768]{1,0:T(8,128)(2,1)S(1)} %get-tuple-element.165.refs_0_), channel_id=1, source_target_pairs={{0,2},{1,3},{2,0},{3,1},{4,6},{5,7},{6,4},{7,5},{8,10},{9,11},{10,... | collective-permute-start | bytes 442376 | tf_op jit(solution)/shard_map/ppermute | solution.py:865
  35.0 24.3 %collective-permute-start = (bf16[96,768]{1,0:T(8,128)(2,1)S(1)}, bf16[96,768]{1,0:T(8,128)(2,1)S(1)}, u32[]{:S(2)}, u32[]{:S(2)}) collective-permute-start(bf16[96,768]{1,0:T(8,128)(2,1)S(1)} %get-tuple-element.165.refs_0_), channel_id=1, source_target_pairs={{0,1},{1,0},{2,3},{3,2},{4,5},{5,4},{6,7},{7,6},{8,9},{9,8},{10,11... | collective-permute-start | bytes 442376 | tf_op jit(solution)/shard_map/ppermute | solution.py:865
  63.3 20.0 %collective-permute-start.9 = (bf16[96,768]{1,0:T(8,128)(2,1)S(1)}, bf16[96,768]{1,0:T(8,128)(2,1)S(1)}, u32[]{:S(2)}, u32[]{:S(2)}) collective-permute-start(bf16[96,768]{1,0:T(8,128)(2,1)S(1)} %get-tuple-element.167.refs_0_), channel_id=1, source_target_pairs={{0,2},{1,3},{2,0},{3,1},{4,6},{5,7},{6,4},{7,5},{8,10},{9,11},{10,... | collective-permute-start | bytes 442376 | tf_op jit(solution)/shard_map/ppermute | solution.py:865
  63.3 20.0 %collective-permute-start.8 = (bf16[96,768]{1,0:T(8,128)(2,1)S(1)}, bf16[96,768]{1,0:T(8,128)(2,1)S(1)}, u32[]{:S(2)}, u32[]{:S(2)}) collective-permute-start(bf16[96,768]{1,0:T(8,128)(2,1)S(1)} %get-tuple-element.167.refs_0_), channel_id=1, source_target_pairs={{0,1},{1,0},{2,3},{3,2},{4,5},{5,4},{6,7},{7,6},{8,9},{9,8},{10,11... | collective-permute-start | bytes 442376 | tf_op jit(solution)/shard_map/ppermute | solution.py:865
  84.3 26.6 %collective-permute-start.11 = (bf16[384,576]{1,0:T(8,128)(2,1)S(1)}, bf16[384,576]{1,0:T(8,128)(2,1)S(1)}, u32[]{:S(2)}, u32[]{:S(2)}) collective-permute-start(bf16[384,576]{1,0:T(8,128)(2,1)S(1)} %get-tuple-element.180.half_ref), channel_id=1, source_target_pairs={{0,4},{4,0},{1,5},{5,1},{2,6},{6,2},{3,7},{7,3},{8,12},{12,8},{9,1... | collective-permute-start | bytes 1327112 | tf_op jit(solution)/shard_map/ppermute | solution.py:865
  84.4 29.8 %collective-permute-start.16 = (bf16[384,384]{1,0:T(8,128)(2,1)S(1)}, bf16[384,384]{1,0:T(8,128)(2,1)S(1)}, u32[]{:S(2)}, u32[]{:S(2)}) collective-permute-start(bf16[384,384]{1,0:T(8,128)(2,1)S(1)} %get-tuple-element.190.refs_0_), channel_id=1, source_target_pairs={{0,24},{8,16},{16,8},{24,0},{1,25},{9,17},{17,9},{25,1},{2,26},{10... | collective-permute-start | bytes 884744 | tf_op jit(solution)/shard_map/ppermute | solution.py:865
  87.0 27.2 %collective-permute-start.15 = (bf16[384,384]{1,0:T(8,128)(2,1)S(1)}, bf16[384,384]{1,0:T(8,128)(2,1)S(1)}, u32[]{:S(2)}, u32[]{:S(2)}) collective-permute-start(bf16[384,384]{1,0:T(8,128)(2,1)S(1)} %get-tuple-element.190.refs_0_), channel_id=1, source_target_pairs={{0,16},{8,24},{16,0},{24,8},{1,17},{9,25},{17,1},{25,9},{2,18},{10... | collective-permute-start | bytes 884744 | tf_op jit(solution)/shard_map/ppermute | solution.py:865
  87.5 26.7 %collective-permute-start.14 = (bf16[384,384]{1,0:T(8,128)(2,1)S(1)}, bf16[384,384]{1,0:T(8,128)(2,1)S(1)}, u32[]{:S(2)}, u32[]{:S(2)}) collective-permute-start(bf16[384,384]{1,0:T(8,128)(2,1)S(1)} %get-tuple-element.190.refs_0_), channel_id=1, source_target_pairs={{0,8},{8,0},{16,24},{24,16},{1,9},{9,1},{17,25},{25,17},{2,10},{10... | collective-permute-start | bytes 884744 | tf_op jit(solution)/shard_map/ppermute | solution.py:865
  128.0 34.8 %collective-permute-start.27 = (bf16[256,768]{1,0:T(8,128)(2,1)}, bf16[256,768]{1,0:T(8,128)(2,1)}, u32[]{:S(2)}, u32[]{:S(2)}) collective-permute-start(bf16[256,768]{1,0:T(8,128)(2,1)} %get-tuple-element.209.refs_0_), channel_id=1, source_target_pairs={{0,8},{8,0},{16,24},{24,16},{1,9},{9,1},{17,25},{25,17},{2,10},{10... | collective-permute-start | bytes 1179656 | tf_op jit(solution)/shard_map/ppermute | solution.py:865
  129.3 36.8 %collective-permute-start.28 = (bf16[256,768]{1,0:T(8,128)(2,1)}, bf16[256,768]{1,0:T(8,128)(2,1)}, u32[]{:S(2)}, u32[]{:S(2)}) collective-permute-start(bf16[256,768]{1,0:T(8,128)(2,1)} %get-tuple-element.209.refs_0_), channel_id=1, source_target_pairs={{0,16},{8,24},{16,0},{24,8},{1,17},{9,25},{17,1},{25,9},{2,18},{10... | collective-permute-start | bytes 1179656 | tf_op jit(solution)/shard_map/ppermute | solution.py:865
  130.5 38.3 %collective-permute-start.29 = (bf16[256,768]{1,0:T(8,128)(2,1)}, bf16[256,768]{1,0:T(8,128)(2,1)}, u32[]{:S(2)}, u32[]{:S(2)}) collective-permute-start(bf16[256,768]{1,0:T(8,128)(2,1)} %get-tuple-element.209.refs_0_), channel_id=1, source_target_pairs={{0,24},{8,16},{16,8},{24,0},{1,25},{9,17},{17,9},{25,1},{2,26},{10... | collective-permute-start | bytes 1179656 | tf_op jit(solution)/shard_map/ppermute | solution.py:865
  144.3 11.5 %collective-permute-start.25 = (bf16[256,192]{1,0:T(8,128)(2,1)}, bf16[256,192]{1,0:T(8,128)(2,1)}, u32[]{:S(2)}, u32[]{:S(2)}) collective-permute-start(bf16[256,192]{1,0:T(8,128)(2,1)} %get-tuple-element.214), channel_id=1, source_target_pairs={{0,16},{8,24},{16,0},{24,8},{1,17},{9,25},{17,1},{25,9},{2,18},{10... | collective-permute-start | bytes 294920 | tf_op jit(solution)/shard_map/ppermute | solution.py:865
  159.9 27.5 %collective-permute-start.32 = (bf16[256,768]{1,0:T(8,128)(2,1)S(1)}, bf16[256,768]{1,0:T(8,128)(2,1)}, u32[]{:S(2)}, u32[]{:S(2)}) collective-permute-start(bf16[256,768]{1,0:T(8,128)(2,1)S(1)} %get-tuple-element.225.refs_0_.refs_8_), channel_id=1, source_target_pairs={{0,24},{8,16},{16,8},{24,0},{1,25},{9,17},{17,9},{25,1},{2,26},{10... | collective-permute-start | bytes 1179656 | tf_op jit(solution)/shard_map/ppermute | solution.py:865
  161.2 20.2 %collective-permute-start.30 = (bf16[256,768]{1,0:T(8,128)(2,1)S(1)}, bf16[256,768]{1,0:T(8,128)(2,1)}, u32[]{:S(2)}, u32[]{:S(2)}) collective-permute-start(bf16[256,768]{1,0:T(8,128)(2,1)S(1)} %get-tuple-element.225.refs_0_.refs_8_), channel_id=1, source_target_pairs={{0,8},{8,0},{16,24},{24,16},{1,9},{9,1},{17,25},{25,17},{2,10},{10... | collective-permute-start | bytes 1179656 | tf_op jit(solution)/shard_map/ppermute | solution.py:865
  162.8 21.0 %collective-permute-start.31 = (bf16[256,768]{1,0:T(8,128)(2,1)S(1)}, bf16[256,768]{1,0:T(8,128)(2,1)}, u32[]{:S(2)}, u32[]{:S(2)}) collective-permute-start(bf16[256,768]{1,0:T(8,128)(2,1)S(1)} %get-tuple-element.225.refs_0_.refs_8_), channel_id=1, source_target_pairs={{0,16},{8,24},{16,0},{24,8},{1,17},{9,25},{17,1},{25,9},{2,18},{10... | collective-permute-start | bytes 1179656 | tf_op jit(solution)/shard_map/ppermute | solution.py:865
  171.5 18.6 %collective-permute-start.35 = (bf16[256,768]{1,0:T(8,128)(2,1)}, bf16[256,768]{1,0:T(8,128)(2,1)}, u32[]{:S(2)}, u32[]{:S(2)}) collective-permute-start(bf16[256,768]{1,0:T(8,128)(2,1)} %feed.11), channel_id=1, source_target_pairs={{0,24},{8,16},{16,8},{24,0},{1,25},{9,17},{17,9},{25,1},{2,26},{10... | collective-permute-start | bytes 1179656 | tf_op jit(solution)/shard_map/ppermute | solution.py:865
  172.8 22.3 %collective-permute-start.34 = (bf16[256,768]{1,0:T(8,128)(2,1)}, bf16[256,768]{1,0:T(8,128)(2,1)}, u32[]{:S(2)}, u32[]{:S(2)}) collective-permute-start(bf16[256,768]{1,0:T(8,128)(2,1)} %feed.10), channel_id=1, source_target_pairs={{0,16},{8,24},{16,0},{24,8},{1,17},{9,25},{17,1},{25,9},{2,18},{10... | collective-permute-start | bytes 1179656 | tf_op jit(solution)/shard_map/ppermute | solution.py:865
  181.4 16.8 %collective-permute-start.33 = (bf16[256,768]{1,0:T(8,128)(2,1)S(1)}, bf16[256,768]{1,0:T(8,128)(2,1)S(1)}, u32[]{:S(2)}, u32[]{:S(2)}) collective-permute-start(bf16[256,768]{1,0:T(8,128)(2,1)S(1)} %copy-done.65), channel_id=1, source_target_pairs={{0,8},{8,0},{16,24},{24,16},{1,9},{9,1},{17,25},{25,17},{2,10},{10... | collective-permute-start | bytes 1179656 | tf_op jit(solution)/shard_map/ppermute | solution.py:865
  183.8 22.8 %collective-permute-start.36 = (bf16[256,768]{1,0:T(8,128)(2,1)S(1)}, bf16[256,768]{1,0:T(8,128)(2,1)S(1)}, u32[]{:S(2)}, u32[]{:S(2)}) collective-permute-start(bf16[256,768]{1,0:T(8,128)(2,1)S(1)} %get-tuple-element.230), channel_id=1, source_target_pairs={{0,8},{8,0},{16,24},{24,16},{1,9},{9,1},{17,25},{25,17},{2,10},{10... | collective-permute-start | bytes 1179656 | tf_op jit(solution)/shard_map/ppermute | solution.py:865
  187.4 19.2 %collective-permute-start.37 = (bf16[256,768]{1,0:T(8,128)(2,1)S(1)}, bf16[256,768]{1,0:T(8,128)(2,1)S(1)}, u32[]{:S(2)}, u32[]{:S(2)}) collective-permute-start(bf16[256,768]{1,0:T(8,128)(2,1)S(1)} %get-tuple-element.232), channel_id=1, source_target_pairs={{0,16},{8,24},{16,0},{24,8},{1,17},{9,25},{17,1},{25,9},{2,18},{10... | collective-permute-start | bytes 1179656 | tf_op jit(solution)/shard_map/ppermute | solution.py:865
  190.1 21.6 %collective-permute-start.38 = (bf16[256,768]{1,0:T(8,128)(2,1)S(1)}, bf16[256,768]{1,0:T(8,128)(2,1)S(1)}, u32[]{:S(2)}, u32[]{:S(2)}) collective-permute-start(bf16[256,768]{1,0:T(8,128)(2,1)S(1)} %get-tuple-element.234), channel_id=1, source_target_pairs={{0,24},{8,16},{16,8},{24,0},{1,25},{9,17},{17,9},{25,1},{2,26},{10... | collective-permute-start | bytes 1179656 | tf_op jit(solution)/shard_map/ppermute | solution.py:865
  214.1 23.3 %collective-permute-start.42 = (bf16[256,768]{1,0:T(8,128)(2,1)S(1)}, bf16[256,768]{1,0:T(8,128)(2,1)S(1)}, u32[]{:S(2)}, u32[]{:S(2)}) collective-permute-start(bf16[256,768]{1,0:T(8,128)(2,1)S(1)} %get-tuple-element.240.refs_0_.refs_4_), channel_id=1, source_target_pairs={{0,24},{8,16},{16,8},{24,0},{1,25},{9,17},{17,9},{25,1},{2,26},{10... | collective-permute-start | bytes 1179656 | tf_op jit(solution)/shard_map/ppermute | solution.py:865
  215.4 19.6 %collective-permute-start.41 = (bf16[256,768]{1,0:T(8,128)(2,1)S(1)}, bf16[256,768]{1,0:T(8,128)(2,1)S(1)}, u32[]{:S(2)}, u32[]{:S(2)}) collective-permute-start(bf16[256,768]{1,0:T(8,128)(2,1)S(1)} %get-tuple-element.240.refs_0_.refs_4_), channel_id=1, source_target_pairs={{0,16},{8,24},{16,0},{24,8},{1,17},{9,25},{17,1},{25,9},{2,18},{10... | collective-permute-start | bytes 1179656 | tf_op jit(solution)/shard_map/ppermute | solution.py:865
  217.2 15.1 %collective-permute-start.40 = (bf16[256,768]{1,0:T(8,128)(2,1)S(1)}, bf16[256,768]{1,0:T(8,128)(2,1)S(1)}, u32[]{:S(2)}, u32[]{:S(2)}) collective-permute-start(bf16[256,768]{1,0:T(8,128)(2,1)S(1)} %get-tuple-element.240.refs_0_.refs_4_), channel_id=1, source_target_pairs={{0,8},{8,0},{16,24},{24,16},{1,9},{9,1},{17,25},{25,17},{2,10},{10... | collective-permute-start | bytes 1179656 | tf_op jit(solution)/shard_map/ppermute | solution.py:865
  245.8 117.9 %all-gather.8.cloned.1.call-start = ((), (), s32[]{:S(2)}) async-start(), calls=%async_computation.4 | async-start | bytes 2654208 | tf_op jit(solution)/shard_map/all_gather | solution.py:1103
  245.9 12.9 %collective-permute-start.45 = (bf16[256,768]{1,0:T(8,128)(2,1)}, bf16[256,768]{1,0:T(8,128)(2,1)S(1)}, u32[]{:S(2)}, u32[]{:S(2)}) collective-permute-start(bf16[256,768]{1,0:T(8,128)(2,1)} %copy-done.93), channel_id=1, source_target_pairs={{0,24},{8,16},{16,8},{24,0},{1,25},{9,17},{17,9},{25,1},{2,26},{10... | collective-permute-start | bytes 1179656 | tf_op jit(solution)/shard_map/ppermute | solution.py:865
  246.7 16.1 %collective-permute-start.44 = (bf16[256,768]{1,0:T(8,128)(2,1)}, bf16[256,768]{1,0:T(8,128)(2,1)S(1)}, u32[]{:S(2)}, u32[]{:S(2)}) collective-permute-start(bf16[256,768]{1,0:T(8,128)(2,1)} %copy-done.92), channel_id=1, source_target_pairs={{0,16},{8,24},{16,0},{24,8},{1,17},{9,25},{17,1},{25,9},{2,18},{10... | collective-permute-start | bytes 1179656 | tf_op jit(solution)/shard_map/ppermute | solution.py:865
  247.0 15.9 %collective-permute-start.43 = (bf16[256,768]{1,0:T(8,128)(2,1)}, bf16[256,768]{1,0:T(8,128)(2,1)S(1)}, u32[]{:S(2)}, u32[]{:S(2)}) collective-permute-start(bf16[256,768]{1,0:T(8,128)(2,1)} %copy-done.91), channel_id=1, source_target_pairs={{0,8},{8,0},{16,24},{24,16},{1,9},{9,1},{17,25},{25,17},{2,10},{10... | collective-permute-start | bytes 1179656 | tf_op jit(solution)/shard_map/ppermute | solution.py:865
  287.3 26.2 %collective-permute-start.49 = (bf16[384,384]{1,0:T(8,128)(2,1)}, bf16[384,384]{1,0:T(8,128)(2,1)S(1)}, u32[]{:S(2)}, u32[]{:S(2)}) collective-permute-start(bf16[384,384]{1,0:T(8,128)(2,1)} %copy-done.96), channel_id=1, source_target_pairs={{0,8},{8,0},{16,24},{24,16},{1,9},{9,1},{17,25},{25,17},{2,10},{10... | collective-permute-start | bytes 884744 | tf_op jit(solution)/shard_map/ppermute | solution.py:865
  287.7 25.7 %collective-permute-start.50 = (bf16[384,384]{1,0:T(8,128)(2,1)}, bf16[384,384]{1,0:T(8,128)(2,1)S(1)}, u32[]{:S(2)}, u32[]{:S(2)}) collective-permute-start(bf16[384,384]{1,0:T(8,128)(2,1)} %copy-done.95), channel_id=1, source_target_pairs={{0,16},{8,24},{16,0},{24,8},{1,17},{9,25},{17,1},{25,9},{2,18},{10... | collective-permute-start | bytes 884744 | tf_op jit(solution)/shard_map/ppermute | solution.py:865
  289.4 24.0 %collective-permute-start.51 = (bf16[384,384]{1,0:T(8,128)(2,1)}, bf16[384,384]{1,0:T(8,128)(2,1)S(1)}, u32[]{:S(2)}, u32[]{:S(2)}) collective-permute-start(bf16[384,384]{1,0:T(8,128)(2,1)} %copy-done.94), channel_id=1, source_target_pairs={{0,24},{8,16},{16,8},{24,0},{1,25},{9,17},{17,9},{25,1},{2,26},{10... | collective-permute-start | bytes 884744 | tf_op jit(solution)/shard_map/ppermute | solution.py:865
  319.9 12.0 %collective-permute-start.53 = (bf16[256,768]{1,0:T(8,128)(2,1)S(1)}, bf16[256,768]{1,0:T(8,128)(2,1)S(1)}, u32[]{:S(2)}, u32[]{:S(2)}) collective-permute-start(bf16[256,768]{1,0:T(8,128)(2,1)S(1)} %get-tuple-element.299), channel_id=1, source_target_pairs={{0,8},{8,0},{16,24},{24,16},{1,9},{9,1},{17,25},{25,17},{2,10},{10... | collective-permute-start | bytes 1179656 | tf_op jit(solution)/shard_map/ppermute | solution.py:865
  320.3 19.7 %collective-permute-start.54 = (bf16[256,768]{1,0:T(8,128)(2,1)S(1)}, bf16[256,768]{1,0:T(8,128)(2,1)S(1)}, u32[]{:S(2)}, u32[]{:S(2)}) collective-permute-start(bf16[256,768]{1,0:T(8,128)(2,1)S(1)} %get-tuple-element.300), channel_id=1, source_target_pairs={{0,16},{8,24},{16,0},{24,8},{1,17},{9,25},{17,1},{25,9},{2,18},{10... | collective-permute-start | bytes 1179656 | tf_op jit(solution)/shard_map/ppermute | solution.py:865
  322.0 18.0 %collective-permute-start.55 = (bf16[256,768]{1,0:T(8,128)(2,1)S(1)}, bf16[256,768]{1,0:T(8,128)(2,1)S(1)}, u32[]{:S(2)}, u32[]{:S(2)}) collective-permute-start(bf16[256,768]{1,0:T(8,128)(2,1)S(1)} %get-tuple-element.301), channel_id=1, source_target_pairs={{0,24},{8,16},{16,8},{24,0},{1,25},{9,17},{17,9},{25,1},{2,26},{10... | collective-permute-start | bytes 1179656 | tf_op jit(solution)/shard_map/ppermute | solution.py:865
  340.8 21.5 %collective-permute-start.59 = (f32[128,768]{1,0:T(8,128)S(1)}, f32[128,768]{1,0:T(8,128)S(1)}, u32[]{:S(2)}, u32[]{:S(2)}) collective-permute-start(f32[128,768]{1,0:T(8,128)S(1)} %get-tuple-element.308), channel_id=1, source_target_pairs={{0,4},{4,0},{1,5},{5,1},{2,6},{6,2},{3,7},{7,3},{8,12},{12,8},{9,1... | collective-permute-start | bytes 1179656 | tf_op jit(solution)/shard_map/ppermute | solution.py:865
  340.8 10.7 %collective-permute-start.56 = (bf16[128,768]{1,0:T(8,128)(2,1)S(1)}, bf16[128,768]{1,0:T(8,128)(2,1)S(1)}, u32[]{:S(2)}, u32[]{:S(2)}) collective-permute-start(bf16[128,768]{1,0:T(8,128)(2,1)S(1)} %get-tuple-element.304), channel_id=1, source_target_pairs={{0,1},{1,0},{2,3},{3,2},{4,5},{5,4},{6,7},{7,6},{8,9},{9,8},{10,11... | collective-permute-start | bytes 589832 | tf_op jit(solution)/shard_map/ppermute | solution.py:865
  340.9 17.2 %collective-permute-start.57 = (bf16[128,768]{1,0:T(8,128)(2,1)S(1)}, bf16[128,768]{1,0:T(8,128)(2,1)S(1)}, u32[]{:S(2)}, u32[]{:S(2)}) collective-permute-start(bf16[128,768]{1,0:T(8,128)(2,1)S(1)} %get-tuple-element.305), channel_id=1, source_target_pairs={{0,2},{1,3},{2,0},{3,1},{4,6},{5,7},{6,4},{7,5},{8,10},{9,11},{10,... | collective-permute-start | bytes 589832 | tf_op jit(solution)/shard_map/ppermute | solution.py:865
  343.3 14.8 %collective-permute-start.58 = (bf16[128,768]{1,0:T(8,128)(2,1)S(1)}, bf16[128,768]{1,0:T(8,128)(2,1)S(1)}, u32[]{:S(2)}, u32[]{:S(2)}) collective-permute-start(bf16[128,768]{1,0:T(8,128)(2,1)S(1)} %get-tuple-element.306), channel_id=1, source_target_pairs={{0,3},{1,2},{2,1},{3,0},{4,7},{5,6},{6,5},{7,4},{8,11},{9,10},{10,... | collective-permute-start | bytes 589832 | tf_op jit(solution)/shard_map/ppermute | solution.py:865
  358.7 11.9 %collective-permute-start.62 = (bf16[128,768]{1,0:T(8,128)(2,1)S(1)}, bf16[128,768]{1,0:T(8,128)(2,1)S(1)}, u32[]{:S(2)}, u32[]{:S(2)}) collective-permute-start(bf16[128,768]{1,0:T(8,128)(2,1)S(1)} %early_sum.1.refs_0_), channel_id=1, source_target_pairs={{0,24},{8,16},{16,8},{24,0},{1,25},{9,17},{17,9},{25,1},{2,26},{10... | collective-permute-start | bytes 589832 | tf_op jit(solution)/shard_map/ppermute | solution.py:865
  360.3 10.4 %collective-permute-start.61 = (bf16[128,768]{1,0:T(8,128)(2,1)S(1)}, bf16[128,768]{1,0:T(8,128)(2,1)S(1)}, u32[]{:S(2)}, u32[]{:S(2)}) collective-permute-start(bf16[128,768]{1,0:T(8,128)(2,1)S(1)} %early_sum.1.refs_0_), channel_id=1, source_target_pairs={{0,16},{8,24},{16,0},{24,8},{1,17},{9,25},{17,1},{25,9},{2,18},{10... | collective-permute-start | bytes 589832 | tf_op jit(solution)/shard_map/ppermute | solution.py:865
  361.9 8.8 %collective-permute-start.60 = (bf16[128,768]{1,0:T(8,128)(2,1)S(1)}, bf16[128,768]{1,0:T(8,128)(2,1)S(1)}, u32[]{:S(2)}, u32[]{:S(2)}) collective-permute-start(bf16[128,768]{1,0:T(8,128)(2,1)S(1)} %early_sum.1.refs_0_), channel_id=1, source_target_pairs={{0,8},{8,0},{16,24},{24,16},{1,9},{9,1},{17,25},{25,17},{2,10},{10... | collective-permute-start | bytes 589832 | tf_op jit(solution)/shard_map/ppermute | solution.py:865
  (121 other events, 1096.8 us)
Sparse Core Ops, SparseCore 0:
  13.4 46.6 all-gather.3
  61.8 35.6 all-gather.5
  246.0 34.1 reduce-scatter.1
  287.4 31.3 all-gather.7

commit v4 on v3

--- a/solution.py
+++ b/solution.py
@@ -32,10 +32,12 @@
 f32 = jnp.float32
 
 IZ, IK, IJ, IR = 0, 1, 2, 3
-ROW_BO, ROW_B2, ROW_G1, ROW_C1, ROW_G2, ROW_C2, ROW_STATS, ROW_B1, ROW_QV = range(9)
-VEC_ROWS = 16
+ROW_BO, ROW_B2, ROW_G1, ROW_C1, ROW_G2, ROW_C2, ROW_B1, ROW_QV = range(8)
+VEC_ROWS = 8
+EXTRA = 16
 
 SMEM_SPEC = pl.BlockSpec(memory_space=pltpu.SMEM)
+HBM_SPEC = pl.BlockSpec(memory_space=pltpu.HBM)
 VMEM_SPEC = pl.BlockSpec(memory_space=pltpu.VMEM)
 
 
@@ -115,40 +117,18 @@
     return value
 
 
-def sums_kernel(ids_ref, attn_ref, in_ref, out_ref, sums_ref):
-    @pl.when(pl.program_id(0) == 0)
-    def _():
-        sums_ref[...] = jnp.zeros_like(sums_ref)
-
-    for number in range(4):
-        sums_ref[number : number + 1, :] += jnp.sum(
-            jnp.abs(attn_ref[number]), axis=0, keepdims=True
-        )
-    for number in range(FF // D):
-        sums_ref[4 + number : 5 + number, :] += jnp.sum(
-            jnp.abs(in_ref[:, number * D : (number + 1) * D]), axis=0, keepdims=True
-        )
-    last = 4 + FF // D
-    sums_ref[last : last + 1, :] += jnp.sum(jnp.abs(out_ref[...]), axis=0, keepdims=True)
-
-
-def column_sums(ids, attn, w_in, w_down, steps=4):
-    return pl.pallas_call(
-        sums_kernel,
-        out_shape=shape((16, D), f32),
-        grid_spec=pltpu.PrefetchScalarGridSpec(
-            num_scalar_prefetch=1,
-            grid=(steps,),
-            in_specs=[
-                pl.BlockSpec((4, attn.shape[1] // steps, D), lambda i, ids: (0, i, 0)),
-                pl.BlockSpec((w_in.shape[0] // steps, FF), lambda i, ids: (i, 0)),
-                pl.BlockSpec((w_down.shape[0] // steps, D), lambda i, ids: (i, 0)),
-            ],
-            out_specs=pl.BlockSpec((16, D), lambda i, ids: (0, 0)),
-        ),
-        compiler_params=pltpu.CompilerParams(vmem_limit_bytes=16 * 2**20),
-        name="column_sums",
-    )(ids, attn, w_in, w_down)
+def split_three(values):
+    high = values.astype(bf16)
+    rest = values - high.astype(f32)
+    middle = rest.astype(bf16)
+    return high, middle, (rest - middle.astype(f32)).astype(bf16)
+
+
+def join_three(ref, row, *index):
+    return tree_sum(
+        [ref[(*index, slice(row + part, row + part + 1))].astype(f32) for part in range(3)]
+        + [0.0]
+    )
 
 
 def sign_of(values):
@@ -161,57 +141,115 @@
     return jnp.where(place == goal, 1.0, 0.0).astype(bf16)
 
 
-def pieces_kernel(n_shard, student, ids_ref, attn_ref, in_ref, down_ref, early_ref, late_ref):
+def early_pieces_kernel(student, ids_ref, attn_hbm, early_ref, attn_ref, sem):
+    k, j = ids_ref[IK], ids_ref[IJ]
+    rows_z = attn_hbm.shape[1]
+    half = rows_z // CORES
+    if student:
+        copy = pltpu.make_async_copy(attn_hbm, attn_ref, sem)
+    else:
+        copy = pltpu.make_async_copy(attn_hbm.at[:, aligned(k * half, half), :], attn_ref, sem)
+    copy.start()
+    chosen = choose(D, COLS, j * COLS)
+    if student:
+        early_ref[half:, :] = jnp.zeros((EXTRA, D), bf16)
+    copy.wait()
+    for number in range(4):
+        lanes = slice(number * COLS, (number + 1) * COLS)
+        if student:
+            full = sign_of(attn_ref[number, aligned(k * half, half), :]).astype(bf16)
+            sums = column_total(jnp.abs(attn_ref[number]))
+            sums = pick(j, [sums[:, chip * COLS : (chip + 1) * COLS] for chip in range(CHIPS)])
+            for part, row in enumerate(split_three(sums)):
+                early_ref[half + part : half + part + 1, lanes] = row
+        else:
+            full = attn_ref[number]
+        early_ref[0:half, lanes] = dot(full, chosen).astype(bf16)
+
+
+def early_pieces(line, student, attn):
+    half = attn.shape[1] // CORES
+    result = pl.pallas_call(
+        functools.partial(early_pieces_kernel, student),
+        out_shape=shape((half + EXTRA * student, D)),
+        in_specs=[SMEM_SPEC, HBM_SPEC],
+        out_specs=VMEM_SPEC,
+        scratch_shapes=[
+            pltpu.VMEM((4, attn.shape[1] if student else half, D), attn.dtype),
+            pltpu.SemaphoreType.DMA,
+        ],
+        compiler_params=pltpu.CompilerParams(vmem_limit_bytes=12 * 2**20),
+        name="early_pieces",
+    )(line.ids, attn)
+    line.wait(result)
+    return result
+
+
+def late_pieces_kernel(
+    n_shard, student, ids_ref, in_hbm, down_hbm, late_ref, in_ref, down_ref, sems
+):
     k, j = ids_ref[IK], ids_ref[IJ]
     units = FF // n_shard
     few = units // GROUP
     rows_z = in_ref.shape[0]
-
-    def travels(values):
-        return sign_of(values).astype(bf16) if student else values
-
-    chosen = choose(D, COLS, j * COLS)
-    for number in range(4):
-        early_ref[:, number * COLS : (number + 1) * COLS] = dot(
-            travels(attn_ref[number]), chosen
-        ).astype(bf16)
-    chosen = choose(units, few, (j * CORES + k) * few)
+    each = rows_z + 2 * few
+    number = j * CORES + k
+    mine = aligned(number * few, few)
+    down_hbm = down_hbm if student else down_hbm.at[mine, :]
+    copies = [
+        pltpu.make_async_copy(in_hbm, in_ref, sems.at[0]),
+        pltpu.make_async_copy(down_hbm, down_ref, sems.at[1]),
+    ]
+    for copy in copies:
+        copy.start()
+    chosen = choose(units, few, number * few)
+    copies[1].wait()
+    if student:
+        full = sign_of(down_ref[mine, :]).astype(bf16)
+        late_ref[each:, :] = jnp.zeros((EXTRA, HALF), bf16)
+        for part, row in enumerate(split_three(column_total(jnp.abs(down_ref[...])))):
+            low = each + 3 + part
+            late_ref[low : low + 1, :] = row[:, :HALF]
+            late_ref[low + 3 : low + 4, :] = row[:, HALF:]
+    else:
+        full = down_ref[...]
+    late_ref[rows_z : rows_z + few, :] = full[:, :HALF]
+    late_ref[rows_z + few : each, :] = full[:, HALF:]
+    copies[0].wait()
     for place in range(n_shard):
-        late_ref[0:rows_z, place * few : (place + 1) * few] = dot(
-            travels(in_ref[:, place * units : (place + 1) * units]), chosen
-        ).astype(bf16)
-    full = travels(down_ref[...])
-    late_ref[rows_z : rows_z + few, :] = full[:, :HALF]
-    late_ref[rows_z + few : rows_z + 2 * few, :] = full[:, HALF:]
-
-
-def weight_pieces(n_shard, student, ids, attn, w_in, w_down):
-    half = attn.shape[1] // CORES
+        lanes = slice(place * few, (place + 1) * few)
+        full = in_ref[:, place * units : (place + 1) * units]
+        if student:
+            sums = column_total(jnp.abs(full))
+            sums = pick(number, [sums[:, n * few : (n + 1) * few] for n in range(GROUP)])
+            for part, row in enumerate(split_three(sums)):
+                late_ref[each + part : each + part + 1, lanes] = row
+            full = sign_of(full).astype(bf16)
+        late_ref[0:rows_z, lanes] = dot(full, chosen).astype(bf16)
+
+
+def late_pieces(line, n_shard, student, w_in, w_down):
     few = FF // n_shard // GROUP
     rows_z = w_in.shape[0]
-    return pl.pallas_call(
-        functools.partial(pieces_kernel, n_shard, student),
-        out_shape=(shape((half, D)), shape((rows_z + 2 * few, HALF))),
-        grid_spec=pltpu.PrefetchScalarGridSpec(
-            num_scalar_prefetch=1,
-            grid=(1,),
-            in_specs=[
-                pl.BlockSpec((4, half, D), lambda i, ids: (0, ids[IK], 0)),
-                pl.BlockSpec((rows_z, FF), lambda i, ids: (0, 0)),
-                pl.BlockSpec((few, D), lambda i, ids: (CORES * ids[IJ] + ids[IK], 0)),
-            ],
-            out_specs=(
-                pl.BlockSpec((half, D), lambda i, ids: (0, 0)),
-                pl.BlockSpec((rows_z + 2 * few, HALF), lambda i, ids: (0, 0)),
-            ),
-        ),
-        compiler_params=pltpu.CompilerParams(vmem_limit_bytes=24 * 2**20),
-        name="student_pieces" if student else "teacher_pieces",
-    )(ids, attn, w_in, w_down)
-
-
-def scale_row(sums_ref, row, gain, fan_in):
-    return gain * (sums_ref[row : row + 1, :] / fan_in) * fan_in ** (-0.5)
+    result = pl.pallas_call(
+        functools.partial(late_pieces_kernel, n_shard, student),
+        out_shape=shape((rows_z + 2 * few + EXTRA * student, HALF)),
+        in_specs=[SMEM_SPEC, HBM_SPEC, HBM_SPEC],
+        out_specs=VMEM_SPEC,
+        scratch_shapes=[
+            pltpu.VMEM((rows_z, FF), w_in.dtype),
+            pltpu.VMEM((w_down.shape[0] if student else few, D), w_down.dtype),
+            pltpu.SemaphoreType.DMA((2,)),
+        ],
+        compiler_params=pltpu.CompilerParams(vmem_limit_bytes=20 * 2**20),
+        name="late_pieces",
+    )(line.ids, w_in, w_down)
+    line.wait(result)
+    return result
+
+
+def scale_row(sums, gain, fan_in):
+    return gain * (sums / fan_in) * fan_in ** (-0.5)
 
 
 def scaled(values, scale):
@@ -222,31 +260,39 @@
     group, refs = refs[:n_shard], refs[n_shard:]
     qkv_ref, out_ref = refs[-2:]
     z = ids_ref[IZ]
-    half = group[0].shape[0]
+    half = D // n_shard // CORES
     fold = n_shard // 2
     base = model * fold * half
     if model:
         out_ref[0:base, :] = refs[0][...]
+        sums = tree_sum(join_three(ref, half) for ref in group)
+        scale = jnp.concatenate(
+            [
+                scale_row(sums[:, number * COLS : (number + 1) * COLS], attn_gains[number], D)
+                for number in range(4)
+            ],
+            axis=1,
+        )
     for mask, ref in enumerate(group):
         place = z ^ mask
-        qkv_ref[aligned(place * half, half), :] = ref[:, :QKV]
+        piece = ref[0:half, :]
+        if model:
+            piece = scaled(piece, scale)
+        qkv_ref[aligned(place * half, half), :] = piece[:, :QKV]
         low = pl.ds(pl.multiple_of(base + lax.rem(place, fold) * half, half), half)
 
         @pl.when(place < fold)
         def _():
-            out_ref[low, 0:COLS] = ref[:, QKV:]
+            out_ref[low, 0:COLS] = piece[:, QKV:]
 
         @pl.when(place >= fold)
         def _():
-            out_ref[low, COLS:] = ref[:, QKV:]
+            out_ref[low, COLS:] = piece[:, QKV:]
 
 
 def out_weight_kernel(n_shard, ids_ref, *refs):
     k, j = ids_ref[IK], ids_ref[IJ]
-    sums_ref, t_ref, s_ref, scale_ref = refs[2 * CHIPS :]
-    scale = scale_row(sums_ref, 3, attn_gains[3], D)
-    for chip in range(CHIPS):
-        scale_ref[chip] = scale[:, chip * COLS : (chip + 1) * COLS]
+    t_ref, s_ref = refs[2 * CHIPS :]
     half = D // n_shard // CORES
     span = n_shard * half // 2
     for core in range(CORES):
@@ -260,23 +306,26 @@
                     rows = pl.ds(
                         pl.multiple_of((place * CORES + (k ^ core)) * half, half), half
                     )
-                    piece = ref[low : low + half, lanes]
-                    if model:
-                        piece = scaled(piece, scale_ref[j ^ mask])
-                    goal[j ^ mask, rows, :] = piece
-
-
-def late_kernel(n_shard, student, ids_ref, all_ref, vec_ref, *refs):
-    if student:
-        sums_ref, in_ref, down_ref, b1_ref = refs
-        down_scale = scale_row(sums_ref, 4 + FF // D, 1.0, FF)
-    else:
-        in_ref, down_ref, b1_ref = refs
-    j = ids_ref[IJ]
+                    goal[j ^ mask, rows, :] = ref[low : low + half, lanes]
+
+
+def merge_kernel(bit, ids_ref, own_ref, got_ref, both_ref):
+    size = own_ref.shape[0]
+    mine = (ids_ref[IZ] >> bit) & 1
+    both_ref[pl.ds(mine * size, size)] = own_ref[...]
+    both_ref[pl.ds((1 - mine) * size, size)] = got_ref[...]
+
+
+def late_kernel(n_shard, student, ids_ref, *refs):
+    groups, vec_ref, refs = refs[:4], refs[4], refs[5:]
+    in_ref, down_ref, b1_ref = refs
+    z, k, j = ids_ref[IZ], ids_ref[IK], ids_ref[IJ]
     units = FF // n_shard
     few = units // GROUP
     rows_z = D // n_shard
     each = rows_z + 2 * few
+    fold = n_shard // 2
+    side = lax.div(z, fold)
 
     def mine(ref, row, core, place):
         options = []
@@ -287,90 +336,109 @@
         return pick(j, options)
 
     for core in range(CORES):
-        lanes = slice(core * HALF, (core + 1) * HALF)
+        for place in range(n_shard):
+            goal = slice(core * HALF + place * few, core * HALF + (place + 1) * few)
+            b1_ref[0:1, goal] = mine(vec_ref, 8, core, place)
+    if student:
+        sums = [
+            tree_sum(
+                join_three(groups[far], each + 3 * part, number)
+                for far in range(2)
+                for number in range(fold)
+            )
+            for part in (1, 2)
+        ]
+        left_scale, right_scale = (scale_row(row, 1.0, FF) for row in sums)
+    for core in range(CORES):
+        which = k ^ core
+        lanes = aligned(which * HALF, HALF)
         if student:
-            scale = jnp.concatenate(
-                [mine(sums_ref, 4, core, place) for place in range(n_shard)], axis=1
+            scale = tree_sum(
+                join_three(groups[core * 2 + far], each, number)
+                for far in range(2)
+                for number in range(fold)
             )
-            scale = (scale / D) * D ** (-0.5)
-        for place in range(n_shard):
-            base = (place * CORES + core) * each
-            piece = all_ref[base : base + rows_z, :]
-            rows = slice(core * HALF + place * few, core * HALF + (place + 1) * few)
-            left = all_ref[base + rows_z : base + rows_z + few, :]
-            right = all_ref[base + rows_z + few : base + each, :]
-            if student:
-                piece = scaled(piece, scale)
-                left = scaled(left, down_scale[:, :HALF])
-                right = scaled(right, down_scale[:, HALF:])
-            in_ref[place * rows_z : (place + 1) * rows_z, lanes] = piece
-            down_ref[rows, 0:HALF] = left
-            down_ref[rows, HALF:] = right
-            b1_ref[0:1, rows] = mine(vec_ref, 8, core, place)
-
-
-def places_kernel(rest, ids_ref, block_ref, lengths_ref, row_ref, col_ref, valid_ref, *, seqs, rows):
-    z, k, j, r = ids_ref[IZ], ids_ref[IK], ids_ref[IJ], ids_ref[IR]
-    length = lengths_ref[z * seqs + k]
+            scale = scale_row(scale, 1.0, D)
+        for far in range(2):
+            ref = groups[core * 2 + far]
+            for number in range(fold):
+                place = (side ^ far) * fold + number
+                piece = ref[number, 0:rows_z, :]
+                left = ref[number, rows_z : rows_z + few, :]
+                right = ref[number, rows_z + few : each, :]
+                if student:
+                    piece = scaled(piece, scale)
+                    left = scaled(left, left_scale)
+                    right = scaled(right, right_scale)
+                in_ref[aligned(place * rows_z, rows_z), lanes] = piece
+                rows = pl.ds(pl.multiple_of(which * HALF + place * few, few), few)
+                down_ref[rows, 0:HALF] = left
+                down_ref[rows, HALF:] = right
+
+
+def block_place(rest, per, ids_ref, block_ref, far, mask, core, part):
+    k, j, r = ids_ref[IK], ids_ref[IJ], ids_ref[IR]
+    chip = (r ^ far) * CHIPS + (j ^ mask)
+    return block_ref[(chip * CORES + (k ^ core)) * per + part]
+
+
+def places_kernel(rest, ids_ref, block_ref, lengths_ref, valid_ref, *outs, seqs, rows):
+    length = lengths_ref[ids_ref[IZ] * seqs + ids_ref[IK]]
     per = rows // BLK
     number = 0
     for far in range(rest):
         for mask in range(CHIPS):
-            for half in range(CORES):
+            for core in range(CORES):
                 for part in range(per):
-                    block = ((((r ^ far) * CHIPS + (j ^ mask)) * CORES + (k ^ half)) * per) + part
-                    base = block_ref[block] * BLK
                     goal = slice(number * BLK, (number + 1) * BLK)
+                    number += 1
+                    if not outs and mask:
+                        continue
+                    base = block_place(rest, per, ids_ref, block_ref, far, mask, core, part) * BLK
                     col = base + lax.broadcasted_iota(jnp.int32, (BLK, 1), 0)
-                    col_ref[goal, :] = col
-                    if far == 0:
-                        row_ref[:, goal] = base + lax.broadcasted_iota(jnp.int32, (1, BLK), 1)
                     if far == 0 and mask == 0:
                         valid_ref[goal, :] = jnp.where(col < length, 1.0, 0.0)
-                    number += 1
-
-
-def input_kernel(ids_ref, *refs):
+                    if outs:
+                        outs[1][goal, :] = col
+                        if far == 0:
+                            row = lax.broadcasted_iota(jnp.int32, (1, BLK), 1)
+                            outs[0][:, goal] = base + row
+
+
+def input_kernel(ids_ref, here_ref, x_ref, y_ref, xy0_ref, xy1_ref, own_ref, send_ref):
     k = ids_ref[IK]
-    own_ref, send_ref = refs[CHIPS:]
-    rows = refs[0].shape[1]
-    for mask in range(CHIPS):
+    rows = here_ref.shape[1]
+    for mask, ref in enumerate((here_ref, x_ref, y_ref)):
         goal = slice(mask * rows, (mask + 1) * rows)
-        own_ref[goal, :] = refs[mask][k]
-        send_ref[goal, :] = refs[mask][1 - k]
-
-
-def qkv_kernel(n_shard, student, ids_ref, own_ref, oth_ref, half_ref, peer_ref, vec_ref, *outs):
+        own_ref[goal, :] = ref[k]
+        send_ref[goal, :] = ref[1 - k]
+    goal = slice(3 * rows, 4 * rows)
+
+    @pl.when(k == 0)
+    def _():
+        own_ref[goal, :] = xy0_ref[...]
+        send_ref[goal, :] = xy1_ref[...]
+
+    @pl.when(k == 1)
+    def _():
+        own_ref[goal, :] = xy1_ref[...]
+        send_ref[goal, :] = xy0_ref[...]
+
+
+def qkv_kernel(n_shard, rest, ids_ref, block_ref, own_ref, oth_ref, half_ref, peer_ref, vec_ref, *outs):
     k, j = ids_ref[IK], ids_ref[IJ]
-    if student:
-        sums_ref, outs = outs[0], outs[1:]
-        scale = jnp.concatenate(
-            [
-                pick(
-                    j,
-                    [
-                        scale_row(sums_ref, number, attn_gains[number], D)[
-                            :, chip * COLS : (chip + 1) * COLS
-                        ]
-                        for chip in range(CHIPS)
-                    ],
-                )
-                for number in range(3)
-            ],
-            axis=1,
-        )
     q_ref, k_ref, v_ref, w_ref = outs
     half = D // n_shard // CORES
     for core, ref in enumerate((half_ref, peer_ref)):
         for place in range(n_shard):
             rows = pl.ds(pl.multiple_of((place * CORES + (k ^ core)) * half, half), half)
-            piece = ref[place * half : (place + 1) * half, :]
-            w_ref[rows, :] = scaled(piece, scale) if student else piece
+            w_ref[rows, :] = ref[place * half : (place + 1) * half, :]
     weight = w_ref[...]
     chips = [slice(chip * COLS, (chip + 1) * COLS) for chip in range(CHIPS)]
     q_bias = pick(j, [vec_ref[0:1, chip] for chip in chips])
     v_bias = pick(j, [vec_ref[1:2, chip] for chip in chips])
     rows = own_ref.shape[0] // CHIPS
+    per = rows // BLK
     for core, ref in enumerate((own_ref, oth_ref)):
         for mask in range(CHIPS):
             result = dot(ref[mask * rows : (mask + 1) * rows, :], weight)
@@ -381,9 +449,17 @@
                 (v_ref, result[:, 2 * COLS :] + v_bias),
             )
             for goal_ref, values in sets:
+                values = values.astype(bf16)
                 for head in range(HEADS_HERE):
                     span = slice(head * HEAD_DIM, (head + 1) * HEAD_DIM)
-                    goal_ref[head, goal, :] = values[:, span].astype(bf16)
+                    if rest > 1:
+                        goal_ref[head, goal, :] = values[:, span]
+                        continue
+                    for part in range(per):
+                        place = block_place(rest, per, ids_ref, block_ref, 0, mask, core, part)
+                        goal_ref[head, aligned(place * BLK, BLK), :] = values[
+                            part * BLK : (part + 1) * BLK, span
+                        ]
 
 
 def attend_kernel(q_ref, k_ref, v_ref, pq_ref, pk_ref, *outs, tile):
@@ -412,6 +488,57 @@
         span = slice(head * HEAD_DIM, (head + 1) * HEAD_DIM)
         for mask in range(CHIPS):
             o_refs[mask][:, span] = all_ref[head, mask * own : (mask + 1) * own, :]
+
+
+def sorted_blocks(ids_ref, block_ref, rows):
+    per = rows // BLK
+    for mask in range(CHIPS):
+        for core in range(CORES):
+            for part in range(per):
+                place = block_place(1, per, ids_ref, block_ref, 0, mask, core, part)
+                yield mask, core * rows + part * BLK, aligned(place * BLK, BLK)
+
+
+def below_diagonal(tile):
+    key = lax.broadcasted_iota(jnp.int32, (tile, tile), 0)
+    query = lax.broadcasted_iota(jnp.int32, (tile, tile), 1)
+    return key <= query
+
+
+def causal_kernel(ids_ref, block_ref, q_ref, k_ref, v_ref, *outs, tile):
+    o_refs, lse_ref, all_ref = outs[:CHIPS], outs[CHIPS], outs[CHIPS + 1]
+    tokens = q_ref.shape[1]
+    rows = tokens // GROUP
+    allowed = below_diagonal(tile)
+
+    def one_head(head, carry):
+        v_turned = v_ref[head].T
+        for t in range(tokens // tile):
+            here = slice(t * tile, (t + 1) * tile)
+            q_tile = q_ref[head, here, :]
+            scores = dot_right(k_ref[head, here, :], q_tile) * (score_scale * log2_e)
+            scores = jnp.where(allowed, scores, masked_score)
+            peak = jnp.max(scores, axis=0, keepdims=True)
+            if t:
+                before = slice(0, t * tile)
+                earlier = dot_right(k_ref[head, before, :], q_tile) * (score_scale * log2_e)
+                peak = jnp.maximum(peak, jnp.max(earlier, axis=0, keepdims=True))
+            powers = jnp.exp2(scores - peak)
+            total = jnp.sum(powers, axis=0, keepdims=True)
+            mixed = dot(v_turned[:, here], powers.astype(bf16))
+            if t:
+                powers = jnp.exp2(earlier - peak)
+                total = total + jnp.sum(powers, axis=0, keepdims=True)
+                mixed = mixed + dot(v_turned[:, before], powers.astype(bf16))
+            all_ref[head, here, :] = (mixed / total).T.astype(bf16)
+            lse_ref[head, :, here] = peak + jnp.log2(total)
+        return carry
+
+    lax.fori_loop(0, HEADS_HERE, one_head, 0)
+    for head in range(HEADS_HERE):
+        span = slice(head * HEAD_DIM, (head + 1) * HEAD_DIM)
+        for mask, low, place in sorted_blocks(ids_ref, block_ref, rows):
+            o_refs[mask][low : low + BLK, span] = all_ref[head, place, :]
 
 
 def norm_parts(values):
@@ -470,8 +597,15 @@
             sums_ref[0:1, :] += column_total(valid_ref[goal, :] * branch * branch)
 
 
-def feed_kernel(student, piece_ref, in_ref, down_ref, b1_ref, part_ref, *outs):
-    inner = dot(piece_ref[...], in_ref[...]) + b1_ref[0:1, :]
+def whole(refs):
+    if len(refs) == 1:
+        return refs[0][...]
+    return jnp.concatenate([ref[...] for ref in refs])
+
+
+def feed_kernel(student, count, *refs):
+    pieces, (in_ref, down_ref, b1_ref, part_ref, *outs) = refs[:count], refs[count:]
+    inner = dot(whole(pieces), in_ref[...]) + b1_ref[0:1, :]
     act = (inner * normal_cdf(inner)).astype(bf16)
     if student:
         outs[0][...] = inner
@@ -522,10 +656,12 @@
     )
 
 
-def feed_back_kernel(piece_ref, inner_ref, in_ref, down_ref, part_ref, grad_ref, sum_ref):
+def feed_back_kernel(count, *refs):
+    pieces, refs = refs[:count], refs[count:]
+    inner_ref, in_ref, down_ref, part_ref, grad_ref, sum_ref = refs
     inner = inner_ref[...]
     slope = normal_cdf(inner) + inner * jnp.exp(-0.5 * inner * inner) * 0.3989422804014327
-    grad = dot_right(piece_ref[...], down_ref[...]) * slope
+    grad = dot_right(whole(pieces), down_ref[...]) * slope
     sum_ref[...] = jnp.broadcast_to(column_total(grad), sum_ref.shape)
     grad = grad.astype(bf16)
     grad_ref[...] = grad
@@ -608,6 +744,61 @@
         sums_ref[1:2, span] = column_total(grad_value)
 
 
+def causal_back_kernel(ids_ref, block_ref, *refs, tile):
+    q_ref, k_ref, v_ref = refs[:3]
+    g_refs, refs = refs[3 : 3 + CHIPS], refs[3 + CHIPS :]
+    lse_ref, gq_ref, gk_ref, gv_ref, sums_ref, g_all, aq_ref, ak_ref, av_ref = refs
+    tokens = q_ref.shape[1]
+    rows = tokens // GROUP
+    own = tokens // CHIPS
+    allowed = below_diagonal(tile)
+    for head in range(HEADS_HERE):
+        span = slice(head * HEAD_DIM, (head + 1) * HEAD_DIM)
+        for mask, low, place in sorted_blocks(ids_ref, block_ref, rows):
+            g_all[head, place, :] = g_refs[mask][low : low + BLK, span]
+
+    def one_head(head, carry):
+        k_turned = k_ref[head].T
+        for t in range(tokens // tile):
+            here = slice(t * tile, (t + 1) * tile)
+            q_tile = q_ref[head, here, :]
+            g_tile = g_all[head, here, :]
+            lse = lse_ref[head, :, here]
+            scores = dot_right(k_ref[head, here, :], q_tile) * (score_scale * log2_e)
+            probs = jnp.exp2(jnp.where(allowed, scores, masked_score) - lse)
+            grads = dot_right(v_ref[head, here, :], g_tile)
+            delta = jnp.sum(probs * grads, axis=0, keepdims=True)
+            if t:
+                before = slice(0, t * tile)
+                earlier = dot_right(k_ref[head, before, :], q_tile) * (score_scale * log2_e)
+                early_probs = jnp.exp2(earlier - lse)
+                early_grads = dot_right(v_ref[head, before, :], g_tile)
+                delta = delta + jnp.sum(early_probs * early_grads, axis=0, keepdims=True)
+            grad_scores = (probs * (grads - delta)).astype(bf16)
+            grad_query = dot(k_turned[:, here], grad_scores)
+            ak_ref[head, here, :] = dot(grad_scores, q_tile)
+            av_ref[head, here, :] = dot(probs.astype(bf16), g_tile)
+            if t:
+                grad_scores = (early_probs * (early_grads - delta)).astype(bf16)
+                grad_query = grad_query + dot(k_turned[:, before], grad_scores)
+                ak_ref[head, before, :] += dot(grad_scores, q_tile)
+                av_ref[head, before, :] += dot(early_probs.astype(bf16), g_tile)
+            aq_ref[head, here, :] = grad_query.T * score_scale
+        return carry
+
+    lax.fori_loop(0, HEADS_HERE, one_head, 0)
+    sums_ref[...] = jnp.zeros_like(sums_ref)
+    for head in range(HEADS_HERE):
+        span = slice(head * HEAD_DIM, (head + 1) * HEAD_DIM)
+        sums_ref[0:1, span] = column_total(aq_ref[head])
+        sums_ref[1:2, span] = column_total(av_ref[head])
+        for mask, low, place in sorted_blocks(ids_ref, block_ref, rows):
+            goal = slice(mask * own + low, mask * own + low + BLK)
+            gq_ref[goal, span] = aq_ref[head, place, :].astype(bf16)
+            gk_ref[goal, span] = (ak_ref[head, place, :] * score_scale).astype(bf16)
+            gv_ref[goal, span] = av_ref[head, place, :].astype(bf16)
+
+
 def qkv_back_kernel(gq_ref, gk_ref, gv_ref, w_ref, *part_refs):
     own = gq_ref.shape[0] // CHIPS
     for mask in range(CHIPS):
@@ -627,41 +818,61 @@
     send_ref[...] = total[rows:, :]
 
 
-def late_grad_kernel(n_shard, *refs):
-    acts, feeds, firsts, inners = (refs[i * CHIPS : (i + 1) * CHIPS] for i in range(4))
-    all_ref, down_ref, in_ref = refs[4 * CHIPS :]
-    down_ref[...] = tree_sum(dot_left(a[...], g[...]) for a, g in zip(acts, feeds)).astype(bf16)
-    in_ref[...] = tree_sum(dot_left(a[...], g[...]) for a, g in zip(firsts, inners)).astype(bf16)
+def late_grad_kernel(n_shard, counts, ids_ref, *refs):
+    k = ids_ref[IK]
+    groups = []
+    for count in counts:
+        groups.append(refs[:count])
+        refs = refs[count:]
+    acts, feeds, firsts, inners = (groups[i * CHIPS : (i + 1) * CHIPS] for i in range(4))
+    own_ref, send_ref, down_ref, in_ref = refs
+    down_ref[...] = tree_sum(dot_left(whole(a), whole(g)) for a, g in zip(acts, feeds))
+    in_ref[...] = tree_sum(dot_left(whole(a), whole(g)) for a, g in zip(firsts, inners))
     few = FF // n_shard // GROUP
     rows_z = D // n_shard
     each = rows_z + 2 * few
-    for core in range(CORES):
-        lanes = slice(core * HALF, (core + 1) * HALF)
+    for goal_ref, half in ((own_ref, k), (send_ref, 1 - k)):
+        kind = goal_ref.dtype
+        lanes = aligned(half * HALF, HALF)
         for place in range(n_shard):
-            base = (place * CORES + core) * each
-            all_ref[base : base + rows_z, :] = in_ref[place * rows_z : (place + 1) * rows_z, lanes]
-            rows = slice(core * HALF + place * few, core * HALF + (place + 1) * few)
-            all_ref[base + rows_z : base + rows_z + few, :] = down_ref[rows, :HALF]
-            all_ref[base + rows_z + few : base + each, :] = down_ref[rows, HALF:]
-
-
-def late_final_kernel(n_shard, all_ref, in_latent_ref, down_latent_ref, in_ref, down_ref):
+            goal_ref[place, 0:rows_z, :] = in_ref[
+                place * rows_z : (place + 1) * rows_z, lanes
+            ].astype(kind)
+            rows = pl.ds(pl.multiple_of(half * HALF + place * few, few), few)
+            goal_ref[place, rows_z : rows_z + few, :] = down_ref[rows, :HALF].astype(kind)
+            goal_ref[place, rows_z + few : each, :] = down_ref[rows, HALF:].astype(kind)
+
+
+def late_split_kernel(n_shard, ids_ref, own_ref, got_ref, *outs):
+    for mask in range(n_shard):
+        place = ids_ref[IZ] ^ mask
+        outs[mask][...] = (own_ref[place] + got_ref[place].astype(f32)).astype(outs[mask].dtype)
+
+
+def sum_kernel(*refs):
+    refs[-1][...] = tree_sum(ref[...].astype(f32) for ref in refs[:-1]).astype(bf16)
+
+
+def late_final_kernel(n_shard, ids_ref, *refs):
+    k, j = ids_ref[IK], ids_ref[IJ]
+    pieces, (in_latent_ref, down_latent_ref, in_ref, down_ref, all_ref) = refs[:GROUP], refs[GROUP:]
     few = FF // n_shard // GROUP
     rows_z = D // n_shard
-    each = rows_z + 2 * few
+    for core in range(CORES):
+        for mask in range(CHIPS):
+            all_ref[(j ^ mask) * CORES + (k ^ core)] = pieces[core * CHIPS + mask][...]
     for number in range(GROUP):
-        base = number * each
         for place in range(n_shard):
             goal = (place * GROUP + number) * few
             lanes = slice(goal, goal + few)
-            grad = all_ref[base : base + rows_z, place * few : (place + 1) * few].astype(f32)
+            grad = all_ref[number, 0:rows_z, place * few : (place + 1) * few].astype(f32)
             keep = jnp.abs(in_latent_ref[:, lanes]) <= 1.0
             in_ref[:, lanes] = jnp.where(keep, grad, 0.0)
         rows = slice(number * few, (number + 1) * few)
         for part in range(2):
             lanes = slice(part * HALF, (part + 1) * HALF)
-            low = base + rows_z + part * few
-            grad = all_ref[low : low + few, :].astype(f32)
+            low = rows_z + part * few
+            grad = all_ref[number, low : low + few, :].astype(f32)
             keep = jnp.abs(down_latent_ref[rows, lanes]) <= 1.0
             down_ref[rows, lanes] = jnp.where(keep, grad, 0.0)
 
@@ -720,8 +931,8 @@
         theirs = pl.ds(pl.multiple_of((place * CORES + 1 - k) * half, half), half)
         own_ref[goal, :] = full_ref[mine, :]
         send_ref[goal, :] = full_ref[theirs, :].astype(bf16)
-    lane = lax.broadcasted_iota(jnp.int32, (1, D), 1)
-    stats = jnp.zeros((1, D), f32)
+    lane = lax.broadcasted_iota(jnp.int32, (1, 2 * COLS), 1)
+    stats = jnp.zeros((1, 2 * COLS), f32)
     for number, row in enumerate(
         (loss_sums[3:4, :], branch_sums[0:1, :], loss_sums[4:5, :], loss_sums[5:6, :])
     ):
@@ -732,12 +943,8 @@
             loss_sums[0:1, :],
             res_sums[1:3, :],
             loss_sums[1:3, :],
-            stats,
             tree_sum(ref[0:1, :] for ref in b1_sums),
-            jnp.concatenate(
-                [qv_sums[0:1, :], qv_sums[1:2, :], jnp.zeros((1, D - 2 * COLS), f32)], axis=1
-            ),
-            jnp.zeros((VEC_ROWS - 9, D), f32),
+            jnp.concatenate([qv_sums[0:1, :], qv_sums[1:2, :], stats], axis=1),
         ]
     )
     high, low = split_hi_lo(table)
@@ -811,7 +1018,7 @@
     for number in range(1, lengths_ref.shape[0]):
         count = count + lengths_ref[number]
     scale = count.astype(f32) * D
-    stats = total[ROW_STATS : ROW_STATS + 1, 0:128] / scale
+    stats = total[ROW_QV : ROW_QV + 1, 2 * COLS : 2 * COLS + 128] / scale
     lane = lax.broadcasted_iota(jnp.int32, (1, 128), 1)
     stats_ref[...] = jnp.where(lane == 0, stats, jnp.sqrt(stats))
     vec_ref[1:7, :] = total[0:6, :]
@@ -873,32 +1080,44 @@
     def swap(piece):
         return flip(piece, "core", 1)
 
-    t_early, t_late = weight_pieces(
-        n_shard, False, line.ids, teacher_attn, teacher_ffn_in, teacher_ffn_out
-    )
-    line.wait(t_early)
-    s_early, s_late = weight_pieces(
-        n_shard, True, line.ids, attn_latent, ffn_in_latent, ffn_out_latent
-    )
-    line.wait(s_early)
-    sums = column_sums(line.ids, attn_latent, ffn_in_latent, ffn_out_latent)
-    line.wait(sums)
-    pos_row, pos_col, valid = line(
+    def near_rows(piece):
+        return [piece, flip(piece, "chip", 1), flip(piece, "chip", 2)]
+
+    def all_rows(near):
+        near = [near[0], *line.behind(*near[1:])]
+        half = near[0].shape[0] // 2
+        far = (flip(near[2][:half], "chip", 1), flip(near[1][half:], "chip", 2))
+        return [(near[0],), (near[1],), (near[2],), far]
+
+    def spread_z(piece):
+        bits = n_shard.bit_length() - 1
+        own = piece[None]
+        for bit in range(bits):
+            got = flip(own, "shard", 1 << bit)
+            if bit == bits - 1:
+                return own, got
+            own = line(
+                functools.partial(merge_kernel, bit),
+                "merge",
+                shape((2 * own.shape[0], *own.shape[1:])),
+                (),
+                (own, got),
+                limit=6,
+            )
+
+    near = near_rows(hidden_in)
+    t_early = early_pieces(line, False, teacher_attn)
+    s_early = early_pieces(line, True, attn_latent)
+    outs = [shape((own, 1), f32)]
+    if rest > 1:
+        outs += [shape((1, tokens), jnp.int32), shape((keys, 1), jnp.int32)]
+    valid, *positions = line(
         functools.partial(places_kernel, rest, seqs=seqs, rows=rows),
         "places",
-        (
-            shape((1, tokens), jnp.int32),
-            shape((keys, 1), jnp.int32),
-            shape((own, 1), f32),
-        ),
+        tuple(outs),
         (block_of, lengths),
         (),
     )
-    for mask in (1 << bit for bit in range(n_shard.bit_length() - 1)):
-        sums = sums + flip(sums, "shard", mask)
-    t_late = lax.all_gather(t_late, ("shard", "core"), axis=0, tiled=True)
-    s_late = lax.all_gather(s_late, ("shard", "core"), axis=0, tiled=True)
-
     t_qkv_half, t_out_half = line(
         functools.partial(early_kernel, n_shard, 0),
         "early_weights",
@@ -906,15 +1125,18 @@
         (),
         gather(t_early, "shard"),
     )
+    pieces = [piece for group in all_rows(near) for piece in group]
+    t_late = late_pieces(line, n_shard, False, teacher_ffn_in, teacher_ffn_out)
+    s_late = late_pieces(line, n_shard, True, ffn_in_latent, ffn_out_latent)
+    pieces = pieces[:3] + [piece[0] for piece in pieces[3:]]
     x_own, x_send = line(
         input_kernel,
         "input",
         (shape((tokens // CORES, D)), shape((tokens // CORES, D))),
         (),
-        gather(hidden_in, "chip"),
+        pieces,
     )
     x_oth = swap(x_send)
-
     def rest_gather(values):
         if rest == 1:
             return values
@@ -929,28 +1151,40 @@
             + [flip(view[m].astype(bf16), "rest", m).astype(f32) for m in range(1, rest)]
         ).astype(bf16)
 
-    def project(student, qkv_half, vector):
+    def project(qkv_half, vector):
         heads = shape((HEADS_HERE, tokens, HEAD_DIM))
         query, key, value, w_qkv = line(
-            functools.partial(qkv_kernel, n_shard, student),
+            functools.partial(qkv_kernel, n_shard, rest),
             "qkv",
             (heads, heads, heads, shape((D, QKV))),
-            (),
-            [x_own, x_oth, qkv_half, swap(qkv_half), vector] + [sums] * student,
+            (block_of,),
+            [x_own, x_oth, qkv_half, swap(qkv_half), vector],
         )
         return query, rest_gather(key), rest_gather(value), w_qkv
 
     def attend(query, key, value):
-        *heads, lse = line(
-            functools.partial(attend_kernel, tile=own),
-            "attend",
-            tuple([shape((own, COLS))] * CHIPS + [shape((HEADS_HERE, 1, tokens), f32)]),
-            (),
-            (query, key, value, pos_row, pos_col),
-            (pltpu.VMEM((HEADS_HERE, tokens, HEAD_DIM), bf16),),
-            limit=20 if rest == 1 else 48,
-            bare=True,
-        )
+        outs = tuple([shape((own, COLS))] * CHIPS + [shape((HEADS_HERE, 1, tokens), f32)])
+        scratch = (pltpu.VMEM((HEADS_HERE, tokens, HEAD_DIM), bf16),)
+        if rest == 1:
+            *heads, lse = line(
+                functools.partial(causal_kernel, tile=own),
+                "attend",
+                outs,
+                (block_of,),
+                (query, key, value),
+                scratch,
+            )
+        else:
+            *heads, lse = line(
+                functools.partial(attend_kernel, tile=own),
+                "attend",
+                outs,
+                (),
+                (query, key, value, *positions),
+                scratch,
+                limit=48,
+                bare=True,
+            )
         return exchange(heads, "chip"), lse
 
     def branch(student, heads, w_out, vector):
@@ -965,29 +1199,29 @@
             (*heads, w_out, x_own, x_oth, vector, valid),
         )
 
-    def late_weights(student, gathered, vector):
+    def late_weights(student, near_far, vector):
         return line(
             functools.partial(late_kernel, n_shard, student),
             "late_weights",
             (shape((D, UNITS)), shape((UNITS, D)), shape((8, UNITS), f32)),
             (),
-            [gathered, vector] + [sums] * student,
+            [*near_far, *[swap(piece) for piece in near_far], vector],
         )
 
-    def feed(student, piece, mask, late):
+    def feed(student, pieces, mask, late):
         outs = [shape((own, D), f32 if mask == 0 else bf16)]
         if student:
             outs += [shape((own, UNITS), f32), shape((own, UNITS))]
         return line(
-            functools.partial(feed_kernel, student),
+            functools.partial(feed_kernel, student, len(pieces)),
             "feed",
             tuple(outs),
             (),
-            (piece, *late),
+            (*pieces, *late),
             bare=True,
         )
 
-    t_query, t_key, t_value, _ = project(False, t_qkv_half, teacher_vec)
+    t_query, t_key, t_value, _ = project(t_qkv_half, teacher_vec)
     s_qkv_half, out_half = line(
         functools.partial(early_kernel, n_shard, 1),
         "early_weights",
@@ -995,29 +1229,36 @@
         (),
         gather(s_early, "shard") + [t_out_half],
     )
+    t_late = spread_z(t_late)
     t_heads, _ = attend(t_query, t_key, t_value)
-    query, key, value, w_qkv = project(True, s_qkv_half, student_vec)
+    (s_late,) = line.behind(s_late)
     out_all = list(line.behind(*gather(out_half, "chip")))
+    query, key, value, w_qkv = project(s_qkv_half, student_vec)
+    s_late = spread_z(s_late)
     t_out, s_out = line(
         functools.partial(out_weight_kernel, n_shard),
         "out_weights",
         (shape((CHIPS, D, COLS)), shape((CHIPS, D, COLS))),
         (),
-        out_all + [swap(piece) for piece in out_all] + [sums],
-        (pltpu.VMEM((CHIPS, 1, COLS), f32),),
+        out_all + [swap(piece) for piece in out_all],
     )
     t_first, t_sent = branch(False, t_heads, t_out, teacher_vec)
-    t_firsts = gather(t_sent, "chip")
+    t_near = near_rows(t_sent)
     heads, lse = attend(query, key, value)
-    t_late = late_weights(False, t_late, teacher_vec)
-    t_parts = [feed(False, t_firsts[0], 0, t_late)[0]]
+    t_late = late_weights(False, line.behind(*t_late), teacher_vec)
+    t_parts = [feed(False, (t_sent,), 0, t_late)[0]]
+    t_firsts = all_rows(t_near)
     first, sent, residual, branch_sums = branch(True, heads, s_out, student_vec)
-    firsts = gather(sent, "chip")
-    t_parts += [feed(False, t_firsts[m], m, t_late)[0] for m in range(1, CHIPS)]
+    near = near_rows(sent)
+    for m in (1, 2):
+        t_parts.append(feed(False, t_firsts[m], m, t_late)[0])
+    s_late = late_weights(True, line.behind(*s_late), student_vec)
+    w_in, w_down, _ = s_late
+    fed = [feed(True, (sent,), 0, s_late)]
+    t_parts.append(feed(False, t_firsts[3], 3, t_late)[0])
     t_parts = exchange(t_parts, "chip")
-    s_late = late_weights(True, s_late, student_vec)
-    w_in, w_down, _ = s_late
-    fed = [feed(True, firsts[m], m, s_late) for m in range(CHIPS)]
+    firsts = all_rows(near)
+    fed += [feed(True, firsts[m], m, s_late) for m in range(1, CHIPS)]
     parts, inners, acts = ([f[i] for f in fed] for i in range(3))
     target = line(
         target_kernel,
@@ -1035,7 +1276,7 @@
         (*exchange(parts, "chip"), first, student_vec, target, valid),
     )
 
-    feeds = gather(sent, "chip")
+    near = near_rows(sent)
 
     def to_owners(here, there):
         return line(
@@ -1047,9 +1288,9 @@
         )
 
     output = to_owners(out[:rows], out[rows:])
-    backs = [
-        line(
-            feed_back_kernel,
+    def feed_back(pieces, m):
+        return line(
+            functools.partial(feed_back_kernel, len(pieces)),
             "feed_back",
             (
                 shape((own, D), f32 if m == 0 else bf16),
@@ -1057,21 +1298,23 @@
                 shape((8, UNITS), f32),
             ),
             (),
-            (feeds[m], inners[m], w_in, w_down),
+            (*pieces, inners[m], w_in, w_down),
             bare=True,
         )
-        for m in range(CHIPS)
-    ]
+
+    backs = [feed_back((sent,), 0)]
+    feeds = all_rows(near)
+    backs += [feed_back(feeds[m], m) for m in range(1, CHIPS)]
     parts, grad_inners, b1_sums = ([b[i] for b in backs] for i in range(3))
-    late_grad = line(
-        functools.partial(late_grad_kernel, n_shard),
+    groups = [(act,) for act in acts] + feeds + firsts + [(inner,) for inner in grad_inners]
+    keep, send = line(
+        functools.partial(late_grad_kernel, n_shard, [len(group) for group in groups]),
         "late_grad",
-        shape((n_shard * CORES * each, HALF)),
+        (shape((n_shard, each, HALF), f32), shape((n_shard, each, HALF))),
         (),
-        (*acts, *feeds, *firsts, *grad_inners),
-        (pltpu.VMEM((UNITS, D), bf16), pltpu.VMEM((D, UNITS), bf16)),
+        [piece for group in groups for piece in group],
+        (pltpu.VMEM((UNITS, D), f32), pltpu.VMEM((D, UNITS), f32)),
         limit=24,
-        bare=True,
     )
     grad_res, grad_branch, *rest_outs = line(
         branch_back_kernel,
@@ -1085,6 +1328,21 @@
         (*exchange(parts, "chip"), grad_second, residual, student_vec, s_out),
     )
     grad_heads, res_sums = exchange(rest_outs[:CHIPS], "chip"), rest_outs[CHIPS]
+    late_pieces_out = line(
+        functools.partial(late_split_kernel, n_shard),
+        "late_split",
+        tuple(shape((each, HALF), f32 if m == 0 else bf16) for m in range(n_shard)),
+        (),
+        (keep, swap(*line.behind(send))),
+    )
+    late_got = [late_pieces_out[0]]
+
+    def late_exchange(*masks):
+        for m in masks:
+            if m < n_shard:
+                late_got.append(flip(*line.behind(late_pieces_out[m]), "shard", m))
+
+    late_exchange(1)
     line.wait(*grad_heads)
     out_parts = line(
         functools.partial(out_grad_kernel, n_shard),
@@ -1096,33 +1354,43 @@
         (*heads, grad_branch),
         (pltpu.VMEM((CHIPS, own, COLS), bf16), pltpu.VMEM((D, COLS), f32)),
     )
-    late = lax.psum_scatter(late_grad, ("shard", "core"), scatter_dimension=0, tiled=True)
-    (late,) = line.behind(late)
-    if rest > 1:
-        late = lax.psum(late, "rest")
-    late = lax.all_gather(late, ("chip", "core"), axis=0, tiled=True)
-    kind = bf16 if rest == 1 else f32
-    grad_query, grad_key, grad_value, qv_sums = line(
-        functools.partial(attend_back_kernel, tile=own),
-        "attend_back",
-        (
-            shape((tokens, COLS)),
-            shape((keys, COLS), kind),
-            shape((keys, COLS), kind),
-            shape((8, COLS), f32),
-        ),
-        (),
-        (query, key, value, *grad_heads, lse, pos_row, pos_col),
-        (
-            pltpu.VMEM((HEADS_HERE, tokens, HEAD_DIM), bf16),
-            pltpu.VMEM((HEADS_HERE, tokens, HEAD_DIM), f32),
-            pltpu.VMEM((HEADS_HERE, keys, HEAD_DIM), f32),
-            pltpu.VMEM((HEADS_HERE, keys, HEAD_DIM), f32),
-        ),
-        limit=28 if rest == 1 else 56,
-        bare=True,
-    )
+    line.wait(late_got[-1])
+    late_exchange(2)
+    outs = (
+        shape((tokens, COLS)),
+        shape((keys, COLS), bf16 if rest == 1 else f32),
+        shape((keys, COLS), bf16 if rest == 1 else f32),
+        shape((8, COLS), f32),
+    )
+    scratch = (
+        pltpu.VMEM((HEADS_HERE, tokens, HEAD_DIM), bf16),
+        pltpu.VMEM((HEADS_HERE, tokens, HEAD_DIM), f32),
+        pltpu.VMEM((HEADS_HERE, keys, HEAD_DIM), f32),
+        pltpu.VMEM((HEADS_HERE, keys, HEAD_DIM), f32),
+    )
+    if rest == 1:
+        grad_query, grad_key, grad_value, qv_sums = line(
+            functools.partial(causal_back_kernel, tile=own),
+            "attend_back",
+            outs,
+            (block_of,),
+            (query, key, value, *grad_heads, lse),
+            scratch,
+            limit=28,
+        )
+    else:
+        grad_query, grad_key, grad_value, qv_sums = line(
+            functools.partial(attend_back_kernel, tile=own),
+            "attend_back",
+            outs,
+            (),
+            (query, key, value, *grad_heads, lse, *positions),
+            scratch,
+            limit=56,
+            bare=True,
+        )
     grad_key, grad_value = rest_scatter(grad_key), rest_scatter(grad_value)
+    line.wait(late_got[-1])
     mine, table, send = line(
         functools.partial(early_grad_kernel, n_shard),
         "early_grad",
@@ -1165,6 +1433,20 @@
         (),
         (mine, table, swap(send)),
     )
+    parts = line.behind(*parts)
+    early = line(
+        early_sum_kernel,
+        "early_sum",
+        shape((half + 2 * VEC_ROWS, D)),
+        (),
+        exchange(pieces, "shard"),
+        bare=True,
+    )
+    if rest > 1:
+        early = line(
+            early_sum_kernel, "rest_sum", shape(early.shape), (), gather(early, "rest"), bare=True
+        )
+    late_exchange(*range(3, n_shard))
     here, there = line(
         hidden_kernel,
         "hidden",
@@ -1173,29 +1455,20 @@
         (grad_res, *exchange(parts, "chip")),
         bare=True,
     )
-    early = line(
-        early_sum_kernel,
-        "early_sum",
-        shape((half + 2 * VEC_ROWS, D)),
-        (),
-        exchange(pieces, "shard"),
-        bare=True,
-    )
+    late = line(sum_kernel, "late_sum", shape((each, HALF)), (), late_got, bare=True)
     if rest > 1:
-        early = line(
-            early_sum_kernel, "rest_sum", shape(early.shape), (), gather(early, "rest"), bare=True
-        )
-    early = gather(early, "chip")
+        late = line(sum_kernel, "rest_sum", shape(late.shape), (), gather(late, "rest"), bare=True)
+    late = gather(late, "chip")
     grad_hidden = to_owners(here, there)
     in_grad, down_grad = line(
         functools.partial(late_final_kernel, n_shard),
         "late_final",
         (shape(ffn_in_latent.shape, f32), shape(ffn_out_latent.shape, f32)),
         (),
-        (late, ffn_in_latent, ffn_out_latent),
-        bare=True,
-    )
-    early = list(line.behind(*early))
+        (*late, *[swap(piece) for piece in late], ffn_in_latent, ffn_out_latent),
+        (pltpu.VMEM((GROUP, each, HALF), bf16),),
+    )
+    early = gather(early, "chip")
     attn_grad, vec_grad, query_grad, stats = line(
         functools.partial(early_final_kernel, n_shard),
         "early_final",

time: 391 us -> 325 us (0.83)
  the two profiles are of different devices: /device:TPU:0 before, /device:TPU:9 now
where the time goes in v4:
time: 325 us; the launch traced here: 320 us
  waiting for transfers between devices  136 us (42%)
  Pallas kernels  91.5 us (28%)
  starting transfers between devices  86.6 us (27%)
  local copies, waits for them, and re-layouts  3.64 us (1%)
    ppermute x88, waiting for transfers between devices, flip(): return lax.ppermute(piece, axis, [(a, a ^ mask) for a in range(size)])  136 us
    ppermute x88, starting transfers between devices, flip(): return lax.ppermute(piece, axis, [(a, a ^ mask) for a in range(size)])  86.6 us
    pallas_call x44, Pallas kernels, call(): pl.pallas_call(kernel, out_shape=outs, in_specs=[SMEM_SPEC] * len(scalars...  85.2 us
  transfers between devices with their start and end apart: 88, of which 34 were waited for; matrix products, arithmetic and copies ran while one was open for 0% of the time, Pallas kernels for 25%

profile of v4, /device:TPU:9, one launch (start us, length us, event | category | flops | bytes accessed | tf_op | source)
XLA Modules:
  0.0 319.7 jit_solution(15280324710309945130)
XLA Ops:
  12.9 3.6 %collective-permute-done.2.refs_3_ = bf16[96,768]{1,0:T(8,128)(2,1)S(1)} collective-permute-done((bf16[96,768]{1,0:T(8,128)(2,1)S(1)}, bf16[96,768]{1,0:T(8,128)(2,1)S(1)}, u32[]{:S(2)}, u32[]{:S(2)}) %collective-permute-start.2) | collective-permute-done | bytes 147488 | tf_op jit(solution)/shard_map/ppermute | solution.py:1072
  16.5 1.9 collective-permute-done.1.refs_2_
  21.4 2.1 late_pieces.3
  24.8 3.7 %collective-permute-start.7 = (bf16[512,768]{1,0:T(8,128)(2,1)S(1)}, bf16[512,768]{1,0:T(8,128)(2,1)S(1)}, u32[]{:S(2)}, u32[]{:S(2)}) collective-permute-start(bf16[512,768]{1,0:T(8,128)(2,1)S(1)} %get-tuple-element.198), channel_id=1, source_target_pairs={{0,4},{4,0},{1,5},{5,1},{2,6},{6,2},{3,7},{7,3},{8,12},{12,8},{9,1... | collective-permute-start | bytes 2359304 | tf_op jit(solution)/shard_map/ppermute | solution.py:1072
  29.1 3.5 %collective-permute-start.10 = (bf16[112,768]{1,0:T(8,128)(2,1)S(1)}, bf16[112,768]{1,0:T(8,128)(2,1)S(1)}, u32[]{:S(2)}, u32[]{:S(2)}) collective-permute-start(bf16[112,768]{1,0:T(8,128)(2,1)S(1)} %early_pieces.3.refs_0_), channel_id=1, source_target_pairs={{0,2},{1,3},{2,0},{3,1},{4,6},{5,7},{6,4},{7,5},{8,10},{9,11},{10,... | collective-permute-start | bytes 516104 | tf_op jit(solution)/shard_map/ppermute | solution.py:1072
  34.2 3.0 qkv.2
  37.2 7.1 %collective-permute-done.10.refs_2_ = bf16[112,768]{1,0:T(8,128)(2,1)S(1)} collective-permute-done((bf16[112,768]{1,0:T(8,128)(2,1)S(1)}, bf16[112,768]{1,0:T(8,128)(2,1)S(1)}, u32[]{:S(2)}, u32[]{:S(2)}) %collective-permute-start.10) | collective-permute-done | bytes 172064 | tf_op jit(solution)/shard_map/ppermute | solution.py:1072
  46.6 2.4 collective-permute-start.13
  51.2 6.6 %attend.2 = (bf16[256,192]{1,0:T(8,128)(2,1)S(1)}, bf16[256,192]{1,0:T(8,128)(2,1)S(1)}, bf16[256,192]{1,0:T(8,128)(2,1)S(1)}, bf16[256,192]{1,0:T(8,128)(2,1)S(1)}, f32[3,1,1024]{2,1,0:T(1,128)}) custom-call(s32[4]{0:T(128)S(1)} %pad_add_fusion.ids_ref, s32[16]{0:T(128)S(1)} %copy-done.10, bf16[3,1024,64]{2,1,0:T(8,128)(2,1)S(1)} %get-tuple-element.199.q_ref, ...), custom_call_target="tpu_custom_call" | custom-call | tf_op jit(solution)/shard_map/attend/pallas_call | solution.py:80
  57.8 1.9 collective-permute-start.14
  62.2 5.3 %collective-permute-done.16.refs_2_ = bf16[384,384]{1,0:T(8,128)(2,1)S(1)} collective-permute-done((bf16[384,384]{1,0:T(8,128)(2,1)S(1)}, bf16[384,384]{1,0:T(8,128)(2,1)S(1)}, u32[]{:S(2)}, u32[]{:S(2)}) %collective-permute-start.16) | collective-permute-done | bytes 294944 | tf_op jit(solution)/shard_map/ppermute | solution.py:1072
  67.5 1.9 collective-permute-start.18
  72.1 2.2 collective-permute-start.22
  75.6 2.2 qkv.3
  79.5 2.1 collective-permute-done.23.refs_2_
  83.1 6.4 %attend.3 = (bf16[256,192]{1,0:T(8,128)(2,1)S(1)}, bf16[256,192]{1,0:T(8,128)(2,1)S(1)}, bf16[256,192]{1,0:T(8,128)(2,1)S(1)}, bf16[256,192]{1,0:T(8,128)(2,1)S(1)}, f32[3,1,1024]{2,1,0:T(1,128)S(1)}) custom-call(s32[4]{0:T(128)S(1)} %pad_add_fusion.ids_ref, s32[16]{0:T(128)S(1)} %copy-done.10, bf16[3,1024,64]{2,1,0:T(8,128)(2,1)S(1)} %get-tuple-element.209.q_ref.refs_0_, ...), custom_call_target="tpu_custom_call" | custom-call | tf_op jit(solution)/shard_map/attend/pallas_call | solution.py:80
  91.2 2.2 collective-permute-start.33
  94.6 8.8 %collective-permute-done.32.refs_0_ = bf16[256,768]{1,0:T(8,128)(2,1)S(1)} collective-permute-done((bf16[256,768]{1,0:T(8,128)(2,1)S(1)}, bf16[256,768]{1,0:T(8,128)(2,1)S(1)}, u32[]{:S(2)}, u32[]{:S(2)}) %collective-permute-start.32) | collective-permute-done | bytes 393248 | tf_op jit(solution)/shard_map/ppermute | solution.py:1072
  108.4 2.0 collective-permute-done.30.refs_3_
  115.0 4.9 %collective-permute-done.33.refs_1_ = bf16[2,400,384]{2,1,0:T(8,128)(2,1)S(1)} collective-permute-done((bf16[2,400,384]{2,1,0:T(8,128)(2,1)S(1)}, bf16[2,400,384]{2,1,0:T(8,128)(2,1)S(1)}, u32[]{:S(2)}, u32[]{:S(2)}) %collective-permute-start.33) | collective-permute-done | bytes 614432 | tf_op jit(solution)/shard_map/ppermute | solution.py:1072
  126.3 8.2 %collective-permute-done.36.refs_0_ = bf16[128,768]{1,0:T(8,128)(2,1)S(1)} collective-permute-done((bf16[128,768]{1,0:T(8,128)(2,1)S(1)}, bf16[128,768]{1,0:T(8,128)(2,1)S(1)}, u32[]{:S(2)}, u32[]{:S(2)}) %collective-permute-start.36) | collective-permute-done | bytes 196640 | tf_op jit(solution)/shard_map/ppermute | solution.py:1072
  143.6 3.9 %collective-permute-done.41.refs_1_.refs_13_ = bf16[128,768]{1,0:T(8,128)(2,1)S(1)} collective-permute-done((bf16[128,768]{1,0:T(8,128)(2,1)S(1)}, bf16[128,768]{1,0:T(8,128)(2,1)S(1)}, u32[]{:S(2)}, u32[]{:S(2)}) %collective-permute-start.41) | collective-permute-done | bytes 196640 | tf_op jit(solution)/shard_map/ppermute | solution.py:1072
  150.2 8.6 %collective-permute-done.44.refs_3_ = bf16[256,768]{1,0:T(8,128)(2,1)S(1)} collective-permute-done((bf16[256,768]{1,0:T(8,128)(2,1)S(1)}, bf16[256,768]{1,0:T(8,128)(2,1)S(1)}, u32[]{:S(2)}, u32[]{:S(2)}) %collective-permute-start.44) | collective-permute-done | bytes 393248 | tf_op jit(solution)/shard_map/ppermute | solution.py:1072
  159.9 5.9 %collective-permute-done.45.refs_1_ = bf16[256,768]{1,0:T(8,128)(2,1)S(1)} collective-permute-done((bf16[256,768]{1,0:T(8,128)(2,1)S(1)}, bf16[256,768]{1,0:T(8,128)(2,1)S(1)}, u32[]{:S(2)}, u32[]{:S(2)}) %collective-permute-start.45) | collective-permute-done | bytes 393248 | tf_op jit(solution)/shard_map/ppermute | solution.py:1072
  165.9 9.8 %collective-permute-done.47.refs_3_ = bf16[256,768]{1,0:T(8,128)(2,1)S(1)} collective-permute-done((bf16[256,768]{1,0:T(8,128)(2,1)S(1)}, bf16[256,768]{1,0:T(8,128)(2,1)S(1)}, u32[]{:S(2)}, u32[]{:S(2)}) %collective-permute-start.47) | collective-permute-done | bytes 393248 | tf_op jit(solution)/shard_map/ppermute | solution.py:1072
  175.7 1.8 loss.1
  178.8 3.2 collective-permute-start.48
  184.4 1.7 feed_back.4
  195.4 3.6 %late_grad.1 = (f32[4,384,384]{2,1,0:T(8,128)S(1)}, bf16[4,384,384]{2,1,0:T(8,128)(2,1)S(1)}) custom-call(s32[4]{0:T(128)S(1)} %pad_add_fusion.ids_ref, bf16[256,768]{1,0:T(8,128)(2,1)S(1)} %get-tuple-element.284.refs_0_, bf16[256,768]{1,0:T(8,128)(2,1)S(1)} %get-tuple-element.285.refs_1_, bf16[256,768]{1,0:T(8,128)(2,1)S(1)} %get-tuple-element.286.refs_2_, ...), custom_call_target="tpu_custom_call" | custom-call | tf_op jit(solution)/shard_map/late_grad/pallas_call | solution.py:80
  198.9 3.6 %collective-permute-done.54.refs_2_ = bf16[256,768]{1,0:T(8,128)(2,1)S(1)} collective-permute-done((bf16[256,768]{1,0:T(8,128)(2,1)S(1)}, bf16[256,768]{1,0:T(8,128)(2,1)S(1)}, u32[]{:S(2)}, u32[]{:S(2)}) %collective-permute-start.54) | collective-permute-done | bytes 393248 | tf_op jit(solution)/shard_map/ppermute | solution.py:1072
  202.5 7.4 %collective-permute-done.55.refs_3_ = bf16[256,768]{1,0:T(8,128)(2,1)S(1)} collective-permute-done((bf16[256,768]{1,0:T(8,128)(2,1)S(1)}, bf16[256,768]{1,0:T(8,128)(2,1)S(1)}, u32[]{:S(2)}, u32[]{:S(2)}) %collective-permute-start.55) | collective-permute-done | bytes 393248 | tf_op jit(solution)/shard_map/ppermute | solution.py:1072
  209.9 2.0 branch_back.1
  211.9 3.6 %collective-permute-start.56 = (bf16[4,384,384]{2,1,0:T(8,128)(2,1)S(1)}, bf16[4,384,384]{2,1,0:T(8,128)(2,1)S(1)}, u32[]{:S(2)}, u32[]{:S(2)}) collective-permute-start(bf16[4,384,384]{2,1,0:T(8,128)(2,1)S(1)} %get-tuple-element.299), channel_id=1, source_target_pairs={{0,4},{4,0},{1,5},{5,1},{2,6},{6,2},{3,7},{7,3},{8,12},{12,8},{9,1... | collective-permute-start | bytes 3538952 | tf_op jit(solution)/shard_map/ppermute | solution.py:1072
  215.6 2.5 collective-permute-done.56.got_ref
  218.8 2.4 collective-permute-start.60
  223.9 1.7 collective-permute-done.57.refs_4_
  225.6 2.7 collective-permute-done.59.refs_6_
  228.3 1.7 out_grad.1
  233.9 10.1 %attend_back.1 = (bf16[1024,192]{1,0:T(8,128)(2,1)S(1)}, bf16[1024,192]{1,0:T(8,128)(2,1)S(1)}, bf16[1024,192]{1,0:T(8,128)(2,1)S(1)}, f32[8,192]{1,0:T(8,128)S(1)}) custom-call(s32[4]{0:T(128)S(1)} %pad_add_fusion.ids_ref, s32[16]{0:T(128)S(1)} %copy-done.10, bf16[3,1024,64]{2,1,0:T(8,128)(2,1)S(1)} %get-tuple-element.209.q_ref.refs_0_, ...), custom_call_target="tpu_custom_call" | custom-call | tf_op jit(solution)/shard_map/attend_back/pallas_call | solution.py:80
  245.6 3.4 %early_grad.1 = (f32[384,768]{1,0:T(8,128)S(1)}, f32[8,768]{1,0:T(8,128)S(1)}, bf16[400,768]{1,0:T(8,128)(2,1)S(1)}) custom-call(s32[4]{0:T(128)S(1)} %pad_add_fusion.ids_ref, bf16[512,768]{1,0:T(8,128)(2,1)S(1)} %get-tuple-element.196.own_ref.refs_5_.refs_0_, bf16[512,768]{1,0:T(8,128)(2,1)S(1)} %collective-permute-done.7.oth_ref.refs_6_.refs_1_, ...), custom_call_target="tpu_custom_call" | custom-call | tf_op jit(solution)/shard_map/early_grad/pallas_call | solution.py:80
  249.0 2.5 collective-permute-start.65
  251.5 2.0 qkv_back.1
  258.7 3.2 collective-permute-done.66.refs_1_
  264.2 8.1 %collective-permute-done.68.refs_3_ = bf16[112,768]{1,0:T(8,128)(2,1)S(1)} collective-permute-done((bf16[112,768]{1,0:T(8,128)(2,1)S(1)}, bf16[112,768]{1,0:T(8,128)(2,1)S(1)}, u32[]{:S(2)}, u32[]{:S(2)}) %collective-permute-start.68) | collective-permute-done | bytes 172064 | tf_op jit(solution)/shard_map/ppermute | solution.py:1072
  276.0 10.3 %collective-permute-done.72.refs_3_ = bf16[384,384]{1,0:T(8,128)(2,1)S(1)} collective-permute-done((bf16[384,384]{1,0:T(8,128)(2,1)S(1)}, bf16[384,384]{1,0:T(8,128)(2,1)S(1)}, u32[]{:S(2)}, u32[]{:S(2)}) %collective-permute-start.72) | collective-permute-done | bytes 294944 | tf_op jit(solution)/shard_map/ppermute | solution.py:1072
  291.5 15.4 %collective-permute-done.82.refs_2_ = bf16[112,768]{1,0:T(8,128)(2,1)S(1)} collective-permute-done((bf16[112,768]{1,0:T(8,128)(2,1)S(1)}, bf16[112,768]{1,0:T(8,128)(2,1)S(1)}, u32[]{:S(2)}, u32[]{:S(2)}) %collective-permute-start.82) | collective-permute-done | bytes 172064 | tf_op jit(solution)/shard_map/ppermute | solution.py:1072
  311.9 3.8 %late_final.1 = (f32[192,3072]{1,0:T(8,128)}, f32[768,768]{1,0:T(8,128)}) custom-call(s32[4]{0:T(128)S(1)} %pad_add_fusion.ids_ref, bf16[384,384]{1,0:T(8,128)(2,1)S(1)} %late_sum.1.refs_0_, bf16[384,384]{1,0:T(8,128)(2,1)S(1)} %collective-permute-done.74.refs_1_, bf16[384,384]{1,0:T(8,128)(2,1)S(1)} %collective-permute-done.75.refs_2_, ...), custom_call_target="tpu_custom_call" | custom-call | tf_op jit(solution)/shard_map/late_final/pallas_call | solution.py:80
  315.7 2.6 early_final.1
  (212 shorter events, 108.6 us)
Async XLA Ops:
  0.6 18.6 %collective-permute-start.3 = (bf16[2,128,768]{2,1,0:T(8,128)(2,1)}, bf16[2,128,768]{2,1,0:T(8,128)(2,1)S(1)}, u32[]{:S(2)}, u32[]{:S(2)}) collective-permute-start(bf16[2,128,768]{2,1,0:T(8,128)(2,1)} %here_ref.1), channel_id=1, source_target_pairs={{0,8},{8,0},{16,24},{24,16},{1,9},{9,1},{17,25},{25,17},{2,10},{10... | collective-permute-start | bytes 1179656 | tf_op jit(solution)/shard_map/ppermute | solution.py:1072
  1.9 17.3 %collective-permute-start.4 = (bf16[2,128,768]{2,1,0:T(8,128)(2,1)}, bf16[2,128,768]{2,1,0:T(8,128)(2,1)S(1)}, u32[]{:S(2)}, u32[]{:S(2)}) collective-permute-start(bf16[2,128,768]{2,1,0:T(8,128)(2,1)} %here_ref.1), channel_id=1, source_target_pairs={{0,16},{8,24},{16,0},{24,8},{1,17},{9,25},{17,1},{25,9},{2,18},{10... | collective-permute-start | bytes 1179656 | tf_op jit(solution)/shard_map/ppermute | solution.py:1072
  5.7 10.8 %collective-permute-start.2 = (bf16[96,768]{1,0:T(8,128)(2,1)S(1)}, bf16[96,768]{1,0:T(8,128)(2,1)S(1)}, u32[]{:S(2)}, u32[]{:S(2)}) collective-permute-start(bf16[96,768]{1,0:T(8,128)(2,1)S(1)} %early_pieces.2.refs_0_), channel_id=1, source_target_pairs={{0,3},{1,2},{2,1},{3,0},{4,7},{5,6},{6,5},{7,4},{8,11},{9,10},{10,... | collective-permute-start | bytes 442376 | tf_op jit(solution)/shard_map/ppermute | solution.py:1072
  7.0 11.4 %collective-permute-start.1 = (bf16[96,768]{1,0:T(8,128)(2,1)S(1)}, bf16[96,768]{1,0:T(8,128)(2,1)S(1)}, u32[]{:S(2)}, u32[]{:S(2)}) collective-permute-start(bf16[96,768]{1,0:T(8,128)(2,1)S(1)} %early_pieces.2.refs_0_), channel_id=1, source_target_pairs={{0,2},{1,3},{2,0},{3,1},{4,6},{5,7},{6,4},{7,5},{8,10},{9,11},{10,... | collective-permute-start | bytes 442376 | tf_op jit(solution)/shard_map/ppermute | solution.py:1072
  8.1 10.3 %collective-permute-start = (bf16[96,768]{1,0:T(8,128)(2,1)S(1)}, bf16[96,768]{1,0:T(8,128)(2,1)S(1)}, u32[]{:S(2)}, u32[]{:S(2)}) collective-permute-start(bf16[96,768]{1,0:T(8,128)(2,1)S(1)} %early_pieces.2.refs_0_), channel_id=1, source_target_pairs={{0,1},{1,0},{2,3},{3,2},{4,5},{5,4},{6,7},{7,6},{8,9},{9,8},{10,11... | collective-permute-start | bytes 442376 | tf_op jit(solution)/shard_map/ppermute | solution.py:1072
  24.8 9.4 %collective-permute-start.7 = (bf16[512,768]{1,0:T(8,128)(2,1)S(1)}, bf16[512,768]{1,0:T(8,128)(2,1)S(1)}, u32[]{:S(2)}, u32[]{:S(2)}) collective-permute-start(bf16[512,768]{1,0:T(8,128)(2,1)S(1)} %get-tuple-element.198), channel_id=1, source_target_pairs={{0,4},{4,0},{1,5},{5,1},{2,6},{6,2},{3,7},{7,3},{8,12},{12,8},{9,1... | collective-permute-start | bytes 2359304 | tf_op jit(solution)/shard_map/ppermute | solution.py:1072
  29.1 15.1 %collective-permute-start.10 = (bf16[112,768]{1,0:T(8,128)(2,1)S(1)}, bf16[112,768]{1,0:T(8,128)(2,1)S(1)}, u32[]{:S(2)}, u32[]{:S(2)}) collective-permute-start(bf16[112,768]{1,0:T(8,128)(2,1)S(1)} %early_pieces.3.refs_0_), channel_id=1, source_target_pairs={{0,2},{1,3},{2,0},{3,1},{4,6},{5,7},{6,4},{7,5},{8,10},{9,11},{10,... | collective-permute-start | bytes 516104 | tf_op jit(solution)/shard_map/ppermute | solution.py:1072
  32.7 11.6 %collective-permute-start.9 = (bf16[112,768]{1,0:T(8,128)(2,1)S(1)}, bf16[112,768]{1,0:T(8,128)(2,1)S(1)}, u32[]{:S(2)}, u32[]{:S(2)}) collective-permute-start(bf16[112,768]{1,0:T(8,128)(2,1)S(1)} %early_pieces.3.refs_0_), channel_id=1, source_target_pairs={{0,1},{1,0},{2,3},{3,2},{4,5},{5,4},{6,7},{7,6},{8,9},{9,8},{10,11... | collective-permute-start | bytes 516104 | tf_op jit(solution)/shard_map/ppermute | solution.py:1072
  32.8 17.8 %collective-permute-start.12 = (bf16[1,384,384]{2,1,0:T(8,128)(2,1)S(1)}, bf16[1,384,384]{2,1,0:T(8,128)(2,1)S(1)}, u32[]{:S(2)}, u32[]{:S(2)}) collective-permute-start(bf16[1,384,384]{2,1,0:T(8,128)(2,1)S(1)} %bitcast.11), channel_id=1, source_target_pairs={{0,1},{1,0},{2,3},{3,2},{4,5},{5,4},{6,7},{7,6},{8,9},{9,8},{10,11... | collective-permute-start | bytes 884744 | tf_op jit(solution)/shard_map/ppermute | solution.py:1072
  45.4 15.8 %collective-permute-start.17 = (bf16[384,384]{1,0:T(8,128)(2,1)S(1)}, bf16[384,384]{1,0:T(8,128)(2,1)S(1)}, u32[]{:S(2)}, u32[]{:S(2)}) collective-permute-start(bf16[384,384]{1,0:T(8,128)(2,1)S(1)} %get-tuple-element.214.refs_0_), channel_id=1, source_target_pairs={{0,24},{8,16},{16,8},{24,0},{1,25},{9,17},{17,9},{25,1},{2,26},{10... | collective-permute-start | bytes 884744 | tf_op jit(solution)/shard_map/ppermute | solution.py:1072
  46.6 25.5 %collective-permute-start.13 = (bf16[384,576]{1,0:T(8,128)(2,1)S(1)}, bf16[384,576]{1,0:T(8,128)(2,1)S(1)}, u32[]{:S(2)}, u32[]{:S(2)}) collective-permute-start(bf16[384,576]{1,0:T(8,128)(2,1)S(1)} %get-tuple-element.202.half_ref), channel_id=1, source_target_pairs={{0,4},{4,0},{1,5},{5,1},{2,6},{6,2},{3,7},{7,3},{8,12},{12,8},{9,1... | collective-permute-start | bytes 1327112 | tf_op jit(solution)/shard_map/ppermute | solution.py:1072
  57.8 12.9 %collective-permute-start.14 = (bf16[1,400,384]{2,1,0:T(8,128)(2,1)S(1)}, bf16[1,400,384]{2,1,0:T(8,128)(2,1)S(1)}, u32[]{:S(2)}, u32[]{:S(2)}) collective-permute-start(bf16[1,400,384]{2,1,0:T(8,128)(2,1)S(1)} %bitcast.9), channel_id=1, source_target_pairs={{0,1},{1,0},{2,3},{3,2},{4,5},{5,4},{6,7},{7,6},{8,9},{9,8},{10,11... | collective-permute-start | bytes 921608 | tf_op jit(solution)/shard_map/ppermute | solution.py:1072
  61.1 28.4 %collective-permute-start.25 = (bf16[2,384,384]{2,1,0:T(8,128)(2,1)S(1)}, bf16[2,384,384]{2,1,0:T(8,128)(2,1)S(1)}, u32[]{:S(2)}, u32[]{:S(2)}) collective-permute-start(bf16[2,384,384]{2,1,0:T(8,128)(2,1)S(1)} %merge.2.refs_0_), channel_id=1, source_target_pairs={{0,2},{1,3},{2,0},{3,1},{4,6},{5,7},{6,4},{7,5},{8,10},{9,11},{10,... | collective-permute-start | bytes 1769480 | tf_op jit(solution)/shard_map/ppermute | solution.py:1072
  89.6 13.9 %collective-permute-start.26 = (bf16[2,384,384]{2,1,0:T(8,128)(2,1)S(1)}, bf16[2,384,384]{2,1,0:T(8,128)(2,1)S(1)}, u32[]{:S(2)}, u32[]{:S(2)}) collective-permute-start(bf16[2,384,384]{2,1,0:T(8,128)(2,1)S(1)} %merge.2.refs_0_), channel_id=1, source_target_pairs={{0,4},{4,0},{1,5},{5,1},{2,6},{6,2},{3,7},{7,3},{8,12},{12,8},{9,1... | collective-permute-start | bytes 1769480 | tf_op jit(solution)/shard_map/ppermute | solution.py:1072
  91.1 13.4 %collective-permute-start.27 = (bf16[2,384,384]{2,1,0:T(8,128)(2,1)S(1)}, bf16[2,384,384]{2,1,0:T(8,128)(2,1)S(1)}, u32[]{:S(2)}, u32[]{:S(2)}) collective-permute-start(bf16[2,384,384]{2,1,0:T(8,128)(2,1)S(1)} %collective-permute-done.25.refs_1_), channel_id=1, source_target_pairs={{0,4},{4,0},{1,5},{5,1},{2,6},{6,2},{3,7},{7,3},{8,12},{12,8},{9,1... | collective-permute-start | bytes 1769480 | tf_op jit(solution)/shard_map/ppermute | solution.py:1072
  91.2 28.7 %collective-permute-start.33 = (bf16[2,400,384]{2,1,0:T(8,128)(2,1)S(1)}, bf16[2,400,384]{2,1,0:T(8,128)(2,1)S(1)}, u32[]{:S(2)}, u32[]{:S(2)}) collective-permute-start(bf16[2,400,384]{2,1,0:T(8,128)(2,1)S(1)} %merge.3.refs_0_), channel_id=1, source_target_pairs={{0,2},{1,3},{2,0},{3,1},{4,6},{5,7},{6,4},{7,5},{8,10},{9,11},{10,... | collective-permute-start | bytes 1843208 | tf_op jit(solution)/shard_map/ppermute | solution.py:1072
  93.4 9.9 %collective-permute-start.32 = (bf16[256,768]{1,0:T(8,128)(2,1)S(1)}, bf16[256,768]{1,0:T(8,128)(2,1)S(1)}, u32[]{:S(2)}, u32[]{:S(2)}) collective-permute-start(bf16[256,768]{1,0:T(8,128)(2,1)S(1)} %get-tuple-element.233.refs_0_), channel_id=1, source_target_pairs={{0,16},{8,24},{16,0},{24,8},{1,17},{9,25},{17,1},{25,9},{2,18},{10... | collective-permute-start | bytes 1179656 | tf_op jit(solution)/shard_map/ppermute | solution.py:1072
  93.4 15.0 %collective-permute-start.31 = (bf16[256,768]{1,0:T(8,128)(2,1)S(1)}, bf16[256,768]{1,0:T(8,128)(2,1)S(1)}, u32[]{:S(2)}, u32[]{:S(2)}) collective-permute-start(bf16[256,768]{1,0:T(8,128)(2,1)S(1)} %get-tuple-element.233.refs_0_), channel_id=1, source_target_pairs={{0,8},{8,0},{16,24},{24,16},{1,9},{9,1},{17,25},{25,17},{2,10},{10... | collective-permute-start | bytes 1179656 | tf_op jit(solution)/shard_map/ppermute | solution.py:1072
  120.4 15.9 %collective-permute-start.39 = (bf16[256,768]{1,0:T(8,128)(2,1)S(1)}, bf16[256,768]{1,0:T(8,128)(2,1)S(1)}, u32[]{:S(2)}, u32[]{:S(2)}) collective-permute-start(bf16[256,768]{1,0:T(8,128)(2,1)S(1)} %get-tuple-element.251.refs_0_.refs_9_), channel_id=1, source_target_pairs={{0,16},{8,24},{16,0},{24,8},{1,17},{9,25},{17,1},{25,9},{2,18},{10... | collective-permute-start | bytes 1179656 | tf_op jit(solution)/shard_map/ppermute | solution.py:1072
  120.4 15.9 %collective-permute-start.38 = (bf16[256,768]{1,0:T(8,128)(2,1)S(1)}, bf16[256,768]{1,0:T(8,128)(2,1)S(1)}, u32[]{:S(2)}, u32[]{:S(2)}) collective-permute-start(bf16[256,768]{1,0:T(8,128)(2,1)S(1)} %get-tuple-element.251.refs_0_.refs_9_), channel_id=1, source_target_pairs={{0,8},{8,0},{16,24},{24,16},{1,9},{9,1},{17,25},{25,17},{2,10},{10... | collective-permute-start | bytes 1179656 | tf_op jit(solution)/shard_map/ppermute | solution.py:1072
  121.6 12.9 %collective-permute-start.36 = (bf16[128,768]{1,0:T(8,128)(2,1)S(1)}, bf16[128,768]{1,0:T(8,128)(2,1)S(1)}, u32[]{:S(2)}, u32[]{:S(2)}) collective-permute-start(bf16[128,768]{1,0:T(8,128)(2,1)S(1)} %slice.35), channel_id=1, source_target_pairs={{0,8},{8,0},{16,24},{24,16},{1,9},{9,1},{17,25},{25,17},{2,10},{10... | collective-permute-start | bytes 589832 | tf_op jit(solution)/shard_map/ppermute | solution.py:1072
  122.0 12.8 %collective-permute-start.37 = (bf16[128,768]{1,0:T(8,128)(2,1)S(1)}, bf16[128,768]{1,0:T(8,128)(2,1)S(1)}, u32[]{:S(2)}, u32[]{:S(2)}) collective-permute-start(bf16[128,768]{1,0:T(8,128)(2,1)S(1)} %slice.36), channel_id=1, source_target_pairs={{0,16},{8,24},{16,0},{24,8},{1,17},{9,25},{17,1},{25,9},{2,18},{10... | collective-permute-start | bytes 589832 | tf_op jit(solution)/shard_map/ppermute | solution.py:1072
  123.4 25.5 %collective-permute-start.43 = (bf16[256,768]{1,0:T(8,128)(2,1)S(1)}, bf16[256,768]{1,0:T(8,128)(2,1)S(1)}, u32[]{:S(2)}, u32[]{:S(2)}) collective-permute-start(bf16[256,768]{1,0:T(8,128)(2,1)S(1)} %feed.10), channel_id=1, source_target_pairs={{0,16},{8,24},{16,0},{24,8},{1,17},{9,25},{17,1},{25,9},{2,18},{10... | collective-permute-start | bytes 1179656 | tf_op jit(solution)/shard_map/ppermute | solution.py:1072
  137.3 10.2 %collective-permute-start.41 = (bf16[128,768]{1,0:T(8,128)(2,1)S(1)}, bf16[128,768]{1,0:T(8,128)(2,1)S(1)}, u32[]{:S(2)}, u32[]{:S(2)}) collective-permute-start(bf16[128,768]{1,0:T(8,128)(2,1)S(1)} %slice.38), channel_id=1, source_target_pairs={{0,16},{8,24},{16,0},{24,8},{1,17},{9,25},{17,1},{25,9},{2,18},{10... | collective-permute-start | bytes 589832 | tf_op jit(solution)/shard_map/ppermute | solution.py:1072
  137.7 12.6 %collective-permute-start.42 = (bf16[256,768]{1,0:T(8,128)(2,1)S(1)}, bf16[256,768]{1,0:T(8,128)(2,1)S(1)}, u32[]{:S(2)}, u32[]{:S(2)}) collective-permute-start(bf16[256,768]{1,0:T(8,128)(2,1)S(1)} %feed.9), channel_id=1, source_target_pairs={{0,8},{8,0},{16,24},{24,16},{1,9},{9,1},{17,25},{25,17},{2,10},{10... | collective-permute-start | bytes 1179656 | tf_op jit(solution)/shard_map/ppermute | solution.py:1072
  139.1 19.8 %collective-permute-start.44 = (bf16[256,768]{1,0:T(8,128)(2,1)S(1)}, bf16[256,768]{1,0:T(8,128)(2,1)S(1)}, u32[]{:S(2)}, u32[]{:S(2)}) collective-permute-start(bf16[256,768]{1,0:T(8,128)(2,1)S(1)} %feed.12), channel_id=1, source_target_pairs={{0,24},{8,16},{16,8},{24,0},{1,25},{9,17},{17,9},{25,1},{2,26},{10... | collective-permute-start | bytes 1179656 | tf_op jit(solution)/shard_map/ppermute | solution.py:1072
  142.9 22.9 %collective-permute-start.45 = (bf16[256,768]{1,0:T(8,128)(2,1)S(1)}, bf16[256,768]{1,0:T(8,128)(2,1)S(1)}, u32[]{:S(2)}, u32[]{:S(2)}) collective-permute-start(bf16[256,768]{1,0:T(8,128)(2,1)S(1)} %get-tuple-element.258), channel_id=1, source_target_pairs={{0,8},{8,0},{16,24},{24,16},{1,9},{9,1},{17,25},{25,17},{2,10},{10... | collective-permute-start | bytes 1179656 | tf_op jit(solution)/shard_map/ppermute | solution.py:1072
  147.4 18.5 %collective-permute-start.46 = (bf16[256,768]{1,0:T(8,128)(2,1)S(1)}, bf16[256,768]{1,0:T(8,128)(2,1)S(1)}, u32[]{:S(2)}, u32[]{:S(2)}) collective-permute-start(bf16[256,768]{1,0:T(8,128)(2,1)S(1)} %get-tuple-element.261), channel_id=1, source_target_pairs={{0,16},{8,24},{16,0},{24,8},{1,17},{9,25},{17,1},{25,9},{2,18},{10... | collective-permute-start | bytes 1179656 | tf_op jit(solution)/shard_map/ppermute | solution.py:1072
  148.9 26.8 %collective-permute-start.47 = (bf16[256,768]{1,0:T(8,128)(2,1)S(1)}, bf16[256,768]{1,0:T(8,128)(2,1)S(1)}, u32[]{:S(2)}, u32[]{:S(2)}) collective-permute-start(bf16[256,768]{1,0:T(8,128)(2,1)S(1)} %get-tuple-element.263), channel_id=1, source_target_pairs={{0,24},{8,16},{16,8},{24,0},{1,25},{9,17},{17,9},{25,1},{2,26},{10... | collective-permute-start | bytes 1179656 | tf_op jit(solution)/shard_map/ppermute | solution.py:1072
  191.0 11.4 %collective-permute-start.54 = (bf16[256,768]{1,0:T(8,128)(2,1)S(1)}, bf16[256,768]{1,0:T(8,128)(2,1)S(1)}, u32[]{:S(2)}, u32[]{:S(2)}) collective-permute-start(bf16[256,768]{1,0:T(8,128)(2,1)S(1)} %get-tuple-element.279), channel_id=1, source_target_pairs={{0,16},{8,24},{16,0},{24,8},{1,17},{9,25},{17,1},{25,9},{2,18},{10... | collective-permute-start | bytes 1179656 | tf_op jit(solution)/shard_map/ppermute | solution.py:1072
  191.4 11.1 %collective-permute-start.53 = (bf16[256,768]{1,0:T(8,128)(2,1)S(1)}, bf16[256,768]{1,0:T(8,128)(2,1)S(1)}, u32[]{:S(2)}, u32[]{:S(2)}) collective-permute-start(bf16[256,768]{1,0:T(8,128)(2,1)S(1)} %get-tuple-element.275), channel_id=1, source_target_pairs={{0,8},{8,0},{16,24},{24,16},{1,9},{9,1},{17,25},{25,17},{2,10},{10... | collective-permute-start | bytes 1179656 | tf_op jit(solution)/shard_map/ppermute | solution.py:1072
  193.8 16.1 %collective-permute-start.55 = (bf16[256,768]{1,0:T(8,128)(2,1)S(1)}, bf16[256,768]{1,0:T(8,128)(2,1)S(1)}, u32[]{:S(2)}, u32[]{:S(2)}) collective-permute-start(bf16[256,768]{1,0:T(8,128)(2,1)S(1)} %get-tuple-element.282), channel_id=1, source_target_pairs={{0,24},{8,16},{16,8},{24,0},{1,25},{9,17},{17,9},{25,1},{2,26},{10... | collective-permute-start | bytes 1179656 | tf_op jit(solution)/shard_map/ppermute | solution.py:1072
  218.8 11.2 %collective-permute-start.60 = (bf16[384,384]{1,0:T(8,128)(2,1)S(1)}, bf16[384,384]{1,0:T(8,128)(2,1)S(1)}, u32[]{:S(2)}, u32[]{:S(2)}) collective-permute-start(bf16[384,384]{1,0:T(8,128)(2,1)S(1)} %get-tuple-element.311), channel_id=1, source_target_pairs={{0,1},{1,0},{2,3},{3,2},{4,5},{5,4},{6,7},{7,6},{8,9},{9,8},{10,11... | collective-permute-start | bytes 884744 | tf_op jit(solution)/shard_map/ppermute | solution.py:1072
  230.0 13.9 %collective-permute-start.61 = (bf16[384,384]{1,0:T(8,128)(2,1)S(1)}, bf16[384,384]{1,0:T(8,128)(2,1)S(1)}, u32[]{:S(2)}, u32[]{:S(2)}) collective-permute-start(bf16[384,384]{1,0:T(8,128)(2,1)S(1)} %get-tuple-element.317), channel_id=1, source_target_pairs={{0,2},{1,3},{2,0},{3,1},{4,6},{5,7},{6,4},{7,5},{8,10},{9,11},{10,... | collective-permute-start | bytes 884744 | tf_op jit(solution)/shard_map/ppermute | solution.py:1072
  231.2 12.7 %collective-permute-start.62 = (bf16[384,384]{1,0:T(8,128)(2,1)S(1)}, bf16[384,384]{1,0:T(8,128)(2,1)S(1)}, u32[]{:S(2)}, u32[]{:S(2)}) collective-permute-start(bf16[384,384]{1,0:T(8,128)(2,1)S(1)} %get-tuple-element.321), channel_id=1, source_target_pairs={{0,8},{8,0},{16,24},{24,16},{1,9},{9,1},{17,25},{25,17},{2,10},{10... | collective-permute-start | bytes 884744 | tf_op jit(solution)/shard_map/ppermute | solution.py:1072
  232.1 11.8 %collective-permute-start.63 = (bf16[384,384]{1,0:T(8,128)(2,1)S(1)}, bf16[384,384]{1,0:T(8,128)(2,1)S(1)}, u32[]{:S(2)}, u32[]{:S(2)}) collective-permute-start(bf16[384,384]{1,0:T(8,128)(2,1)S(1)} %get-tuple-element.322), channel_id=1, source_target_pairs={{0,16},{8,24},{16,0},{24,8},{1,17},{9,25},{17,1},{25,9},{2,18},{10... | collective-permute-start | bytes 884744 | tf_op jit(solution)/shard_map/ppermute | solution.py:1072
  232.6 13.1 %collective-permute-start.64 = (bf16[384,384]{1,0:T(8,128)(2,1)S(1)}, bf16[384,384]{1,0:T(8,128)(2,1)S(1)}, u32[]{:S(2)}, u32[]{:S(2)}) collective-permute-start(bf16[384,384]{1,0:T(8,128)(2,1)S(1)} %get-tuple-element.323), channel_id=1, source_target_pairs={{0,24},{8,16},{16,8},{24,0},{1,25},{9,17},{17,9},{25,1},{2,26},{10... | collective-permute-start | bytes 884744 | tf_op jit(solution)/shard_map/ppermute | solution.py:1072
  255.9 16.3 %collective-permute-start.68 = (bf16[112,768]{1,0:T(8,128)(2,1)S(1)}, bf16[112,768]{1,0:T(8,128)(2,1)S(1)}, u32[]{:S(2)}, u32[]{:S(2)}) collective-permute-start(bf16[112,768]{1,0:T(8,128)(2,1)S(1)} %get-tuple-element.343), channel_id=1, source_target_pairs={{0,3},{1,2},{2,1},{3,0},{4,7},{5,6},{6,5},{7,4},{8,11},{9,10},{10,... | collective-permute-start | bytes 516104 | tf_op jit(solution)/shard_map/ppermute | solution.py:1072
  257.0 17.9 %collective-permute-start.69 = (bf16[256,768]{1,0:T(8,128)(2,1)S(1)}, bf16[256,768]{1,0:T(8,128)(2,1)S(1)}, u32[]{:S(2)}, u32[]{:S(2)}) collective-permute-start(bf16[256,768]{1,0:T(8,128)(2,1)S(1)} %get-tuple-element.349), channel_id=1, source_target_pairs={{0,8},{8,0},{16,24},{24,16},{1,9},{9,1},{17,25},{25,17},{2,10},{10... | collective-permute-start | bytes 1179656 | tf_op jit(solution)/shard_map/ppermute | solution.py:1072
  257.4 17.5 %collective-permute-start.70 = (bf16[256,768]{1,0:T(8,128)(2,1)S(1)}, bf16[256,768]{1,0:T(8,128)(2,1)S(1)}, u32[]{:S(2)}, u32[]{:S(2)}) collective-permute-start(bf16[256,768]{1,0:T(8,128)(2,1)S(1)} %get-tuple-element.350), channel_id=1, source_target_pairs={{0,16},{8,24},{16,0},{24,8},{1,17},{9,25},{17,1},{25,9},{2,18},{10... | collective-permute-start | bytes 1179656 | tf_op jit(solution)/shard_map/ppermute | solution.py:1072
  261.9 13.3 %collective-permute-start.71 = (bf16[256,768]{1,0:T(8,128)(2,1)S(1)}, bf16[256,768]{1,0:T(8,128)(2,1)S(1)}, u32[]{:S(2)}, u32[]{:S(2)}) collective-permute-start(bf16[256,768]{1,0:T(8,128)(2,1)S(1)} %get-tuple-element.351), channel_id=1, source_target_pairs={{0,24},{8,16},{16,8},{24,0},{1,25},{9,17},{17,9},{25,1},{2,26},{10... | collective-permute-start | bytes 1179656 | tf_op jit(solution)/shard_map/ppermute | solution.py:1072
  272.9 13.4 %collective-permute-start.72 = (bf16[384,384]{1,0:T(8,128)(2,1)S(1)}, bf16[384,384]{1,0:T(8,128)(2,1)S(1)}, u32[]{:S(2)}, u32[]{:S(2)}) collective-permute-start(bf16[384,384]{1,0:T(8,128)(2,1)S(1)} %get-tuple-element.355), channel_id=1, source_target_pairs={{0,3},{1,2},{2,1},{3,0},{4,7},{5,6},{6,5},{7,4},{8,11},{9,10},{10,... | collective-permute-start | bytes 884744 | tf_op jit(solution)/shard_map/ppermute | solution.py:1072
  273.4 16.6 %collective-permute-start.83 = (bf16[112,768]{1,0:T(8,128)(2,1)S(1)}, bf16[112,768]{1,0:T(8,128)(2,1)S(1)}, u32[]{:S(2)}, u32[]{:S(2)}) collective-permute-start(bf16[112,768]{1,0:T(8,128)(2,1)S(1)} %early_sum.1.refs_0_), channel_id=1, source_target_pairs={{0,24},{8,16},{16,8},{24,0},{1,25},{9,17},{17,9},{25,1},{2,26},{10... | collective-permute-start | bytes 516104 | tf_op jit(solution)/shard_map/ppermute | solution.py:1072
  287.1 20.4 %collective-permute-start.76 = (bf16[384,384]{1,0:T(8,128)(2,1)S(1)}, bf16[384,384]{1,0:T(8,128)(2,1)S(1)}, u32[]{:S(2)}, u32[]{:S(2)}) collective-permute-start(bf16[384,384]{1,0:T(8,128)(2,1)S(1)} %late_sum.1.refs_0_), channel_id=1, source_target_pairs={{0,24},{8,16},{16,8},{24,0},{1,25},{9,17},{17,9},{25,1},{2,26},{10... | collective-permute-start | bytes 884744 | tf_op jit(solution)/shard_map/ppermute | solution.py:1072
  288.6 19.4 %collective-permute-start.75 = (bf16[384,384]{1,0:T(8,128)(2,1)S(1)}, bf16[384,384]{1,0:T(8,128)(2,1)S(1)}, u32[]{:S(2)}, u32[]{:S(2)}) collective-permute-start(bf16[384,384]{1,0:T(8,128)(2,1)S(1)} %late_sum.1.refs_0_), channel_id=1, source_target_pairs={{0,16},{8,24},{16,0},{24,8},{1,17},{9,25},{17,1},{25,9},{2,18},{10... | collective-permute-start | bytes 884744 | tf_op jit(solution)/shard_map/ppermute | solution.py:1072
  288.7 18.2 %collective-permute-start.82 = (bf16[112,768]{1,0:T(8,128)(2,1)S(1)}, bf16[112,768]{1,0:T(8,128)(2,1)S(1)}, u32[]{:S(2)}, u32[]{:S(2)}) collective-permute-start(bf16[112,768]{1,0:T(8,128)(2,1)S(1)} %early_sum.1.refs_0_), channel_id=1, source_target_pairs={{0,16},{8,24},{16,0},{24,8},{1,17},{9,25},{17,1},{25,9},{2,18},{10... | collective-permute-start | bytes 516104 | tf_op jit(solution)/shard_map/ppermute | solution.py:1072
  290.1 17.4 %collective-permute-start.81 = (bf16[112,768]{1,0:T(8,128)(2,1)S(1)}, bf16[112,768]{1,0:T(8,128)(2,1)S(1)}, u32[]{:S(2)}, u32[]{:S(2)}) collective-permute-start(bf16[112,768]{1,0:T(8,128)(2,1)S(1)} %early_sum.1.refs_0_), channel_id=1, source_target_pairs={{0,8},{8,0},{16,24},{24,16},{1,9},{9,1},{17,25},{25,17},{2,10},{10... | collective-permute-start | bytes 516104 | tf_op jit(solution)/shard_map/ppermute | solution.py:1072
  290.1 18.0 %collective-permute-start.74 = (bf16[384,384]{1,0:T(8,128)(2,1)S(1)}, bf16[384,384]{1,0:T(8,128)(2,1)S(1)}, u32[]{:S(2)}, u32[]{:S(2)}) collective-permute-start(bf16[384,384]{1,0:T(8,128)(2,1)S(1)} %late_sum.1.refs_0_), channel_id=1, source_target_pairs={{0,8},{8,0},{16,24},{24,16},{1,9},{9,1},{17,25},{25,17},{2,10},{10... | collective-permute-start | bytes 884744 | tf_op jit(solution)/shard_map/ppermute | solution.py:1072
  (52 other events, 313.6 us)

commit v5 on v4

--- a/solution.py
+++ b/solution.py
@@ -440,8 +440,9 @@
     rows = own_ref.shape[0] // CHIPS
     per = rows // BLK
     for core, ref in enumerate((own_ref, oth_ref)):
+        full = dot(ref[...], weight)
         for mask in range(CHIPS):
-            result = dot(ref[mask * rows : (mask + 1) * rows, :], weight)
+            result = full[mask * rows : (mask + 1) * rows, :]
             goal = slice((mask * CORES + core) * rows, (mask * CORES + core + 1) * rows)
             sets = (
                 (q_ref, result[:, :COLS] + q_bias),
@@ -1232,7 +1233,7 @@
     t_late = spread_z(t_late)
     t_heads, _ = attend(t_query, t_key, t_value)
     (s_late,) = line.behind(s_late)
-    out_all = list(line.behind(*gather(out_half, "chip")))
+    out_all = gather(out_half, "chip")
     query, key, value, w_qkv = project(s_qkv_half, student_vec)
     s_late = spread_z(s_late)
     t_out, s_out = line(
@@ -1244,8 +1245,9 @@
     )
     t_first, t_sent = branch(False, t_heads, t_out, teacher_vec)
     t_near = near_rows(t_sent)
+    t_late = line.behind(*t_late)
     heads, lse = attend(query, key, value)
-    t_late = late_weights(False, line.behind(*t_late), teacher_vec)
+    t_late = late_weights(False, t_late, teacher_vec)
     t_parts = [feed(False, (t_sent,), 0, t_late)[0]]
     t_firsts = all_rows(t_near)
     first, sent, residual, branch_sums = branch(True, heads, s_out, student_vec)
@@ -1255,9 +1257,9 @@
     s_late = late_weights(True, line.behind(*s_late), student_vec)
     w_in, w_down, _ = s_late
     fed = [feed(True, (sent,), 0, s_late)]
+    firsts = all_rows(near)
     t_parts.append(feed(False, t_firsts[3], 3, t_late)[0])
     t_parts = exchange(t_parts, "chip")
-    firsts = all_rows(near)
     fed += [feed(True, firsts[m], m, s_late) for m in range(1, CHIPS)]
     parts, inners, acts = ([f[i] for f in fed] for i in range(3))
     target = line(
@@ -1287,7 +1289,6 @@
             (here, swap(there)),
         )
 
-    output = to_owners(out[:rows], out[rows:])
     def feed_back(pieces, m):
         return line(
             functools.partial(feed_back_kernel, len(pieces)),
@@ -1305,6 +1306,7 @@
     backs = [feed_back((sent,), 0)]
     feeds = all_rows(near)
     backs += [feed_back(feeds[m], m) for m in range(1, CHIPS)]
+    output = to_owners(out[:rows], out[rows:])
     parts, grad_inners, b1_sums = ([b[i] for b in backs] for i in range(3))
     groups = [(act,) for act in acts] + feeds + firsts + [(inner,) for inner in grad_inners]
     keep, send = line(
@@ -1343,7 +1345,6 @@
                 late_got.append(flip(*line.behind(late_pieces_out[m]), "shard", m))
 
     late_exchange(1)
-    line.wait(*grad_heads)
     out_parts = line(
         functools.partial(out_grad_kernel, n_shard),
         "out_grad",
@@ -1354,7 +1355,8 @@
         (*heads, grad_branch),
         (pltpu.VMEM((CHIPS, own, COLS), bf16), pltpu.VMEM((D, COLS), f32)),
     )
-    line.wait(late_got[-1])
+    line.wait(*grad_heads)
+    out_parts = list(line.behind(*out_parts))
     late_exchange(2)
     outs = (
         shape((tokens, COLS)),
@@ -1460,14 +1462,6 @@
         late = line(sum_kernel, "rest_sum", shape(late.shape), (), gather(late, "rest"), bare=True)
     late = gather(late, "chip")
     grad_hidden = to_owners(here, there)
-    in_grad, down_grad = line(
-        functools.partial(late_final_kernel, n_shard),
-        "late_final",
-        (shape(ffn_in_latent.shape, f32), shape(ffn_out_latent.shape, f32)),
-        (),
-        (*late, *[swap(piece) for piece in late], ffn_in_latent, ffn_out_latent),
-        (pltpu.VMEM((GROUP, each, HALF), bf16),),
-    )
     early = gather(early, "chip")
     attn_grad, vec_grad, query_grad, stats = line(
         functools.partial(early_final_kernel, n_shard),
@@ -1486,6 +1480,14 @@
             pltpu.VMEM((8, D), f32),
         ),
     )
+    in_grad, down_grad = line(
+        functools.partial(late_final_kernel, n_shard),
+        "late_final",
+        (shape(ffn_in_latent.shape, f32), shape(ffn_out_latent.shape, f32)),
+        (),
+        (*late, *[swap(piece) for piece in late], ffn_in_latent, ffn_out_latent),
+        (pltpu.VMEM((GROUP, each, HALF), bf16),),
+    )
     return (
         output,
         stats[0, :4],

time: 325 us -> 313 us (0.963)
  the two profiles are of different devices: /device:TPU:9 before, /device:TPU:0 now
where the time goes in v5:
time: 313 us; the launch traced here: 308 us
  waiting for transfers between devices  125 us (40%)
  Pallas kernels  91.8 us (29%)
  starting transfers between devices  83.9 us (27%)
  local copies, waits for them, and re-layouts  5.3 us (2%)
    ppermute x88, waiting for transfers between devices, flip(): return lax.ppermute(piece, axis, [(a, a ^ mask) for a in range(size)])  125 us
    pallas_call x44, Pallas kernels, call(): pl.pallas_call(kernel, out_shape=outs, in_specs=[SMEM_SPEC] * len(scalars...  85.6 us
    ppermute x88, starting transfers between devices, flip(): return lax.ppermute(piece, axis, [(a, a ^ mask) for a in range(size)])  83.9 us
  transfers between devices with their start and end apart: 88, of which 40 were waited for; matrix products, arithmetic and copies ran while one was open for 0% of the time, Pallas kernels for 26%

profile of v5, /device:TPU:0, one launch (start us, length us, event | category | flops | bytes accessed | tf_op | source)
XLA Modules:
  0.0 308.1 jit_solution(17638779432662920302)
XLA Ops:
  0.6 3.0 collective-permute-start.3
  7.7 3.7 %collective-permute-start.2 = (bf16[96,768]{1,0:T(8,128)(2,1)S(1)}, bf16[96,768]{1,0:T(8,128)(2,1)S(1)}, u32[]{:S(2)}, u32[]{:S(2)}) collective-permute-start(bf16[96,768]{1,0:T(8,128)(2,1)S(1)} %early_pieces.2.refs_0_), channel_id=1, source_target_pairs={{0,3},{1,2},{2,1},{3,0},{4,7},{5,6},{6,5},{7,4},{8,11},{9,10},{10,... | collective-permute-start | bytes 442376 | tf_op jit(solution)/shard_map/ppermute | solution.py:1073
  16.3 6.9 %collective-permute-done.1.refs_2_ = bf16[96,768]{1,0:T(8,128)(2,1)S(1)} collective-permute-done((bf16[96,768]{1,0:T(8,128)(2,1)S(1)}, bf16[96,768]{1,0:T(8,128)(2,1)S(1)}, u32[]{:S(2)}, u32[]{:S(2)}) %collective-permute-start.1) | collective-permute-done | bytes 147488 | tf_op jit(solution)/shard_map/ppermute | solution.py:1073
  26.9 2.1 late_pieces.3
  31.6 2.5 collective-permute-start.11
  34.1 1.9 collective-permute-start.9
  36.1 3.0 qkv.2
  40.8 7.5 %collective-permute-done.10.refs_2_ = bf16[112,768]{1,0:T(8,128)(2,1)S(1)} collective-permute-done((bf16[112,768]{1,0:T(8,128)(2,1)S(1)}, bf16[112,768]{1,0:T(8,128)(2,1)S(1)}, u32[]{:S(2)}, u32[]{:S(2)}) %collective-permute-start.10) | collective-permute-done | bytes 172064 | tf_op jit(solution)/shard_map/ppermute | solution.py:1073
  54.2 6.6 %attend.2 = (bf16[256,192]{1,0:T(8,128)(2,1)S(1)}, bf16[256,192]{1,0:T(8,128)(2,1)S(1)}, bf16[256,192]{1,0:T(8,128)(2,1)S(1)}, bf16[256,192]{1,0:T(8,128)(2,1)S(1)}, f32[3,1,1024]{2,1,0:T(1,128)}) custom-call(s32[4]{0:T(128)S(1)} %pad_add_fusion.ids_ref, s32[16]{0:T(128)S(1)} %copy-done.11, bf16[3,1024,64]{2,1,0:T(8,128)(2,1)S(1)} %get-tuple-element.198.q_ref, ...), custom_call_target="tpu_custom_call" | custom-call | tf_op jit(solution)/shard_map/attend/pallas_call | solution.py:80
  61.5 2.4 collective-permute-start.25
  63.9 2.2 collective-permute-done.16.refs_2_
  66.6 9.7 %collective-permute-done.14.got_ref = bf16[1,400,384]{2,1,0:T(8,128)(2,1)S(1)} collective-permute-done((bf16[1,400,384]{2,1,0:T(8,128)(2,1)S(1)}, bf16[1,400,384]{2,1,0:T(8,128)(2,1)S(1)}, u32[]{:S(2)}, u32[]{:S(2)}) %collective-permute-start.14) | collective-permute-done | bytes 307232 | tf_op jit(solution)/shard_map/ppermute | solution.py:1073
  79.8 2.1 qkv.3
  83.6 2.7 collective-permute-done.23.refs_2_
  87.8 1.9 collective-permute-done.25.refs_1_
  92.3 6.4 %attend.3 = (bf16[256,192]{1,0:T(8,128)(2,1)S(1)}, bf16[256,192]{1,0:T(8,128)(2,1)S(1)}, bf16[256,192]{1,0:T(8,128)(2,1)S(1)}, bf16[256,192]{1,0:T(8,128)(2,1)S(1)}, f32[3,1,1024]{2,1,0:T(1,128)S(1)}) custom-call(s32[4]{0:T(128)S(1)} %pad_add_fusion.ids_ref, s32[16]{0:T(128)S(1)} %copy-done.11, bf16[3,1024,64]{2,1,0:T(8,128)(2,1)S(1)} %get-tuple-element.208.q_ref.refs_0_, ...), custom_call_target="tpu_custom_call" | custom-call | tf_op jit(solution)/shard_map/attend/pallas_call | solution.py:80
  98.7 2.6 collective-permute-done.32.refs_0_
  107.2 2.8 collective-permute-done.29.refs_2_
  114.6 5.2 %collective-permute-done.33.refs_1_ = bf16[2,400,384]{2,1,0:T(8,128)(2,1)S(1)} collective-permute-done((bf16[2,400,384]{2,1,0:T(8,128)(2,1)S(1)}, bf16[2,400,384]{2,1,0:T(8,128)(2,1)S(1)}, u32[]{:S(2)}, u32[]{:S(2)}) %collective-permute-start.33) | collective-permute-done | bytes 614432 | tf_op jit(solution)/shard_map/ppermute | solution.py:1073
  127.8 4.5 %collective-permute-done.39.refs_0_.refs_11_ = bf16[256,768]{1,0:T(8,128)(2,1)S(1)} collective-permute-done((bf16[256,768]{1,0:T(8,128)(2,1)S(1)}, bf16[256,768]{1,0:T(8,128)(2,1)S(1)}, u32[]{:S(2)}, u32[]{:S(2)}) %collective-permute-start.39) | collective-permute-done | bytes 393248 | tf_op jit(solution)/shard_map/ppermute | solution.py:1073
  138.6 6.4 %collective-permute-done.37.refs_1_ = bf16[128,768]{1,0:T(8,128)(2,1)S(1)} collective-permute-done((bf16[128,768]{1,0:T(8,128)(2,1)S(1)}, bf16[128,768]{1,0:T(8,128)(2,1)S(1)}, u32[]{:S(2)}, u32[]{:S(2)}) %collective-permute-start.37) | collective-permute-done | bytes 196640 | tf_op jit(solution)/shard_map/ppermute | solution.py:1073
  155.9 3.5 %collective-permute-done.44.refs_3_ = bf16[256,768]{1,0:T(8,128)(2,1)S(1)} collective-permute-done((bf16[256,768]{1,0:T(8,128)(2,1)S(1)}, bf16[256,768]{1,0:T(8,128)(2,1)S(1)}, u32[]{:S(2)}, u32[]{:S(2)}) %collective-permute-start.44) | collective-permute-done | bytes 393248 | tf_op jit(solution)/shard_map/ppermute | solution.py:1073
  160.4 6.5 %collective-permute-done.45.refs_1_ = bf16[256,768]{1,0:T(8,128)(2,1)S(1)} collective-permute-done((bf16[256,768]{1,0:T(8,128)(2,1)S(1)}, bf16[256,768]{1,0:T(8,128)(2,1)S(1)}, u32[]{:S(2)}, u32[]{:S(2)}) %collective-permute-start.45) | collective-permute-done | bytes 393248 | tf_op jit(solution)/shard_map/ppermute | solution.py:1073
  167.8 6.9 %collective-permute-done.47.refs_3_ = bf16[256,768]{1,0:T(8,128)(2,1)S(1)} collective-permute-done((bf16[256,768]{1,0:T(8,128)(2,1)S(1)}, bf16[256,768]{1,0:T(8,128)(2,1)S(1)}, u32[]{:S(2)}, u32[]{:S(2)}) %collective-permute-start.47) | collective-permute-done | bytes 393248 | tf_op jit(solution)/shard_map/ppermute | solution.py:1073
  174.7 1.8 loss.1
  180.1 6.0 %collective-permute-done.49.refs_0_.refs_6_ = bf16[256,768]{1,0:T(8,128)(2,1)S(1)} collective-permute-done((bf16[256,768]{1,0:T(8,128)(2,1)S(1)}, bf16[256,768]{1,0:T(8,128)(2,1)S(1)}, u32[]{:S(2)}, u32[]{:S(2)}) %collective-permute-start.49) | collective-permute-done | bytes 393248 | tf_op jit(solution)/shard_map/ppermute | solution.py:1073
  196.7 2.0 collective-permute-start.55
  201.6 3.5 %late_grad.1 = (f32[4,384,384]{2,1,0:T(8,128)S(1)}, bf16[4,384,384]{2,1,0:T(8,128)(2,1)S(1)}) custom-call(s32[4]{0:T(128)S(1)} %pad_add_fusion.ids_ref, bf16[256,768]{1,0:T(8,128)(2,1)S(1)} %get-tuple-element.279.refs_0_, bf16[256,768]{1,0:T(8,128)(2,1)S(1)} %get-tuple-element.280.refs_1_, bf16[256,768]{1,0:T(8,128)(2,1)S(1)} %get-tuple-element.281.refs_2_, ...), custom_call_target="tpu_custom_call" | custom-call | tf_op jit(solution)/shard_map/late_grad/pallas_call | solution.py:80
  205.1 5.4 %collective-permute-done.54.refs_2_ = bf16[256,768]{1,0:T(8,128)(2,1)S(1)} collective-permute-done((bf16[256,768]{1,0:T(8,128)(2,1)S(1)}, bf16[256,768]{1,0:T(8,128)(2,1)S(1)}, u32[]{:S(2)}, u32[]{:S(2)}) %collective-permute-start.54) | collective-permute-done | bytes 393248 | tf_op jit(solution)/shard_map/ppermute | solution.py:1073
  210.5 2.0 branch_back.1
  214.3 1.8 collective-permute-start.59
  216.9 1.7 out_grad.1
  219.7 2.3 collective-permute-done.59.refs_6_
  225.5 10.1 %attend_back.1 = (bf16[1024,192]{1,0:T(8,128)(2,1)S(1)}, bf16[1024,192]{1,0:T(8,128)(2,1)S(1)}, bf16[1024,192]{1,0:T(8,128)(2,1)S(1)}, f32[8,192]{1,0:T(8,128)S(1)}) custom-call(s32[4]{0:T(128)S(1)} %pad_add_fusion.ids_ref, s32[16]{0:T(128)S(1)} %copy-done.11, bf16[3,1024,64]{2,1,0:T(8,128)(2,1)S(1)} %get-tuple-element.208.q_ref.refs_0_, ...), custom_call_target="tpu_custom_call" | custom-call | tf_op jit(solution)/shard_map/attend_back/pallas_call | solution.py:80
  237.1 3.4 %early_grad.1 = (f32[384,768]{1,0:T(8,128)S(1)}, f32[8,768]{1,0:T(8,128)S(1)}, bf16[400,768]{1,0:T(8,128)(2,1)S(1)}) custom-call(s32[4]{0:T(128)S(1)} %pad_add_fusion.ids_ref, bf16[512,768]{1,0:T(8,128)(2,1)S(1)} %get-tuple-element.195.own_ref.refs_5_.refs_0_, bf16[512,768]{1,0:T(8,128)(2,1)S(1)} %collective-permute-done.7.oth_ref.refs_6_.refs_1_, ...), custom_call_target="tpu_custom_call" | custom-call | tf_op jit(solution)/shard_map/early_grad/pallas_call | solution.py:80
  240.6 2.0 qkv_back.1
  243.4 1.8 collective-permute-start.65
  246.2 1.9 collective-permute-start.71
  251.1 2.8 collective-permute-done.65.refs_1_
  255.1 1.9 collective-permute-done.66.refs_2_
  257.0 1.8 collective-permute-start.70
  258.8 7.4 %collective-permute-done.67.refs_3_ = bf16[112,768]{1,0:T(8,128)(2,1)S(1)} collective-permute-done((bf16[112,768]{1,0:T(8,128)(2,1)S(1)}, bf16[112,768]{1,0:T(8,128)(2,1)S(1)}, u32[]{:S(2)}, u32[]{:S(2)}) %collective-permute-start.67) | collective-permute-done | bytes 172064 | tf_op jit(solution)/shard_map/ppermute | solution.py:1073
  268.3 1.8 collective-permute-start.76
  270.1 4.9 %collective-permute-done.76.refs_3_ = bf16[112,768]{1,0:T(8,128)(2,1)S(1)} collective-permute-done((bf16[112,768]{1,0:T(8,128)(2,1)S(1)}, bf16[112,768]{1,0:T(8,128)(2,1)S(1)}, u32[]{:S(2)}, u32[]{:S(2)}) %collective-permute-start.76) | collective-permute-done | bytes 172064 | tf_op jit(solution)/shard_map/ppermute | solution.py:1073
  285.7 5.0 %collective-permute-done.83.refs_3_ = bf16[384,384]{1,0:T(8,128)(2,1)S(1)} collective-permute-done((bf16[384,384]{1,0:T(8,128)(2,1)S(1)}, bf16[384,384]{1,0:T(8,128)(2,1)S(1)}, u32[]{:S(2)}, u32[]{:S(2)}) %collective-permute-start.83) | collective-permute-done | bytes 294944 | tf_op jit(solution)/shard_map/ppermute | solution.py:1073
  290.7 5.3 %collective-permute-done.82.refs_2_ = bf16[384,384]{1,0:T(8,128)(2,1)S(1)} collective-permute-done((bf16[384,384]{1,0:T(8,128)(2,1)S(1)}, bf16[384,384]{1,0:T(8,128)(2,1)S(1)}, u32[]{:S(2)}, u32[]{:S(2)}) %collective-permute-start.82) | collective-permute-done | bytes 294944 | tf_op jit(solution)/shard_map/ppermute | solution.py:1073
  298.1 2.5 early_final.1
  303.5 4.4 %late_final.1 = (f32[192,3072]{1,0:T(8,128)}, f32[768,768]{1,0:T(8,128)}) custom-call(s32[4]{0:T(128)S(1)} %pad_add_fusion.ids_ref, bf16[384,384]{1,0:T(8,128)(2,1)S(1)} %late_sum.1.refs_0_, bf16[384,384]{1,0:T(8,128)(2,1)S(1)} %collective-permute-done.81.refs_1_, bf16[384,384]{1,0:T(8,128)(2,1)S(1)} %collective-permute-done.82.refs_2_, ...), custom_call_target="tpu_custom_call" | custom-call | tf_op jit(solution)/shard_map/late_final/pallas_call | solution.py:80
  (214 shorter events, 119.8 us)
Async XLA Ops:
  0.6 23.4 %collective-permute-start.3 = (bf16[2,128,768]{2,1,0:T(8,128)(2,1)}, bf16[2,128,768]{2,1,0:T(8,128)(2,1)S(1)}, u32[]{:S(2)}, u32[]{:S(2)}) collective-permute-start(bf16[2,128,768]{2,1,0:T(8,128)(2,1)} %here_ref.1), channel_id=1, source_target_pairs={{0,8},{8,0},{16,24},{24,16},{1,9},{9,1},{17,25},{25,17},{2,10},{10... | collective-permute-start | bytes 1179656 | tf_op jit(solution)/shard_map/ppermute | solution.py:1073
  3.6 20.4 %collective-permute-start.4 = (bf16[2,128,768]{2,1,0:T(8,128)(2,1)}, bf16[2,128,768]{2,1,0:T(8,128)(2,1)S(1)}, u32[]{:S(2)}, u32[]{:S(2)}) collective-permute-start(bf16[2,128,768]{2,1,0:T(8,128)(2,1)} %here_ref.1), channel_id=1, source_target_pairs={{0,16},{8,24},{16,0},{24,8},{1,17},{9,25},{17,1},{25,9},{2,18},{10... | collective-permute-start | bytes 1179656 | tf_op jit(solution)/shard_map/ppermute | solution.py:1073
  11.4 11.9 %collective-permute-start.1 = (bf16[96,768]{1,0:T(8,128)(2,1)S(1)}, bf16[96,768]{1,0:T(8,128)(2,1)S(1)}, u32[]{:S(2)}, u32[]{:S(2)}) collective-permute-start(bf16[96,768]{1,0:T(8,128)(2,1)S(1)} %early_pieces.2.refs_0_), channel_id=1, source_target_pairs={{0,2},{1,3},{2,0},{3,1},{4,6},{5,7},{6,4},{7,5},{8,10},{9,11},{10,... | collective-permute-start | bytes 442376 | tf_op jit(solution)/shard_map/ppermute | solution.py:1073
  11.4 11.9 %collective-permute-start = (bf16[96,768]{1,0:T(8,128)(2,1)S(1)}, bf16[96,768]{1,0:T(8,128)(2,1)S(1)}, u32[]{:S(2)}, u32[]{:S(2)}) collective-permute-start(bf16[96,768]{1,0:T(8,128)(2,1)S(1)} %early_pieces.2.refs_0_), channel_id=1, source_target_pairs={{0,1},{1,0},{2,3},{3,2},{4,5},{5,4},{6,7},{7,6},{8,9},{9,8},{10,11... | collective-permute-start | bytes 442376 | tf_op jit(solution)/shard_map/ppermute | solution.py:1073
  34.1 14.2 %collective-permute-start.10 = (bf16[112,768]{1,0:T(8,128)(2,1)S(1)}, bf16[112,768]{1,0:T(8,128)(2,1)S(1)}, u32[]{:S(2)}, u32[]{:S(2)}) collective-permute-start(bf16[112,768]{1,0:T(8,128)(2,1)S(1)} %early_pieces.3.refs_0_), channel_id=1, source_target_pairs={{0,2},{1,3},{2,0},{3,1},{4,6},{5,7},{6,4},{7,5},{8,10},{9,11},{10,... | collective-permute-start | bytes 516104 | tf_op jit(solution)/shard_map/ppermute | solution.py:1073
  34.1 14.2 %collective-permute-start.9 = (bf16[112,768]{1,0:T(8,128)(2,1)S(1)}, bf16[112,768]{1,0:T(8,128)(2,1)S(1)}, u32[]{:S(2)}, u32[]{:S(2)}) collective-permute-start(bf16[112,768]{1,0:T(8,128)(2,1)S(1)} %early_pieces.3.refs_0_), channel_id=1, source_target_pairs={{0,1},{1,0},{2,3},{3,2},{4,5},{5,4},{6,7},{7,6},{8,9},{9,8},{10,11... | collective-permute-start | bytes 516104 | tf_op jit(solution)/shard_map/ppermute | solution.py:1073
  36.0 17.6 %collective-permute-start.12 = (bf16[1,384,384]{2,1,0:T(8,128)(2,1)S(1)}, bf16[1,384,384]{2,1,0:T(8,128)(2,1)S(1)}, u32[]{:S(2)}, u32[]{:S(2)}) collective-permute-start(bf16[1,384,384]{2,1,0:T(8,128)(2,1)S(1)} %bitcast.11), channel_id=1, source_target_pairs={{0,1},{1,0},{2,3},{3,2},{4,5},{5,4},{6,7},{7,6},{8,9},{9,8},{10,11... | collective-permute-start | bytes 884744 | tf_op jit(solution)/shard_map/ppermute | solution.py:1073
  49.4 12.1 %collective-permute-start.18 = (bf16[384,384]{1,0:T(8,128)(2,1)S(1)}, bf16[384,384]{1,0:T(8,128)(2,1)S(1)}, u32[]{:S(2)}, u32[]{:S(2)}) collective-permute-start(bf16[384,384]{1,0:T(8,128)(2,1)S(1)} %get-tuple-element.212.refs_0_), channel_id=1, source_target_pairs={{0,4},{4,0},{1,5},{5,1},{2,6},{6,2},{3,7},{7,3},{8,12},{12,8},{9,1... | collective-permute-start | bytes 884744 | tf_op jit(solution)/shard_map/ppermute | solution.py:1073
  49.4 14.4 %collective-permute-start.17 = (bf16[384,384]{1,0:T(8,128)(2,1)S(1)}, bf16[384,384]{1,0:T(8,128)(2,1)S(1)}, u32[]{:S(2)}, u32[]{:S(2)}) collective-permute-start(bf16[384,384]{1,0:T(8,128)(2,1)S(1)} %get-tuple-element.212.refs_0_), channel_id=1, source_target_pairs={{0,24},{8,16},{16,8},{24,0},{1,25},{9,17},{17,9},{25,1},{2,26},{10... | collective-permute-start | bytes 884744 | tf_op jit(solution)/shard_map/ppermute | solution.py:1073
  50.9 15.1 %collective-permute-start.16 = (bf16[384,384]{1,0:T(8,128)(2,1)S(1)}, bf16[384,384]{1,0:T(8,128)(2,1)S(1)}, u32[]{:S(2)}, u32[]{:S(2)}) collective-permute-start(bf16[384,384]{1,0:T(8,128)(2,1)S(1)} %get-tuple-element.212.refs_0_), channel_id=1, source_target_pairs={{0,16},{8,24},{16,0},{24,8},{1,17},{9,25},{17,1},{25,9},{2,18},{10... | collective-permute-start | bytes 884744 | tf_op jit(solution)/shard_map/ppermute | solution.py:1073
  52.5 13.7 %collective-permute-start.15 = (bf16[384,384]{1,0:T(8,128)(2,1)S(1)}, bf16[384,384]{1,0:T(8,128)(2,1)S(1)}, u32[]{:S(2)}, u32[]{:S(2)}) collective-permute-start(bf16[384,384]{1,0:T(8,128)(2,1)S(1)} %get-tuple-element.212.refs_0_), channel_id=1, source_target_pairs={{0,8},{8,0},{16,24},{24,16},{1,9},{9,1},{17,25},{25,17},{2,10},{10... | collective-permute-start | bytes 884744 | tf_op jit(solution)/shard_map/ppermute | solution.py:1073
  60.8 15.5 %collective-permute-start.14 = (bf16[1,400,384]{2,1,0:T(8,128)(2,1)S(1)}, bf16[1,400,384]{2,1,0:T(8,128)(2,1)S(1)}, u32[]{:S(2)}, u32[]{:S(2)}) collective-permute-start(bf16[1,400,384]{2,1,0:T(8,128)(2,1)S(1)} %bitcast.9), channel_id=1, source_target_pairs={{0,1},{1,0},{2,3},{3,2},{4,5},{5,4},{6,7},{7,6},{8,9},{9,8},{10,11... | collective-permute-start | bytes 921608 | tf_op jit(solution)/shard_map/ppermute | solution.py:1073
  61.5 28.3 %collective-permute-start.25 = (bf16[2,384,384]{2,1,0:T(8,128)(2,1)S(1)}, bf16[2,384,384]{2,1,0:T(8,128)(2,1)S(1)}, u32[]{:S(2)}, u32[]{:S(2)}) collective-permute-start(bf16[2,384,384]{2,1,0:T(8,128)(2,1)S(1)} %merge.2.refs_0_), channel_id=1, source_target_pairs={{0,2},{1,3},{2,0},{3,1},{4,6},{5,7},{6,4},{7,5},{8,10},{9,11},{10,... | collective-permute-start | bytes 1769480 | tf_op jit(solution)/shard_map/ppermute | solution.py:1073
  63.8 12.5 %collective-permute-start.13 = (bf16[384,576]{1,0:T(8,128)(2,1)S(1)}, bf16[384,576]{1,0:T(8,128)(2,1)S(1)}, u32[]{:S(2)}, u32[]{:S(2)}) collective-permute-start(bf16[384,576]{1,0:T(8,128)(2,1)S(1)} %get-tuple-element.201.half_ref), channel_id=1, source_target_pairs={{0,4},{4,0},{1,5},{5,1},{2,6},{6,2},{3,7},{7,3},{8,12},{12,8},{9,1... | collective-permute-start | bytes 1327112 | tf_op jit(solution)/shard_map/ppermute | solution.py:1073
  66.1 12.2 %collective-permute-start.20 = (bf16[384,384]{1,0:T(8,128)(2,1)S(1)}, bf16[384,384]{1,0:T(8,128)(2,1)S(1)}, u32[]{:S(2)}, u32[]{:S(2)}) collective-permute-start(bf16[384,384]{1,0:T(8,128)(2,1)S(1)} %collective-permute-done.16.refs_2_), channel_id=1, source_target_pairs={{0,4},{4,0},{1,5},{5,1},{2,6},{6,2},{3,7},{7,3},{8,12},{12,8},{9,1... | collective-permute-start | bytes 884744 | tf_op jit(solution)/shard_map/ppermute | solution.py:1073
  89.8 13.0 %collective-permute-start.26 = (bf16[2,384,384]{2,1,0:T(8,128)(2,1)S(1)}, bf16[2,384,384]{2,1,0:T(8,128)(2,1)S(1)}, u32[]{:S(2)}, u32[]{:S(2)}) collective-permute-start(bf16[2,384,384]{2,1,0:T(8,128)(2,1)S(1)} %merge.2.refs_0_), channel_id=1, source_target_pairs={{0,4},{4,0},{1,5},{5,1},{2,6},{6,2},{3,7},{7,3},{8,12},{12,8},{9,1... | collective-permute-start | bytes 1769480 | tf_op jit(solution)/shard_map/ppermute | solution.py:1073
  89.8 13.5 %collective-permute-start.27 = (bf16[2,384,384]{2,1,0:T(8,128)(2,1)S(1)}, bf16[2,384,384]{2,1,0:T(8,128)(2,1)S(1)}, u32[]{:S(2)}, u32[]{:S(2)}) collective-permute-start(bf16[2,384,384]{2,1,0:T(8,128)(2,1)S(1)} %collective-permute-done.25.refs_1_), channel_id=1, source_target_pairs={{0,4},{4,0},{1,5},{5,1},{2,6},{6,2},{3,7},{7,3},{8,12},{12,8},{9,1... | collective-permute-start | bytes 1769480 | tf_op jit(solution)/shard_map/ppermute | solution.py:1073
  90.3 29.5 %collective-permute-start.33 = (bf16[2,400,384]{2,1,0:T(8,128)(2,1)S(1)}, bf16[2,400,384]{2,1,0:T(8,128)(2,1)S(1)}, u32[]{:S(2)}, u32[]{:S(2)}) collective-permute-start(bf16[2,400,384]{2,1,0:T(8,128)(2,1)S(1)} %merge.3.refs_0_), channel_id=1, source_target_pairs={{0,2},{1,3},{2,0},{3,1},{4,6},{5,7},{6,4},{7,5},{8,10},{9,11},{10,... | collective-permute-start | bytes 1843208 | tf_op jit(solution)/shard_map/ppermute | solution.py:1073
  90.8 16.4 %collective-permute-start.31 = (bf16[256,768]{1,0:T(8,128)(2,1)S(1)}, bf16[256,768]{1,0:T(8,128)(2,1)S(1)}, u32[]{:S(2)}, u32[]{:S(2)}) collective-permute-start(bf16[256,768]{1,0:T(8,128)(2,1)S(1)} %get-tuple-element.228.refs_0_), channel_id=1, source_target_pairs={{0,8},{8,0},{16,24},{24,16},{1,9},{9,1},{17,25},{25,17},{2,10},{10... | collective-permute-start | bytes 1179656 | tf_op jit(solution)/shard_map/ppermute | solution.py:1073
  120.3 12.0 %collective-permute-start.39 = (bf16[256,768]{1,0:T(8,128)(2,1)S(1)}, bf16[256,768]{1,0:T(8,128)(2,1)S(1)}, u32[]{:S(2)}, u32[]{:S(2)}) collective-permute-start(bf16[256,768]{1,0:T(8,128)(2,1)S(1)} %get-tuple-element.246.refs_0_.refs_9_), channel_id=1, source_target_pairs={{0,16},{8,24},{16,0},{24,8},{1,17},{9,25},{17,1},{25,9},{2,18},{10... | collective-permute-start | bytes 1179656 | tf_op jit(solution)/shard_map/ppermute | solution.py:1073
  120.8 12.0 %collective-permute-start.38 = (bf16[256,768]{1,0:T(8,128)(2,1)S(1)}, bf16[256,768]{1,0:T(8,128)(2,1)S(1)}, u32[]{:S(2)}, u32[]{:S(2)}) collective-permute-start(bf16[256,768]{1,0:T(8,128)(2,1)S(1)} %get-tuple-element.246.refs_0_.refs_9_), channel_id=1, source_target_pairs={{0,8},{8,0},{16,24},{24,16},{1,9},{9,1},{17,25},{25,17},{2,10},{10... | collective-permute-start | bytes 1179656 | tf_op jit(solution)/shard_map/ppermute | solution.py:1073
  122.3 32.1 %collective-permute-start.43 = (bf16[256,768]{1,0:T(8,128)(2,1)S(1)}, bf16[256,768]{1,0:T(8,128)(2,1)S(1)}, u32[]{:S(2)}, u32[]{:S(2)}) collective-permute-start(bf16[256,768]{1,0:T(8,128)(2,1)S(1)} %feed.10), channel_id=1, source_target_pairs={{0,16},{8,24},{16,0},{24,8},{1,17},{9,25},{17,1},{25,9},{2,18},{10... | collective-permute-start | bytes 1179656 | tf_op jit(solution)/shard_map/ppermute | solution.py:1073
  123.9 13.2 %collective-permute-start.36 = (bf16[128,768]{1,0:T(8,128)(2,1)S(1)}, bf16[128,768]{1,0:T(8,128)(2,1)S(1)}, u32[]{:S(2)}, u32[]{:S(2)}) collective-permute-start(bf16[128,768]{1,0:T(8,128)(2,1)S(1)} %slice.35), channel_id=1, source_target_pairs={{0,8},{8,0},{16,24},{24,16},{1,9},{9,1},{17,25},{25,17},{2,10},{10... | collective-permute-start | bytes 589832 | tf_op jit(solution)/shard_map/ppermute | solution.py:1073
  124.5 20.4 %collective-permute-start.37 = (bf16[128,768]{1,0:T(8,128)(2,1)S(1)}, bf16[128,768]{1,0:T(8,128)(2,1)S(1)}, u32[]{:S(2)}, u32[]{:S(2)}) collective-permute-start(bf16[128,768]{1,0:T(8,128)(2,1)S(1)} %slice.36), channel_id=1, source_target_pairs={{0,16},{8,24},{16,0},{24,8},{1,17},{9,25},{17,1},{25,9},{2,18},{10... | collective-permute-start | bytes 589832 | tf_op jit(solution)/shard_map/ppermute | solution.py:1073
  132.9 18.0 %collective-permute-start.40 = (bf16[128,768]{1,0:T(8,128)(2,1)S(1)}, bf16[128,768]{1,0:T(8,128)(2,1)S(1)}, u32[]{:S(2)}, u32[]{:S(2)}) collective-permute-start(bf16[128,768]{1,0:T(8,128)(2,1)S(1)} %slice.37), channel_id=1, source_target_pairs={{0,8},{8,0},{16,24},{24,16},{1,9},{9,1},{17,25},{25,17},{2,10},{10... | collective-permute-start | bytes 589832 | tf_op jit(solution)/shard_map/ppermute | solution.py:1073
  134.4 17.0 %collective-permute-start.41 = (bf16[128,768]{1,0:T(8,128)(2,1)S(1)}, bf16[128,768]{1,0:T(8,128)(2,1)S(1)}, u32[]{:S(2)}, u32[]{:S(2)}) collective-permute-start(bf16[128,768]{1,0:T(8,128)(2,1)S(1)} %slice.38), channel_id=1, source_target_pairs={{0,16},{8,24},{16,0},{24,8},{1,17},{9,25},{17,1},{25,9},{2,18},{10... | collective-permute-start | bytes 589832 | tf_op jit(solution)/shard_map/ppermute | solution.py:1073
  137.1 18.9 %collective-permute-start.42 = (bf16[256,768]{1,0:T(8,128)(2,1)S(1)}, bf16[256,768]{1,0:T(8,128)(2,1)S(1)}, u32[]{:S(2)}, u32[]{:S(2)}) collective-permute-start(bf16[256,768]{1,0:T(8,128)(2,1)S(1)} %feed.9), channel_id=1, source_target_pairs={{0,8},{8,0},{16,24},{24,16},{1,9},{9,1},{17,25},{25,17},{2,10},{10... | collective-permute-start | bytes 1179656 | tf_op jit(solution)/shard_map/ppermute | solution.py:1073
  146.4 13.1 %collective-permute-start.44 = (bf16[256,768]{1,0:T(8,128)(2,1)S(1)}, bf16[256,768]{1,0:T(8,128)(2,1)S(1)}, u32[]{:S(2)}, u32[]{:S(2)}) collective-permute-start(bf16[256,768]{1,0:T(8,128)(2,1)S(1)} %feed.12), channel_id=1, source_target_pairs={{0,24},{8,16},{16,8},{24,0},{1,25},{9,17},{17,9},{25,1},{2,26},{10... | collective-permute-start | bytes 1179656 | tf_op jit(solution)/shard_map/ppermute | solution.py:1073
  150.8 16.1 %collective-permute-start.45 = (bf16[256,768]{1,0:T(8,128)(2,1)S(1)}, bf16[256,768]{1,0:T(8,128)(2,1)S(1)}, u32[]{:S(2)}, u32[]{:S(2)}) collective-permute-start(bf16[256,768]{1,0:T(8,128)(2,1)S(1)} %get-tuple-element.253), channel_id=1, source_target_pairs={{0,8},{8,0},{16,24},{24,16},{1,9},{9,1},{17,25},{25,17},{2,10},{10... | collective-permute-start | bytes 1179656 | tf_op jit(solution)/shard_map/ppermute | solution.py:1073
  151.5 16.4 %collective-permute-start.46 = (bf16[256,768]{1,0:T(8,128)(2,1)S(1)}, bf16[256,768]{1,0:T(8,128)(2,1)S(1)}, u32[]{:S(2)}, u32[]{:S(2)}) collective-permute-start(bf16[256,768]{1,0:T(8,128)(2,1)S(1)} %get-tuple-element.256), channel_id=1, source_target_pairs={{0,16},{8,24},{16,0},{24,8},{1,17},{9,25},{17,1},{25,9},{2,18},{10... | collective-permute-start | bytes 1179656 | tf_op jit(solution)/shard_map/ppermute | solution.py:1073
  154.4 20.3 %collective-permute-start.47 = (bf16[256,768]{1,0:T(8,128)(2,1)S(1)}, bf16[256,768]{1,0:T(8,128)(2,1)S(1)}, u32[]{:S(2)}, u32[]{:S(2)}) collective-permute-start(bf16[256,768]{1,0:T(8,128)(2,1)S(1)} %get-tuple-element.258), channel_id=1, source_target_pairs={{0,24},{8,16},{16,8},{24,0},{1,25},{9,17},{17,9},{25,1},{2,26},{10... | collective-permute-start | bytes 1179656 | tf_op jit(solution)/shard_map/ppermute | solution.py:1073
  192.7 17.8 %collective-permute-start.54 = (bf16[256,768]{1,0:T(8,128)(2,1)S(1)}, bf16[256,768]{1,0:T(8,128)(2,1)S(1)}, u32[]{:S(2)}, u32[]{:S(2)}) collective-permute-start(bf16[256,768]{1,0:T(8,128)(2,1)S(1)} %get-tuple-element.273), channel_id=1, source_target_pairs={{0,16},{8,24},{16,0},{24,8},{1,17},{9,25},{17,1},{25,9},{2,18},{10... | collective-permute-start | bytes 1179656 | tf_op jit(solution)/shard_map/ppermute | solution.py:1073
  193.3 17.2 %collective-permute-start.53 = (bf16[256,768]{1,0:T(8,128)(2,1)S(1)}, bf16[256,768]{1,0:T(8,128)(2,1)S(1)}, u32[]{:S(2)}, u32[]{:S(2)}) collective-permute-start(bf16[256,768]{1,0:T(8,128)(2,1)S(1)} %get-tuple-element.269), channel_id=1, source_target_pairs={{0,8},{8,0},{16,24},{24,16},{1,9},{9,1},{17,25},{25,17},{2,10},{10... | collective-permute-start | bytes 1179656 | tf_op jit(solution)/shard_map/ppermute | solution.py:1073
  196.7 13.7 %collective-permute-start.55 = (bf16[256,768]{1,0:T(8,128)(2,1)S(1)}, bf16[256,768]{1,0:T(8,128)(2,1)S(1)}, u32[]{:S(2)}, u32[]{:S(2)}) collective-permute-start(bf16[256,768]{1,0:T(8,128)(2,1)S(1)} %get-tuple-element.276), channel_id=1, source_target_pairs={{0,24},{8,16},{16,8},{24,0},{1,25},{9,17},{17,9},{25,1},{2,26},{10... | collective-permute-start | bytes 1179656 | tf_op jit(solution)/shard_map/ppermute | solution.py:1073
  222.0 14.6 %collective-permute-start.60 = (bf16[384,384]{1,0:T(8,128)(2,1)S(1)}, bf16[384,384]{1,0:T(8,128)(2,1)S(1)}, u32[]{:S(2)}, u32[]{:S(2)}) collective-permute-start(bf16[384,384]{1,0:T(8,128)(2,1)S(1)} %get-tuple-element.309), channel_id=1, source_target_pairs={{0,2},{1,3},{2,0},{3,1},{4,6},{5,7},{6,4},{7,5},{8,10},{9,11},{10,... | collective-permute-start | bytes 884744 | tf_op jit(solution)/shard_map/ppermute | solution.py:1073
  222.0 14.6 %collective-permute-start.61 = (bf16[384,384]{1,0:T(8,128)(2,1)S(1)}, bf16[384,384]{1,0:T(8,128)(2,1)S(1)}, u32[]{:S(2)}, u32[]{:S(2)}) collective-permute-start(bf16[384,384]{1,0:T(8,128)(2,1)S(1)} %get-tuple-element.317), channel_id=1, source_target_pairs={{0,8},{8,0},{16,24},{24,16},{1,9},{9,1},{17,25},{25,17},{2,10},{10... | collective-permute-start | bytes 884744 | tf_op jit(solution)/shard_map/ppermute | solution.py:1073
  223.1 13.5 %collective-permute-start.62 = (bf16[384,384]{1,0:T(8,128)(2,1)S(1)}, bf16[384,384]{1,0:T(8,128)(2,1)S(1)}, u32[]{:S(2)}, u32[]{:S(2)}) collective-permute-start(bf16[384,384]{1,0:T(8,128)(2,1)S(1)} %get-tuple-element.318), channel_id=1, source_target_pairs={{0,16},{8,24},{16,0},{24,8},{1,17},{9,25},{17,1},{25,9},{2,18},{10... | collective-permute-start | bytes 884744 | tf_op jit(solution)/shard_map/ppermute | solution.py:1073
  224.2 12.9 %collective-permute-start.63 = (bf16[384,384]{1,0:T(8,128)(2,1)S(1)}, bf16[384,384]{1,0:T(8,128)(2,1)S(1)}, u32[]{:S(2)}, u32[]{:S(2)}) collective-permute-start(bf16[384,384]{1,0:T(8,128)(2,1)S(1)} %get-tuple-element.319), channel_id=1, source_target_pairs={{0,24},{8,16},{16,8},{24,0},{1,25},{9,17},{17,9},{25,1},{2,26},{10... | collective-permute-start | bytes 884744 | tf_op jit(solution)/shard_map/ppermute | solution.py:1073
  245.2 11.8 %collective-permute-start.66 = (bf16[112,768]{1,0:T(8,128)(2,1)S(1)}, bf16[112,768]{1,0:T(8,128)(2,1)S(1)}, u32[]{:S(2)}, u32[]{:S(2)}) collective-permute-start(bf16[112,768]{1,0:T(8,128)(2,1)S(1)} %get-tuple-element.338), channel_id=1, source_target_pairs={{0,2},{1,3},{2,0},{3,1},{4,6},{5,7},{6,4},{7,5},{8,10},{9,11},{10,... | collective-permute-start | bytes 516104 | tf_op jit(solution)/shard_map/ppermute | solution.py:1073
  246.2 22.1 %collective-permute-start.71 = (bf16[384,384]{1,0:T(8,128)(2,1)S(1)}, bf16[384,384]{1,0:T(8,128)(2,1)S(1)}, u32[]{:S(2)}, u32[]{:S(2)}) collective-permute-start(bf16[384,384]{1,0:T(8,128)(2,1)S(1)} %get-tuple-element.351), channel_id=1, source_target_pairs={{0,1},{1,0},{2,3},{3,2},{4,5},{5,4},{6,7},{7,6},{8,9},{9,8},{10,11... | collective-permute-start | bytes 884744 | tf_op jit(solution)/shard_map/ppermute | solution.py:1073
  248.1 18.0 %collective-permute-start.67 = (bf16[112,768]{1,0:T(8,128)(2,1)S(1)}, bf16[112,768]{1,0:T(8,128)(2,1)S(1)}, u32[]{:S(2)}, u32[]{:S(2)}) collective-permute-start(bf16[112,768]{1,0:T(8,128)(2,1)S(1)} %get-tuple-element.339), channel_id=1, source_target_pairs={{0,3},{1,2},{2,1},{3,0},{4,7},{5,6},{6,5},{7,4},{8,11},{9,10},{10,... | collective-permute-start | bytes 516104 | tf_op jit(solution)/shard_map/ppermute | solution.py:1073
  249.6 25.4 %collective-permute-start.68 = (bf16[256,768]{1,0:T(8,128)(2,1)S(1)}, bf16[256,768]{1,0:T(8,128)(2,1)S(1)}, u32[]{:S(2)}, u32[]{:S(2)}) collective-permute-start(bf16[256,768]{1,0:T(8,128)(2,1)S(1)} %get-tuple-element.345), channel_id=1, source_target_pairs={{0,8},{8,0},{16,24},{24,16},{1,9},{9,1},{17,25},{25,17},{2,10},{10... | collective-permute-start | bytes 1179656 | tf_op jit(solution)/shard_map/ppermute | solution.py:1073
  253.8 22.5 %collective-permute-start.69 = (bf16[256,768]{1,0:T(8,128)(2,1)S(1)}, bf16[256,768]{1,0:T(8,128)(2,1)S(1)}, u32[]{:S(2)}, u32[]{:S(2)}) collective-permute-start(bf16[256,768]{1,0:T(8,128)(2,1)S(1)} %get-tuple-element.346), channel_id=1, source_target_pairs={{0,16},{8,24},{16,0},{24,8},{1,17},{9,25},{17,1},{25,9},{2,18},{10... | collective-permute-start | bytes 1179656 | tf_op jit(solution)/shard_map/ppermute | solution.py:1073
  257.0 20.7 %collective-permute-start.70 = (bf16[256,768]{1,0:T(8,128)(2,1)S(1)}, bf16[256,768]{1,0:T(8,128)(2,1)S(1)}, u32[]{:S(2)}, u32[]{:S(2)}) collective-permute-start(bf16[256,768]{1,0:T(8,128)(2,1)S(1)} %get-tuple-element.347), channel_id=1, source_target_pairs={{0,24},{8,16},{16,8},{24,0},{1,25},{9,17},{17,9},{25,1},{2,26},{10... | collective-permute-start | bytes 1179656 | tf_op jit(solution)/shard_map/ppermute | solution.py:1073
  278.6 18.0 %collective-permute-start.73 = (f32[128,768]{1,0:T(8,128)S(1)}, f32[128,768]{1,0:T(8,128)S(1)}, u32[]{:S(2)}, u32[]{:S(2)}) collective-permute-start(f32[128,768]{1,0:T(8,128)S(1)} %get-tuple-element.355), channel_id=1, source_target_pairs={{0,4},{4,0},{1,5},{5,1},{2,6},{6,2},{3,7},{7,3},{8,12},{12,8},{9,1... | collective-permute-start | bytes 1179656 | tf_op jit(solution)/shard_map/ppermute | solution.py:1073
  281.8 14.3 %collective-permute-start.82 = (bf16[384,384]{1,0:T(8,128)(2,1)S(1)}, bf16[384,384]{1,0:T(8,128)(2,1)S(1)}, u32[]{:S(2)}, u32[]{:S(2)}) collective-permute-start(bf16[384,384]{1,0:T(8,128)(2,1)S(1)} %late_sum.1.refs_0_), channel_id=1, source_target_pairs={{0,16},{8,24},{16,0},{24,8},{1,17},{9,25},{17,1},{25,9},{2,18},{10... | collective-permute-start | bytes 884744 | tf_op jit(solution)/shard_map/ppermute | solution.py:1073
  283.1 13.0 %collective-permute-start.81 = (bf16[384,384]{1,0:T(8,128)(2,1)S(1)}, bf16[384,384]{1,0:T(8,128)(2,1)S(1)}, u32[]{:S(2)}, u32[]{:S(2)}) collective-permute-start(bf16[384,384]{1,0:T(8,128)(2,1)S(1)} %late_sum.1.refs_0_), channel_id=1, source_target_pairs={{0,8},{8,0},{16,24},{24,16},{1,9},{9,1},{17,25},{25,17},{2,10},{10... | collective-permute-start | bytes 884744 | tf_op jit(solution)/shard_map/ppermute | solution.py:1073
  285.5 12.6 %collective-permute-start.78 = (bf16[112,768]{1,0:T(8,128)(2,1)S(1)}, bf16[112,768]{1,0:T(8,128)(2,1)S(1)}, u32[]{:S(2)}, u32[]{:S(2)}) collective-permute-start(bf16[112,768]{1,0:T(8,128)(2,1)S(1)} %collective-permute-done.74.refs_1_), channel_id=1, source_target_pairs={{0,4},{4,0},{1,5},{5,1},{2,6},{6,2},{3,7},{7,3},{8,12},{12,8},{9,1... | collective-permute-start | bytes 516104 | tf_op jit(solution)/shard_map/ppermute | solution.py:1073
  (53 other events, 397.1 us)

commit v6 on v5

--- a/solution.py
+++ b/solution.py
@@ -1223,6 +1223,7 @@
         )
 
     t_query, t_key, t_value, _ = project(t_qkv_half, teacher_vec)
+    (s_late,) = line.behind(s_late)
     s_qkv_half, out_half = line(
         functools.partial(early_kernel, n_shard, 1),
         "early_weights",
@@ -1232,7 +1233,6 @@
     )
     t_late = spread_z(t_late)
     t_heads, _ = attend(t_query, t_key, t_value)
-    (s_late,) = line.behind(s_late)
     out_all = gather(out_half, "chip")
     query, key, value, w_qkv = project(s_qkv_half, student_vec)
     s_late = spread_z(s_late)
@@ -1435,6 +1435,7 @@
         (),
         (mine, table, swap(send)),
     )
+    late_exchange(*range(3, n_shard))
     parts = line.behind(*parts)
     early = line(
         early_sum_kernel,
@@ -1448,7 +1449,6 @@
         early = line(
             early_sum_kernel, "rest_sum", shape(early.shape), (), gather(early, "rest"), bare=True
         )
-    late_exchange(*range(3, n_shard))
     here, there = line(
         hidden_kernel,
         "hidden",

time: 313 us -> 310 us (level)
  starting transfers between devices: 83.9 us -> 80.7 us
    ppermute x88, starting transfers between devices: 83.9 us -> 80.7 us  [flip(): return lax.ppermute(piece, axis, [(a, a ^ mask) for a in range(size)])]
  transfers between devices with their start and end apart: 88 -> 88, of which waited for: 40 -> 41; matrix products, arithmetic and copies ran while one was open for 0% -> 0% of each run, Pallas kernels for 26% -> 26%
where the time goes in v6:
time: 310 us; the launch traced here: 305 us
  waiting for transfers between devices  125 us (40%)
  Pallas kernels  91.8 us (30%)
  starting transfers between devices  80.7 us (26%)
  local copies, waits for them, and re-layouts  5.3 us (2%)
    ppermute x88, waiting for transfers between devices, flip(): return lax.ppermute(piece, axis, [(a, a ^ mask) for a in range(size)])  125 us
    pallas_call x44, Pallas kernels, call(): pl.pallas_call(kernel, out_shape=outs, in_specs=[SMEM_SPEC] * len(scalars...  85.5 us
    ppermute x88, starting transfers between devices, flip(): return lax.ppermute(piece, axis, [(a, a ^ mask) for a in range(size)])  80.7 us
  transfers between devices with their start and end apart: 88, of which 41 were waited for; matrix products, arithmetic and copies ran while one was open for 0% of the time, Pallas kernels for 26%

profile of v6, /device:TPU:0, one launch (start us, length us, event | category | flops | bytes accessed | tf_op | source)
XLA Modules:
  0.0 304.6 jit_solution(4166626079725697259)
XLA Ops:
  0.6 3.0 collective-permute-start.3
  7.7 3.7 %collective-permute-start.2 = (bf16[96,768]{1,0:T(8,128)(2,1)S(1)}, bf16[96,768]{1,0:T(8,128)(2,1)S(1)}, u32[]{:S(2)}, u32[]{:S(2)}) collective-permute-start(bf16[96,768]{1,0:T(8,128)(2,1)S(1)} %early_pieces.2.refs_0_), channel_id=1, source_target_pairs={{0,3},{1,2},{2,1},{3,0},{4,7},{5,6},{6,5},{7,4},{8,11},{9,10},{10,... | collective-permute-start | bytes 442376 | tf_op jit(solution)/shard_map/ppermute | solution.py:1073
  16.3 6.9 %collective-permute-done.1.refs_2_ = bf16[96,768]{1,0:T(8,128)(2,1)S(1)} collective-permute-done((bf16[96,768]{1,0:T(8,128)(2,1)S(1)}, bf16[96,768]{1,0:T(8,128)(2,1)S(1)}, u32[]{:S(2)}, u32[]{:S(2)}) %collective-permute-start.1) | collective-permute-done | bytes 147488 | tf_op jit(solution)/shard_map/ppermute | solution.py:1073
  26.9 2.1 late_pieces.3
  31.6 2.5 collective-permute-start.11
  34.1 1.9 collective-permute-start.9
  36.1 3.0 qkv.2
  40.8 7.5 %collective-permute-done.10.refs_2_ = bf16[112,768]{1,0:T(8,128)(2,1)S(1)} collective-permute-done((bf16[112,768]{1,0:T(8,128)(2,1)S(1)}, bf16[112,768]{1,0:T(8,128)(2,1)S(1)}, u32[]{:S(2)}, u32[]{:S(2)}) %collective-permute-start.10) | collective-permute-done | bytes 172064 | tf_op jit(solution)/shard_map/ppermute | solution.py:1073
  54.9 2.4 collective-permute-start.25
  57.3 3.0 collective-permute-done.17.refs_3_
  60.3 5.8 %collective-permute-done.16.refs_2_ = bf16[384,384]{1,0:T(8,128)(2,1)S(1)} collective-permute-done((bf16[384,384]{1,0:T(8,128)(2,1)S(1)}, bf16[384,384]{1,0:T(8,128)(2,1)S(1)}, u32[]{:S(2)}, u32[]{:S(2)}) %collective-permute-start.16) | collective-permute-done | bytes 294944 | tf_op jit(solution)/shard_map/ppermute | solution.py:1073
  66.6 1.8 collective-permute-done.14.got_ref
  68.4 6.6 %attend.2 = (bf16[256,192]{1,0:T(8,128)(2,1)S(1)}, bf16[256,192]{1,0:T(8,128)(2,1)S(1)}, bf16[256,192]{1,0:T(8,128)(2,1)S(1)}, bf16[256,192]{1,0:T(8,128)(2,1)S(1)}, f32[3,1,1024]{2,1,0:T(1,128)}) custom-call(s32[4]{0:T(128)S(1)} %pad_add_fusion.ids_ref, s32[16]{0:T(128)S(1)} %copy-done.11, bf16[3,1024,64]{2,1,0:T(8,128)(2,1)S(1)} %get-tuple-element.198.q_ref, ...), custom_call_target="tpu_custom_call" | custom-call | tf_op jit(solution)/shard_map/attend/pallas_call | solution.py:80
  78.6 2.1 qkv.3
  82.3 2.7 collective-permute-done.23.refs_2_
  88.9 6.4 %attend.3 = (bf16[256,192]{1,0:T(8,128)(2,1)S(1)}, bf16[256,192]{1,0:T(8,128)(2,1)S(1)}, bf16[256,192]{1,0:T(8,128)(2,1)S(1)}, bf16[256,192]{1,0:T(8,128)(2,1)S(1)}, f32[3,1,1024]{2,1,0:T(1,128)S(1)}) custom-call(s32[4]{0:T(128)S(1)} %pad_add_fusion.ids_ref, s32[16]{0:T(128)S(1)} %copy-done.11, bf16[3,1024,64]{2,1,0:T(8,128)(2,1)S(1)} %get-tuple-element.208.q_ref.refs_0_, ...), custom_call_target="tpu_custom_call" | custom-call | tf_op jit(solution)/shard_map/attend/pallas_call | solution.py:80
  95.3 2.9 collective-permute-done.32.refs_0_
  100.0 1.8 collective-permute-start.30
  104.3 2.1 collective-permute-done.29.refs_2_
  110.9 5.1 %collective-permute-done.33.refs_1_ = bf16[2,400,384]{2,1,0:T(8,128)(2,1)S(1)} collective-permute-done((bf16[2,400,384]{2,1,0:T(8,128)(2,1)S(1)}, bf16[2,400,384]{2,1,0:T(8,128)(2,1)S(1)}, u32[]{:S(2)}, u32[]{:S(2)}) %collective-permute-start.33) | collective-permute-done | bytes 614432 | tf_op jit(solution)/shard_map/ppermute | solution.py:1073
  124.0 4.5 %collective-permute-done.39.refs_0_.refs_11_ = bf16[256,768]{1,0:T(8,128)(2,1)S(1)} collective-permute-done((bf16[256,768]{1,0:T(8,128)(2,1)S(1)}, bf16[256,768]{1,0:T(8,128)(2,1)S(1)}, u32[]{:S(2)}, u32[]{:S(2)}) %collective-permute-start.39) | collective-permute-done | bytes 393248 | tf_op jit(solution)/shard_map/ppermute | solution.py:1073
  131.3 2.0 collective-permute-done.36.refs_0_
  134.5 6.7 %collective-permute-done.37.refs_1_ = bf16[128,768]{1,0:T(8,128)(2,1)S(1)} collective-permute-done((bf16[128,768]{1,0:T(8,128)(2,1)S(1)}, bf16[128,768]{1,0:T(8,128)(2,1)S(1)}, u32[]{:S(2)}, u32[]{:S(2)}) %collective-permute-start.37) | collective-permute-done | bytes 196640 | tf_op jit(solution)/shard_map/ppermute | solution.py:1073
  151.9 3.8 %collective-permute-done.44.refs_3_ = bf16[256,768]{1,0:T(8,128)(2,1)S(1)} collective-permute-done((bf16[256,768]{1,0:T(8,128)(2,1)S(1)}, bf16[256,768]{1,0:T(8,128)(2,1)S(1)}, u32[]{:S(2)}, u32[]{:S(2)}) %collective-permute-start.44) | collective-permute-done | bytes 393248 | tf_op jit(solution)/shard_map/ppermute | solution.py:1073
  156.7 6.5 %collective-permute-done.45.refs_1_ = bf16[256,768]{1,0:T(8,128)(2,1)S(1)} collective-permute-done((bf16[256,768]{1,0:T(8,128)(2,1)S(1)}, bf16[256,768]{1,0:T(8,128)(2,1)S(1)}, u32[]{:S(2)}, u32[]{:S(2)}) %collective-permute-start.45) | collective-permute-done | bytes 393248 | tf_op jit(solution)/shard_map/ppermute | solution.py:1073
  164.0 6.9 %collective-permute-done.47.refs_3_ = bf16[256,768]{1,0:T(8,128)(2,1)S(1)} collective-permute-done((bf16[256,768]{1,0:T(8,128)(2,1)S(1)}, bf16[256,768]{1,0:T(8,128)(2,1)S(1)}, u32[]{:S(2)}, u32[]{:S(2)}) %collective-permute-start.47) | collective-permute-done | bytes 393248 | tf_op jit(solution)/shard_map/ppermute | solution.py:1073
  170.9 1.8 loss.1
  176.1 6.3 %collective-permute-done.49.refs_0_.refs_6_ = bf16[256,768]{1,0:T(8,128)(2,1)S(1)} collective-permute-done((bf16[256,768]{1,0:T(8,128)(2,1)S(1)}, bf16[256,768]{1,0:T(8,128)(2,1)S(1)}, u32[]{:S(2)}, u32[]{:S(2)}) %collective-permute-start.49) | collective-permute-done | bytes 393248 | tf_op jit(solution)/shard_map/ppermute | solution.py:1073
  193.2 1.7 collective-permute-start.55
  197.8 3.5 %late_grad.1 = (f32[4,384,384]{2,1,0:T(8,128)S(1)}, bf16[4,384,384]{2,1,0:T(8,128)(2,1)S(1)}) custom-call(s32[4]{0:T(128)S(1)} %pad_add_fusion.ids_ref, bf16[256,768]{1,0:T(8,128)(2,1)S(1)} %get-tuple-element.279.refs_0_, bf16[256,768]{1,0:T(8,128)(2,1)S(1)} %get-tuple-element.280.refs_1_, bf16[256,768]{1,0:T(8,128)(2,1)S(1)} %get-tuple-element.281.refs_2_, ...), custom_call_target="tpu_custom_call" | custom-call | tf_op jit(solution)/shard_map/late_grad/pallas_call | solution.py:80
  201.3 5.0 %collective-permute-done.54.refs_2_ = bf16[256,768]{1,0:T(8,128)(2,1)S(1)} collective-permute-done((bf16[256,768]{1,0:T(8,128)(2,1)S(1)}, bf16[256,768]{1,0:T(8,128)(2,1)S(1)}, u32[]{:S(2)}, u32[]{:S(2)}) %collective-permute-start.54) | collective-permute-done | bytes 393248 | tf_op jit(solution)/shard_map/ppermute | solution.py:1073
  206.3 2.0 branch_back.1
  214.8 3.0 collective-permute-done.58.refs_5_
  221.3 10.1 %attend_back.1 = (bf16[1024,192]{1,0:T(8,128)(2,1)S(1)}, bf16[1024,192]{1,0:T(8,128)(2,1)S(1)}, bf16[1024,192]{1,0:T(8,128)(2,1)S(1)}, f32[8,192]{1,0:T(8,128)S(1)}) custom-call(s32[4]{0:T(128)S(1)} %pad_add_fusion.ids_ref, s32[16]{0:T(128)S(1)} %copy-done.11, bf16[3,1024,64]{2,1,0:T(8,128)(2,1)S(1)} %get-tuple-element.208.q_ref.refs_0_, ...), custom_call_target="tpu_custom_call" | custom-call | tf_op jit(solution)/shard_map/attend_back/pallas_call | solution.py:80
  233.3 3.4 %early_grad.1 = (f32[384,768]{1,0:T(8,128)S(1)}, f32[8,768]{1,0:T(8,128)S(1)}, bf16[400,768]{1,0:T(8,128)(2,1)S(1)}) custom-call(s32[4]{0:T(128)S(1)} %pad_add_fusion.ids_ref, bf16[512,768]{1,0:T(8,128)(2,1)S(1)} %get-tuple-element.195.own_ref.refs_5_.refs_0_, bf16[512,768]{1,0:T(8,128)(2,1)S(1)} %collective-permute-done.7.oth_ref.refs_6_.refs_1_, ...), custom_call_target="tpu_custom_call" | custom-call | tf_op jit(solution)/shard_map/early_grad/pallas_call | solution.py:80
  236.8 2.0 qkv_back.1
  239.6 2.5 collective-permute-start.65
  242.4 1.9 collective-permute-start.71
  244.3 2.2 collective-permute-start.67
  247.4 2.6 collective-permute-done.65.refs_1_
  251.0 3.0 collective-permute-done.66.refs_2_
  255.4 6.9 %collective-permute-done.67.refs_3_ = bf16[112,768]{1,0:T(8,128)(2,1)S(1)} collective-permute-done((bf16[112,768]{1,0:T(8,128)(2,1)S(1)}, bf16[112,768]{1,0:T(8,128)(2,1)S(1)}, u32[]{:S(2)}, u32[]{:S(2)}) %collective-permute-start.67) | collective-permute-done | bytes 172064 | tf_op jit(solution)/shard_map/ppermute | solution.py:1073
  262.4 2.2 collective-permute-start.72
  266.7 5.2 %collective-permute-done.76.refs_3_ = bf16[112,768]{1,0:T(8,128)(2,1)S(1)} collective-permute-done((bf16[112,768]{1,0:T(8,128)(2,1)S(1)}, bf16[112,768]{1,0:T(8,128)(2,1)S(1)}, u32[]{:S(2)}, u32[]{:S(2)}) %collective-permute-start.76) | collective-permute-done | bytes 172064 | tf_op jit(solution)/shard_map/ppermute | solution.py:1073
  282.3 4.6 %collective-permute-done.83.refs_3_ = bf16[384,384]{1,0:T(8,128)(2,1)S(1)} collective-permute-done((bf16[384,384]{1,0:T(8,128)(2,1)S(1)}, bf16[384,384]{1,0:T(8,128)(2,1)S(1)}, u32[]{:S(2)}, u32[]{:S(2)}) %collective-permute-start.83) | collective-permute-done | bytes 294944 | tf_op jit(solution)/shard_map/ppermute | solution.py:1073
  286.9 5.7 %collective-permute-done.82.refs_2_ = bf16[384,384]{1,0:T(8,128)(2,1)S(1)} collective-permute-done((bf16[384,384]{1,0:T(8,128)(2,1)S(1)}, bf16[384,384]{1,0:T(8,128)(2,1)S(1)}, u32[]{:S(2)}, u32[]{:S(2)}) %collective-permute-start.82) | collective-permute-done | bytes 294944 | tf_op jit(solution)/shard_map/ppermute | solution.py:1073
  294.6 2.5 early_final.1
  300.0 4.4 %late_final.1 = (f32[192,3072]{1,0:T(8,128)}, f32[768,768]{1,0:T(8,128)}) custom-call(s32[4]{0:T(128)S(1)} %pad_add_fusion.ids_ref, bf16[384,384]{1,0:T(8,128)(2,1)S(1)} %late_sum.1.refs_0_, bf16[384,384]{1,0:T(8,128)(2,1)S(1)} %collective-permute-done.81.refs_1_, bf16[384,384]{1,0:T(8,128)(2,1)S(1)} %collective-permute-done.82.refs_2_, ...), custom_call_target="tpu_custom_call" | custom-call | tf_op jit(solution)/shard_map/late_final/pallas_call | solution.py:80
  (214 shorter events, 116.7 us)
Async XLA Ops:
  0.6 23.4 %collective-permute-start.3 = (bf16[2,128,768]{2,1,0:T(8,128)(2,1)}, bf16[2,128,768]{2,1,0:T(8,128)(2,1)S(1)}, u32[]{:S(2)}, u32[]{:S(2)}) collective-permute-start(bf16[2,128,768]{2,1,0:T(8,128)(2,1)} %here_ref.1), channel_id=1, source_target_pairs={{0,8},{8,0},{16,24},{24,16},{1,9},{9,1},{17,25},{25,17},{2,10},{10... | collective-permute-start | bytes 1179656 | tf_op jit(solution)/shard_map/ppermute | solution.py:1073
  3.6 20.4 %collective-permute-start.4 = (bf16[2,128,768]{2,1,0:T(8,128)(2,1)}, bf16[2,128,768]{2,1,0:T(8,128)(2,1)S(1)}, u32[]{:S(2)}, u32[]{:S(2)}) collective-permute-start(bf16[2,128,768]{2,1,0:T(8,128)(2,1)} %here_ref.1), channel_id=1, source_target_pairs={{0,16},{8,24},{16,0},{24,8},{1,17},{9,25},{17,1},{25,9},{2,18},{10... | collective-permute-start | bytes 1179656 | tf_op jit(solution)/shard_map/ppermute | solution.py:1073
  11.4 11.9 %collective-permute-start.1 = (bf16[96,768]{1,0:T(8,128)(2,1)S(1)}, bf16[96,768]{1,0:T(8,128)(2,1)S(1)}, u32[]{:S(2)}, u32[]{:S(2)}) collective-permute-start(bf16[96,768]{1,0:T(8,128)(2,1)S(1)} %early_pieces.2.refs_0_), channel_id=1, source_target_pairs={{0,2},{1,3},{2,0},{3,1},{4,6},{5,7},{6,4},{7,5},{8,10},{9,11},{10,... | collective-permute-start | bytes 442376 | tf_op jit(solution)/shard_map/ppermute | solution.py:1073
  11.4 11.9 %collective-permute-start = (bf16[96,768]{1,0:T(8,128)(2,1)S(1)}, bf16[96,768]{1,0:T(8,128)(2,1)S(1)}, u32[]{:S(2)}, u32[]{:S(2)}) collective-permute-start(bf16[96,768]{1,0:T(8,128)(2,1)S(1)} %early_pieces.2.refs_0_), channel_id=1, source_target_pairs={{0,1},{1,0},{2,3},{3,2},{4,5},{5,4},{6,7},{7,6},{8,9},{9,8},{10,11... | collective-permute-start | bytes 442376 | tf_op jit(solution)/shard_map/ppermute | solution.py:1073
  34.1 14.2 %collective-permute-start.10 = (bf16[112,768]{1,0:T(8,128)(2,1)S(1)}, bf16[112,768]{1,0:T(8,128)(2,1)S(1)}, u32[]{:S(2)}, u32[]{:S(2)}) collective-permute-start(bf16[112,768]{1,0:T(8,128)(2,1)S(1)} %early_pieces.3.refs_0_), channel_id=1, source_target_pairs={{0,2},{1,3},{2,0},{3,1},{4,6},{5,7},{6,4},{7,5},{8,10},{9,11},{10,... | collective-permute-start | bytes 516104 | tf_op jit(solution)/shard_map/ppermute | solution.py:1073
  34.1 14.2 %collective-permute-start.9 = (bf16[112,768]{1,0:T(8,128)(2,1)S(1)}, bf16[112,768]{1,0:T(8,128)(2,1)S(1)}, u32[]{:S(2)}, u32[]{:S(2)}) collective-permute-start(bf16[112,768]{1,0:T(8,128)(2,1)S(1)} %early_pieces.3.refs_0_), channel_id=1, source_target_pairs={{0,1},{1,0},{2,3},{3,2},{4,5},{5,4},{6,7},{7,6},{8,9},{9,8},{10,11... | collective-permute-start | bytes 516104 | tf_op jit(solution)/shard_map/ppermute | solution.py:1073
  36.0 17.6 %collective-permute-start.12 = (bf16[1,384,384]{2,1,0:T(8,128)(2,1)S(1)}, bf16[1,384,384]{2,1,0:T(8,128)(2,1)S(1)}, u32[]{:S(2)}, u32[]{:S(2)}) collective-permute-start(bf16[1,384,384]{2,1,0:T(8,128)(2,1)S(1)} %bitcast.11), channel_id=1, source_target_pairs={{0,1},{1,0},{2,3},{3,2},{4,5},{5,4},{6,7},{7,6},{8,9},{9,8},{10,11... | collective-permute-start | bytes 884744 | tf_op jit(solution)/shard_map/ppermute | solution.py:1073
  50.9 15.1 %collective-permute-start.16 = (bf16[384,384]{1,0:T(8,128)(2,1)S(1)}, bf16[384,384]{1,0:T(8,128)(2,1)S(1)}, u32[]{:S(2)}, u32[]{:S(2)}) collective-permute-start(bf16[384,384]{1,0:T(8,128)(2,1)S(1)} %get-tuple-element.212.refs_0_), channel_id=1, source_target_pairs={{0,16},{8,24},{16,0},{24,8},{1,17},{9,25},{17,1},{25,9},{2,18},{10... | collective-permute-start | bytes 884744 | tf_op jit(solution)/shard_map/ppermute | solution.py:1073
  52.5 13.7 %collective-permute-start.15 = (bf16[384,384]{1,0:T(8,128)(2,1)S(1)}, bf16[384,384]{1,0:T(8,128)(2,1)S(1)}, u32[]{:S(2)}, u32[]{:S(2)}) collective-permute-start(bf16[384,384]{1,0:T(8,128)(2,1)S(1)} %get-tuple-element.212.refs_0_), channel_id=1, source_target_pairs={{0,8},{8,0},{16,24},{24,16},{1,9},{9,1},{17,25},{25,17},{2,10},{10... | collective-permute-start | bytes 884744 | tf_op jit(solution)/shard_map/ppermute | solution.py:1073
  53.6 14.9 %collective-permute-start.14 = (bf16[1,400,384]{2,1,0:T(8,128)(2,1)S(1)}, bf16[1,400,384]{2,1,0:T(8,128)(2,1)S(1)}, u32[]{:S(2)}, u32[]{:S(2)}) collective-permute-start(bf16[1,400,384]{2,1,0:T(8,128)(2,1)S(1)} %bitcast.9), channel_id=1, source_target_pairs={{0,1},{1,0},{2,3},{3,2},{4,5},{5,4},{6,7},{7,6},{8,9},{9,8},{10,11... | collective-permute-start | bytes 921608 | tf_op jit(solution)/shard_map/ppermute | solution.py:1073
  54.9 31.7 %collective-permute-start.25 = (bf16[2,384,384]{2,1,0:T(8,128)(2,1)S(1)}, bf16[2,384,384]{2,1,0:T(8,128)(2,1)S(1)}, u32[]{:S(2)}, u32[]{:S(2)}) collective-permute-start(bf16[2,384,384]{2,1,0:T(8,128)(2,1)S(1)} %merge.2.refs_0_), channel_id=1, source_target_pairs={{0,2},{1,3},{2,0},{3,1},{4,6},{5,7},{6,4},{7,5},{8,10},{9,11},{10,... | collective-permute-start | bytes 1769480 | tf_op jit(solution)/shard_map/ppermute | solution.py:1073
  60.3 14.8 %collective-permute-start.13 = (bf16[384,576]{1,0:T(8,128)(2,1)S(1)}, bf16[384,576]{1,0:T(8,128)(2,1)S(1)}, u32[]{:S(2)}, u32[]{:S(2)}) collective-permute-start(bf16[384,576]{1,0:T(8,128)(2,1)S(1)} %get-tuple-element.201.half_ref), channel_id=1, source_target_pairs={{0,4},{4,0},{1,5},{5,1},{2,6},{6,2},{3,7},{7,3},{8,12},{12,8},{9,1... | collective-permute-start | bytes 1327112 | tf_op jit(solution)/shard_map/ppermute | solution.py:1073
  68.4 12.9 %collective-permute-start.19 = (bf16[384,384]{1,0:T(8,128)(2,1)S(1)}, bf16[384,384]{1,0:T(8,128)(2,1)S(1)}, u32[]{:S(2)}, u32[]{:S(2)}) collective-permute-start(bf16[384,384]{1,0:T(8,128)(2,1)S(1)} %collective-permute-done.15.refs_1_), channel_id=1, source_target_pairs={{0,4},{4,0},{1,5},{5,1},{2,6},{6,2},{3,7},{7,3},{8,12},{12,8},{9,1... | collective-permute-start | bytes 884744 | tf_op jit(solution)/shard_map/ppermute | solution.py:1073
  86.6 12.2 %collective-permute-start.26 = (bf16[2,384,384]{2,1,0:T(8,128)(2,1)S(1)}, bf16[2,384,384]{2,1,0:T(8,128)(2,1)S(1)}, u32[]{:S(2)}, u32[]{:S(2)}) collective-permute-start(bf16[2,384,384]{2,1,0:T(8,128)(2,1)S(1)} %merge.2.refs_0_), channel_id=1, source_target_pairs={{0,4},{4,0},{1,5},{5,1},{2,6},{6,2},{3,7},{7,3},{8,12},{12,8},{9,1... | collective-permute-start | bytes 1769480 | tf_op jit(solution)/shard_map/ppermute | solution.py:1073
  86.6 13.3 %collective-permute-start.27 = (bf16[2,384,384]{2,1,0:T(8,128)(2,1)S(1)}, bf16[2,384,384]{2,1,0:T(8,128)(2,1)S(1)}, u32[]{:S(2)}, u32[]{:S(2)}) collective-permute-start(bf16[2,384,384]{2,1,0:T(8,128)(2,1)S(1)} %collective-permute-done.25.refs_1_), channel_id=1, source_target_pairs={{0,4},{4,0},{1,5},{5,1},{2,6},{6,2},{3,7},{7,3},{8,12},{12,8},{9,1... | collective-permute-start | bytes 1769480 | tf_op jit(solution)/shard_map/ppermute | solution.py:1073
  87.1 28.9 %collective-permute-start.33 = (bf16[2,400,384]{2,1,0:T(8,128)(2,1)S(1)}, bf16[2,400,384]{2,1,0:T(8,128)(2,1)S(1)}, u32[]{:S(2)}, u32[]{:S(2)}) collective-permute-start(bf16[2,400,384]{2,1,0:T(8,128)(2,1)S(1)} %merge.3.refs_0_), channel_id=1, source_target_pairs={{0,2},{1,3},{2,0},{3,1},{4,6},{5,7},{6,4},{7,5},{8,10},{9,11},{10,... | collective-permute-start | bytes 1843208 | tf_op jit(solution)/shard_map/ppermute | solution.py:1073
  87.6 16.5 %collective-permute-start.31 = (bf16[256,768]{1,0:T(8,128)(2,1)S(1)}, bf16[256,768]{1,0:T(8,128)(2,1)S(1)}, u32[]{:S(2)}, u32[]{:S(2)}) collective-permute-start(bf16[256,768]{1,0:T(8,128)(2,1)S(1)} %get-tuple-element.228.refs_0_), channel_id=1, source_target_pairs={{0,8},{8,0},{16,24},{24,16},{1,9},{9,1},{17,25},{25,17},{2,10},{10... | collective-permute-start | bytes 1179656 | tf_op jit(solution)/shard_map/ppermute | solution.py:1073
  116.5 12.0 %collective-permute-start.39 = (bf16[256,768]{1,0:T(8,128)(2,1)S(1)}, bf16[256,768]{1,0:T(8,128)(2,1)S(1)}, u32[]{:S(2)}, u32[]{:S(2)}) collective-permute-start(bf16[256,768]{1,0:T(8,128)(2,1)S(1)} %get-tuple-element.246.refs_0_.refs_9_), channel_id=1, source_target_pairs={{0,16},{8,24},{16,0},{24,8},{1,17},{9,25},{17,1},{25,9},{2,18},{10... | collective-permute-start | bytes 1179656 | tf_op jit(solution)/shard_map/ppermute | solution.py:1073
  117.0 12.0 %collective-permute-start.38 = (bf16[256,768]{1,0:T(8,128)(2,1)S(1)}, bf16[256,768]{1,0:T(8,128)(2,1)S(1)}, u32[]{:S(2)}, u32[]{:S(2)}) collective-permute-start(bf16[256,768]{1,0:T(8,128)(2,1)S(1)} %get-tuple-element.246.refs_0_.refs_9_), channel_id=1, source_target_pairs={{0,8},{8,0},{16,24},{24,16},{1,9},{9,1},{17,25},{25,17},{2,10},{10... | collective-permute-start | bytes 1179656 | tf_op jit(solution)/shard_map/ppermute | solution.py:1073
  118.3 32.4 %collective-permute-start.43 = (bf16[256,768]{1,0:T(8,128)(2,1)S(1)}, bf16[256,768]{1,0:T(8,128)(2,1)S(1)}, u32[]{:S(2)}, u32[]{:S(2)}) collective-permute-start(bf16[256,768]{1,0:T(8,128)(2,1)S(1)} %feed.10), channel_id=1, source_target_pairs={{0,16},{8,24},{16,0},{24,8},{1,17},{9,25},{17,1},{25,9},{2,18},{10... | collective-permute-start | bytes 1179656 | tf_op jit(solution)/shard_map/ppermute | solution.py:1073
  119.1 14.1 %collective-permute-start.36 = (bf16[128,768]{1,0:T(8,128)(2,1)S(1)}, bf16[128,768]{1,0:T(8,128)(2,1)S(1)}, u32[]{:S(2)}, u32[]{:S(2)}) collective-permute-start(bf16[128,768]{1,0:T(8,128)(2,1)S(1)} %slice.35), channel_id=1, source_target_pairs={{0,8},{8,0},{16,24},{24,16},{1,9},{9,1},{17,25},{25,17},{2,10},{10... | collective-permute-start | bytes 589832 | tf_op jit(solution)/shard_map/ppermute | solution.py:1073
  120.7 20.4 %collective-permute-start.37 = (bf16[128,768]{1,0:T(8,128)(2,1)S(1)}, bf16[128,768]{1,0:T(8,128)(2,1)S(1)}, u32[]{:S(2)}, u32[]{:S(2)}) collective-permute-start(bf16[128,768]{1,0:T(8,128)(2,1)S(1)} %slice.36), channel_id=1, source_target_pairs={{0,16},{8,24},{16,0},{24,8},{1,17},{9,25},{17,1},{25,9},{2,18},{10... | collective-permute-start | bytes 589832 | tf_op jit(solution)/shard_map/ppermute | solution.py:1073
  129.1 17.7 %collective-permute-start.40 = (bf16[128,768]{1,0:T(8,128)(2,1)S(1)}, bf16[128,768]{1,0:T(8,128)(2,1)S(1)}, u32[]{:S(2)}, u32[]{:S(2)}) collective-permute-start(bf16[128,768]{1,0:T(8,128)(2,1)S(1)} %slice.37), channel_id=1, source_target_pairs={{0,8},{8,0},{16,24},{24,16},{1,9},{9,1},{17,25},{25,17},{2,10},{10... | collective-permute-start | bytes 589832 | tf_op jit(solution)/shard_map/ppermute | solution.py:1073
  130.4 17.3 %collective-permute-start.41 = (bf16[128,768]{1,0:T(8,128)(2,1)S(1)}, bf16[128,768]{1,0:T(8,128)(2,1)S(1)}, u32[]{:S(2)}, u32[]{:S(2)}) collective-permute-start(bf16[128,768]{1,0:T(8,128)(2,1)S(1)} %slice.38), channel_id=1, source_target_pairs={{0,16},{8,24},{16,0},{24,8},{1,17},{9,25},{17,1},{25,9},{2,18},{10... | collective-permute-start | bytes 589832 | tf_op jit(solution)/shard_map/ppermute | solution.py:1073
  133.3 18.6 %collective-permute-start.42 = (bf16[256,768]{1,0:T(8,128)(2,1)S(1)}, bf16[256,768]{1,0:T(8,128)(2,1)S(1)}, u32[]{:S(2)}, u32[]{:S(2)}) collective-permute-start(bf16[256,768]{1,0:T(8,128)(2,1)S(1)} %feed.9), channel_id=1, source_target_pairs={{0,8},{8,0},{16,24},{24,16},{1,9},{9,1},{17,25},{25,17},{2,10},{10... | collective-permute-start | bytes 1179656 | tf_op jit(solution)/shard_map/ppermute | solution.py:1073
  142.6 13.1 %collective-permute-start.44 = (bf16[256,768]{1,0:T(8,128)(2,1)S(1)}, bf16[256,768]{1,0:T(8,128)(2,1)S(1)}, u32[]{:S(2)}, u32[]{:S(2)}) collective-permute-start(bf16[256,768]{1,0:T(8,128)(2,1)S(1)} %feed.12), channel_id=1, source_target_pairs={{0,24},{8,16},{16,8},{24,0},{1,25},{9,17},{17,9},{25,1},{2,26},{10... | collective-permute-start | bytes 1179656 | tf_op jit(solution)/shard_map/ppermute | solution.py:1073
  146.8 16.4 %collective-permute-start.45 = (bf16[256,768]{1,0:T(8,128)(2,1)S(1)}, bf16[256,768]{1,0:T(8,128)(2,1)S(1)}, u32[]{:S(2)}, u32[]{:S(2)}) collective-permute-start(bf16[256,768]{1,0:T(8,128)(2,1)S(1)} %get-tuple-element.253), channel_id=1, source_target_pairs={{0,8},{8,0},{16,24},{24,16},{1,9},{9,1},{17,25},{25,17},{2,10},{10... | collective-permute-start | bytes 1179656 | tf_op jit(solution)/shard_map/ppermute | solution.py:1073
  147.7 16.4 %collective-permute-start.46 = (bf16[256,768]{1,0:T(8,128)(2,1)S(1)}, bf16[256,768]{1,0:T(8,128)(2,1)S(1)}, u32[]{:S(2)}, u32[]{:S(2)}) collective-permute-start(bf16[256,768]{1,0:T(8,128)(2,1)S(1)} %get-tuple-element.256), channel_id=1, source_target_pairs={{0,16},{8,24},{16,0},{24,8},{1,17},{9,25},{17,1},{25,9},{2,18},{10... | collective-permute-start | bytes 1179656 | tf_op jit(solution)/shard_map/ppermute | solution.py:1073
  150.7 20.3 %collective-permute-start.47 = (bf16[256,768]{1,0:T(8,128)(2,1)S(1)}, bf16[256,768]{1,0:T(8,128)(2,1)S(1)}, u32[]{:S(2)}, u32[]{:S(2)}) collective-permute-start(bf16[256,768]{1,0:T(8,128)(2,1)S(1)} %get-tuple-element.258), channel_id=1, source_target_pairs={{0,24},{8,16},{16,8},{24,0},{1,25},{9,17},{17,9},{25,1},{2,26},{10... | collective-permute-start | bytes 1179656 | tf_op jit(solution)/shard_map/ppermute | solution.py:1073
  187.9 18.4 %collective-permute-start.54 = (bf16[256,768]{1,0:T(8,128)(2,1)S(1)}, bf16[256,768]{1,0:T(8,128)(2,1)S(1)}, u32[]{:S(2)}, u32[]{:S(2)}) collective-permute-start(bf16[256,768]{1,0:T(8,128)(2,1)S(1)} %get-tuple-element.273), channel_id=1, source_target_pairs={{0,16},{8,24},{16,0},{24,8},{1,17},{9,25},{17,1},{25,9},{2,18},{10... | collective-permute-start | bytes 1179656 | tf_op jit(solution)/shard_map/ppermute | solution.py:1073
  189.2 17.1 %collective-permute-start.53 = (bf16[256,768]{1,0:T(8,128)(2,1)S(1)}, bf16[256,768]{1,0:T(8,128)(2,1)S(1)}, u32[]{:S(2)}, u32[]{:S(2)}) collective-permute-start(bf16[256,768]{1,0:T(8,128)(2,1)S(1)} %get-tuple-element.269), channel_id=1, source_target_pairs={{0,8},{8,0},{16,24},{24,16},{1,9},{9,1},{17,25},{25,17},{2,10},{10... | collective-permute-start | bytes 1179656 | tf_op jit(solution)/shard_map/ppermute | solution.py:1073
  193.2 13.1 %collective-permute-start.55 = (bf16[256,768]{1,0:T(8,128)(2,1)S(1)}, bf16[256,768]{1,0:T(8,128)(2,1)S(1)}, u32[]{:S(2)}, u32[]{:S(2)}) collective-permute-start(bf16[256,768]{1,0:T(8,128)(2,1)S(1)} %get-tuple-element.276), channel_id=1, source_target_pairs={{0,24},{8,16},{16,8},{24,0},{1,25},{9,17},{17,9},{25,1},{2,26},{10... | collective-permute-start | bytes 1179656 | tf_op jit(solution)/shard_map/ppermute | solution.py:1073
  217.8 15.1 %collective-permute-start.60 = (bf16[384,384]{1,0:T(8,128)(2,1)S(1)}, bf16[384,384]{1,0:T(8,128)(2,1)S(1)}, u32[]{:S(2)}, u32[]{:S(2)}) collective-permute-start(bf16[384,384]{1,0:T(8,128)(2,1)S(1)} %get-tuple-element.309), channel_id=1, source_target_pairs={{0,2},{1,3},{2,0},{3,1},{4,6},{5,7},{6,4},{7,5},{8,10},{9,11},{10,... | collective-permute-start | bytes 884744 | tf_op jit(solution)/shard_map/ppermute | solution.py:1073
  217.8 15.1 %collective-permute-start.61 = (bf16[384,384]{1,0:T(8,128)(2,1)S(1)}, bf16[384,384]{1,0:T(8,128)(2,1)S(1)}, u32[]{:S(2)}, u32[]{:S(2)}) collective-permute-start(bf16[384,384]{1,0:T(8,128)(2,1)S(1)} %get-tuple-element.317), channel_id=1, source_target_pairs={{0,8},{8,0},{16,24},{24,16},{1,9},{9,1},{17,25},{25,17},{2,10},{10... | collective-permute-start | bytes 884744 | tf_op jit(solution)/shard_map/ppermute | solution.py:1073
  218.9 14.4 %collective-permute-start.62 = (bf16[384,384]{1,0:T(8,128)(2,1)S(1)}, bf16[384,384]{1,0:T(8,128)(2,1)S(1)}, u32[]{:S(2)}, u32[]{:S(2)}) collective-permute-start(bf16[384,384]{1,0:T(8,128)(2,1)S(1)} %get-tuple-element.318), channel_id=1, source_target_pairs={{0,16},{8,24},{16,0},{24,8},{1,17},{9,25},{17,1},{25,9},{2,18},{10... | collective-permute-start | bytes 884744 | tf_op jit(solution)/shard_map/ppermute | solution.py:1073
  219.9 13.5 %collective-permute-start.63 = (bf16[384,384]{1,0:T(8,128)(2,1)S(1)}, bf16[384,384]{1,0:T(8,128)(2,1)S(1)}, u32[]{:S(2)}, u32[]{:S(2)}) collective-permute-start(bf16[384,384]{1,0:T(8,128)(2,1)S(1)} %get-tuple-element.319), channel_id=1, source_target_pairs={{0,24},{8,16},{16,8},{24,0},{1,25},{9,17},{17,9},{25,1},{2,26},{10... | collective-permute-start | bytes 884744 | tf_op jit(solution)/shard_map/ppermute | solution.py:1073
  242.1 11.8 %collective-permute-start.66 = (bf16[112,768]{1,0:T(8,128)(2,1)S(1)}, bf16[112,768]{1,0:T(8,128)(2,1)S(1)}, u32[]{:S(2)}, u32[]{:S(2)}) collective-permute-start(bf16[112,768]{1,0:T(8,128)(2,1)S(1)} %get-tuple-element.338), channel_id=1, source_target_pairs={{0,2},{1,3},{2,0},{3,1},{4,6},{5,7},{6,4},{7,5},{8,10},{9,11},{10,... | collective-permute-start | bytes 516104 | tf_op jit(solution)/shard_map/ppermute | solution.py:1073
  242.4 22.8 %collective-permute-start.71 = (bf16[384,384]{1,0:T(8,128)(2,1)S(1)}, bf16[384,384]{1,0:T(8,128)(2,1)S(1)}, u32[]{:S(2)}, u32[]{:S(2)}) collective-permute-start(bf16[384,384]{1,0:T(8,128)(2,1)S(1)} %get-tuple-element.351), channel_id=1, source_target_pairs={{0,1},{1,0},{2,3},{3,2},{4,5},{5,4},{6,7},{7,6},{8,9},{9,8},{10,11... | collective-permute-start | bytes 884744 | tf_op jit(solution)/shard_map/ppermute | solution.py:1073
  244.3 18.0 %collective-permute-start.67 = (bf16[112,768]{1,0:T(8,128)(2,1)S(1)}, bf16[112,768]{1,0:T(8,128)(2,1)S(1)}, u32[]{:S(2)}, u32[]{:S(2)}) collective-permute-start(bf16[112,768]{1,0:T(8,128)(2,1)S(1)} %get-tuple-element.339), channel_id=1, source_target_pairs={{0,3},{1,2},{2,1},{3,0},{4,7},{5,6},{6,5},{7,4},{8,11},{9,10},{10,... | collective-permute-start | bytes 516104 | tf_op jit(solution)/shard_map/ppermute | solution.py:1073
  246.5 25.4 %collective-permute-start.68 = (bf16[256,768]{1,0:T(8,128)(2,1)S(1)}, bf16[256,768]{1,0:T(8,128)(2,1)S(1)}, u32[]{:S(2)}, u32[]{:S(2)}) collective-permute-start(bf16[256,768]{1,0:T(8,128)(2,1)S(1)} %get-tuple-element.345), channel_id=1, source_target_pairs={{0,8},{8,0},{16,24},{24,16},{1,9},{9,1},{17,25},{25,17},{2,10},{10... | collective-permute-start | bytes 1179656 | tf_op jit(solution)/shard_map/ppermute | solution.py:1073
  250.1 22.9 %collective-permute-start.69 = (bf16[256,768]{1,0:T(8,128)(2,1)S(1)}, bf16[256,768]{1,0:T(8,128)(2,1)S(1)}, u32[]{:S(2)}, u32[]{:S(2)}) collective-permute-start(bf16[256,768]{1,0:T(8,128)(2,1)S(1)} %get-tuple-element.346), channel_id=1, source_target_pairs={{0,16},{8,24},{16,0},{24,8},{1,17},{9,25},{17,1},{25,9},{2,18},{10... | collective-permute-start | bytes 1179656 | tf_op jit(solution)/shard_map/ppermute | solution.py:1073
  254.0 20.0 %collective-permute-start.70 = (bf16[256,768]{1,0:T(8,128)(2,1)S(1)}, bf16[256,768]{1,0:T(8,128)(2,1)S(1)}, u32[]{:S(2)}, u32[]{:S(2)}) collective-permute-start(bf16[256,768]{1,0:T(8,128)(2,1)S(1)} %get-tuple-element.347), channel_id=1, source_target_pairs={{0,24},{8,16},{16,8},{24,0},{1,25},{9,17},{17,9},{25,1},{2,26},{10... | collective-permute-start | bytes 1179656 | tf_op jit(solution)/shard_map/ppermute | solution.py:1073
  262.4 12.4 %collective-permute-start.72 = (bf16[384,384]{1,0:T(8,128)(2,1)S(1)}, bf16[384,384]{1,0:T(8,128)(2,1)S(1)}, u32[]{:S(2)}, u32[]{:S(2)}) collective-permute-start(bf16[384,384]{1,0:T(8,128)(2,1)S(1)} %get-tuple-element.353), channel_id=1, source_target_pairs={{0,3},{1,2},{2,1},{3,0},{4,7},{5,6},{6,5},{7,4},{8,11},{9,10},{10,... | collective-permute-start | bytes 884744 | tf_op jit(solution)/shard_map/ppermute | solution.py:1073
  274.7 18.3 %collective-permute-start.73 = (f32[128,768]{1,0:T(8,128)S(1)}, f32[128,768]{1,0:T(8,128)S(1)}, u32[]{:S(2)}, u32[]{:S(2)}) collective-permute-start(f32[128,768]{1,0:T(8,128)S(1)} %get-tuple-element.355), channel_id=1, source_target_pairs={{0,4},{4,0},{1,5},{5,1},{2,6},{6,2},{3,7},{7,3},{8,12},{12,8},{9,1... | collective-permute-start | bytes 1179656 | tf_op jit(solution)/shard_map/ppermute | solution.py:1073
  278.7 13.8 %collective-permute-start.82 = (bf16[384,384]{1,0:T(8,128)(2,1)S(1)}, bf16[384,384]{1,0:T(8,128)(2,1)S(1)}, u32[]{:S(2)}, u32[]{:S(2)}) collective-permute-start(bf16[384,384]{1,0:T(8,128)(2,1)S(1)} %late_sum.1.refs_0_), channel_id=1, source_target_pairs={{0,16},{8,24},{16,0},{24,8},{1,17},{9,25},{17,1},{25,9},{2,18},{10... | collective-permute-start | bytes 884744 | tf_op jit(solution)/shard_map/ppermute | solution.py:1073
  279.6 13.0 %collective-permute-start.81 = (bf16[384,384]{1,0:T(8,128)(2,1)S(1)}, bf16[384,384]{1,0:T(8,128)(2,1)S(1)}, u32[]{:S(2)}, u32[]{:S(2)}) collective-permute-start(bf16[384,384]{1,0:T(8,128)(2,1)S(1)} %late_sum.1.refs_0_), channel_id=1, source_target_pairs={{0,8},{8,0},{16,24},{24,16},{1,9},{9,1},{17,25},{25,17},{2,10},{10... | collective-permute-start | bytes 884744 | tf_op jit(solution)/shard_map/ppermute | solution.py:1073
  282.1 12.5 %collective-permute-start.78 = (bf16[112,768]{1,0:T(8,128)(2,1)S(1)}, bf16[112,768]{1,0:T(8,128)(2,1)S(1)}, u32[]{:S(2)}, u32[]{:S(2)}) collective-permute-start(bf16[112,768]{1,0:T(8,128)(2,1)S(1)} %collective-permute-done.74.refs_1_), channel_id=1, source_target_pairs={{0,4},{4,0},{1,5},{5,1},{2,6},{6,2},{3,7},{7,3},{8,12},{12,8},{9,1... | collective-permute-start | bytes 516104 | tf_op jit(solution)/shard_map/ppermute | solution.py:1073
  286.9 11.4 %collective-permute-start.84 = (bf16[384,384]{1,0:T(8,128)(2,1)S(1)}, bf16[384,384]{1,0:T(8,128)(2,1)}, u32[]{:S(2)}, u32[]{:S(2)}) collective-permute-start(bf16[384,384]{1,0:T(8,128)(2,1)S(1)} %late_sum.1.refs_0_), channel_id=1, source_target_pairs={{0,4},{4,0},{1,5},{5,1},{2,6},{6,2},{3,7},{7,3},{8,12},{12,8},{9,1... | collective-permute-start | bytes 884744 | tf_op jit(solution)/shard_map/ppermute | solution.py:1073
  (53 other events, 380.2 us)

commit v7 on v6

--- a/solution.py
+++ b/solution.py
@@ -37,7 +37,6 @@
 EXTRA = 16
 
 SMEM_SPEC = pl.BlockSpec(memory_space=pltpu.SMEM)
-HBM_SPEC = pl.BlockSpec(memory_space=pltpu.HBM)
 VMEM_SPEC = pl.BlockSpec(memory_space=pltpu.VMEM)
 
 
@@ -141,19 +140,13 @@
     return jnp.where(place == goal, 1.0, 0.0).astype(bf16)
 
 
-def early_pieces_kernel(student, ids_ref, attn_hbm, early_ref, attn_ref, sem):
+def early_pieces_kernel(student, ids_ref, attn_ref, early_ref):
     k, j = ids_ref[IK], ids_ref[IJ]
-    rows_z = attn_hbm.shape[1]
+    rows_z = attn_ref.shape[1]
     half = rows_z // CORES
-    if student:
-        copy = pltpu.make_async_copy(attn_hbm, attn_ref, sem)
-    else:
-        copy = pltpu.make_async_copy(attn_hbm.at[:, aligned(k * half, half), :], attn_ref, sem)
-    copy.start()
     chosen = choose(D, COLS, j * COLS)
     if student:
         early_ref[half:, :] = jnp.zeros((EXTRA, D), bf16)
-    copy.wait()
     for number in range(4):
         lanes = slice(number * COLS, (number + 1) * COLS)
         if student:
@@ -163,7 +156,7 @@
             for part, row in enumerate(split_three(sums)):
                 early_ref[half + part : half + part + 1, lanes] = row
         else:
-            full = attn_ref[number]
+            full = attn_ref[number, aligned(k * half, half), :]
         early_ref[0:half, lanes] = dot(full, chosen).astype(bf16)
 
 
@@ -172,12 +165,8 @@
     result = pl.pallas_call(
         functools.partial(early_pieces_kernel, student),
         out_shape=shape((half + EXTRA * student, D)),
-        in_specs=[SMEM_SPEC, HBM_SPEC],
+        in_specs=[SMEM_SPEC, VMEM_SPEC],
         out_specs=VMEM_SPEC,
-        scratch_shapes=[
-            pltpu.VMEM((4, attn.shape[1] if student else half, D), attn.dtype),
-            pltpu.SemaphoreType.DMA,
-        ],
         compiler_params=pltpu.CompilerParams(vmem_limit_bytes=12 * 2**20),
         name="early_pieces",
     )(line.ids, attn)
@@ -186,7 +175,7 @@
 
 
 def late_pieces_kernel(
-    n_shard, student, ids_ref, in_hbm, down_hbm, late_ref, in_ref, down_ref, sems
+    n_shard, student, ids_ref, in_ref, down_ref, late_ref
 ):
     k, j = ids_ref[IK], ids_ref[IJ]
     units = FF // n_shard
@@ -195,15 +184,7 @@
     each = rows_z + 2 * few
     number = j * CORES + k
     mine = aligned(number * few, few)
-    down_hbm = down_hbm if student else down_hbm.at[mine, :]
-    copies = [
-        pltpu.make_async_copy(in_hbm, in_ref, sems.at[0]),
-        pltpu.make_async_copy(down_hbm, down_ref, sems.at[1]),
-    ]
-    for copy in copies:
-        copy.start()
     chosen = choose(units, few, number * few)
-    copies[1].wait()
     if student:
         full = sign_of(down_ref[mine, :]).astype(bf16)
         late_ref[each:, :] = jnp.zeros((EXTRA, HALF), bf16)
@@ -212,10 +193,9 @@
             late_ref[low : low + 1, :] = row[:, :HALF]
             late_ref[low + 3 : low + 4, :] = row[:, HALF:]
     else:
-        full = down_ref[...]
+        full = down_ref[mine, :]
     late_ref[rows_z : rows_z + few, :] = full[:, :HALF]
     late_ref[rows_z + few : each, :] = full[:, HALF:]
-    copies[0].wait()
     for place in range(n_shard):
         lanes = slice(place * few, (place + 1) * few)
         full = in_ref[:, place * units : (place + 1) * units]
@@ -234,13 +214,8 @@
     result = pl.pallas_call(
         functools.partial(late_pieces_kernel, n_shard, student),
         out_shape=shape((rows_z + 2 * few + EXTRA * student, HALF)),
-        in_specs=[SMEM_SPEC, HBM_SPEC, HBM_SPEC],
+        in_specs=[SMEM_SPEC, VMEM_SPEC, VMEM_SPEC],
         out_specs=VMEM_SPEC,
-        scratch_shapes=[
-            pltpu.VMEM((rows_z, FF), w_in.dtype),
-            pltpu.VMEM((w_down.shape[0] if student else few, D), w_down.dtype),
-            pltpu.SemaphoreType.DMA((2,)),
-        ],
         compiler_params=pltpu.CompilerParams(vmem_limit_bytes=20 * 2**20),
         name="late_pieces",
     )(line.ids, w_in, w_down)

time: 310 us -> 309 us (level)
  transfers between devices with their start and end apart: 88 -> 88, of which waited for: 41 -> 41; matrix products, arithmetic and copies ran while one was open for 0% -> 0% of each run, Pallas kernels for 26% -> 25%
where the time goes in v7:
time: 309 us; the launch traced here: 304 us
  waiting for transfers between devices  126 us (41%)
  Pallas kernels  90.4 us (29%)
  starting transfers between devices  80.7 us (26%)
  local copies, waits for them, and re-layouts  5.3 us (2%)
    ppermute x88, waiting for transfers between devices, flip(): return lax.ppermute(piece, axis, [(a, a ^ mask) for a in range(size)])  126 us
    pallas_call x44, Pallas kernels, call(): pl.pallas_call(kernel, out_shape=outs, in_specs=[SMEM_SPEC] * len(scalars...  85.5 us
    ppermute x88, starting transfers between devices, flip(): return lax.ppermute(piece, axis, [(a, a ^ mask) for a in range(size)])  80.7 us
  transfers between devices with their start and end apart: 88, of which 41 were waited for; matrix products, arithmetic and copies ran while one was open for 0% of the time, Pallas kernels for 25%

profile of v7, /device:TPU:0, one launch (start us, length us, event | category | flops | bytes accessed | tf_op | source)
XLA Modules:
  0.0 304.5 jit_solution(2427952391970639121)
XLA Ops:
  0.6 3.0 collective-permute-start.3
  7.5 3.7 %collective-permute-start.2 = (bf16[96,768]{1,0:T(8,128)(2,1)S(1)}, bf16[96,768]{1,0:T(8,128)(2,1)S(1)}, u32[]{:S(2)}, u32[]{:S(2)}) collective-permute-start(bf16[96,768]{1,0:T(8,128)(2,1)S(1)} %early_pieces.2.refs_0_), channel_id=1, source_target_pairs={{0,3},{1,2},{2,1},{3,0},{4,7},{5,6},{6,5},{7,4},{8,11},{9,10},{10,... | collective-permute-start | bytes 442376 | tf_op jit(solution)/shard_map/ppermute | solution.py:1048
  16.2 6.9 %collective-permute-done.1.refs_2_ = bf16[96,768]{1,0:T(8,128)(2,1)S(1)} collective-permute-done((bf16[96,768]{1,0:T(8,128)(2,1)S(1)}, bf16[96,768]{1,0:T(8,128)(2,1)S(1)}, u32[]{:S(2)}, u32[]{:S(2)}) %collective-permute-start.1) | collective-permute-done | bytes 147488 | tf_op jit(solution)/shard_map/ppermute | solution.py:1048
  27.8 2.1 collective-permute-done.5
  31.5 2.5 collective-permute-start.11
  33.9 1.9 collective-permute-start.9
  36.0 3.0 qkv.2
  40.6 7.5 %collective-permute-done.10.refs_2_ = bf16[112,768]{1,0:T(8,128)(2,1)S(1)} collective-permute-done((bf16[112,768]{1,0:T(8,128)(2,1)S(1)}, bf16[112,768]{1,0:T(8,128)(2,1)S(1)}, u32[]{:S(2)}, u32[]{:S(2)}) %collective-permute-start.10) | collective-permute-done | bytes 172064 | tf_op jit(solution)/shard_map/ppermute | solution.py:1048
  54.7 2.4 collective-permute-start.25
  57.1 3.0 collective-permute-done.17.refs_3_
  60.1 5.8 %collective-permute-done.16.refs_2_ = bf16[384,384]{1,0:T(8,128)(2,1)S(1)} collective-permute-done((bf16[384,384]{1,0:T(8,128)(2,1)S(1)}, bf16[384,384]{1,0:T(8,128)(2,1)S(1)}, u32[]{:S(2)}, u32[]{:S(2)}) %collective-permute-start.16) | collective-permute-done | bytes 294944 | tf_op jit(solution)/shard_map/ppermute | solution.py:1048
  66.4 1.8 collective-permute-done.14.got_ref
  68.3 6.6 %attend.2 = (bf16[256,192]{1,0:T(8,128)(2,1)S(1)}, bf16[256,192]{1,0:T(8,128)(2,1)S(1)}, bf16[256,192]{1,0:T(8,128)(2,1)S(1)}, bf16[256,192]{1,0:T(8,128)(2,1)S(1)}, f32[3,1,1024]{2,1,0:T(1,128)}) custom-call(s32[4]{0:T(128)S(1)} %pad_add_fusion.ids_ref, s32[16]{0:T(128)S(1)} %copy-done.11, bf16[3,1024,64]{2,1,0:T(8,128)(2,1)S(1)} %get-tuple-element.198.q_ref, ...), custom_call_target="tpu_custom_call" | custom-call | tf_op jit(solution)/shard_map/attend/pallas_call | solution.py:79
  78.4 2.1 qkv.3
  82.2 2.7 collective-permute-done.23.refs_2_
  88.7 6.4 %attend.3 = (bf16[256,192]{1,0:T(8,128)(2,1)S(1)}, bf16[256,192]{1,0:T(8,128)(2,1)S(1)}, bf16[256,192]{1,0:T(8,128)(2,1)S(1)}, bf16[256,192]{1,0:T(8,128)(2,1)S(1)}, f32[3,1,1024]{2,1,0:T(1,128)S(1)}) custom-call(s32[4]{0:T(128)S(1)} %pad_add_fusion.ids_ref, s32[16]{0:T(128)S(1)} %copy-done.11, bf16[3,1024,64]{2,1,0:T(8,128)(2,1)S(1)} %get-tuple-element.208.q_ref.refs_0_, ...), custom_call_target="tpu_custom_call" | custom-call | tf_op jit(solution)/shard_map/attend/pallas_call | solution.py:79
  95.1 2.9 collective-permute-done.32.refs_0_
  99.8 1.8 collective-permute-start.30
  104.2 2.1 collective-permute-done.29.refs_2_
  110.8 5.1 %collective-permute-done.33.refs_1_ = bf16[2,400,384]{2,1,0:T(8,128)(2,1)S(1)} collective-permute-done((bf16[2,400,384]{2,1,0:T(8,128)(2,1)S(1)}, bf16[2,400,384]{2,1,0:T(8,128)(2,1)S(1)}, u32[]{:S(2)}, u32[]{:S(2)}) %collective-permute-start.33) | collective-permute-done | bytes 614432 | tf_op jit(solution)/shard_map/ppermute | solution.py:1048
  123.9 4.5 %collective-permute-done.39.refs_0_.refs_11_ = bf16[256,768]{1,0:T(8,128)(2,1)S(1)} collective-permute-done((bf16[256,768]{1,0:T(8,128)(2,1)S(1)}, bf16[256,768]{1,0:T(8,128)(2,1)S(1)}, u32[]{:S(2)}, u32[]{:S(2)}) %collective-permute-start.39) | collective-permute-done | bytes 393248 | tf_op jit(solution)/shard_map/ppermute | solution.py:1048
  131.1 2.0 collective-permute-done.36.refs_0_
  134.3 6.7 %collective-permute-done.37.refs_1_ = bf16[128,768]{1,0:T(8,128)(2,1)S(1)} collective-permute-done((bf16[128,768]{1,0:T(8,128)(2,1)S(1)}, bf16[128,768]{1,0:T(8,128)(2,1)S(1)}, u32[]{:S(2)}, u32[]{:S(2)}) %collective-permute-start.37) | collective-permute-done | bytes 196640 | tf_op jit(solution)/shard_map/ppermute | solution.py:1048
  151.7 3.8 %collective-permute-done.44.refs_3_ = bf16[256,768]{1,0:T(8,128)(2,1)S(1)} collective-permute-done((bf16[256,768]{1,0:T(8,128)(2,1)S(1)}, bf16[256,768]{1,0:T(8,128)(2,1)S(1)}, u32[]{:S(2)}, u32[]{:S(2)}) %collective-permute-start.44) | collective-permute-done | bytes 393248 | tf_op jit(solution)/shard_map/ppermute | solution.py:1048
  156.5 6.5 %collective-permute-done.45.refs_1_ = bf16[256,768]{1,0:T(8,128)(2,1)S(1)} collective-permute-done((bf16[256,768]{1,0:T(8,128)(2,1)S(1)}, bf16[256,768]{1,0:T(8,128)(2,1)S(1)}, u32[]{:S(2)}, u32[]{:S(2)}) %collective-permute-start.45) | collective-permute-done | bytes 393248 | tf_op jit(solution)/shard_map/ppermute | solution.py:1048
  163.8 6.9 %collective-permute-done.47.refs_3_ = bf16[256,768]{1,0:T(8,128)(2,1)S(1)} collective-permute-done((bf16[256,768]{1,0:T(8,128)(2,1)S(1)}, bf16[256,768]{1,0:T(8,128)(2,1)S(1)}, u32[]{:S(2)}, u32[]{:S(2)}) %collective-permute-start.47) | collective-permute-done | bytes 393248 | tf_op jit(solution)/shard_map/ppermute | solution.py:1048
  170.8 1.8 loss.1
  175.9 6.3 %collective-permute-done.49.refs_0_.refs_6_ = bf16[256,768]{1,0:T(8,128)(2,1)S(1)} collective-permute-done((bf16[256,768]{1,0:T(8,128)(2,1)S(1)}, bf16[256,768]{1,0:T(8,128)(2,1)S(1)}, u32[]{:S(2)}, u32[]{:S(2)}) %collective-permute-start.49) | collective-permute-done | bytes 393248 | tf_op jit(solution)/shard_map/ppermute | solution.py:1048
  193.0 1.7 collective-permute-start.55
  197.6 3.5 %late_grad.1 = (f32[4,384,384]{2,1,0:T(8,128)S(1)}, bf16[4,384,384]{2,1,0:T(8,128)(2,1)S(1)}) custom-call(s32[4]{0:T(128)S(1)} %pad_add_fusion.ids_ref, bf16[256,768]{1,0:T(8,128)(2,1)S(1)} %get-tuple-element.279.refs_0_, bf16[256,768]{1,0:T(8,128)(2,1)S(1)} %get-tuple-element.280.refs_1_, bf16[256,768]{1,0:T(8,128)(2,1)S(1)} %get-tuple-element.281.refs_2_, ...), custom_call_target="tpu_custom_call" | custom-call | tf_op jit(solution)/shard_map/late_grad/pallas_call | solution.py:79
  201.2 5.0 %collective-permute-done.54.refs_2_ = bf16[256,768]{1,0:T(8,128)(2,1)S(1)} collective-permute-done((bf16[256,768]{1,0:T(8,128)(2,1)S(1)}, bf16[256,768]{1,0:T(8,128)(2,1)S(1)}, u32[]{:S(2)}, u32[]{:S(2)}) %collective-permute-start.54) | collective-permute-done | bytes 393248 | tf_op jit(solution)/shard_map/ppermute | solution.py:1048
  206.2 2.0 branch_back.1
  214.6 3.0 collective-permute-done.58.refs_5_
  221.1 10.1 %attend_back.1 = (bf16[1024,192]{1,0:T(8,128)(2,1)S(1)}, bf16[1024,192]{1,0:T(8,128)(2,1)S(1)}, bf16[1024,192]{1,0:T(8,128)(2,1)S(1)}, f32[8,192]{1,0:T(8,128)S(1)}) custom-call(s32[4]{0:T(128)S(1)} %pad_add_fusion.ids_ref, s32[16]{0:T(128)S(1)} %copy-done.11, bf16[3,1024,64]{2,1,0:T(8,128)(2,1)S(1)} %get-tuple-element.208.q_ref.refs_0_, ...), custom_call_target="tpu_custom_call" | custom-call | tf_op jit(solution)/shard_map/attend_back/pallas_call | solution.py:79
  233.2 3.4 %early_grad.1 = (f32[384,768]{1,0:T(8,128)S(1)}, f32[8,768]{1,0:T(8,128)S(1)}, bf16[400,768]{1,0:T(8,128)(2,1)S(1)}) custom-call(s32[4]{0:T(128)S(1)} %pad_add_fusion.ids_ref, bf16[512,768]{1,0:T(8,128)(2,1)S(1)} %get-tuple-element.195.own_ref.refs_5_.refs_0_, bf16[512,768]{1,0:T(8,128)(2,1)S(1)} %collective-permute-done.7.oth_ref.refs_6_.refs_1_, ...), custom_call_target="tpu_custom_call" | custom-call | tf_op jit(solution)/shard_map/early_grad/pallas_call | solution.py:79
  236.7 2.0 qkv_back.1
  239.4 2.5 collective-permute-start.65
  242.3 1.9 collective-permute-start.71
  244.2 2.2 collective-permute-start.67
  247.3 2.6 collective-permute-done.65.refs_1_
  250.8 3.0 collective-permute-done.66.refs_2_
  255.3 6.9 %collective-permute-done.67.refs_3_ = bf16[112,768]{1,0:T(8,128)(2,1)S(1)} collective-permute-done((bf16[112,768]{1,0:T(8,128)(2,1)S(1)}, bf16[112,768]{1,0:T(8,128)(2,1)S(1)}, u32[]{:S(2)}, u32[]{:S(2)}) %collective-permute-start.67) | collective-permute-done | bytes 172064 | tf_op jit(solution)/shard_map/ppermute | solution.py:1048
  262.2 2.2 collective-permute-start.72
  266.5 5.2 %collective-permute-done.76.refs_3_ = bf16[112,768]{1,0:T(8,128)(2,1)S(1)} collective-permute-done((bf16[112,768]{1,0:T(8,128)(2,1)S(1)}, bf16[112,768]{1,0:T(8,128)(2,1)S(1)}, u32[]{:S(2)}, u32[]{:S(2)}) %collective-permute-start.76) | collective-permute-done | bytes 172064 | tf_op jit(solution)/shard_map/ppermute | solution.py:1048
  282.1 4.6 %collective-permute-done.83.refs_3_ = bf16[384,384]{1,0:T(8,128)(2,1)S(1)} collective-permute-done((bf16[384,384]{1,0:T(8,128)(2,1)S(1)}, bf16[384,384]{1,0:T(8,128)(2,1)S(1)}, u32[]{:S(2)}, u32[]{:S(2)}) %collective-permute-start.83) | collective-permute-done | bytes 294944 | tf_op jit(solution)/shard_map/ppermute | solution.py:1048
  286.7 5.7 %collective-permute-done.82.refs_2_ = bf16[384,384]{1,0:T(8,128)(2,1)S(1)} collective-permute-done((bf16[384,384]{1,0:T(8,128)(2,1)S(1)}, bf16[384,384]{1,0:T(8,128)(2,1)S(1)}, u32[]{:S(2)}, u32[]{:S(2)}) %collective-permute-start.82) | collective-permute-done | bytes 294944 | tf_op jit(solution)/shard_map/ppermute | solution.py:1048
  294.4 2.5 early_final.1
  299.8 4.4 %late_final.1 = (f32[192,3072]{1,0:T(8,128)}, f32[768,768]{1,0:T(8,128)}) custom-call(s32[4]{0:T(128)S(1)} %pad_add_fusion.ids_ref, bf16[384,384]{1,0:T(8,128)(2,1)S(1)} %late_sum.1.refs_0_, bf16[384,384]{1,0:T(8,128)(2,1)S(1)} %collective-permute-done.81.refs_1_, bf16[384,384]{1,0:T(8,128)(2,1)S(1)} %collective-permute-done.82.refs_2_, ...), custom_call_target="tpu_custom_call" | custom-call | tf_op jit(solution)/shard_map/late_final/pallas_call | solution.py:79
  (214 shorter events, 116.5 us)
Async XLA Ops:
  0.6 23.2 %collective-permute-start.3 = (bf16[2,128,768]{2,1,0:T(8,128)(2,1)}, bf16[2,128,768]{2,1,0:T(8,128)(2,1)S(1)}, u32[]{:S(2)}, u32[]{:S(2)}) collective-permute-start(bf16[2,128,768]{2,1,0:T(8,128)(2,1)} %here_ref.1), channel_id=1, source_target_pairs={{0,8},{8,0},{16,24},{24,16},{1,9},{9,1},{17,25},{25,17},{2,10},{10... | collective-permute-start | bytes 1179656 | tf_op jit(solution)/shard_map/ppermute | solution.py:1048
  3.6 20.2 %collective-permute-start.4 = (bf16[2,128,768]{2,1,0:T(8,128)(2,1)}, bf16[2,128,768]{2,1,0:T(8,128)(2,1)S(1)}, u32[]{:S(2)}, u32[]{:S(2)}) collective-permute-start(bf16[2,128,768]{2,1,0:T(8,128)(2,1)} %here_ref.1), channel_id=1, source_target_pairs={{0,16},{8,24},{16,0},{24,8},{1,17},{9,25},{17,1},{25,9},{2,18},{10... | collective-permute-start | bytes 1179656 | tf_op jit(solution)/shard_map/ppermute | solution.py:1048
  11.2 11.9 %collective-permute-start.1 = (bf16[96,768]{1,0:T(8,128)(2,1)S(1)}, bf16[96,768]{1,0:T(8,128)(2,1)S(1)}, u32[]{:S(2)}, u32[]{:S(2)}) collective-permute-start(bf16[96,768]{1,0:T(8,128)(2,1)S(1)} %early_pieces.2.refs_0_), channel_id=1, source_target_pairs={{0,2},{1,3},{2,0},{3,1},{4,6},{5,7},{6,4},{7,5},{8,10},{9,11},{10,... | collective-permute-start | bytes 442376 | tf_op jit(solution)/shard_map/ppermute | solution.py:1048
  11.2 11.9 %collective-permute-start = (bf16[96,768]{1,0:T(8,128)(2,1)S(1)}, bf16[96,768]{1,0:T(8,128)(2,1)S(1)}, u32[]{:S(2)}, u32[]{:S(2)}) collective-permute-start(bf16[96,768]{1,0:T(8,128)(2,1)S(1)} %early_pieces.2.refs_0_), channel_id=1, source_target_pairs={{0,1},{1,0},{2,3},{3,2},{4,5},{5,4},{6,7},{7,6},{8,9},{9,8},{10,11... | collective-permute-start | bytes 442376 | tf_op jit(solution)/shard_map/ppermute | solution.py:1048
  33.9 14.2 %collective-permute-start.10 = (bf16[112,768]{1,0:T(8,128)(2,1)S(1)}, bf16[112,768]{1,0:T(8,128)(2,1)S(1)}, u32[]{:S(2)}, u32[]{:S(2)}) collective-permute-start(bf16[112,768]{1,0:T(8,128)(2,1)S(1)} %early_pieces.3.refs_0_), channel_id=1, source_target_pairs={{0,2},{1,3},{2,0},{3,1},{4,6},{5,7},{6,4},{7,5},{8,10},{9,11},{10,... | collective-permute-start | bytes 516104 | tf_op jit(solution)/shard_map/ppermute | solution.py:1048
  33.9 14.2 %collective-permute-start.9 = (bf16[112,768]{1,0:T(8,128)(2,1)S(1)}, bf16[112,768]{1,0:T(8,128)(2,1)S(1)}, u32[]{:S(2)}, u32[]{:S(2)}) collective-permute-start(bf16[112,768]{1,0:T(8,128)(2,1)S(1)} %early_pieces.3.refs_0_), channel_id=1, source_target_pairs={{0,1},{1,0},{2,3},{3,2},{4,5},{5,4},{6,7},{7,6},{8,9},{9,8},{10,11... | collective-permute-start | bytes 516104 | tf_op jit(solution)/shard_map/ppermute | solution.py:1048
  35.8 17.6 %collective-permute-start.12 = (bf16[1,384,384]{2,1,0:T(8,128)(2,1)S(1)}, bf16[1,384,384]{2,1,0:T(8,128)(2,1)S(1)}, u32[]{:S(2)}, u32[]{:S(2)}) collective-permute-start(bf16[1,384,384]{2,1,0:T(8,128)(2,1)S(1)} %bitcast.11), channel_id=1, source_target_pairs={{0,1},{1,0},{2,3},{3,2},{4,5},{5,4},{6,7},{7,6},{8,9},{9,8},{10,11... | collective-permute-start | bytes 884744 | tf_op jit(solution)/shard_map/ppermute | solution.py:1048
  50.7 15.2 %collective-permute-start.16 = (bf16[384,384]{1,0:T(8,128)(2,1)S(1)}, bf16[384,384]{1,0:T(8,128)(2,1)S(1)}, u32[]{:S(2)}, u32[]{:S(2)}) collective-permute-start(bf16[384,384]{1,0:T(8,128)(2,1)S(1)} %get-tuple-element.212.refs_0_), channel_id=1, source_target_pairs={{0,16},{8,24},{16,0},{24,8},{1,17},{9,25},{17,1},{25,9},{2,18},{10... | collective-permute-start | bytes 884744 | tf_op jit(solution)/shard_map/ppermute | solution.py:1048
  52.3 13.7 %collective-permute-start.15 = (bf16[384,384]{1,0:T(8,128)(2,1)S(1)}, bf16[384,384]{1,0:T(8,128)(2,1)S(1)}, u32[]{:S(2)}, u32[]{:S(2)}) collective-permute-start(bf16[384,384]{1,0:T(8,128)(2,1)S(1)} %get-tuple-element.212.refs_0_), channel_id=1, source_target_pairs={{0,8},{8,0},{16,24},{24,16},{1,9},{9,1},{17,25},{25,17},{2,10},{10... | collective-permute-start | bytes 884744 | tf_op jit(solution)/shard_map/ppermute | solution.py:1048
  53.4 14.9 %collective-permute-start.14 = (bf16[1,400,384]{2,1,0:T(8,128)(2,1)S(1)}, bf16[1,400,384]{2,1,0:T(8,128)(2,1)S(1)}, u32[]{:S(2)}, u32[]{:S(2)}) collective-permute-start(bf16[1,400,384]{2,1,0:T(8,128)(2,1)S(1)} %bitcast.9), channel_id=1, source_target_pairs={{0,1},{1,0},{2,3},{3,2},{4,5},{5,4},{6,7},{7,6},{8,9},{9,8},{10,11... | collective-permute-start | bytes 921608 | tf_op jit(solution)/shard_map/ppermute | solution.py:1048
  54.7 31.7 %collective-permute-start.25 = (bf16[2,384,384]{2,1,0:T(8,128)(2,1)S(1)}, bf16[2,384,384]{2,1,0:T(8,128)(2,1)S(1)}, u32[]{:S(2)}, u32[]{:S(2)}) collective-permute-start(bf16[2,384,384]{2,1,0:T(8,128)(2,1)S(1)} %merge.2.refs_0_), channel_id=1, source_target_pairs={{0,2},{1,3},{2,0},{3,1},{4,6},{5,7},{6,4},{7,5},{8,10},{9,11},{10,... | collective-permute-start | bytes 1769480 | tf_op jit(solution)/shard_map/ppermute | solution.py:1048
  60.1 14.8 %collective-permute-start.13 = (bf16[384,576]{1,0:T(8,128)(2,1)S(1)}, bf16[384,576]{1,0:T(8,128)(2,1)S(1)}, u32[]{:S(2)}, u32[]{:S(2)}) collective-permute-start(bf16[384,576]{1,0:T(8,128)(2,1)S(1)} %get-tuple-element.201.half_ref), channel_id=1, source_target_pairs={{0,4},{4,0},{1,5},{5,1},{2,6},{6,2},{3,7},{7,3},{8,12},{12,8},{9,1... | collective-permute-start | bytes 1327112 | tf_op jit(solution)/shard_map/ppermute | solution.py:1048
  68.3 12.8 %collective-permute-start.19 = (bf16[384,384]{1,0:T(8,128)(2,1)S(1)}, bf16[384,384]{1,0:T(8,128)(2,1)S(1)}, u32[]{:S(2)}, u32[]{:S(2)}) collective-permute-start(bf16[384,384]{1,0:T(8,128)(2,1)S(1)} %collective-permute-done.15.refs_1_), channel_id=1, source_target_pairs={{0,4},{4,0},{1,5},{5,1},{2,6},{6,2},{3,7},{7,3},{8,12},{12,8},{9,1... | collective-permute-start | bytes 884744 | tf_op jit(solution)/shard_map/ppermute | solution.py:1048
  86.4 12.2 %collective-permute-start.26 = (bf16[2,384,384]{2,1,0:T(8,128)(2,1)S(1)}, bf16[2,384,384]{2,1,0:T(8,128)(2,1)S(1)}, u32[]{:S(2)}, u32[]{:S(2)}) collective-permute-start(bf16[2,384,384]{2,1,0:T(8,128)(2,1)S(1)} %merge.2.refs_0_), channel_id=1, source_target_pairs={{0,4},{4,0},{1,5},{5,1},{2,6},{6,2},{3,7},{7,3},{8,12},{12,8},{9,1... | collective-permute-start | bytes 1769480 | tf_op jit(solution)/shard_map/ppermute | solution.py:1048
  86.5 13.3 %collective-permute-start.27 = (bf16[2,384,384]{2,1,0:T(8,128)(2,1)S(1)}, bf16[2,384,384]{2,1,0:T(8,128)(2,1)S(1)}, u32[]{:S(2)}, u32[]{:S(2)}) collective-permute-start(bf16[2,384,384]{2,1,0:T(8,128)(2,1)S(1)} %collective-permute-done.25.refs_1_), channel_id=1, source_target_pairs={{0,4},{4,0},{1,5},{5,1},{2,6},{6,2},{3,7},{7,3},{8,12},{12,8},{9,1... | collective-permute-start | bytes 1769480 | tf_op jit(solution)/shard_map/ppermute | solution.py:1048
  87.0 28.9 %collective-permute-start.33 = (bf16[2,400,384]{2,1,0:T(8,128)(2,1)S(1)}, bf16[2,400,384]{2,1,0:T(8,128)(2,1)S(1)}, u32[]{:S(2)}, u32[]{:S(2)}) collective-permute-start(bf16[2,400,384]{2,1,0:T(8,128)(2,1)S(1)} %merge.3.refs_0_), channel_id=1, source_target_pairs={{0,2},{1,3},{2,0},{3,1},{4,6},{5,7},{6,4},{7,5},{8,10},{9,11},{10,... | collective-permute-start | bytes 1843208 | tf_op jit(solution)/shard_map/ppermute | solution.py:1048
  87.5 16.5 %collective-permute-start.31 = (bf16[256,768]{1,0:T(8,128)(2,1)S(1)}, bf16[256,768]{1,0:T(8,128)(2,1)S(1)}, u32[]{:S(2)}, u32[]{:S(2)}) collective-permute-start(bf16[256,768]{1,0:T(8,128)(2,1)S(1)} %get-tuple-element.228.refs_0_), channel_id=1, source_target_pairs={{0,8},{8,0},{16,24},{24,16},{1,9},{9,1},{17,25},{25,17},{2,10},{10... | collective-permute-start | bytes 1179656 | tf_op jit(solution)/shard_map/ppermute | solution.py:1048
  116.4 12.0 %collective-permute-start.39 = (bf16[256,768]{1,0:T(8,128)(2,1)S(1)}, bf16[256,768]{1,0:T(8,128)(2,1)S(1)}, u32[]{:S(2)}, u32[]{:S(2)}) collective-permute-start(bf16[256,768]{1,0:T(8,128)(2,1)S(1)} %get-tuple-element.246.refs_0_.refs_9_), channel_id=1, source_target_pairs={{0,16},{8,24},{16,0},{24,8},{1,17},{9,25},{17,1},{25,9},{2,18},{10... | collective-permute-start | bytes 1179656 | tf_op jit(solution)/shard_map/ppermute | solution.py:1048
  116.9 12.0 %collective-permute-start.38 = (bf16[256,768]{1,0:T(8,128)(2,1)S(1)}, bf16[256,768]{1,0:T(8,128)(2,1)S(1)}, u32[]{:S(2)}, u32[]{:S(2)}) collective-permute-start(bf16[256,768]{1,0:T(8,128)(2,1)S(1)} %get-tuple-element.246.refs_0_.refs_9_), channel_id=1, source_target_pairs={{0,8},{8,0},{16,24},{24,16},{1,9},{9,1},{17,25},{25,17},{2,10},{10... | collective-permute-start | bytes 1179656 | tf_op jit(solution)/shard_map/ppermute | solution.py:1048
  118.1 32.4 %collective-permute-start.43 = (bf16[256,768]{1,0:T(8,128)(2,1)S(1)}, bf16[256,768]{1,0:T(8,128)(2,1)S(1)}, u32[]{:S(2)}, u32[]{:S(2)}) collective-permute-start(bf16[256,768]{1,0:T(8,128)(2,1)S(1)} %feed.10), channel_id=1, source_target_pairs={{0,16},{8,24},{16,0},{24,8},{1,17},{9,25},{17,1},{25,9},{2,18},{10... | collective-permute-start | bytes 1179656 | tf_op jit(solution)/shard_map/ppermute | solution.py:1048
  119.0 14.1 %collective-permute-start.36 = (bf16[128,768]{1,0:T(8,128)(2,1)S(1)}, bf16[128,768]{1,0:T(8,128)(2,1)S(1)}, u32[]{:S(2)}, u32[]{:S(2)}) collective-permute-start(bf16[128,768]{1,0:T(8,128)(2,1)S(1)} %slice.35), channel_id=1, source_target_pairs={{0,8},{8,0},{16,24},{24,16},{1,9},{9,1},{17,25},{25,17},{2,10},{10... | collective-permute-start | bytes 589832 | tf_op jit(solution)/shard_map/ppermute | solution.py:1048
  120.5 20.4 %collective-permute-start.37 = (bf16[128,768]{1,0:T(8,128)(2,1)S(1)}, bf16[128,768]{1,0:T(8,128)(2,1)S(1)}, u32[]{:S(2)}, u32[]{:S(2)}) collective-permute-start(bf16[128,768]{1,0:T(8,128)(2,1)S(1)} %slice.36), channel_id=1, source_target_pairs={{0,16},{8,24},{16,0},{24,8},{1,17},{9,25},{17,1},{25,9},{2,18},{10... | collective-permute-start | bytes 589832 | tf_op jit(solution)/shard_map/ppermute | solution.py:1048
  128.9 17.7 %collective-permute-start.40 = (bf16[128,768]{1,0:T(8,128)(2,1)S(1)}, bf16[128,768]{1,0:T(8,128)(2,1)S(1)}, u32[]{:S(2)}, u32[]{:S(2)}) collective-permute-start(bf16[128,768]{1,0:T(8,128)(2,1)S(1)} %slice.37), channel_id=1, source_target_pairs={{0,8},{8,0},{16,24},{24,16},{1,9},{9,1},{17,25},{25,17},{2,10},{10... | collective-permute-start | bytes 589832 | tf_op jit(solution)/shard_map/ppermute | solution.py:1048
  130.2 17.3 %collective-permute-start.41 = (bf16[128,768]{1,0:T(8,128)(2,1)S(1)}, bf16[128,768]{1,0:T(8,128)(2,1)S(1)}, u32[]{:S(2)}, u32[]{:S(2)}) collective-permute-start(bf16[128,768]{1,0:T(8,128)(2,1)S(1)} %slice.38), channel_id=1, source_target_pairs={{0,16},{8,24},{16,0},{24,8},{1,17},{9,25},{17,1},{25,9},{2,18},{10... | collective-permute-start | bytes 589832 | tf_op jit(solution)/shard_map/ppermute | solution.py:1048
  133.1 18.6 %collective-permute-start.42 = (bf16[256,768]{1,0:T(8,128)(2,1)S(1)}, bf16[256,768]{1,0:T(8,128)(2,1)S(1)}, u32[]{:S(2)}, u32[]{:S(2)}) collective-permute-start(bf16[256,768]{1,0:T(8,128)(2,1)S(1)} %feed.9), channel_id=1, source_target_pairs={{0,8},{8,0},{16,24},{24,16},{1,9},{9,1},{17,25},{25,17},{2,10},{10... | collective-permute-start | bytes 1179656 | tf_op jit(solution)/shard_map/ppermute | solution.py:1048
  142.4 13.1 %collective-permute-start.44 = (bf16[256,768]{1,0:T(8,128)(2,1)S(1)}, bf16[256,768]{1,0:T(8,128)(2,1)S(1)}, u32[]{:S(2)}, u32[]{:S(2)}) collective-permute-start(bf16[256,768]{1,0:T(8,128)(2,1)S(1)} %feed.12), channel_id=1, source_target_pairs={{0,24},{8,16},{16,8},{24,0},{1,25},{9,17},{17,9},{25,1},{2,26},{10... | collective-permute-start | bytes 1179656 | tf_op jit(solution)/shard_map/ppermute | solution.py:1048
  146.6 16.4 %collective-permute-start.45 = (bf16[256,768]{1,0:T(8,128)(2,1)S(1)}, bf16[256,768]{1,0:T(8,128)(2,1)S(1)}, u32[]{:S(2)}, u32[]{:S(2)}) collective-permute-start(bf16[256,768]{1,0:T(8,128)(2,1)S(1)} %get-tuple-element.253), channel_id=1, source_target_pairs={{0,8},{8,0},{16,24},{24,16},{1,9},{9,1},{17,25},{25,17},{2,10},{10... | collective-permute-start | bytes 1179656 | tf_op jit(solution)/shard_map/ppermute | solution.py:1048
  147.5 16.4 %collective-permute-start.46 = (bf16[256,768]{1,0:T(8,128)(2,1)S(1)}, bf16[256,768]{1,0:T(8,128)(2,1)S(1)}, u32[]{:S(2)}, u32[]{:S(2)}) collective-permute-start(bf16[256,768]{1,0:T(8,128)(2,1)S(1)} %get-tuple-element.256), channel_id=1, source_target_pairs={{0,16},{8,24},{16,0},{24,8},{1,17},{9,25},{17,1},{25,9},{2,18},{10... | collective-permute-start | bytes 1179656 | tf_op jit(solution)/shard_map/ppermute | solution.py:1048
  150.5 20.3 %collective-permute-start.47 = (bf16[256,768]{1,0:T(8,128)(2,1)S(1)}, bf16[256,768]{1,0:T(8,128)(2,1)S(1)}, u32[]{:S(2)}, u32[]{:S(2)}) collective-permute-start(bf16[256,768]{1,0:T(8,128)(2,1)S(1)} %get-tuple-element.258), channel_id=1, source_target_pairs={{0,24},{8,16},{16,8},{24,0},{1,25},{9,17},{17,9},{25,1},{2,26},{10... | collective-permute-start | bytes 1179656 | tf_op jit(solution)/shard_map/ppermute | solution.py:1048
  187.8 18.4 %collective-permute-start.54 = (bf16[256,768]{1,0:T(8,128)(2,1)S(1)}, bf16[256,768]{1,0:T(8,128)(2,1)S(1)}, u32[]{:S(2)}, u32[]{:S(2)}) collective-permute-start(bf16[256,768]{1,0:T(8,128)(2,1)S(1)} %get-tuple-element.273), channel_id=1, source_target_pairs={{0,16},{8,24},{16,0},{24,8},{1,17},{9,25},{17,1},{25,9},{2,18},{10... | collective-permute-start | bytes 1179656 | tf_op jit(solution)/shard_map/ppermute | solution.py:1048
  189.0 17.1 %collective-permute-start.53 = (bf16[256,768]{1,0:T(8,128)(2,1)S(1)}, bf16[256,768]{1,0:T(8,128)(2,1)S(1)}, u32[]{:S(2)}, u32[]{:S(2)}) collective-permute-start(bf16[256,768]{1,0:T(8,128)(2,1)S(1)} %get-tuple-element.269), channel_id=1, source_target_pairs={{0,8},{8,0},{16,24},{24,16},{1,9},{9,1},{17,25},{25,17},{2,10},{10... | collective-permute-start | bytes 1179656 | tf_op jit(solution)/shard_map/ppermute | solution.py:1048
  193.0 13.1 %collective-permute-start.55 = (bf16[256,768]{1,0:T(8,128)(2,1)S(1)}, bf16[256,768]{1,0:T(8,128)(2,1)S(1)}, u32[]{:S(2)}, u32[]{:S(2)}) collective-permute-start(bf16[256,768]{1,0:T(8,128)(2,1)S(1)} %get-tuple-element.276), channel_id=1, source_target_pairs={{0,24},{8,16},{16,8},{24,0},{1,25},{9,17},{17,9},{25,1},{2,26},{10... | collective-permute-start | bytes 1179656 | tf_op jit(solution)/shard_map/ppermute | solution.py:1048
  217.6 15.1 %collective-permute-start.60 = (bf16[384,384]{1,0:T(8,128)(2,1)S(1)}, bf16[384,384]{1,0:T(8,128)(2,1)S(1)}, u32[]{:S(2)}, u32[]{:S(2)}) collective-permute-start(bf16[384,384]{1,0:T(8,128)(2,1)S(1)} %get-tuple-element.309), channel_id=1, source_target_pairs={{0,2},{1,3},{2,0},{3,1},{4,6},{5,7},{6,4},{7,5},{8,10},{9,11},{10,... | collective-permute-start | bytes 884744 | tf_op jit(solution)/shard_map/ppermute | solution.py:1048
  217.6 15.1 %collective-permute-start.61 = (bf16[384,384]{1,0:T(8,128)(2,1)S(1)}, bf16[384,384]{1,0:T(8,128)(2,1)S(1)}, u32[]{:S(2)}, u32[]{:S(2)}) collective-permute-start(bf16[384,384]{1,0:T(8,128)(2,1)S(1)} %get-tuple-element.317), channel_id=1, source_target_pairs={{0,8},{8,0},{16,24},{24,16},{1,9},{9,1},{17,25},{25,17},{2,10},{10... | collective-permute-start | bytes 884744 | tf_op jit(solution)/shard_map/ppermute | solution.py:1048
  218.8 14.4 %collective-permute-start.62 = (bf16[384,384]{1,0:T(8,128)(2,1)S(1)}, bf16[384,384]{1,0:T(8,128)(2,1)S(1)}, u32[]{:S(2)}, u32[]{:S(2)}) collective-permute-start(bf16[384,384]{1,0:T(8,128)(2,1)S(1)} %get-tuple-element.318), channel_id=1, source_target_pairs={{0,16},{8,24},{16,0},{24,8},{1,17},{9,25},{17,1},{25,9},{2,18},{10... | collective-permute-start | bytes 884744 | tf_op jit(solution)/shard_map/ppermute | solution.py:1048
  219.7 13.5 %collective-permute-start.63 = (bf16[384,384]{1,0:T(8,128)(2,1)S(1)}, bf16[384,384]{1,0:T(8,128)(2,1)S(1)}, u32[]{:S(2)}, u32[]{:S(2)}) collective-permute-start(bf16[384,384]{1,0:T(8,128)(2,1)S(1)} %get-tuple-element.319), channel_id=1, source_target_pairs={{0,24},{8,16},{16,8},{24,0},{1,25},{9,17},{17,9},{25,1},{2,26},{10... | collective-permute-start | bytes 884744 | tf_op jit(solution)/shard_map/ppermute | solution.py:1048
  242.0 11.8 %collective-permute-start.66 = (bf16[112,768]{1,0:T(8,128)(2,1)S(1)}, bf16[112,768]{1,0:T(8,128)(2,1)S(1)}, u32[]{:S(2)}, u32[]{:S(2)}) collective-permute-start(bf16[112,768]{1,0:T(8,128)(2,1)S(1)} %get-tuple-element.338), channel_id=1, source_target_pairs={{0,2},{1,3},{2,0},{3,1},{4,6},{5,7},{6,4},{7,5},{8,10},{9,11},{10,... | collective-permute-start | bytes 516104 | tf_op jit(solution)/shard_map/ppermute | solution.py:1048
  242.3 22.8 %collective-permute-start.71 = (bf16[384,384]{1,0:T(8,128)(2,1)S(1)}, bf16[384,384]{1,0:T(8,128)(2,1)S(1)}, u32[]{:S(2)}, u32[]{:S(2)}) collective-permute-start(bf16[384,384]{1,0:T(8,128)(2,1)S(1)} %get-tuple-element.351), channel_id=1, source_target_pairs={{0,1},{1,0},{2,3},{3,2},{4,5},{5,4},{6,7},{7,6},{8,9},{9,8},{10,11... | collective-permute-start | bytes 884744 | tf_op jit(solution)/shard_map/ppermute | solution.py:1048
  244.2 18.0 %collective-permute-start.67 = (bf16[112,768]{1,0:T(8,128)(2,1)S(1)}, bf16[112,768]{1,0:T(8,128)(2,1)S(1)}, u32[]{:S(2)}, u32[]{:S(2)}) collective-permute-start(bf16[112,768]{1,0:T(8,128)(2,1)S(1)} %get-tuple-element.339), channel_id=1, source_target_pairs={{0,3},{1,2},{2,1},{3,0},{4,7},{5,6},{6,5},{7,4},{8,11},{9,10},{10,... | collective-permute-start | bytes 516104 | tf_op jit(solution)/shard_map/ppermute | solution.py:1048
  246.4 25.4 %collective-permute-start.68 = (bf16[256,768]{1,0:T(8,128)(2,1)S(1)}, bf16[256,768]{1,0:T(8,128)(2,1)S(1)}, u32[]{:S(2)}, u32[]{:S(2)}) collective-permute-start(bf16[256,768]{1,0:T(8,128)(2,1)S(1)} %get-tuple-element.345), channel_id=1, source_target_pairs={{0,8},{8,0},{16,24},{24,16},{1,9},{9,1},{17,25},{25,17},{2,10},{10... | collective-permute-start | bytes 1179656 | tf_op jit(solution)/shard_map/ppermute | solution.py:1048
  249.9 22.9 %collective-permute-start.69 = (bf16[256,768]{1,0:T(8,128)(2,1)S(1)}, bf16[256,768]{1,0:T(8,128)(2,1)S(1)}, u32[]{:S(2)}, u32[]{:S(2)}) collective-permute-start(bf16[256,768]{1,0:T(8,128)(2,1)S(1)} %get-tuple-element.346), channel_id=1, source_target_pairs={{0,16},{8,24},{16,0},{24,8},{1,17},{9,25},{17,1},{25,9},{2,18},{10... | collective-permute-start | bytes 1179656 | tf_op jit(solution)/shard_map/ppermute | solution.py:1048
  253.8 20.0 %collective-permute-start.70 = (bf16[256,768]{1,0:T(8,128)(2,1)S(1)}, bf16[256,768]{1,0:T(8,128)(2,1)S(1)}, u32[]{:S(2)}, u32[]{:S(2)}) collective-permute-start(bf16[256,768]{1,0:T(8,128)(2,1)S(1)} %get-tuple-element.347), channel_id=1, source_target_pairs={{0,24},{8,16},{16,8},{24,0},{1,25},{9,17},{17,9},{25,1},{2,26},{10... | collective-permute-start | bytes 1179656 | tf_op jit(solution)/shard_map/ppermute | solution.py:1048
  262.2 12.4 %collective-permute-start.72 = (bf16[384,384]{1,0:T(8,128)(2,1)S(1)}, bf16[384,384]{1,0:T(8,128)(2,1)S(1)}, u32[]{:S(2)}, u32[]{:S(2)}) collective-permute-start(bf16[384,384]{1,0:T(8,128)(2,1)S(1)} %get-tuple-element.353), channel_id=1, source_target_pairs={{0,3},{1,2},{2,1},{3,0},{4,7},{5,6},{6,5},{7,4},{8,11},{9,10},{10,... | collective-permute-start | bytes 884744 | tf_op jit(solution)/shard_map/ppermute | solution.py:1048
  274.6 18.3 %collective-permute-start.73 = (f32[128,768]{1,0:T(8,128)S(1)}, f32[128,768]{1,0:T(8,128)S(1)}, u32[]{:S(2)}, u32[]{:S(2)}) collective-permute-start(f32[128,768]{1,0:T(8,128)S(1)} %get-tuple-element.355), channel_id=1, source_target_pairs={{0,4},{4,0},{1,5},{5,1},{2,6},{6,2},{3,7},{7,3},{8,12},{12,8},{9,1... | collective-permute-start | bytes 1179656 | tf_op jit(solution)/shard_map/ppermute | solution.py:1048
  278.5 13.8 %collective-permute-start.82 = (bf16[384,384]{1,0:T(8,128)(2,1)S(1)}, bf16[384,384]{1,0:T(8,128)(2,1)S(1)}, u32[]{:S(2)}, u32[]{:S(2)}) collective-permute-start(bf16[384,384]{1,0:T(8,128)(2,1)S(1)} %late_sum.1.refs_0_), channel_id=1, source_target_pairs={{0,16},{8,24},{16,0},{24,8},{1,17},{9,25},{17,1},{25,9},{2,18},{10... | collective-permute-start | bytes 884744 | tf_op jit(solution)/shard_map/ppermute | solution.py:1048
  279.5 12.9 %collective-permute-start.81 = (bf16[384,384]{1,0:T(8,128)(2,1)S(1)}, bf16[384,384]{1,0:T(8,128)(2,1)S(1)}, u32[]{:S(2)}, u32[]{:S(2)}) collective-permute-start(bf16[384,384]{1,0:T(8,128)(2,1)S(1)} %late_sum.1.refs_0_), channel_id=1, source_target_pairs={{0,8},{8,0},{16,24},{24,16},{1,9},{9,1},{17,25},{25,17},{2,10},{10... | collective-permute-start | bytes 884744 | tf_op jit(solution)/shard_map/ppermute | solution.py:1048
  282.0 12.5 %collective-permute-start.78 = (bf16[112,768]{1,0:T(8,128)(2,1)S(1)}, bf16[112,768]{1,0:T(8,128)(2,1)S(1)}, u32[]{:S(2)}, u32[]{:S(2)}) collective-permute-start(bf16[112,768]{1,0:T(8,128)(2,1)S(1)} %collective-permute-done.74.refs_1_), channel_id=1, source_target_pairs={{0,4},{4,0},{1,5},{5,1},{2,6},{6,2},{3,7},{7,3},{8,12},{12,8},{9,1... | collective-permute-start | bytes 516104 | tf_op jit(solution)/shard_map/ppermute | solution.py:1048
  286.7 11.4 %collective-permute-start.84 = (bf16[384,384]{1,0:T(8,128)(2,1)S(1)}, bf16[384,384]{1,0:T(8,128)(2,1)}, u32[]{:S(2)}, u32[]{:S(2)}) collective-permute-start(bf16[384,384]{1,0:T(8,128)(2,1)S(1)} %late_sum.1.refs_0_), channel_id=1, source_target_pairs={{0,4},{4,0},{1,5},{5,1},{2,6},{6,2},{3,7},{7,3},{8,12},{12,8},{9,1... | collective-permute-start | bytes 884744 | tf_op jit(solution)/shard_map/ppermute | solution.py:1048
  (53 other events, 379.9 us)
